TPU v7x, 128 devices: a whole 4x4x4 slice. The times are simulated.
128 devices in a mesh: dp: 4 (over x), expert: 32 (over z, y, core).
Axes of the slice: x: 4, y: 4, z: 4, core: 2. Of those that a mesh axis runs over, the one named last changes fastest.
Arguments:
- tokens: bfloat16 [16384, 2048], P(('dp', 'expert')), may hold values from -6 to 6
- out_grad: bfloat16 [16384, 2048], P(('dp', 'expert')), may hold values from -6 to 6
- expert_ids: int32 [16384, 8], P(('dp', 'expert')), may hold values from 0 to 63, all different within a row
- route_probs: bfloat16 [16384, 8], P(('dp', 'expert')), may hold values from 0.019897461 to 0.5
- w_gate: bfloat16 [64, 2048, 768], P('expert'), may hold values from -0.125 to 0.125
- w_up: bfloat16 [64, 2048, 768], P('expert'), may hold values from -0.125 to 0.125
- w_down: bfloat16 [64, 2048, 768], P('expert'), may hold values from -0.21875 to 0.21875
- decay_mask: int32 [64, 3], P('expert'), may hold values from 0 to 1
Outputs:
- grad_tokens: bfloat16 [16384, 2048], P(('dp', 'expert'))
- grad_probs: bfloat16 [16384, 8], P(('dp', 'expert'))
- new_gate: bfloat16 [64, 2048, 768], P('expert', 'dp')
- new_up: bfloat16 [64, 2048, 768], P('expert', 'dp')
- new_down: bfloat16 [64, 2048, 768], P('expert', 'dp')
All inputs are finite; a program needn't handle non-finite values.
Results may differ from a plain program's by a relative error of at most 0.015.
Values may be sent and summed in bfloat16 or wider, within the bound.
No kernel may reach another device: no remote copies, remote signals or barrier semaphores. Data moves between devices by JAX's collectives and lax.ppermute only.
A program may use at most 192 MiB of HBM per device.

v0:
```python
import jax
import jax.numpy as jnp
from jax import lax
from jax.sharding import PartitionSpec as P

step_size = 0.004
shrink_rate = 0.1


def body(tokens, out_grad, expert_ids, route_probs, w_gate, w_up, w_down, decay_mask):
    n_owner = lax.axis_size("expert")
    n_group = lax.axis_size("dp")
    local_exp = w_gate.shape[0]
    width = tokens.shape[1]
    hidden = w_gate.shape[2]
    tok_rows = tokens.shape[0]
    topk = expert_ids.shape[1]
    n_experts = n_owner * local_exp
    capacity = tok_rows * topk // n_experts
    assigns = tok_rows * topk
    flat_ids = expert_ids.reshape(assigns)
    onehot = (flat_ids[:, None] == jnp.arange(n_experts, dtype=jnp.int32)[None, :]).astype(
        jnp.int32
    )
    before = jnp.cumsum(onehot, axis=0) - onehot
    position = jnp.sum(before * onehot, axis=1)
    slots = jnp.where(position < capacity, flat_ids * capacity + position, n_experts * capacity)
    order = jnp.arange(assigns, dtype=jnp.int32)
    slot_token = (
        jnp.full((n_experts * capacity + 1,), tok_rows, jnp.int32).at[slots].set(order // topk)[:-1]
    )
    slot_assign = (
        jnp.full((n_experts * capacity + 1,), assigns, jnp.int32).at[slots].set(order)[:-1]
    )
    zero_row = jnp.zeros((1, width), jnp.bfloat16)
    tok_pad = jnp.concatenate([tokens, zero_row], axis=0)
    grad_pad = jnp.concatenate([out_grad, zero_row], axis=0)
    prob_pad = jnp.concatenate(
        [route_probs.reshape(assigns), jnp.zeros((1,), jnp.bfloat16)], axis=0
    )
    send_x = tok_pad[slot_token].reshape(n_owner, local_exp * capacity, width)
    send_dy = grad_pad[slot_token].reshape(n_owner, local_exp * capacity, width)
    send_p = prob_pad[slot_assign].reshape(n_owner, local_exp * capacity)
    got_x, got_dy, got_p = (
        lax.all_to_all(send_x, "expert", split_axis=0, concat_axis=0, tiled=True),
        lax.all_to_all(send_dy, "expert", split_axis=0, concat_axis=0, tiled=True),
        lax.all_to_all(send_p, "expert", split_axis=0, concat_axis=0, tiled=True),
    )
    rows_x = got_x.reshape(n_owner, local_exp, capacity, width)
    rows_dy = got_dy.reshape(n_owner, local_exp, capacity, width)
    rows_p = got_p.reshape(n_owner, local_exp, capacity)
    gate = jnp.einsum("sjcd,jdh->sjch", rows_x, w_gate, preferred_element_type=jnp.float32)
    upper = jnp.einsum("sjcd,jdh->sjch", rows_x, w_up, preferred_element_type=jnp.float32)
    sig = jax.nn.sigmoid(gate)
    act = gate * sig
    hid = (act * upper).astype(jnp.bfloat16)
    outs = jnp.einsum("sjch,jdh->sjcd", hid, w_down, preferred_element_type=jnp.float32).astype(
        jnp.bfloat16
    )
    dout = (rows_p[..., None].astype(jnp.float32) * rows_dy.astype(jnp.float32)).astype(
        jnp.bfloat16
    )
    dhid = jnp.einsum("sjcd,jdh->sjch", dout, w_down, preferred_element_type=jnp.float32)
    dgate = (dhid * upper * sig * (1.0 + gate * (1.0 - sig))).astype(jnp.bfloat16)
    dup = (dhid * act).astype(jnp.bfloat16)
    dx_slots = (
        jnp.einsum("sjch,jdh->sjcd", dgate, w_gate, preferred_element_type=jnp.float32)
        + jnp.einsum("sjch,jdh->sjcd", dup, w_up, preferred_element_type=jnp.float32)
    ).astype(jnp.bfloat16)
    dx_send = dx_slots.reshape(n_owner, local_exp * capacity, width)
    back_out = lax.all_to_all(
        outs.reshape(n_owner, local_exp * capacity, width),
        "expert",
        split_axis=0,
        concat_axis=0,
        tiled=True,
    )
    out_pad = jnp.concatenate([back_out.reshape(n_experts * capacity, width), zero_row], axis=0)
    routed_out = out_pad[slots].reshape(tok_rows, topk, width)
    grad_probs = jnp.einsum(
        "tkd,td->tk", routed_out, out_grad, preferred_element_type=jnp.float32
    ).astype(jnp.bfloat16)
    back_dx = lax.all_to_all(dx_send, "expert", split_axis=0, concat_axis=0, tiled=True)
    dx_pad = jnp.concatenate([back_dx.reshape(n_experts * capacity, width), zero_row], axis=0)
    routed_dx = dx_pad[slots].reshape(tok_rows, topk, width)
    grad_tokens = jnp.sum(routed_dx.astype(jnp.float32), axis=1).astype(jnp.bfloat16)
    shard_rows = width // n_group
    grad_g = jnp.einsum("sjcd,sjch->djh", rows_x, dgate, preferred_element_type=jnp.float32)
    grad_u = jnp.einsum("sjcd,sjch->djh", rows_x, dup, preferred_element_type=jnp.float32)
    grad_d = jnp.einsum("sjcd,sjch->djh", dout, hid, preferred_element_type=jnp.float32)
    stacked = jnp.stack([grad_g, grad_u, grad_d], axis=1)
    summed = lax.psum_scatter(
        stacked.reshape(shard_rows * lax.axis_size("dp"), 3 * local_exp * hidden).astype(
            jnp.bfloat16
        ),
        "dp",
        scatter_dimension=0,
        tiled=True,
    ).astype(jnp.float32)
    grads = summed.reshape(shard_rows, 3, local_exp, hidden).transpose(1, 2, 0, 3)
    first_row = lax.axis_index("dp") * shard_rows
    rates = decay_mask.astype(jnp.float32)

    def update(weight, grad_w, column):
        weight_f = lax.dynamic_slice_in_dim(weight, first_row, shard_rows, 1).astype(jnp.float32)
        factor = rates[:, column][:, None, None]
        return (weight_f - step_size * grad_w - shrink_rate * factor * weight_f).astype(
            jnp.bfloat16
        )

    new_gate = update(w_gate, grads[0], 0)
    new_up = update(w_up, grads[1], 1)
    new_down = update(w_down, grads[2], 2)
    return (grad_tokens, grad_probs, new_gate, new_up, new_down)


def solution(mesh):
    placed = (
        P(("dp", "expert"), None),
        P(("dp", "expert"), None),
        P(("dp", "expert"), None),
        P(("dp", "expert"), None),
        P("expert", None, None),
        P("expert", None, None),
        P("expert", None, None),
        P("expert", None),
    )
    return jax.shard_map(
        body,
        mesh=mesh,
        in_specs=placed,
        out_specs=(
            P(("dp", "expert"), None),
            P(("dp", "expert"), None),
            P("expert", "dp", None),
            P("expert", "dp", None),
            P("expert", "dp", None),
        ),
        check_vma=False,
    )
```

profile of v0, /device:TPU:0, one launch (start us, length us, event | category | flops | bytes accessed | tf_op | source)
XLA Modules:
  0.0 418.4 jit_solution(10301693080132725727)
XLA Ops:
  7.2 0.8 copy.87
  8.0 0.1 eq.29
  8.1 0.1 eq.25
  8.2 0.7 broadcast_multiply_fusion
  8.9 18.0 %reduce-window.6 = s32[64,8,128]{2,1,0:T(8,128)S(1)} reduce-window(s32[64,8,128]{2,1,0:T(8,128)S(1)} %fusion.51, s32[]{:T(128)} %constant.21.clone.1), window={size=1x1x128 pad=0_0x0_0x127_0}, to_apply=%region_0.0 | reduce-window | flops 8323072 | bytes 524292 | tf_op jit(solution)/shard_map/reduce-window
  26.9 0.1 slice.50
  27.1 0.1 copy.89
  27.3 0.1 copy.90
  27.3 0.1 broadcast_add_fusion
  27.5 0.1 copy.91
  27.6 0.1 mul.125
  27.7 0.8 copy.86
  28.5 0.1 reshape.148
  28.6 0.1 fusion.50
  28.7 4.3 %scatter_custom_fusion = s32[1025]{0:T(1024)S(1)} fusion(s32[1024]{0:T(1024)S(1)} %bitcast.174, s32[1024]{0:T(1024)S(1)} %iota.13, s32[]{:T(128)} %constant.16.clone.1), kind=kCustom, calls=%fused_computation.99 | custom fusion | bytes 4104 | tf_op jit(solution)/shard_map/scatter | solution.py:33
  33.1 6.8 %gather_fusion = bf16[1024]{0:T(1024)(128)(2,1)S(1)} fusion(bf16[1025]{0:T(1024)(128)(2,1)S(1)} %pad_maximum_fusion.1, s32[1024]{0:T(1024)S(1)} %fusion.54), kind=kCustom, calls=%fused_computation | custom fusion | bytes 8192 | tf_op jit(solution)/shard_map/gather | solution.py:43
  39.9 0.7 all_to_all.24
  40.5 8.4 %all-to-all-start = ((bf16[32,1,32]{2,1,0:T(2,128)(2,1)}), bf16[32,1,32]{2,1,0:T(2,128)(2,1)S(1)}, u32[]{:S(2)}, u32[]{:S(2)}) async-start(bf16[32,1,32]{2,1,0:T(2,128)(2,1)} %all_to_all.24), calls=%async_computation | async-start | bytes 32768 | tf_op jit(solution)/shard_map/all_to_all | solution.py:47
  49.0 4.3 %scatter_custom_fusion.1 = s32[1025]{0:T(1024)S(1)} fusion(s32[1024]{0:T(1024)S(1)} %bitcast.175, s32[1024]{0:T(1024)S(1)} %add_select_fusion, s32[]{:T(128)} %constant.44.clone.1), kind=kCustom, calls=%fused_computation.97 | custom fusion | bytes 4104 | tf_op jit(solution)/shard_map/scatter | solution.py:30
  53.4 6.1 %gather_fusion.2 = bf16[1024,2048]{1,0:T(8,128)(2,1)} fusion(bf16[129,2048]{1,0:T(8,128)(2,1)S(1)} %concatenate.17, s32[1024]{0:T(1024)S(1)} %fusion.55), kind=kCustom, calls=%fused_computation.2 | custom fusion | bytes 8392704 | tf_op jit(solution)/shard_map/gather | solution.py:41
  59.5 7.6 %all-to-all-start.2 = ((bf16[32,32,2048]{2,1,0:T(8,128)(2,1)}), bf16[32,32,2048]{2,1,0:T(8,128)(2,1)}, u32[]{:S(2)}, u32[]{:S(2)}) async-start(bf16[32,32,2048]{2,1,0:T(8,128)(2,1)} %bitcast.161), calls=%async_computation.2 | async-start | bytes 8388608 | tf_op jit(solution)/shard_map/all_to_all | solution.py:45
  67.2 6.0 %gather_fusion.1 = bf16[1024,2048]{1,0:T(8,128)(2,1)} fusion(bf16[129,2048]{1,0:T(8,128)(2,1)S(1)} %concatenate.16, s32[1024]{0:T(1024)S(1)} %fusion.55), kind=kCustom, calls=%fused_computation.1 | custom fusion | bytes 8392704 | tf_op jit(solution)/shard_map/gather | solution.py:42
  73.3 47.4 %all-to-all-done.2 = bf16[32,32,2048]{2,1,0:T(8,128)(2,1)} async-done(((bf16[32,32,2048]{2,1,0:T(8,128)(2,1)}), bf16[32,32,2048]{2,1,0:T(8,128)(2,1)}, u32[]{:S(2)}, u32[]{:S(2)}) %all-to-all-start.2) | async-done | bytes 4194336 | tf_op jit(solution)/shard_map/all_to_all | solution.py:45
  120.6 4.9 %all-to-all-start.1 = ((bf16[32,32,2048]{2,1,0:T(8,128)(2,1)}), bf16[32,32,2048]{2,1,0:T(8,128)(2,1)}, u32[]{:S(2)}, u32[]{:S(2)}) async-start(bf16[32,32,2048]{2,1,0:T(8,128)(2,1)} %bitcast.160), calls=%async_computation.1 | async-start | bytes 8388608 | tf_op jit(solution)/shard_map/all_to_all | solution.py:46
  125.5 0.0 reduce-scatter.2.cloned.1.call-start
  125.5 0.1 copy.93
  125.6 0.1 copy.94
  125.7 9.2 %fusion.6 = f32[2,32,16,768]{3,2,1,0:T(8,128)} fusion(bf16[2,2048,768]{2,1,0:T(8,128)(2,1)} %param.12, bf16[32,2,16,2048]{3,2,1,0:T(8,128)(2,1)} %bitcast.11), kind=kOutput, calls=%fused_computation.20 | convolution fusion | flops 3221225472 | bytes 13631488 | tf_op jit(solution)/shard_map/sjcd,jdh->sjch/dot_general | solution.py:52
  135.0 44.0 %all-to-all-done.1 = bf16[32,32,2048]{2,1,0:T(8,128)(2,1)} async-done(((bf16[32,32,2048]{2,1,0:T(8,128)(2,1)}), bf16[32,32,2048]{2,1,0:T(8,128)(2,1)}, u32[]{:S(2)}, u32[]{:S(2)}) %all-to-all-start.1) | async-done | bytes 4194336 | tf_op jit(solution)/shard_map/all_to_all | solution.py:46
  179.0 7.4 %fusion.10 = f32[2,32,16,768]{3,2,1,0:T(8,128)S(1)} fusion(bf16[2,2048,768]{2,1,0:T(8,128)(2,1)} %param.14, bf16[32,2,16,2048]{3,2,1,0:T(8,128)(2,1)} %bitcast.50, f32[32,2,16]{2,1,0:T(2,128)S(1)} %copy.94), kind=kOutput, calls=%fused_computation.24 | convolution fusion | flops 3227516928 | bytes 13635584 | tf_op jit(solution)/shard_map/sjcd,jdh->sjch/dot_general | solution.py:63
  186.4 7.9 %fusion.41 = (bf16[32,2,16,768]{3,2,0,1:T(8,128)(2,1)S(1)}, bf16[32,2,16,768]{3,2,0,1:T(8,128)(2,1)}, bf16[32,2,16,768]{3,2,0,1:T(8,128)(2,1)S(1)}) fusion(f32[2,32,16,768]{3,2,1,0:T(8,128)S(1)} %copy-done.12, f32[2,32,16,768]{3,2,1,0:T(8,128)S(1)} %fusion.10, bf16[2,2048,768]{2,1,0:T(8,128)(2,1)S(1)} %bitcast.168, bf16[32,2,16,2048]{3,2,1,0:T(8,128)(2,1)} %bitcast.11), kind=kOutput, calls=%fused_computation.67 | convolution fusion | flops 3233021952 | bytes 21495808 | tf_op jit(solution)/shard_map/sjcd,jdh->sjch/dot_general | solution.py:53
  194.3 7.2 %fusion.3 = bf16[2048,1,2,768]{0,3,2,1:T(8,128)(2,1)S(1)} fusion(bf16[32,2,16,768]{3,2,0,1:T(8,128)(2,1)S(1)} %get-tuple-element.31, bf16[32,2,16,2048]{3,2,1,0:T(8,128)(2,1)} %bitcast.50, f32[32,2,16]{2,1,0:T(2,128)S(1)} %copy.94), kind=kOutput, calls=%fused_computation.17 | convolution fusion | flops 3230662656 | bytes 12062720 | tf_op jit(solution)/shard_map/sjcd,sjch->djh/dot_general | solution.py:90
  201.6 6.0 %fusion.2 = bf16[2048,1,2,768]{0,3,2,1:T(8,128)(2,1)S(1)} fusion(bf16[32,2,16,768]{3,2,0,1:T(8,128)(2,1)S(1)} %get-tuple-element.33, bf16[32,2,16,2048]{3,2,1,0:T(8,128)(2,1)} %bitcast.11), kind=kOutput, calls=%fused_computation.16 | convolution fusion | flops 3224371200 | bytes 12058624 | tf_op jit(solution)/shard_map/sjcd,sjch->djh/dot_general | solution.py:89
  207.6 5.9 %fusion.1 = bf16[2048,1,2,768]{0,3,2,1:T(8,128)(2,1)S(1)} fusion(bf16[32,2,16,768]{3,2,0,1:T(8,128)(2,1)S(1)} %copy-done.9, bf16[32,2,16,2048]{3,2,1,0:T(8,128)(2,1)} %bitcast.11), kind=kOutput, calls=%fused_computation.15 | convolution fusion | flops 3224371200 | bytes 12058624 | tf_op jit(solution)/shard_map/sjcd,sjch->djh/dot_general | solution.py:88
  213.6 8.5 %pad_maximum_fusion = bf16[2048,3,2,768]{0,3,2,1:T(8,128)(2,1)} fusion(bf16[2048,1,2,768]{0,3,2,1:T(8,128)(2,1)S(1)} %fusion.3, bf16[2048,1,2,768]{0,3,2,1:T(8,128)(2,1)S(1)} %fusion.2, bf16[2048,1,2,768]{0,3,2,1:T(8,128)(2,1)S(1)} %fusion.1), kind=kLoop, calls=%fused_computation.7 | loop fusion | flops 18874368 | bytes 37748736 | tf_op jit(solution)/shard_map/stack | solution.py:91
  222.1 0.0 reduce-scatter.2.cloned.1.call-update
  222.1 10.2 %fusion.4 = f32[2,32,16,2048]{3,2,1,0:T(8,128)} fusion(bf16[32,2,16,768]{3,2,0,1:T(8,128)(2,1)} %get-tuple-element.32, bf16[2,2048,768]{2,1,0:T(8,128)(2,1)} %param.12), kind=kOutput, calls=%fused_computation.18 | convolution fusion | flops 3221225472 | bytes 16252928 | tf_op jit(solution)/shard_map/sjch,jdh->sjcd/dot_general | solution.py:67
  232.3 6.4 %fusion.16 = bf16[32,2,16,2048]{3,2,0,1:T(8,128)(2,1)S(1)} fusion(f32[2,32,16,2048]{3,2,1,0:T(8,128)} %fusion.4, bf16[32,2,16,768]{3,2,0,1:T(8,128)(2,1)} %copy-done.8, bf16[2,2048,768]{2,1,0:T(8,128)(2,1)S(1)} %bitcast.170), kind=kOutput, calls=%fused_computation.30 | convolution fusion | flops 3225419776 | bytes 20447232 | tf_op jit(solution)/shard_map/sjch,jdh->sjcd/dot_general | solution.py:68
  238.7 2.6 copy.98
  241.2 5.0 %all-to-all-start.3 = ((bf16[32,32,2048]{2,1,0:T(8,128)(2,1)}), bf16[32,32,2048]{2,1,0:T(8,128)(2,1)}, u32[]{:S(2)}, u32[]{:S(2)}) async-start(bf16[32,32,2048]{2,1,0:T(8,128)(2,1)} %bitcast.163), calls=%async_computation.3 | async-start | bytes 8388608 | tf_op jit(solution)/shard_map/all_to_all | solution.py:83
  246.2 6.6 %convert_bitcast_fusion.1 = bf16[32,2,16,2048]{3,2,0,1:T(8,128)(2,1)S(1)} fusion(bf16[32,2,16,768]{3,2,0,1:T(8,128)(2,1)S(1)} %copy-done.11, bf16[2,2048,768]{2,1,0:T(8,128)(2,1)} %param.14), kind=kOutput, calls=%fused_computation.34 | convolution fusion | flops 3223322624 | bytes 12058624 | tf_op jit(solution)/shard_map/sjch,jdh->sjcd/dot_general | solution.py:57
  252.8 2.3 copy.99
  255.1 44.6 %all-to-all-done.3 = bf16[32,32,2048]{2,1,0:T(8,128)(2,1)} async-done(((bf16[32,32,2048]{2,1,0:T(8,128)(2,1)}), bf16[32,32,2048]{2,1,0:T(8,128)(2,1)}, u32[]{:S(2)}, u32[]{:S(2)}) %all-to-all-start.3) | async-done | bytes 4194336 | tf_op jit(solution)/shard_map/all_to_all | solution.py:83
  299.7 5.1 %all-to-all-start.4 = ((bf16[32,32,2048]{2,1,0:T(8,128)(2,1)}), bf16[32,32,2048]{2,1,0:T(8,128)(2,1)}, u32[]{:S(2)}, u32[]{:S(2)}) async-start(bf16[32,32,2048]{2,1,0:T(8,128)(2,1)} %bitcast.162), calls=%async_computation.4 | async-start | bytes 8388608 | tf_op jit(solution)/shard_map/all_to_all | solution.py:71
  304.9 1.6 constant_dynamic-slice_fusion.2
  306.4 0.7 copy.119
  307.2 2.9 constant_dynamic-slice_fusion
  310.0 1.7 copy.118
  311.8 2.7 constant_dynamic-slice_fusion.1
  314.4 2.6 copy.117
  317.0 0.2 multiply_reduce_fusion
  317.3 4.9 %concatenate.18 = bf16[1025,2048]{1,0:T(8,128)(2,1)} pad(bf16[1024,2048]{1,0:T(8,128)(2,1)} %bitcast.21, bf16[]{:T(256)} %constant.18.clone.1), padding=0_1x0_0 | pad | bytes 8392706 | tf_op jit(solution)/shard_map/concatenate | solution.py:84
  322.2 36.1 %all-to-all-done.4 = bf16[32,32,2048]{2,1,0:T(8,128)(2,1)} async-done(((bf16[32,32,2048]{2,1,0:T(8,128)(2,1)}), bf16[32,32,2048]{2,1,0:T(8,128)(2,1)}, u32[]{:S(2)}, u32[]{:S(2)}) %all-to-all-start.4) | async-done | bytes 4194336 | tf_op jit(solution)/shard_map/all_to_all | solution.py:71
  358.3 4.8 %concatenate.19 = bf16[1025,2048]{1,0:T(8,128)(2,1)} pad(bf16[1024,2048]{1,0:T(8,128)(2,1)} %bitcast.26, bf16[]{:T(256)} %constant.18.clone.1), padding=0_1x0_0 | pad | bytes 8392706 | tf_op jit(solution)/shard_map/concatenate | solution.py:78
  363.1 11.6 %gather_fusion.3 = bf16[1024,2048]{1,0:T(8,128)(2,1)} fusion(bf16[1025,2048]{1,0:T(8,128)(2,1)} %concatenate.18, s32[1024]{0:T(1024)S(1)} %broadcast_clamp_fusion), kind=kCustom, calls=%fused_computation.3 | custom fusion | bytes 8392704 | tf_op jit(solution)/shard_map/gather | solution.py:85
  374.7 11.6 %gather_fusion.4 = bf16[1024,2048]{1,0:T(8,128)(2,1)} fusion(bf16[1025,2048]{1,0:T(8,128)(2,1)} %concatenate.19, s32[1024]{0:T(1024)S(1)} %broadcast_clamp_fusion), kind=kCustom, calls=%fused_computation.4 | custom fusion | bytes 8392704 | tf_op jit(solution)/shard_map/gather | solution.py:79
  386.3 5.1 %fusion.17 = bf16[128,1,8]{2,1,0:T(2,128)(2,1)S(1)} fusion(bf16[1024,2048]{1,0:T(8,128)(2,1)} %gather_fusion.4, bf16[128,2048,1]{1,0,2:T(8,128)(2,1)} %bitcast.166), kind=kOutput, calls=%fused_computation.31 | convolution fusion | flops 4194304 | bytes 4720640 | tf_op jit(solution)/shard_map/tkd,td->tk/dot_general | solution.py:80
  391.3 0.7 copy.113
  392.0 5.9 %bitcast_reduce_fusion = bf16[128,2048]{1,0:T(8,128)(2,1)} fusion(bf16[1024,2048]{1,0:T(8,128)(2,1)} %gather_fusion.3), kind=kLoop, calls=%fused_computation.33 | loop fusion | flops 1835008 | bytes 4718592 | tf_op jit(solution)/shard_map/reduce_sum | solution.py:86
  397.9 3.8 convert_bitcast_fusion
  401.7 3.6 fusion.30
  405.2 2.7 copy.106
  408.0 1.6 copy.107
  409.5 1.6 copy.108
  (51 shorter events, 0.3 us)
Async XLA Ops:
  7.2 46.2 %copy-start.3 = (bf16[128,2048]{1,0:T(8,128)(2,1)S(1)}, bf16[128,2048]{1,0:T(8,128)(2,1)}, u32[]{:S(2)}) copy-start(bf16[128,2048]{1,0:T(8,128)(2,1)} %param.8) | copy-start | bytes 1572868
  28.7 24.6 %copy-start.5 = (s32[1024,1]{0,1:T(1,128)}, s32[1024,1]{0,1:T(1,128)S(1)}, u32[]{:S(2)}) copy-start(s32[1024,1]{0,1:T(1,128)S(1)} %compare_select_fusion) | copy-start | bytes 12292
  40.5 18.9 %all-to-all-start = ((bf16[32,1,32]{2,1,0:T(2,128)(2,1)}), bf16[32,1,32]{2,1,0:T(2,128)(2,1)S(1)}, u32[]{:S(2)}, u32[]{:S(2)}) async-start(bf16[32,1,32]{2,1,0:T(2,128)(2,1)} %all_to_all.24), calls=%async_computation | async-start | bytes 32768 | tf_op jit(solution)/shard_map/all_to_all | solution.py:47
  59.5 7.7 %copy-start.4 = (bf16[128,2048]{1,0:T(8,128)(2,1)S(1)}, bf16[128,2048]{1,0:T(8,128)(2,1)}, u32[]{:S(2)}) copy-start(bf16[128,2048]{1,0:T(8,128)(2,1)} %param.9) | copy-start | bytes 1572868
  59.5 61.1 %all-to-all-start.2 = ((bf16[32,32,2048]{2,1,0:T(8,128)(2,1)}), bf16[32,32,2048]{2,1,0:T(8,128)(2,1)}, u32[]{:S(2)}, u32[]{:S(2)}) async-start(bf16[32,32,2048]{2,1,0:T(8,128)(2,1)} %bitcast.161), calls=%async_computation.2 | async-start | bytes 8388608 | tf_op jit(solution)/shard_map/all_to_all | solution.py:45
  120.6 58.3 %all-to-all-start.1 = ((bf16[32,32,2048]{2,1,0:T(8,128)(2,1)}), bf16[32,32,2048]{2,1,0:T(8,128)(2,1)}, u32[]{:S(2)}, u32[]{:S(2)}) async-start(bf16[32,32,2048]{2,1,0:T(8,128)(2,1)} %bitcast.160), calls=%async_computation.1 | async-start | bytes 8388608 | tf_op jit(solution)/shard_map/all_to_all | solution.py:46
  125.5 272.4 %reduce-scatter.2.cloned.1.call-start = ((), (), s32[]{:S(2)}) async-start(), calls=%async_computation.6 | async-start | bytes 23592960 | tf_op jit(solution)/shard_map/reduce_scatter | solution.py:92
  125.7 60.7 %slice-start = ((s8[6291456]{0:T(1024)(128)(4,1)}), s8[2097152]{0:T(1024)(128)(4,1)S(1)}, s32[]{:S(2)}) async-start(s8[6291456]{0:T(1024)(128)(4,1)} %bitcast.167), calls=%async_computation.7 | async-start | bytes 4194304
  179.0 7.4 %slice-start.1 = ((s8[6291456]{0:T(1024)(128)(4,1)}), s8[4194304]{0:T(1024)(128)(4,1)S(1)}, s32[]{:S(2)}) async-start(s8[6291456]{0:T(1024)(128)(4,1)} %bitcast.167), calls=%async_computation.8 | async-start | bytes 8388608
  179.0 7.4 %copy-start.12 = (f32[2,32,16,768]{3,2,1,0:T(8,128)S(1)}, f32[2,32,16,768]{3,2,1,0:T(8,128)}, u32[]{:S(2)}) copy-start(f32[2,32,16,768]{3,2,1,0:T(8,128)} %fusion.6) | copy-start | bytes 9437188
  194.3 7.3 %copy-start.10 = (bf16[32,2,16,768]{3,2,0,1:T(8,128)(2,1)}, bf16[32,2,16,768]{3,2,0,1:T(8,128)(2,1)S(1)}, u32[]{:S(2)}) copy-start(bf16[32,2,16,768]{3,2,0,1:T(8,128)(2,1)S(1)} %get-tuple-element.31) | copy-start | bytes 4718596
  194.3 7.3 %copy-start.8 = (bf16[32,2,16,768]{3,2,0,1:T(8,128)(2,1)}, bf16[32,2,16,768]{3,2,0,1:T(8,128)(2,1)S(1)}, u32[]{:S(2)}) copy-start(bf16[32,2,16,768]{3,2,0,1:T(8,128)(2,1)S(1)} %get-tuple-element.33) | copy-start | bytes 4718596
  201.6 6.1 %copy-start.9 = (bf16[32,2,16,768]{3,2,0,1:T(8,128)(2,1)S(1)}, bf16[32,2,16,768]{3,2,0,1:T(8,128)(2,1)}, u32[]{:S(2)}) copy-start(bf16[32,2,16,768]{3,2,0,1:T(8,128)(2,1)} %get-tuple-element.32) | copy-start | bytes 4718596
  222.0 10.2 %slice-start.2 = ((s8[6291456]{0:T(1024)(128)(4,1)}), s8[2097152]{0:T(1024)(128)(4,1)S(1)}, s32[]{:S(2)}) async-start(s8[6291456]{0:T(1024)(128)(4,1)} %bitcast.169), calls=%async_computation.9 | async-start | bytes 4194304
  222.1 10.2 %slice-start.3 = ((s8[6291456]{0:T(1024)(128)(4,1)}), s8[4194304]{0:T(1024)(128)(4,1)S(1)}, s32[]{:S(2)}) async-start(s8[6291456]{0:T(1024)(128)(4,1)} %bitcast.169), calls=%async_computation.10 | async-start | bytes 8388608
  241.2 5.0 %copy-start.11 = (bf16[32,2,16,768]{3,2,0,1:T(8,128)(2,1)S(1)}, bf16[32,2,16,768]{3,2,0,1:T(8,128)(2,1)}, u32[]{:S(2)}) copy-start(bf16[32,2,16,768]{3,2,0,1:T(8,128)(2,1)} %copy-done.10) | copy-start | bytes 4718596
  241.2 58.5 %all-to-all-start.3 = ((bf16[32,32,2048]{2,1,0:T(8,128)(2,1)}), bf16[32,32,2048]{2,1,0:T(8,128)(2,1)}, u32[]{:S(2)}, u32[]{:S(2)}) async-start(bf16[32,32,2048]{2,1,0:T(8,128)(2,1)} %bitcast.163), calls=%async_computation.3 | async-start | bytes 8388608 | tf_op jit(solution)/shard_map/all_to_all | solution.py:83
  299.7 58.6 %all-to-all-start.4 = ((bf16[32,32,2048]{2,1,0:T(8,128)(2,1)}), bf16[32,32,2048]{2,1,0:T(8,128)(2,1)}, u32[]{:S(2)}, u32[]{:S(2)}) async-start(bf16[32,32,2048]{2,1,0:T(8,128)(2,1)} %bitcast.162), calls=%async_computation.4 | async-start | bytes 8388608 | tf_op jit(solution)/shard_map/all_to_all | solution.py:71
  304.8 2.3 copy-start.7
  310.0 7.2 %copy-start.6 = (s32[1024,1]{0,1:T(1,128)S(1)}, s32[1024,1]{0,1:T(1,128)}, u32[]{:S(2)}) copy-start(s32[1024,1]{0,1:T(1,128)} %copy-done.5) | copy-start | bytes 12292
  397.9 3.8 copy-start
  405.2 2.7 copy-start.2
  405.2 4.3 %copy-start.1 = (bf16[2,512,768]{1,2,0:T(8,128)(2,1)S(1)}, bf16[2,512,768]{1,2,0:T(8,128)(2,1)}, u32[]{:S(2)}) copy-start(bf16[2,512,768]{1,2,0:T(8,128)(2,1)} %get-tuple-element.28) | copy-start | bytes 4718596
Sparse Core Ops, SparseCore 0:
  222.2 161.6 reduce-scatter.1
where the time goes:
time: 426 us; the launch traced here: 418 us
  waiting for transfers between devices  172 us (40%)
  local copies, waits for them, and re-layouts  87.5 us (21%)
  matrix products  71.9 us (17%)
  other arithmetic  40.9 us (10%)
  starting transfers between devices  31.1 us (7%)
  between operations  14.9 us (3%)
    all_to_all x1, waiting for transfers between devices, body(): lax.all_to_all(send_x, 'expert', split_axis=0, concat_axis=0, tiled=True)  47.4 us
    all_to_all x1, waiting for transfers between devices, body(): lax.all_to_all(dx_send, 'expert', split_axis=0, concat_axis=0, tiled=True)  44.6 us
    all_to_all x1, waiting for transfers between devices, body(): lax.all_to_all(send_dy, 'expert', split_axis=0, concat_axis=0, tiled=True)  44 us
    all_to_all x1, waiting for transfers between devices, body(): lax.all_to_all(outs.reshape(n_owner, local_exp * capacity, width), 'exper...  36.1 us
    another operation x3, other arithmetic  18.2 us
    unnamed x42, local copies, waits for them, and re-layouts  12.6 us
    gather x1, local copies, waits for them, and re-layouts, body(): routed_dx = dx_pad[slots].reshape(tok_rows, topk, width)  11.6 us
    gather x1, local copies, waits for them, and re-layouts, body(): routed_out = out_pad[slots].reshape(tok_rows, topk, width)  11.6 us
  transfers between devices with their start and end apart: 6, of which 4 were waited for; matrix products, arithmetic and copies ran while one was open for 26% of the time, Pallas kernels for 0%

commit v1 on v0

v1 whole, which is shorter than its diff:
```python
import functools

import jax
import jax.numpy as jnp
from jax import lax
from jax.experimental import pallas as pl
from jax.experimental.pallas import tpu as pltpu
from jax.sharding import PartitionSpec as P

step_size = 0.004
shrink_rate = 0.1
LANES = 128
F32 = jnp.float32
BF16 = jnp.bfloat16
VMEM_LIMIT = 60 * 1024 * 1024


def dot(a, b, dims):
    return lax.dot_general(a, b, (dims, ((), ())), preferred_element_type=F32)


def cost(flops, moved):
    return pl.CostEstimate(flops=flops, transcendentals=0, bytes_accessed=moved)


NN = ((1,), (0,))
NT = ((1,), (1,))
TN = ((0,), (0,))


def slot_values(ids_t, n_experts, capacity):
    topk, tok = ids_t.shape
    rows = lax.broadcasted_iota(jnp.int32, (n_experts, tok), 0)
    hit = ids_t[0:1, :] == rows
    for k in range(1, topk):
        hit = jnp.logical_or(hit, ids_t[k : k + 1, :] == rows)
    hit_f = jnp.where(hit, 1.0, 0.0)
    earlier = lax.broadcasted_iota(jnp.int32, (tok, tok), 0) < lax.broadcasted_iota(
        jnp.int32, (tok, tok), 1
    )
    count = dot(hit_f.astype(BF16), jnp.where(earlier, 1.0, 0.0).astype(BF16), NN)
    return jnp.where(jnp.logical_and(hit, count < capacity), count, -1.0)


def slot_rows(values, chunk, local_exp, capacity):
    n_experts, tok = values.shape
    n_rows = n_experts // local_exp * capacity
    expert_of = lax.broadcasted_iota(jnp.int32, (n_rows, n_experts), 0) // capacity * local_exp + chunk
    spread = jnp.where(expert_of == lax.broadcasted_iota(jnp.int32, (n_rows, n_experts), 1), 1.0, 0.0)
    spread = spread.astype(BF16)
    at = dot(spread, values.astype(BF16), NN)
    place = (lax.broadcasted_iota(jnp.int32, (n_rows, tok), 0) % capacity).astype(F32)
    return at == place, spread


def dispatch_kernel(local_exp, capacity, ids_ref, probs_ref, tok_ref, grad_ref, *out_refs):
    ids_t = ids_ref[...]
    topk, tok = ids_t.shape
    n_experts = out_refs[0].shape[0] // capacity * local_exp
    width = tok_ref.shape[1]
    values = slot_values(ids_t, n_experts, capacity)
    rows = lax.broadcasted_iota(jnp.int32, (n_experts, tok), 0)
    prob = jnp.zeros((n_experts, tok), F32)
    for k in range(topk):
        prob = prob + jnp.where(ids_t[k : k + 1, :] == rows, probs_ref[k : k + 1, :].astype(F32), 0.0)
    for chunk, out_ref in enumerate(out_refs):
        onehot, spread = slot_rows(values, chunk, local_exp, capacity)
        prob_rows = dot(spread, prob.astype(BF16), NN)
        pick = jnp.where(onehot, 1.0, 0.0).astype(BF16)
        weighted = jnp.where(onehot, prob_rows, 0.0).astype(BF16)
        out_ref[:, :width] = dot(pick, tok_ref[...], NN).astype(BF16)
        out_ref[:, width:] = dot(weighted, grad_ref[...], NN).astype(BF16)


def dispatch(local_exp, capacity, n_experts, ids_t, probs_t, tokens, out_grad):
    tok, width = tokens.shape
    n_rows = n_experts // local_exp * capacity
    return pl.pallas_call(
        functools.partial(dispatch_kernel, local_exp, capacity),
        out_shape=[jax.ShapeDtypeStruct((n_rows, 2 * width), BF16)] * local_exp,
        compiler_params=pltpu.CompilerParams(vmem_limit_bytes=VMEM_LIMIT),
        cost_estimate=cost(4 * local_exp * n_rows * tok * width, 4 * width * (tok + local_exp * n_rows)),
        name="dispatch",
    )(ids_t, probs_t, tokens, out_grad)


def grads_kernel(x_ref, do_ref, wg_ref, wu_ref, wd_ref, g_ref, da_ref, db_ref, s_ref):
    x = x_ref[...]
    do = do_ref[...]
    gate = dot(x, wg_ref[0], NN)
    upper = dot(x, wu_ref[0], NN)
    sig = jax.nn.sigmoid(gate)
    act = gate * sig
    hid = (act * upper).astype(BF16)
    dhid = dot(do, wd_ref[0], NN)
    total = jnp.sum(hid.astype(F32) * dhid, axis=1, keepdims=True)
    high = total.astype(BF16).astype(F32)
    lane = lax.broadcasted_iota(jnp.int32, s_ref.shape, 1)
    s_ref[...] = jnp.where(lane == 0, high, jnp.where(lane == 1, total - high, 0.0)).astype(BF16)
    hidden = hid.shape[1]
    g_ref[:, 2 * hidden :] = dot(do, hid, TN).astype(BF16)
    dgate = (dhid * upper * sig * (1.0 + gate * (1.0 - sig))).astype(BF16)
    da_ref[...] = dgate
    g_ref[:, :hidden] = dot(x, dgate, TN).astype(BF16)
    dup = (dhid * act).astype(BF16)
    db_ref[...] = dup
    g_ref[:, hidden : 2 * hidden] = dot(x, dup, TN).astype(BF16)


def expert_grads(chunk, rows, wg, wu, wd):
    n_rows, width = rows.shape[0], rows.shape[1] // 2
    hidden = wg.shape[2]
    weight = pl.BlockSpec((1, width, hidden), lambda i: (chunk, 0, 0), pipeline_mode=pl.Buffered(1))

    def whole(shape):
        return pl.BlockSpec(shape, lambda i: (0, 0), pipeline_mode=pl.Buffered(1))

    return pl.pallas_call(
        grads_kernel,
        grid=(1,),
        in_specs=[
            pl.BlockSpec((n_rows, width), lambda i: (0, 0), pipeline_mode=pl.Buffered(1)),
            pl.BlockSpec((n_rows, width), lambda i: (0, 1), pipeline_mode=pl.Buffered(1)),
            weight,
            weight,
            weight,
        ],
        out_specs=[
            whole((width, 3 * hidden)),
            whole((n_rows, hidden)),
            whole((n_rows, hidden)),
            whole((n_rows, LANES)),
        ],
        out_shape=[
            jax.ShapeDtypeStruct((width, 3 * hidden), BF16),
            jax.ShapeDtypeStruct((n_rows, hidden), BF16),
            jax.ShapeDtypeStruct((n_rows, hidden), BF16),
            jax.ShapeDtypeStruct((n_rows, LANES), BF16),
        ],
        compiler_params=pltpu.CompilerParams(vmem_limit_bytes=VMEM_LIMIT),
        cost_estimate=cost(12000 * n_rows * width * hidden, 12 * width * hidden + 4 * n_rows * (width + hidden)),
        name=f"grads{chunk}",
    )(rows, rows, wg, wu, wd)


def dx_kernel(da_ref, db_ref, s_ref, wg_ref, wu_ref, out_ref):
    width = wg_ref.shape[1]
    out_ref[:, :width] = (dot(da_ref[...], wg_ref[0], NT) + dot(db_ref[...], wu_ref[0], NT)).astype(BF16)
    out_ref[:, width:] = s_ref[...]


def input_grads(chunk, da, db, s, wg, wu):
    n_rows, hidden = da.shape
    width = wg.shape[1]
    weight = pl.BlockSpec((1, width, hidden), lambda i: (chunk, 0, 0), pipeline_mode=pl.Buffered(1))

    def whole(shape):
        return pl.BlockSpec(shape, lambda i: (0, 0), pipeline_mode=pl.Buffered(1))

    return pl.pallas_call(
        dx_kernel,
        grid=(1,),
        in_specs=[whole((n_rows, hidden)), whole((n_rows, hidden)), whole((n_rows, LANES)), weight, weight],
        out_specs=whole((n_rows, width + LANES)),
        out_shape=jax.ShapeDtypeStruct((n_rows, width + LANES), BF16),
        compiler_params=pltpu.CompilerParams(vmem_limit_bytes=VMEM_LIMIT),
        cost_estimate=cost(4 * n_rows * width * hidden, 4 * width * hidden + 2 * n_rows * (width + 2 * hidden)),
        name=f"dx{chunk}",
    )(da, db, s, wg, wu)


def combine_kernel(local_exp, capacity, ids_ref, *refs):
    ids_t = ids_ref[...]
    back = refs[:local_exp]
    tok_ref, prob_ref = refs[local_exp:]
    topk, tok = ids_t.shape
    n_experts = back[0].shape[0] // capacity * local_exp
    width = tok_ref.shape[1]
    values = slot_values(ids_t, n_experts, capacity)
    total = jnp.zeros((tok, width), F32)
    by_expert = jnp.zeros((n_experts, tok), F32)
    for chunk in range(local_exp):
        onehot, spread = slot_rows(values, chunk, local_exp, capacity)
        pick = jnp.where(onehot, 1.0, 0.0)
        total = total + dot(pick.astype(BF16), back[chunk][:, :width], TN)
        s = back[chunk][:, width:].astype(F32)
        s = s[:, 0:1] + s[:, 1:2]
        placed = pick * s
        high = placed.astype(BF16)
        low = (placed - high.astype(F32)).astype(BF16)
        by_expert = by_expert + dot(spread, high, TN) + dot(spread, low, TN)
    tok_ref[...] = total.astype(BF16)
    rows = lax.broadcasted_iota(jnp.int32, (n_experts, tok), 0)
    for k in range(topk):
        mine = jnp.where(ids_t[k : k + 1, :] == rows, by_expert, 0.0)
        prob_ref[k : k + 1, :] = jnp.sum(mine, axis=0, keepdims=True)


def combine(local_exp, capacity, ids_t, backs, width):
    topk, tok = ids_t.shape
    n_rows = local_exp * backs[0].shape[0]
    return pl.pallas_call(
        functools.partial(combine_kernel, local_exp, capacity),
        out_shape=[
            jax.ShapeDtypeStruct((tok, width), BF16),
            jax.ShapeDtypeStruct((topk, tok), F32),
        ],
        compiler_params=pltpu.CompilerParams(vmem_limit_bytes=VMEM_LIMIT),
        cost_estimate=cost(2000 * n_rows * tok * width, 2 * width * (n_rows + tok)),
        name="combine",
    )(ids_t, *backs)


def body(tokens, out_grad, expert_ids, route_probs, w_gate, w_up, w_down, decay_mask):
    n_owner = lax.axis_size("expert")
    n_group = lax.axis_size("dp")
    local_exp = w_gate.shape[0]
    width = tokens.shape[1]
    hidden = w_gate.shape[2]
    tok_rows, topk = expert_ids.shape
    n_experts = n_owner * local_exp
    capacity = tok_rows * topk // n_experts
    ids_t = expert_ids.T
    probs_t = route_probs.T
    shard_rows = width // n_group
    first_row = lax.axis_index("dp") * shard_rows

    sends = dispatch(local_exp, capacity, n_experts, ids_t, probs_t, tokens, out_grad)
    got = []
    for rows in sends:
        if got:
            rows, got[-1] = lax.optimization_barrier((rows, got[-1]))
        rows = rows.reshape(n_owner, capacity, 2 * width)
        got.append(lax.all_to_all(rows, "expert", split_axis=0, concat_axis=0, tiled=True))
    summed, backs = [], []
    for chunk in range(local_exp):
        rows = got[chunk].reshape(n_owner * capacity, 2 * width)
        g, da, db, s = expert_grads(chunk, rows, w_gate, w_up, w_down)
        summed.append(lax.psum_scatter(g, "dp", scatter_dimension=0, tiled=True))
        if chunk + 1 < local_exp:
            da, got[chunk + 1] = lax.optimization_barrier((da, got[chunk + 1]))
        dx = input_grads(chunk, da, db, s, w_gate, w_up).reshape(n_owner, capacity, width + LANES)
        back = lax.all_to_all(dx, "expert", split_axis=0, concat_axis=0, tiled=True)
        backs.append(back.reshape(n_owner * capacity, width + LANES))
    grad_tokens, scores = combine(local_exp, capacity, ids_t, backs, width)
    grad_probs = (scores / probs_t.astype(F32)).astype(BF16).T

    rates = decay_mask.astype(F32)

    def update(weight, column):
        weight_f = lax.dynamic_slice_in_dim(weight, first_row, shard_rows, 1).astype(F32)
        grad_w = jnp.stack([s[:, column * hidden : (column + 1) * hidden] for s in summed]).astype(F32)
        factor = rates[:, column][:, None, None]
        return (weight_f - step_size * grad_w - shrink_rate * factor * weight_f).astype(BF16)

    return (grad_tokens, grad_probs, update(w_gate, 0), update(w_up, 1), update(w_down, 2))


def solution(mesh):
    placed = (
        P(("dp", "expert"), None),
        P(("dp", "expert"), None),
        P(("dp", "expert"), None),
        P(("dp", "expert"), None),
        P("expert", None, None),
        P("expert", None, None),
        P("expert", None, None),
        P("expert", None),
    )
    return jax.shard_map(
        body,
        mesh=mesh,
        in_specs=placed,
        out_specs=(
            P(("dp", "expert"), None),
            P(("dp", "expert"), None),
            P("expert", "dp", None),
            P("expert", "dp", None),
            P("expert", "dp", None),
        ),
        check_vma=False,
    )
```

time: 426 us -> 296 us (0.69); the launches traced: 418 us -> 295 us
  local copies, waits for them, and re-layouts: 87.5 us -> 5.01 us
  matrix products: 71.9 us -> 0 us
  Pallas kernels: 0 us -> 65.4 us
  blocking collectives: 0 us -> 59.6 us
  waiting for transfers between devices: 172 us -> 127 us
  other arithmetic: 40.9 us -> 9.34 us
  starting transfers between devices: 31.1 us -> 14.5 us
    all_to_all x5 -> x3, waiting for transfers between devices: 172 us -> 68.4 us  [the longest x1 34.3 us: body(): lax.all_to_all(rows, 'expert', split_axis=0, concat_axis=0, tiled=True)]
    dot_general x10 -> x0, matrix products: 71.9 us -> none  [the longest x1 10.2 us: body(): jnp.einsum('sjch,jdh->sjcd', dgate, w_gate, preferred_element_type=jnp.fl...]
    pallas_call x0 -> x6, Pallas kernels: none -> 65.4 us  [the longest x2 38.3 us: expert_grads(): pl.pallas_call(grads_kernel, grid=(1,), in_specs=[pl.BlockSpec((n_rows, w...]
    all_to_all x0 -> x1, blocking collectives: none -> 59.6 us  [body(): lax.all_to_all(rows, 'expert', split_axis=0, concat_axis=0, tiled=True)]
    reduce_scatter x1 -> x2, waiting for transfers between devices: 0.01 us -> 58.2 us  [body(): summed.append(lax.psum_scatter(g, 'dp', scatter_dimension=0, tiled=True))]
    gather x5 -> x0, local copies, waits for them, and re-layouts: 42.1 us -> none  [the longest x1 11.6 us: body(): routed_dx = dx_pad[slots].reshape(tok_rows, topk, width)]
    another operation x4 -> x0, other arithmetic: 26.6 us -> none
    all_to_all x5 -> x3, starting transfers between devices: 31 us -> 13.9 us  [the longest x2 9.07 us: body(): back = lax.all_to_all(dx, 'expert', split_axis=0, concat_axis=0, tiled=True)]
  transfers between devices with their start and end apart: 6 -> 5, of which waited for: 4 -> 4; matrix products, arithmetic and copies ran while one was open for 26% -> 1% of each run, Pallas kernels for 0% -> 20%
where the time goes in v1:
time: 296 us; the launch traced here: 295 us
  waiting for transfers between devices  127 us (43%)
  Pallas kernels  65.4 us (22%)
  blocking collectives  59.6 us (20%)
  starting transfers between devices  14.5 us (5%)
  between operations  14.1 us (5%)
  other arithmetic  9.34 us (3%)
  local copies, waits for them, and re-layouts  5.01 us (2%)
    all_to_all x1, blocking collectives, body(): lax.all_to_all(rows, 'expert', split_axis=0, concat_axis=0, tiled=True)  59.6 us
    reduce_scatter x2, waiting for transfers between devices, body(): summed.append(lax.psum_scatter(g, 'dp', scatter_dimension=0, tiled=True))  58.2 us
    pallas_call x2, Pallas kernels, expert_grads(): pl.pallas_call(grads_kernel, grid=(1,), in_specs=[pl.BlockSpec((n_rows, w...  38.3 us
    all_to_all x1, waiting for transfers between devices, body(): lax.all_to_all(rows, 'expert', split_axis=0, concat_axis=0, tiled=True)  34.3 us
    all_to_all x2, waiting for transfers between devices, body(): back = lax.all_to_all(dx, 'expert', split_axis=0, concat_axis=0, tiled=True)  34.2 us
    pallas_call x2, Pallas kernels, input_grads(): pl.pallas_call(dx_kernel, grid=(1,), in_specs=[whole((n_rows, hidden)), w...  16.6 us
    all_to_all x2, starting transfers between devices, body(): back = lax.all_to_all(dx, 'expert', split_axis=0, concat_axis=0, tiled=True)  9.07 us
    convert_element_type x2, other arithmetic, update(): (weight_f - step_size * grad_w - shrink_rate * factor * weight_f).astype(...  7.32 us
  transfers between devices with their start and end apart: 5, of which 4 were waited for; matrix products, arithmetic and copies ran while one was open for 1% of the time, Pallas kernels for 20%

profile of v1, /device:TPU:0, one launch (start us, length us, event | category | flops | bytes accessed | tf_op | source)
XLA Modules:
  0.0 294.5 jit_solution(11435345410825095228)
XLA Ops:
  7.2 6.1 %dispatch.1 = (bf16[512,4096]{1,0:T(8,128)(2,1)}, bf16[512,4096]{1,0:T(8,128)(2,1)}) custom-call(s32[8,128]{1,0:T(8,128)} %bitcast.33, bf16[8,128]{1,0:T(8,128)(2,1)} %bitcast.32, bf16[128,2048]{1,0:T(8,128)(2,1)} %tok_ref.1, bf16[128,2048]{1,0:T(8,128)(2,1)} %grad_ref.1), custom_call_target="tpu_custom_call" | custom-call | flops 1073741824 | bytes 9437184 | tf_op jit(solution)/shard_map/dispatch/pallas_call | solution.py:78
  13.3 59.6 %all_to_all.20 = bf16[32,16,4096]{2,1,0:T(8,128)(2,1)} all-to-all(bf16[32,16,4096]{2,1,0:T(8,128)(2,1)} %bitcast.30), channel_id=1, replica_groups=mesh['dp'=4,'expert'=32] {'expert'}, dimensions={0} | all-to-all | bytes 8388608 | tf_op jit(solution)/shard_map/all_to_all | solution.py:234
  72.8 4.9 %all-to-all-start.1 = ((bf16[32,16,4096]{2,1,0:T(8,128)(2,1)}), bf16[32,16,4096]{2,1,0:T(8,128)(2,1)}, u32[]{:S(2)}, u32[]{:S(2)}) async-start(bf16[32,16,4096]{2,1,0:T(8,128)(2,1)} %bitcast.27), calls=%async_computation.1 | async-start | bytes 8388608 | tf_op jit(solution)/shard_map/all_to_all | solution.py:234
  77.7 0.2 reduce-scatter.3.cloned.1.call-start
  77.9 19.0 %grads0.1 = (bf16[2048,2304]{1,0:T(8,128)(2,1)}, bf16[512,768]{1,0:T(8,128)(2,1)}, bf16[512,768]{1,0:T(8,128)(2,1)}, bf16[512,128]{1,0:T(8,128)(2,1)}) custom-call(bf16[512,4096]{1,0:T(8,128)(2,1)} %bitcast.28, bf16[512,4096]{1,0:T(8,128)(2,1)} %bitcast.29, bf16[2,2048,768]{2,1,0:T(8,128)(2,1)} %wg_ref.7, bf16[2,2048,768]{2,1,0:T(8,128)(2,1)} %wu_ref.7, ...), custom_call_target="tpu_custom_call" | custom-call | flops 9663676416000 | bytes 24641536 | tf_op jit(solution)/shard_map/grads0/pallas_call | solution.py:118
  96.9 0.0 reduce-scatter.3.cloned.1.call-update
  96.9 34.3 %all-to-all-done.1 = bf16[32,16,4096]{2,1,0:T(8,128)(2,1)} async-done(((bf16[32,16,4096]{2,1,0:T(8,128)(2,1)}), bf16[32,16,4096]{2,1,0:T(8,128)(2,1)}, u32[]{:S(2)}, u32[]{:S(2)}) %all-to-all-start.1) | async-done | bytes 4194336 | tf_op jit(solution)/shard_map/all_to_all | solution.py:234
  131.2 8.3 %dx0.1 = bf16[512,2176]{1,0:T(8,128)(2,1)} custom-call(bf16[512,768]{1,0:T(8,128)(2,1)} %get-tuple-element.26.da_ref, bf16[512,768]{1,0:T(8,128)(2,1)} %get-tuple-element.27.db_ref, bf16[512,128]{1,0:T(8,128)(2,1)} %get-tuple-element.28.s_ref, bf16[2,2048,768]{2,1,0:T(8,128)(2,1)} %wg_ref.7, bf16[2,2048,768]{2,1,0:T(8,128)(2,1)} %wu_ref.7), custom_call_target="tpu_custom_call" | custom-call | flops 3221225472 | bytes 9961472 | tf_op jit(solution)/shard_map/dx0/pallas_call | solution.py:160
  139.5 5.0 %all-to-all-start.2 = ((bf16[32,16,2176]{2,1,0:T(8,128)(2,1)}), bf16[32,16,2176]{2,1,0:T(8,128)(2,1)}, u32[]{:S(2)}, u32[]{:S(2)}) async-start(bf16[32,16,2176]{2,1,0:T(8,128)(2,1)} %bitcast.26), calls=%async_computation.2 | async-start | bytes 4456448 | tf_op jit(solution)/shard_map/all_to_all | solution.py:243
  144.5 19.3 %grads1.1 = (bf16[2048,2304]{1,0:T(8,128)(2,1)}, bf16[512,768]{1,0:T(8,128)(2,1)}, bf16[512,768]{1,0:T(8,128)(2,1)}, bf16[512,128]{1,0:T(8,128)(2,1)}) custom-call(bf16[512,4096]{1,0:T(8,128)(2,1)} %bitcast.7.x_ref.do_ref, bf16[512,4096]{1,0:T(8,128)(2,1)} %bitcast.7.x_ref.do_ref, bf16[2,2048,768]{2,1,0:T(8,128)(2,1)} %wg_ref.7, ...), custom_call_target="tpu_custom_call" | custom-call | flops 9663676416000 | bytes 24641536 | tf_op jit(solution)/shard_map/grads1/pallas_call | solution.py:118
  163.8 8.3 %dx1.1 = bf16[512,2176]{1,0:T(8,128)(2,1)} custom-call(bf16[512,768]{1,0:T(8,128)(2,1)} %get-tuple-element.30.da_ref, bf16[512,768]{1,0:T(8,128)(2,1)} %get-tuple-element.31.db_ref, bf16[512,128]{1,0:T(8,128)(2,1)} %get-tuple-element.32.s_ref, bf16[2,2048,768]{2,1,0:T(8,128)(2,1)} %wg_ref.7, bf16[2,2048,768]{2,1,0:T(8,128)(2,1)} %wu_ref.7), custom_call_target="tpu_custom_call" | custom-call | flops 3221225472 | bytes 9961472 | tf_op jit(solution)/shard_map/dx1/pallas_call | solution.py:160
  172.1 0.0 copy-start.5
  172.1 3.7 %all-to-all-done.2 = bf16[32,16,2176]{2,1,0:T(8,128)(2,1)} async-done(((bf16[32,16,2176]{2,1,0:T(8,128)(2,1)}), bf16[32,16,2176]{2,1,0:T(8,128)(2,1)}, u32[]{:S(2)}, u32[]{:S(2)}) %all-to-all-start.2) | async-done | bytes 2228256 | tf_op jit(solution)/shard_map/all_to_all | solution.py:243
  175.8 4.1 %all-to-all-start.3 = ((bf16[32,16,2176]{2,1,0:T(8,128)(2,1)}), bf16[32,16,2176]{2,1,0:T(8,128)(2,1)S(1)}, u32[]{:S(2)}, u32[]{:S(2)}) async-start(bf16[32,16,2176]{2,1,0:T(8,128)(2,1)} %bitcast.25), calls=%async_computation.3 | async-start | bytes 4456448 | tf_op jit(solution)/shard_map/all_to_all | solution.py:243
  179.9 0.3 reduce-scatter.5.cloned.1.call-start
  180.2 0.0 copy-done.5
  180.2 0.8 multiply_reduce_fusion
  181.0 0.0 reduce-scatter.5.cloned.1.call-update
  181.0 30.4 %all-to-all-done.3 = bf16[32,16,2176]{2,1,0:T(8,128)(2,1)S(1)} async-done(((bf16[32,16,2176]{2,1,0:T(8,128)(2,1)}), bf16[32,16,2176]{2,1,0:T(8,128)(2,1)S(1)}, u32[]{:S(2)}, u32[]{:S(2)}) %all-to-all-start.3) | async-done | bytes 2228256 | tf_op jit(solution)/shard_map/all_to_all | solution.py:243
  211.5 0.0 copy-start
  211.5 1.4 copy-done
  212.9 0.0 copy-start.4
  212.9 4.4 %combine.1 = (bf16[128,2048]{1,0:T(8,128)(2,1)}, f32[8,128]{1,0:T(8,128)}) custom-call(s32[8,128]{1,0:T(8,128)} %bitcast.34, bf16[512,2176]{1,0:T(8,128)(2,1)} %bitcast.6.refs_0_, bf16[512,2176]{1,0:T(8,128)(2,1)} %bitcast.31), custom_call_target="tpu_custom_call" | custom-call | flops 536870912000 | bytes 4718592 | tf_op jit(solution)/shard_map/combine/pallas_call | solution.py:202
  217.3 0.0 copy-done.4
  217.3 1.3 fusion.6
  218.6 0.0 reduce-scatter.3.cloned.1.call-done
  218.6 1.8 slice_bitcast_fusion.1
  220.4 0.0 copy-start.3
  220.4 58.2 %reduce-scatter.5.cloned.1.call-done = bf16[512,2304]{1,0:T(8,128)(2,1)} async-done(((bf16[2048,2304]{1,0:T(8,128)(2,1)}), bf16[512,2304]{1,0:T(8,128)(2,1)}) %reduce-scatter.5.cloned.1.call-update) | async-done | bytes 2359312 | tf_op jit(solution)/shard_map/reduce_scatter | solution.py:239
  278.6 1.8 slice_bitcast_fusion
  280.4 0.0 copy-start.1
  280.4 0.0 copy-start.2
  280.4 0.0 copy-done.3
  280.4 3.3 %fusion.5 = bf16[2,512,768]{2,1,0:T(8,128)(2,1)} fusion(bf16[1,512,768]{2,1,0:T(8,128)(2,1)S(1)} %get-tuple-element.43, bf16[1,512,768]{2,1,0:T(8,128)(2,1)S(1)} %get-tuple-element.40, f32[2]{0:T(128)S(1)} %copy-done.3, bf16[2,2048,768]{2,1,0:T(8,128)(2,1)} %wd_ref.3, s32[]{:T(128)S(6)} %select_n.2), kind=kLoop, calls=%fused_computation.11 | loop fusion | flops 7864320 | bytes 4718604 | tf_op jit(solution)/shard_map/convert_element_type | solution.py:254
  283.7 0.0 copy-done.1
  283.7 0.0 copy-done.2
  283.7 4.0 %fusion.1 = (bf16[2,512,768]{2,1,0:T(8,128)(2,1)}, bf16[2,512,768]{2,1,0:T(8,128)(2,1)}) fusion(bf16[1,512,768]{2,1,0:T(8,128)(2,1)S(1)} %get-tuple-element.45, bf16[1,512,768]{2,1,0:T(8,128)(2,1)S(1)} %get-tuple-element.42, f32[2]{0:T(128)S(1)} %copy-done.2, bf16[2,2048,768]{2,1,0:T(8,128)(2,1)} %wg_ref.7, s32[]{:T(128)S(6)} %select_n.2, f32[2]{0:T(128)S(1)} %copy-done.1, ...), kind=kLoop, calls=%fused_computation.7 | loop fusion | flops 15728640 | bytes 9437204 | tf_op jit(solution)/shard_map/convert_element_type | solution.py:254
  (1 shorter events, 0.0 us)
Async XLA Ops:
  72.8 58.3 %all-to-all-start.1 = ((bf16[32,16,4096]{2,1,0:T(8,128)(2,1)}), bf16[32,16,4096]{2,1,0:T(8,128)(2,1)}, u32[]{:S(2)}, u32[]{:S(2)}) async-start(bf16[32,16,4096]{2,1,0:T(8,128)(2,1)} %bitcast.27), calls=%async_computation.1 | async-start | bytes 8388608 | tf_op jit(solution)/shard_map/all_to_all | solution.py:234
  77.7 140.9 %reduce-scatter.3.cloned.1.call-start = ((), (), s32[]{:S(2)}) async-start(), calls=%async_computation.6 | async-start | bytes 11796480 | tf_op jit(solution)/shard_map/reduce_scatter | solution.py:239
  139.5 36.4 %all-to-all-start.2 = ((bf16[32,16,2176]{2,1,0:T(8,128)(2,1)}), bf16[32,16,2176]{2,1,0:T(8,128)(2,1)}, u32[]{:S(2)}, u32[]{:S(2)}) async-start(bf16[32,16,2176]{2,1,0:T(8,128)(2,1)} %bitcast.26), calls=%async_computation.2 | async-start | bytes 4456448 | tf_op jit(solution)/shard_map/all_to_all | solution.py:243
  172.1 8.1 %copy-start.5 = (s32[2,3]{1,0:T(2,128)S(1)}, s32[2,3]{1,0:T(2,128)}, u32[]{:S(2)}) copy-start(s32[2,3]{1,0:T(2,128)} %param.15) | copy-start | bytes 76
  175.8 35.6 %all-to-all-start.3 = ((bf16[32,16,2176]{2,1,0:T(8,128)(2,1)}), bf16[32,16,2176]{2,1,0:T(8,128)(2,1)S(1)}, u32[]{:S(2)}, u32[]{:S(2)}) async-start(bf16[32,16,2176]{2,1,0:T(8,128)(2,1)} %bitcast.25), calls=%async_computation.3 | async-start | bytes 4456448 | tf_op jit(solution)/shard_map/all_to_all | solution.py:243
  179.9 98.7 %reduce-scatter.5.cloned.1.call-start = ((), (), s32[]{:S(2)}) async-start(), calls=%async_computation.7 | async-start | bytes 11796480 | tf_op jit(solution)/shard_map/reduce_scatter | solution.py:239
  211.5 1.4 copy-start
  212.9 4.4 %copy-start.4 = (bf16[128,8]{0,1:T(8,128)(2,1)S(1)}, bf16[128,8]{0,1:T(8,128)(2,1)}, u32[]{:S(2)}) copy-start(bf16[128,8]{0,1:T(8,128)(2,1)} %param.11) | copy-start | bytes 6148
  220.4 60.0 %copy-start.3 = (f32[2]{0:T(128)S(1)}, f32[2]{0:T(128)}, u32[]{:S(2)}) copy-start(f32[2]{0:T(128)} %get-tuple-element.37) | copy-start | bytes 28
  280.4 3.3 %copy-start.1 = (f32[2]{0:T(128)S(1)}, f32[2]{0:T(128)}, u32[]{:S(2)}) copy-start(f32[2]{0:T(128)} %get-tuple-element.38) | copy-start | bytes 28
  280.4 3.3 %copy-start.2 = (f32[2]{0:T(128)S(1)}, f32[2]{0:T(128)}, u32[]{:S(2)}) copy-start(f32[2]{0:T(128)} %get-tuple-element.39) | copy-start | bytes 28
Sparse Core Ops, SparseCore 0:
  97.0 90.2 reduce-scatter.2
  189.8 88.6 reduce-scatter.4

commit v2 on v0

v2 whole, which is shorter than its diff:
```python
import functools

import jax
import jax.numpy as jnp
from jax import lax
from jax.experimental import pallas as pl
from jax.experimental.pallas import tpu as pltpu
from jax.sharding import PartitionSpec as P

step_size = 0.004
shrink_rate = 0.1
LANES = 128
CORES = 2
F32 = jnp.float32
BF16 = jnp.bfloat16
NN = ((1,), (0,))
NT = ((1,), (1,))
TN = ((0,), (0,))
ANY = pl.BlockSpec(memory_space=pl.ANY)
SMEM = pl.BlockSpec(memory_space=pltpu.SMEM)


def dot(a, b, dims):
    return lax.dot_general(a, b, (dims, ((), ())), preferred_element_type=F32)


def iota(shape, dim):
    return lax.broadcasted_iota(jnp.int32, shape, dim)


def params(mib):
    return pltpu.CompilerParams(vmem_limit_bytes=60 * 1024 * 1024)


def cost(flops, moved):
    return pl.CostEstimate(flops=flops, transcendentals=0, bytes_accessed=moved)


def whole(shape):
    return pl.BlockSpec(shape, lambda *_: (0,) * len(shape), pipeline_mode=pl.Buffered(1))


def routing(meta, topk, n_chip, capacity, stride, plane):
    tok = meta.shape[0]
    eye = jnp.where(iota((tok, tok), 0) == iota((tok, tok), 1), 1.0, 0.0).astype(BF16)
    meta_t = dot(meta, eye, TN)
    expert = (iota((n_chip, tok), 0) * stride + plane).astype(F32)
    hit = jnp.zeros((n_chip, tok), F32)
    prob = jnp.zeros((n_chip, tok), F32)
    for k in range(topk):
        same = meta_t[k : k + 1, :] == expert
        hit = hit + jnp.where(same, 1.0, 0.0)
        prob = prob + jnp.where(same, meta_t[topk + k : topk + k + 1, :], 0.0)
    earlier = jnp.where(iota((tok, tok), 0) < iota((tok, tok), 1), 1.0, 0.0).astype(BF16)
    count = dot(hit.astype(BF16), earlier, NN)
    values = jnp.where(jnp.logical_and(hit > 0.5, count < capacity), count, -1.0)
    rows = n_chip * capacity
    spread = jnp.where(iota((rows, n_chip), 0) // capacity == iota((rows, n_chip), 1), 1.0, 0.0).astype(BF16)
    place = (iota((rows, tok), 0) % capacity).astype(F32)
    onehot = dot(spread, values.astype(BF16), NN) == place
    return onehot, dot(spread, prob.astype(BF16), NN)


def dispatch_kernel(topk, capacity, stride, plane_ref, *refs):
    packed, out_ref = refs[:-1], refs[-1]
    n_chip = out_ref.shape[0]
    width = out_ref.shape[2] // 2
    for g, ref in enumerate(packed):
        onehot, prob_rows = routing(ref[:, 2 * width :], topk, n_chip, capacity, stride, plane_ref[0])
        pick = jnp.where(onehot, 1.0, 0.0).astype(BF16)
        weighted = jnp.where(onehot, prob_rows, 0.0).astype(BF16)
        x = dot(pick, ref[:, :width], NN).astype(BF16)
        do = dot(weighted, ref[:, width : 2 * width], NN).astype(BF16)
        rows = slice(g * capacity, (g + 1) * capacity)
        out_ref[:, rows, :width] = x.reshape(n_chip, capacity, width)
        out_ref[:, rows, width:] = do.reshape(n_chip, capacity, width)


def dispatch(name, plane, packed, n_chip, topk, capacity, stride, width):
    n_rows = len(packed) * capacity
    return pl.pallas_call(
        functools.partial(dispatch_kernel, topk, capacity, stride),
        in_specs=[SMEM] + [pl.BlockSpec(memory_space=pltpu.VMEM)] * len(packed),
        out_shape=jax.ShapeDtypeStruct((n_chip, n_rows, 2 * width), BF16),
        compiler_params=params(32),
        cost_estimate=cost(4 * n_chip * n_rows * LANES * width, 8 * n_chip * n_rows * width),
        name=name,
    )(plane, *packed)


def hidden_kernel(x_ref, do_ref, wg_ref, wu_ref, wd_ref, hid_ref, da_ref, db_ref, s_ref):
    gate = dot(x_ref[...], wg_ref[...], NN)
    upper = dot(x_ref[...], wu_ref[...], NN)
    sig = jax.nn.sigmoid(gate)
    act = gate * sig
    hid = (act * upper).astype(BF16)
    hid_ref[...] = hid
    dhid = dot(do_ref[...], wd_ref[...], NN)
    total = jnp.sum(hid.astype(F32) * dhid, axis=1, keepdims=True)
    high = total.astype(BF16).astype(F32)
    lane = iota(s_ref.shape, 1)
    s_ref[...] = jnp.where(lane == 0, high, jnp.where(lane == 1, total - high, 0.0)).astype(BF16)
    da_ref[...] = (dhid * upper * sig * (1.0 + gate * (1.0 - sig))).astype(BF16)
    db_ref[...] = (dhid * act).astype(BF16)


def hidden_grads(name, rows, wg, wu, wd):
    n_rows, width = rows.shape[0], rows.shape[1] // 2
    hidden = wg.shape[1]
    return pl.pallas_call(
        hidden_kernel,
        grid=(1,),
        in_specs=[
            pl.BlockSpec((n_rows, width), lambda i: (0, 0), pipeline_mode=pl.Buffered(1)),
            pl.BlockSpec((n_rows, width), lambda i: (0, 1), pipeline_mode=pl.Buffered(1)),
            whole((width, hidden)),
            whole((width, hidden)),
            whole((width, hidden)),
        ],
        out_specs=[whole((n_rows, hidden))] * 3 + [whole((n_rows, LANES))],
        out_shape=[jax.ShapeDtypeStruct((n_rows, hidden), BF16)] * 3
        + [jax.ShapeDtypeStruct((n_rows, LANES), BF16)],
        compiler_params=params(32),
        cost_estimate=cost(6 * n_rows * width * hidden, 6 * width * hidden + n_rows * (4 * width + 6 * hidden)),
        name=name,
    )(rows, rows, wg, wu, wd)


def dx_kernel(da_ref, db_ref, s_ref, wg_ref, wu_ref, *refs):
    out_ref = refs[-1]
    n_chip, capacity, hidden = da_ref.shape
    width = wg_ref.shape[0]
    da = da_ref[...].reshape(n_chip * capacity, hidden)
    db = db_ref[...].reshape(n_chip * capacity, hidden)
    dx = (dot(da, wg_ref[...], NT) + dot(db, wu_ref[...], NT)).astype(BF16)
    out_ref[:, :, :width] = dx.reshape(n_chip, capacity, width)
    out_ref[:, :, width:] = s_ref[...]


def input_grads(name, da, db, s, wg, wu, n_chip, capacity, n_group, first, into):
    width, hidden = wg.shape
    count = da.shape[0] // (n_chip * capacity)

    def split(a):
        return a.reshape(n_chip, count * capacity, a.shape[1])

    def group(lanes, shift):
        return pl.BlockSpec((n_chip, capacity, lanes), lambda i: (0, i + shift, 0))

    extra = [] if into is None else [into]
    return pl.pallas_call(
        dx_kernel,
        grid=(count,),
        in_specs=[
            group(hidden, 0),
            group(hidden, 0),
            group(LANES, 0),
            whole((width, hidden)),
            whole((width, hidden)),
        ]
        + [ANY] * len(extra),
        out_specs=group(width + LANES, first),
        out_shape=jax.ShapeDtypeStruct((n_chip, n_group * capacity, width + LANES), BF16),
        input_output_aliases={5: 0} if extra else {},
        compiler_params=params(32),
        cost_estimate=cost(4 * da.shape[0] * width * hidden, 4 * width * hidden + 2 * da.shape[0] * width),
        name=name,
    )(split(da), split(db), split(s), wg, wu, *extra)


def weight_kernel(n_chunk, with_sum, where_ref, *refs):
    xs, dos = refs[:n_chunk], refs[n_chunk : 2 * n_chunk]
    hids, das, dbs = (refs[(2 + i) * n_chunk : (3 + i) * n_chunk] for i in range(3))
    rest = refs[5 * n_chunk :]
    out_ref = rest[-1]
    hidden = hids[0].shape[1]

    def total(lefts, rights):
        out = dot(lefts[0][...], rights[0][...], TN)
        for left, right in zip(lefts[1:], rights[1:]):
            out = out + dot(left[...], right[...], TN)
        return out

    for m, (lefts, rights) in enumerate(((xs, das), (xs, dbs), (dos, hids))):
        part = total(lefts, rights)
        lanes = slice(m * hidden, (m + 1) * hidden)
        if with_sum:
            part = part + rest[0][0, :, lanes].astype(F32)
        out_ref[0, :, lanes] = part.astype(BF16)


def weight_grads(name, where, steps, rows, hids, das, dbs, add=None, add_at=0):
    n_chunk = len(rows)
    width, hidden = rows[0].shape[1] // 2, hids[0].shape[1]
    half = width // 8
    lefts = width // half

    def columns(r, shift):
        return pl.BlockSpec((r.shape[0], half), lambda i, at: (0, at[i] + shift))

    in_specs = [columns(r, 0) for r in rows] + [columns(r, lefts) for r in rows]
    in_specs += [whole(a.shape) for a in hids + das + dbs]
    args = rows + rows + hids + das + dbs
    if add is not None:
        in_specs.append(pl.BlockSpec((1, half, 3 * hidden), lambda i, at: (i + add_at, 0, 0)))
        args.append(add)
    total = sum(r.shape[0] for r in rows)
    return pl.pallas_call(
        functools.partial(weight_kernel, n_chunk, add is not None),
        grid_spec=pltpu.PrefetchScalarGridSpec(
            num_scalar_prefetch=1,
            grid=(steps,),
            in_specs=in_specs,
            out_specs=pl.BlockSpec((1, half, 3 * hidden), lambda i, at: (i, 0, 0)),
        ),
        out_shape=jax.ShapeDtypeStruct((steps, half, 3 * hidden), BF16),
        compiler_params=params(32),
        cost_estimate=cost(6 * steps * total * half * hidden, 6 * total * hidden + 6 * steps * half * hidden),
        name=name,
    )(where, *args)


def pick_kernel(n_out, index_ref, *refs):
    sources, out_refs, sems = refs[: -n_out - 1], refs[-n_out - 1 : -1], refs[-1]
    per = out_refs[0].shape[0]
    for o in range(n_out * per):
        for s, source in enumerate(sources):

            @pl.when(index_ref[o] == s)
            def _():
                pltpu.make_async_copy(source.at[0], out_refs[o // per].at[o % per], sems.at[o]).start()

    for o in range(n_out * per):
        pltpu.make_async_copy(sources[0].at[0], out_refs[o // per].at[o % per], sems.at[o]).wait()


def pick(index, sources, n_out, per):
    shape = (per,) + sources[0].shape[1:]
    return pl.pallas_call(
        functools.partial(pick_kernel, n_out),
        in_specs=[SMEM] + [ANY] * len(sources),
        out_specs=[ANY] * n_out,
        out_shape=[jax.ShapeDtypeStruct(shape, BF16)] * n_out,
        scratch_shapes=[pltpu.SemaphoreType.DMA((n_out * per,))],
        compiler_params=params(16),
        name="pick",
    )(index, *sources)


def update_kernel(where_ref, mask_ref, own_ref, other_ref, *refs):
    weights, outs = refs[:3], refs[3:]
    hidden = weights[0].shape[2]
    j = pl.program_id(1)

    def write(grad_ref):
        for m in range(3):
            rate = mask_ref[j, m].astype(F32)
            weight = weights[m][0].astype(F32)
            grad = grad_ref[0, :, m * hidden : (m + 1) * hidden].astype(F32)
            outs[m][0] = (weight - step_size * grad - shrink_rate * rate * weight).astype(BF16)

    @pl.when(pl.program_id(0) == 0)
    def _():
        write(own_ref)

    @pl.when(pl.program_id(0) == 1)
    def _():
        write(other_ref)


def update(where, mask, own, other, weights, shard_rows):
    local, half, _ = own.shape
    hidden = weights[0].shape[2]
    last = local - 1

    def at(h, w):
        return w[0] * (1 - h) + (1 - w[0]) * h

    weight = pl.BlockSpec((1, half, hidden), lambda h, j, w: (j, CORES * w[1] + at(h, w), 0))
    result = pl.BlockSpec((1, half, hidden), lambda h, j, w: (j, at(h, w), 0))
    return pl.pallas_call(
        update_kernel,
        grid_spec=pltpu.PrefetchScalarGridSpec(
            num_scalar_prefetch=1,
            grid=(CORES, local),
            in_specs=[
                SMEM,
                pl.BlockSpec((1, half, 3 * hidden), lambda h, j, w: (j * (1 - h) + last * h, 0, 0)),
                pl.BlockSpec((1, half, 3 * hidden), lambda h, j, w: (j * h, 0, 0)),
            ]
            + [weight] * 3,
            out_specs=[result] * 3,
        ),
        out_shape=[jax.ShapeDtypeStruct((local, shard_rows, hidden), BF16)] * 3,
        compiler_params=params(32),
        name="update",
    )(where, mask, own, other, *weights)


def combine_kernel(topk, capacity, stride, plane_ref, back_ref, *refs):
    count = len(refs) // 2
    n_chip = back_ref.shape[0]
    width = back_ref.shape[2] - LANES
    for g in range(count):
        meta = refs[g][:, 2 * width :]
        out_ref = refs[count + g]
        tok = meta.shape[0]
        onehot, _ = routing(meta, topk, n_chip, capacity, stride, plane_ref[0])
        pick_f = jnp.where(onehot, 1.0, 0.0)
        n_rows = n_chip * capacity
        rows = slice(g * capacity, (g + 1) * capacity)
        dx = back_ref[:, rows, :width].reshape(n_rows, width)
        out_ref[:, :width] = dot(pick_f.astype(BF16), dx, TN).astype(BF16)
        s = back_ref[:, rows, width:].reshape(n_rows, LANES).astype(F32)
        placed = pick_f * (s[:, 0:1] + s[:, 1:2])
        high = placed.astype(BF16)
        low = (placed - high.astype(F32)).astype(BF16)
        spread = jnp.where(iota((n_rows, LANES), 0) // capacity == iota((n_rows, LANES), 1), 1.0, 0.0)
        spread = spread.astype(BF16)
        by_expert = dot(high, spread, TN) + dot(low, spread, TN)
        lane = iota((tok, LANES), 1)
        expert = (lane * stride + plane_ref[0]).astype(F32)
        ids = meta.astype(F32)
        scores = jnp.zeros((tok, LANES), F32)
        for k in range(topk):
            mine = jnp.where(ids[:, k : k + 1] == expert, by_expert, 0.0)
            mine = jnp.sum(mine, axis=1, keepdims=True)
            top = mine.astype(BF16).astype(F32)
            scores = scores + jnp.where(lane == k, top, 0.0) + jnp.where(lane == topk + k, mine - top, 0.0)
        out_ref[:, width:] = scores.astype(BF16)


def combine(plane, back, packed, topk, capacity, stride):
    tok = packed[0].shape[0]
    lanes = back.shape[2]
    return pl.pallas_call(
        functools.partial(combine_kernel, topk, capacity, stride),
        in_specs=[SMEM] + [pl.BlockSpec(memory_space=pltpu.VMEM)] * (1 + len(packed)),
        out_shape=[jax.ShapeDtypeStruct((tok, lanes), BF16)] * len(packed),
        compiler_params=params(32),
        cost_estimate=cost(2 * back.shape[0] * back.shape[1] * tok * lanes, 4 * back.size),
        name="combine",
    )(plane, back, *packed)


def finish_kernel(topk, probs_ref, *refs):
    parts, (tok_ref, prob_ref) = refs[:-2], refs[-2:]
    width = tok_ref.shape[1]
    total = parts[0][...].astype(F32)
    for part in parts[1:]:
        total = total + part[...].astype(F32)
    tok_ref[...] = total[:, :width].astype(BF16)
    scores = total[:, width : width + topk] + total[:, width + topk : width + 2 * topk]
    prob_ref[...] = (scores / probs_ref[...].astype(F32)).astype(BF16)


def finish(probs, parts, width):
    tok, topk = probs.shape
    return pl.pallas_call(
        functools.partial(finish_kernel, topk),
        out_shape=[jax.ShapeDtypeStruct((tok, width), BF16), jax.ShapeDtypeStruct((tok, topk), BF16)],
        compiler_params=params(32),
        name="finish",
    )(probs, *parts)


def body(tokens, out_grad, expert_ids, route_probs, w_gate, w_up, w_down, decay_mask):
    n_owner = lax.axis_size("expert")
    n_group = lax.axis_size("dp")
    local_exp = w_gate.shape[0]
    width = tokens.shape[1]
    tok_rows, topk = expert_ids.shape
    n_experts = n_owner * local_exp
    capacity = tok_rows * topk // n_experts
    n_chip = n_owner // CORES
    stride = CORES * local_exp
    shard_rows = width // n_group
    p = lax.axis_index("dp").astype(jnp.int32)
    core = lax.axis_index("expert").astype(jnp.int32) % CORES
    plane = p.reshape(1)
    same_core = [[CORES * c + k for c in range(n_chip)] for k in range(CORES)]
    other_core = [(q, q ^ 1) for q in range(n_owner)]

    def across(a, r):
        return lax.ppermute(a, "dp", [(i, (i + r) % n_group) for i in range(n_group)])

    def exchange(a):
        return lax.all_to_all(a, "expert", 0, 0, axis_index_groups=same_core, tiled=True)

    meta = jnp.concatenate(
        [expert_ids.astype(BF16), route_probs, jnp.zeros((tok_rows, LANES - 2 * topk), BF16)], axis=1
    )
    packed = jnp.concatenate([tokens, out_grad, meta], axis=1)
    near, far = (1, n_group - 1), (2,)
    from_near = [across(packed, r) for r in near]
    from_far = [across(packed, r) for r in far]

    mine = core == p // local_exp
    weights = []
    for w in (w_gate, w_up, w_down):
        other = lax.ppermute(w, "expert", other_core)
        pick_of = functools.partial(lax.dynamic_index_in_dim, index=p % local_exp, axis=0, keepdims=False)
        weights.append(jnp.where(mine, pick_of(w), pick_of(other)))
    wg, wu, wd = weights

    got = []
    for name, chunk in (("own", [packed]), ("near", from_near), ("far", from_far)):
        if got:
            chunk = list(chunk)
            chunk[0], got[-1] = lax.optimization_barrier((chunk[0], got[-1])) if False else (chunk[0], got[-1])
        rows = dispatch("send_" + name, plane, chunk, n_chip, topk, capacity, stride, width)
        if got:
            rows, got[-1] = lax.optimization_barrier((rows, got[-1]))
        got.append(exchange(rows))

    rows, hids, das, dbs, sums = [], [], [], [], []
    for name, part in zip(("own", "near", "far"), got):
        part = part.reshape(-1, 2 * width)
        hid, da, db, s = hidden_grads("hidden_" + name, part, wg, wu, wd)
        rows.append(part)
        hids.append(hid)
        das.append(da)
        dbs.append(db)
        sums.append(s)

    order = (2, 1, n_group - 1, 0)
    blocks = jnp.stack([CORES * ((p + r) % n_group) for r in order]).astype(jnp.int32)
    theirs = weight_grads("theirs", blocks + (1 - core), n_group, rows, hids, das, dbs)
    added = lax.ppermute(theirs, "expert", other_core)

    dx, first = None, 0
    for i, name in enumerate(("own", "near", "far")):
        dx = input_grads("dx_" + name, das[i], dbs[i], sums[i], wg, wu, n_chip, capacity, n_group, first, dx)
        first += rows[i].shape[0] // (n_chip * capacity)
    back = exchange(dx)

    landed = [None] * n_group
    for i, r in enumerate(order):
        block = weight_grads(
            f"mine_{r}", blocks[i : i + 1] + core, 1, rows, hids, das, dbs, added, i
        )
        landed[r] = across(block, r) if r else block

    parts = combine(plane, back, [packed] + from_near + from_far, topk, capacity, stride)
    home = [parts[0]] + [across(a, n_group - r) for a, r in zip(parts[1:], near + far)]
    grad_tokens, grad_probs = finish(route_probs, home, width)

    def source(owner, j):
        return (p - (local_exp * owner + j)) % n_group

    index = jnp.stack(
        [source(1 - core, j) for j in range(local_exp)] + [source(core, j) for j in range(local_exp)]
    ).astype(jnp.int32)
    outgoing, own = pick(index, landed, 2, local_exp)
    other = lax.ppermute(outgoing, "expert", other_core)
    where = jnp.stack([core, p]).astype(jnp.int32)
    new = update(where, decay_mask, own, other, (w_gate, w_up, w_down), shard_rows)
    return (grad_tokens, grad_probs, *new)


def solution(mesh):
    placed = (
        P(("dp", "expert"), None),
        P(("dp", "expert"), None),
        P(("dp", "expert"), None),
        P(("dp", "expert"), None),
        P("expert", None, None),
        P("expert", None, None),
        P("expert", None, None),
        P("expert", None),
    )
    return jax.shard_map(
        body,
        mesh=mesh,
        in_specs=placed,
        out_specs=(
            P(("dp", "expert"), None),
            P(("dp", "expert"), None),
            P("expert", "dp", None),
            P("expert", "dp", None),
            P("expert", "dp", None),
        ),
        check_vma=False,
    )
```

time: 426 us -> 474 us (1.11); the launches traced: 418 us -> 473 us
  Pallas kernels: 0 us -> 256 us
  local copies, waits for them, and re-layouts: 87.5 us -> 13.5 us
  matrix products: 71.9 us -> 0 us
  waiting for transfers between devices: 172 us -> 144 us
  other arithmetic: 40.9 us -> 16.6 us
  between operations: 14.9 us -> 0.86 us
  starting transfers between devices: 31.1 us -> 42.4 us
    pallas_call x0 -> x18, Pallas kernels: none -> 256 us  [the longest x1 145 us: pick(): pl.pallas_call(functools.partial(pick_kernel, n_out), in_specs=[SMEM] + [...]
    all_to_all x5 -> x4, waiting for transfers between devices: 172 us -> 30.5 us  [exchange(): lax.all_to_all(a, 'expert', 0, 0, axis_index_groups=same_core, tiled=True)]
    ppermute x0 -> x14, waiting for transfers between devices: none -> 113 us  [the longest x9 113 us: across(): lax.ppermute(a, 'dp', [(i, (i + r) % n_group) for i in range(n_group)])]
    dot_general x10 -> x0, matrix products: 71.9 us -> none  [the longest x1 10.2 us: body(): jnp.einsum('sjch,jdh->sjcd', dgate, w_gate, preferred_element_type=jnp.fl...]
    gather x5 -> x0, local copies, waits for them, and re-layouts: 42.1 us -> none  [the longest x1 11.6 us: body(): routed_dx = dx_pad[slots].reshape(tok_rows, topk, width)]
    another operation x4 -> x2, other arithmetic: 26.6 us -> 1.24 us  [the longest x1 0.67 us: body(): jnp.stack([source(1 - core, j) for j in range(local_exp)] + [source(core,...]
    ppermute x0 -> x14, starting transfers between devices: none -> 15.1 us  [the longest x9 14 us: across(): lax.ppermute(a, 'dp', [(i, (i + r) % n_group) for i in range(n_group)])]
    select_n x2 -> x3, other arithmetic: 0.02 us -> 14 us  [body(): weights.append(jnp.where(mine, pick_of(w), pick_of(other)))]
  transfers between devices with their start and end apart: 6 -> 18, of which waited for: 4 -> 7; matrix products, arithmetic and copies ran while one was open for 26% -> 5% of each run, Pallas kernels for 0% -> 49%
where the time goes in v2:
time: 474 us; the launch traced here: 473 us
  Pallas kernels  256 us (54%)
  waiting for transfers between devices  144 us (30%)
  starting transfers between devices  42.4 us (9%)
  other arithmetic  16.6 us (4%)
  local copies, waits for them, and re-layouts  13.5 us (3%)
    pallas_call x1, Pallas kernels, pick(): pl.pallas_call(functools.partial(pick_kernel, n_out), in_specs=[SMEM] + [...  145 us
    ppermute x9, waiting for transfers between devices, across(): lax.ppermute(a, 'dp', [(i, (i + r) % n_group) for i in range(n_group)])  113 us
    pallas_call x5, Pallas kernels, weight_grads(): pl.pallas_call(functools.partial(weight_kernel, n_chunk, add is not None)...  32.8 us
    all_to_all x4, waiting for transfers between devices, exchange(): lax.all_to_all(a, 'expert', 0, 0, axis_index_groups=same_core, tiled=True)  30.5 us
    pallas_call x3, Pallas kernels, hidden_grads(): pl.pallas_call(hidden_kernel, grid=(1,), in_specs=[pl.BlockSpec((n_rows,...  27.8 us
    all_to_all x4, starting transfers between devices, exchange(): lax.all_to_all(a, 'expert', 0, 0, axis_index_groups=same_core, tiled=True)  27.3 us
    pallas_call x3, Pallas kernels, input_grads(): pl.pallas_call(dx_kernel, grid=(count,), in_specs=[group(hidden, 0), grou...  19.8 us
    ppermute x9, starting transfers between devices, across(): lax.ppermute(a, 'dp', [(i, (i + r) % n_group) for i in range(n_group)])  14 us
  transfers between devices with their start and end apart: 18, of which 7 were waited for; matrix products, arithmetic and copies ran while one was open for 5% of the time, Pallas kernels for 49%

profile of v2, /device:TPU:0, one launch (start us, length us, event | category | flops | bytes accessed | tf_op | source)
XLA Modules:
  0.0 473.3 jit_solution(9832116978037938271)
XLA Ops:
  0.6 0.1 collective-permute-start.3
  0.7 0.8 copy.17.probs_ref
  1.5 0.7 convert_element_type.3
  2.2 0.1 copy.15
  2.4 3.1 concatenate.3.refs_0_
  5.5 3.8 send_own.1
  9.2 8.1 %all-to-all-start = ((bf16[16,16,4096]{2,1,0:T(8,128)(2,1)}), bf16[16,16,4096]{2,1,0:T(8,128)(2,1)S(1)}, u32[]{:S(2)}, u32[]{:S(2)}) async-start(bf16[16,16,4096]{2,1,0:T(8,128)(2,1)} %send_own.1), calls=%async_computation | async-start | bytes 4194304 | tf_op jit(solution)/shard_map/all_to_all | solution.py:388
  17.4 0.3 collective-permute-start.4
  17.6 0.3 collective-permute-start.5
  17.9 1.5 collective-permute-start.1
  19.4 1.7 collective-permute-start.2
  21.2 23.9 %collective-permute-done.1.refs_0_.refs_1_ = bf16[128,4224]{1,0:T(8,128)(2,1)S(1)} collective-permute-done((bf16[128,4224]{1,0:T(8,128)(2,1)S(1)}, bf16[128,4224]{1,0:T(8,128)(2,1)S(1)}, u32[]{:S(2)}, u32[]{:S(2)}) %collective-permute-start.1) | collective-permute-done | bytes 1081376 | tf_op jit(solution)/shard_map/ppermute | solution.py:385
  45.1 1.0 copy-done.3
  46.1 0.0 collective-permute-done.2.refs_1_.refs_2_
  46.1 5.6 %send_near.1 = bf16[16,32,4096]{2,1,0:T(8,128)(2,1)} custom-call(s32[1]{0:T(128)} %bitcast.plane_ref, bf16[128,4224]{1,0:T(8,128)(2,1)} %copy-done.3, bf16[128,4224]{1,0:T(8,128)(2,1)} %collective-permute-done.2.refs_1_.refs_2_), custom_call_target="tpu_custom_call" | custom-call | flops 536870912 | bytes 8388608 | tf_op jit(solution)/shard_map/send_near/pallas_call | solution.py:81
  51.8 0.0 all-to-all-done
  51.8 1.3 copy-done
  53.0 7.1 %all-to-all-start.1 = ((bf16[16,32,4096]{2,1,0:T(8,128)(2,1)}), bf16[16,32,4096]{2,1,0:T(8,128)(2,1)}, u32[]{:S(2)}, u32[]{:S(2)}) async-start(bf16[16,32,4096]{2,1,0:T(8,128)(2,1)} %send_near.1), calls=%async_computation.1 | async-start | bytes 8388608 | tf_op jit(solution)/shard_map/all_to_all | solution.py:388
  60.1 1.9 collective-permute-start
  62.1 24.4 %collective-permute-done.refs_0_.refs_3_ = bf16[128,4224]{1,0:T(8,128)(2,1)S(1)} collective-permute-done((bf16[128,4224]{1,0:T(8,128)(2,1)S(1)}, bf16[128,4224]{1,0:T(8,128)(2,1)S(1)}, u32[]{:S(2)}, u32[]{:S(2)}) %collective-permute-start) | collective-permute-done | bytes 1081376 | tf_op jit(solution)/shard_map/ppermute | solution.py:385
  86.5 1.0 copy-done.4
  87.4 3.7 send_far.1
  91.1 30.4 %all-to-all-done.1 = bf16[16,32,4096]{2,1,0:T(8,128)(2,1)} async-done(((bf16[16,32,4096]{2,1,0:T(8,128)(2,1)}), bf16[16,32,4096]{2,1,0:T(8,128)(2,1)}, u32[]{:S(2)}, u32[]{:S(2)}) %all-to-all-start.1) | async-done | bytes 4194336 | tf_op jit(solution)/shard_map/all_to_all | solution.py:388
  121.5 4.9 %all-to-all-start.2 = ((bf16[16,16,4096]{2,1,0:T(8,128)(2,1)}), bf16[16,16,4096]{2,1,0:T(8,128)(2,1)S(1)}, u32[]{:S(2)}, u32[]{:S(2)}) async-start(bf16[16,16,4096]{2,1,0:T(8,128)(2,1)} %send_far.1), calls=%async_computation.2 | async-start | bytes 4194304 | tf_op jit(solution)/shard_map/all_to_all | solution.py:388
  126.6 0.7 add_add_fusion.where_ref
  127.2 0.0 collective-permute-done.3
  127.2 5.0 %select_bitcast_fusion.2.wg_ref = bf16[2048,768]{1,0:T(8,128)(2,1)} fusion(bf16[2,2048,768]{2,1,0:T(8,128)(2,1)} %collective-permute-done.3, s32[]{:T(128)S(6)} %select_n.86, bf16[2,2048,768]{2,1,0:T(8,128)(2,1)} %refs_0_.1, pred[]{:T(512)S(6)} %eq.16), kind=kLoop, calls=%fused_computation.2 | loop fusion | flops 1572864 | bytes 9437189 | tf_op jit(solution)/shard_map/jit(_where)/select_n | solution.py:403
  132.2 0.0 collective-permute-done.4
  132.2 5.0 %select_bitcast_fusion.1.wu_ref = bf16[2048,768]{1,0:T(8,128)(2,1)} fusion(bf16[2,2048,768]{2,1,0:T(8,128)(2,1)} %collective-permute-done.4, s32[]{:T(128)S(6)} %select_n.86, bf16[2,2048,768]{2,1,0:T(8,128)(2,1)} %refs_1_.1, pred[]{:T(512)S(6)} %eq.16), kind=kLoop, calls=%fused_computation.1 | loop fusion | flops 1572864 | bytes 9437189 | tf_op jit(solution)/shard_map/jit(_where)/select_n | solution.py:403
  137.3 4.0 select_bitcast_fusion.wd_ref
  141.2 8.1 %hidden_own.1 = (bf16[256,768]{1,0:T(8,128)(2,1)}, bf16[256,768]{1,0:T(8,128)(2,1)}, bf16[256,768]{1,0:T(8,128)(2,1)}, bf16[256,128]{1,0:T(8,128)(2,1)}) custom-call(bf16[256,4096]{1,0:T(8,128)(2,1)} %bitcast.28, bf16[256,4096]{1,0:T(8,128)(2,1)} %bitcast.29, bf16[2048,768]{1,0:T(8,128)(2,1)} %select_bitcast_fusion.2.wg_ref, ...), custom_call_target="tpu_custom_call" | custom-call | flops 2415919104 | bytes 12713984 | tf_op jit(solution)/shard_map/hidden_own/pallas_call | solution.py:110
  149.3 11.6 %hidden_near.1 = (bf16[512,768]{1,0:T(8,128)(2,1)}, bf16[512,768]{1,0:T(8,128)(2,1)}, bf16[512,768]{1,0:T(8,128)(2,1)}, bf16[512,128]{1,0:T(8,128)(2,1)}) custom-call(bf16[512,4096]{1,0:T(8,128)(2,1)} %bitcast.8.x_ref.do_ref.refs_1_.refs_4_, bf16[512,4096]{1,0:T(8,128)(2,1)} %bitcast.8.x_ref.do_ref.refs_1_.refs_4_, ...), custom_call_target="tpu_custom_call" | custom-call | flops 4831838208 | bytes 15990784 | tf_op jit(solution)/shard_map/hidden_near/pallas_call | solution.py:110
  160.9 1.3 copy-done.1
  162.3 8.1 %hidden_far.1 = (bf16[256,768]{1,0:T(8,128)(2,1)}, bf16[256,768]{1,0:T(8,128)(2,1)}, bf16[256,768]{1,0:T(8,128)(2,1)}, bf16[256,128]{1,0:T(8,128)(2,1)}) custom-call(bf16[256,4096]{1,0:T(8,128)(2,1)} %bitcast.40, bf16[256,4096]{1,0:T(8,128)(2,1)} %bitcast.41, bf16[2048,768]{1,0:T(8,128)(2,1)} %select_bitcast_fusion.2.wg_ref, ...), custom_call_target="tpu_custom_call" | custom-call | flops 2415919104 | bytes 12713984 | tf_op jit(solution)/shard_map/hidden_far/pallas_call | solution.py:110
  170.3 10.6 %theirs.1 = bf16[4,256,2304]{2,1,0:T(8,128)(2,1)} custom-call(s32[4]{0:T(128)} %add_add_fusion.where_ref, bf16[256,4096]{1,0:T(8,128)(2,1)} %bitcast.30, bf16[512,4096]{1,0:T(8,128)(2,1)} %bitcast.8.x_ref.do_ref.refs_1_.refs_4_, bf16[256,4096]{1,0:T(8,128)(2,1)} %bitcast.42, bf16[256,4096]{1,0:T(8,128)(2,1)} %bitcast.31, ...), custom_call_target="tpu_custom_call" | custom-call | flops 4831838208 | bytes 9437184 | tf_op jit(solution)/shard_map/theirs/pallas_call | solution.py:208
  181.0 0.0 collective-permute-start.9
  181.0 6.0 %dx_own.1.refs_0_ = bf16[16,64,2176]{2,1,0:T(8,128)(2,1)} custom-call(bf16[16,16,768]{2,1,0:T(8,128)(2,1)} %bitcast.56, bf16[16,16,768]{2,1,0:T(8,128)(2,1)} %bitcast.57, bf16[16,16,128]{2,1,0:T(8,128)(2,1)} %bitcast.61, bf16[2048,768]{1,0:T(8,128)(2,1)} %select_bitcast_fusion.2.wg_ref, bf16[2048,768]{1,0:T(8,128)(2,1)} %select_bitcast_fusion.1.wu_ref), custom_call_target="tpu_custom_call" | custom-call | flops 1610612736 | bytes 7340032 | tf_op jit(solution)/shard_map/dx_own/pallas_call | solution.py:151
  187.0 7.8 %dx_near.1.refs_0_ = bf16[16,64,2176]{2,1,0:T(8,128)(2,1)} custom-call(bf16[16,32,768]{2,1,0:T(8,128)(2,1)} %bitcast.52, bf16[16,32,768]{2,1,0:T(8,128)(2,1)} %bitcast.53, bf16[16,32,128]{2,1,0:T(8,128)(2,1)} %bitcast.60, bf16[2048,768]{1,0:T(8,128)(2,1)} %select_bitcast_fusion.2.wg_ref, ...), custom_call_target="tpu_custom_call", output_to_operand_aliasing={{}: (5, {})} | custom-call | flops 3221225472 | bytes 8388608 | tf_op jit(solution)/shard_map/dx_near/pallas_call | solution.py:151
  194.9 5.9 %dx_far.1 = bf16[16,64,2176]{2,1,0:T(8,128)(2,1)} custom-call(bf16[16,16,768]{2,1,0:T(8,128)(2,1)} %bitcast.58, bf16[16,16,768]{2,1,0:T(8,128)(2,1)} %bitcast.59, bf16[16,16,128]{2,1,0:T(8,128)(2,1)} %bitcast.62, bf16[2048,768]{1,0:T(8,128)(2,1)} %select_bitcast_fusion.2.wg_ref, ...), custom_call_target="tpu_custom_call", output_to_operand_aliasing={{}: (5, {})} | custom-call | flops 1610612736 | bytes 7340032 | tf_op jit(solution)/shard_map/dx_far/pallas_call | solution.py:151
  200.8 7.2 %all-to-all-start.3 = ((bf16[16,64,2176]{2,1,0:T(8,128)(2,1)}), bf16[16,64,2176]{2,1,0:T(8,128)(2,1)}, u32[]{:S(2)}, u32[]{:S(2)}) async-start(bf16[16,64,2176]{2,1,0:T(8,128)(2,1)} %dx_far.1), calls=%async_computation.3 | async-start | bytes 8912896 | tf_op jit(solution)/shard_map/all_to_all | solution.py:388
  208.0 5.5 %mine_1.1 = bf16[1,256,2304]{2,1,0:T(8,128)(2,1)} custom-call(s32[1]{0:T(128)S(6)} %add.99.where_ref, bf16[256,4096]{1,0:T(8,128)(2,1)} %bitcast.32, bf16[512,4096]{1,0:T(8,128)(2,1)} %bitcast.8.x_ref.do_ref.refs_1_.refs_4_, bf16[256,4096]{1,0:T(8,128)(2,1)} %bitcast.44, bf16[256,4096]{1,0:T(8,128)(2,1)} %bitcast.33, ...), custom_call_target="tpu_custom_call" | custom-call | flops 1207959552 | bytes 5898240 | tf_op jit(solution)/shard_map/mine_1/pallas_call | solution.py:208
  213.6 5.5 %mine_2.1 = bf16[1,256,2304]{2,1,0:T(8,128)(2,1)} custom-call(s32[1]{0:T(128)S(6)} %add.100.where_ref, bf16[256,4096]{1,0:T(8,128)(2,1)} %bitcast.34, bf16[512,4096]{1,0:T(8,128)(2,1)} %bitcast.8.x_ref.do_ref.refs_1_.refs_4_, bf16[256,4096]{1,0:T(8,128)(2,1)} %bitcast.46, bf16[256,4096]{1,0:T(8,128)(2,1)} %bitcast.35, ...), custom_call_target="tpu_custom_call" | custom-call | flops 1207959552 | bytes 5898240 | tf_op jit(solution)/shard_map/mine_2/pallas_call | solution.py:208
  219.1 2.2 collective-permute-start.11
  221.3 5.6 %mine_3.1 = bf16[1,256,2304]{2,1,0:T(8,128)(2,1)} custom-call(s32[1]{0:T(128)S(6)} %add.101.where_ref, bf16[256,4096]{1,0:T(8,128)(2,1)} %bitcast.36, bf16[512,4096]{1,0:T(8,128)(2,1)} %bitcast.8.x_ref.do_ref.refs_1_.refs_4_, bf16[256,4096]{1,0:T(8,128)(2,1)} %bitcast.48, bf16[256,4096]{1,0:T(8,128)(2,1)} %bitcast.37, ...), custom_call_target="tpu_custom_call" | custom-call | flops 1207959552 | bytes 5898240 | tf_op jit(solution)/shard_map/mine_3/pallas_call | solution.py:208
  226.9 2.5 collective-permute-start.12
  229.4 0.7 pad_add_fusion.1.index_ref
  230.1 5.5 %mine_0.1.refs_0_ = bf16[1,256,2304]{2,1,0:T(8,128)(2,1)} custom-call(s32[1]{0:T(128)S(6)} %add.90.where_ref, bf16[256,4096]{1,0:T(8,128)(2,1)} %bitcast.38, bf16[512,4096]{1,0:T(8,128)(2,1)} %bitcast.8.x_ref.do_ref.refs_1_.refs_4_, bf16[256,4096]{1,0:T(8,128)(2,1)} %bitcast.50, bf16[256,4096]{1,0:T(8,128)(2,1)} %bitcast.39, ...), custom_call_target="tpu_custom_call" | custom-call | flops 1207959552 | bytes 5898240 | tf_op jit(solution)/shard_map/mine_0/pallas_call | solution.py:208
  235.6 32.8 %collective-permute-done.10.refs_1_ = bf16[1,256,2304]{2,1,0:T(8,128)(2,1)S(1)} collective-permute-done((bf16[1,256,2304]{2,1,0:T(8,128)(2,1)}, bf16[1,256,2304]{2,1,0:T(8,128)(2,1)S(1)}, u32[]{:S(2)}, u32[]{:S(2)}) %collective-permute-start.10) | collective-permute-done | bytes 1179680 | tf_op jit(solution)/shard_map/ppermute | solution.py:385
  268.4 6.1 %collective-permute-done.12.refs_3_ = bf16[1,256,2304]{2,1,0:T(8,128)(2,1)S(1)} collective-permute-done((bf16[1,256,2304]{2,1,0:T(8,128)(2,1)}, bf16[1,256,2304]{2,1,0:T(8,128)(2,1)S(1)}, u32[]{:S(2)}, u32[]{:S(2)}) %collective-permute-start.12) | collective-permute-done | bytes 1179680 | tf_op jit(solution)/shard_map/ppermute | solution.py:385
  274.5 1.1 copy-done.8
  275.6 144.7 %pick.1 = (bf16[2,256,2304]{2,1,0:T(8,128)(2,1)}, bf16[2,256,2304]{2,1,0:T(8,128)(2,1)}) custom-call(s32[4]{0:T(128)} %pad_add_fusion.1.index_ref, bf16[1,256,2304]{2,1,0:T(8,128)(2,1)} %mine_0.1.refs_0_, bf16[1,256,2304]{2,1,0:T(8,128)(2,1)} %copy-done.6, bf16[1,256,2304]{2,1,0:T(8,128)(2,1)} %copy-done.7, bf16[1,256,2304]{2,1,0:T(8,128)(2,1)} %copy-done.8), custom_call_target="tpu_custom_call" | custom-call | tf_op jit(solution)/shard_map/pick/pallas_call | solution.py:239
  420.3 0.3 collective-permute-start.13
  420.7 7.6 %combine.1 = (bf16[128,2176]{1,0:T(8,128)(2,1)}, bf16[128,2176]{1,0:T(8,128)(2,1)}, bf16[128,2176]{1,0:T(8,128)(2,1)}, bf16[128,2176]{1,0:T(8,128)(2,1)}) custom-call(s32[1]{0:T(128)} %bitcast.plane_ref, bf16[16,64,2176]{2,1,0:T(8,128)(2,1)} %all-to-all-done.3.back_ref, bf16[128,4224]{1,0:T(8,128)(2,1)} %concatenate.3.refs_0_, bf16[128,4224]{1,0:T(8,128)(2,1)} %copy-done.3, ...), custom_call_target="tpu_custom_call" | custom-call | flops 570425344 | bytes 8912896 | tf_op jit(solution)/shard_map/combine/pallas_call | solution.py:336
  428.3 2.6 collective-permute-start.6
  430.9 1.5 collective-permute-start.8
  432.4 0.6 pad_add_fusion.where_ref
  433.0 22.7 %collective-permute-done.6.refs_1_ = bf16[128,2176]{1,0:T(8,128)(2,1)S(1)} collective-permute-done((bf16[128,2176]{1,0:T(8,128)(2,1)}, bf16[128,2176]{1,0:T(8,128)(2,1)S(1)}, u32[]{:S(2)}, u32[]{:S(2)}) %collective-permute-start.6) | collective-permute-done | bytes 557088 | tf_op jit(solution)/shard_map/ppermute | solution.py:385
  455.7 3.3 collective-permute-done.7.refs_2_
  459.0 0.8 copy-done.10
  459.8 0.2 copy-done.11
  460.0 2.9 finish.1
  462.9 1.4 copy.18
  464.3 1.4 copy-done.5
  465.7 7.6 %update.1 = (bf16[2,512,768]{2,1,0:T(8,128)(2,1)}, bf16[2,512,768]{2,1,0:T(8,128)(2,1)}, bf16[2,512,768]{2,1,0:T(8,128)(2,1)}) custom-call(s32[2]{0:T(128)} %pad_add_fusion.where_ref, s32[2,3]{1,0:T(2,128)} %mask_ref.1, bf16[2,256,2304]{2,1,0:T(8,128)(2,1)} %get-tuple-element.54.own_ref, bf16[2,256,2304]{2,1,0:T(8,128)(2,1)} %copy-done.5, ...), custom_call_target="tpu_custom_call" | custom-call | tf_op jit(solution)/shard_map/update/pallas_call | solution.py:281
  (33 shorter events, 0.1 us)
Async XLA Ops:
  0.6 126.6 %collective-permute-start.3 = (bf16[2,2048,768]{2,1,0:T(8,128)(2,1)}, bf16[2,2048,768]{2,1,0:T(8,128)(2,1)}, u32[]{:S(2)}, u32[]{:S(2)}) collective-permute-start(bf16[2,2048,768]{2,1,0:T(8,128)(2,1)} %refs_0_.1), channel_id=1, source_target_pairs={{0,1},{1,0},{2,3},{3,2},{4,5},{5,4},{6,7},{7,6},{8,9},{9,8},{10,11... | collective-permute-start | bytes 18874376 | tf_op jit(solution)/shard_map/ppermute | solution.py:401
  1.5 7.7 %copy-start.12 = (bf16[128,8]{1,0:T(8,128)(2,1)}, bf16[128,8]{1,0:T(8,128)(2,1)S(1)}, u32[]{:S(2)}) copy-start(bf16[128,8]{1,0:T(8,128)(2,1)S(1)} %copy.17.probs_ref) | copy-start | bytes 6148
  5.5 12.5 %copy-start.2 = (bf16[128,4224]{1,0:T(8,128)(2,1)S(1)}, bf16[128,4224]{1,0:T(8,128)(2,1)}, u32[]{:S(2)}) copy-start(bf16[128,4224]{1,0:T(8,128)(2,1)} %concatenate.3.refs_0_) | copy-start | bytes 3244036
  9.2 42.5 %all-to-all-start = ((bf16[16,16,4096]{2,1,0:T(8,128)(2,1)}), bf16[16,16,4096]{2,1,0:T(8,128)(2,1)S(1)}, u32[]{:S(2)}, u32[]{:S(2)}) async-start(bf16[16,16,4096]{2,1,0:T(8,128)(2,1)} %send_own.1), calls=%async_computation | async-start | bytes 4194304 | tf_op jit(solution)/shard_map/all_to_all | solution.py:388
  17.4 114.9 %collective-permute-start.4 = (bf16[2,2048,768]{2,1,0:T(8,128)(2,1)}, bf16[2,2048,768]{2,1,0:T(8,128)(2,1)}, u32[]{:S(2)}, u32[]{:S(2)}) collective-permute-start(bf16[2,2048,768]{2,1,0:T(8,128)(2,1)} %refs_1_.1), channel_id=1, source_target_pairs={{0,1},{1,0},{2,3},{3,2},{4,5},{5,4},{6,7},{7,6},{8,9},{9,8},{10,11... | collective-permute-start | bytes 18874376 | tf_op jit(solution)/shard_map/ppermute | solution.py:401
  17.6 119.6 %collective-permute-start.5 = (bf16[2,2048,768]{2,1,0:T(8,128)(2,1)}, bf16[2,2048,768]{2,1,0:T(8,128)(2,1)}, u32[]{:S(2)}, u32[]{:S(2)}) collective-permute-start(bf16[2,2048,768]{2,1,0:T(8,128)(2,1)} %refs_2_.1), channel_id=1, source_target_pairs={{0,1},{1,0},{2,3},{3,2},{4,5},{5,4},{6,7},{7,6},{8,9},{9,8},{10,11... | collective-permute-start | bytes 18874376 | tf_op jit(solution)/shard_map/ppermute | solution.py:401
  17.9 27.2 %collective-permute-start.1 = (bf16[128,4224]{1,0:T(8,128)(2,1)S(1)}, bf16[128,4224]{1,0:T(8,128)(2,1)S(1)}, u32[]{:S(2)}, u32[]{:S(2)}) collective-permute-start(bf16[128,4224]{1,0:T(8,128)(2,1)S(1)} %copy-done.2), channel_id=1, source_target_pairs={{0,32},{32,64},{64,96},{96,0},{1,33},{33,65},{65,97},{97,1},{2,34}... | collective-permute-start | bytes 3244040 | tf_op jit(solution)/shard_map/ppermute | solution.py:385
  19.4 26.7 %collective-permute-start.2 = (bf16[128,4224]{1,0:T(8,128)(2,1)S(1)}, bf16[128,4224]{1,0:T(8,128)(2,1)}, u32[]{:S(2)}, u32[]{:S(2)}) collective-permute-start(bf16[128,4224]{1,0:T(8,128)(2,1)S(1)} %copy-done.2), channel_id=1, source_target_pairs={{0,96},{32,0},{64,32},{96,64},{1,97},{33,1},{65,33},{97,65},{2,98}... | collective-permute-start | bytes 3244040 | tf_op jit(solution)/shard_map/ppermute | solution.py:385
  45.1 1.0 copy-start.3
  51.8 1.3 copy-start
  53.0 68.5 %all-to-all-start.1 = ((bf16[16,32,4096]{2,1,0:T(8,128)(2,1)}), bf16[16,32,4096]{2,1,0:T(8,128)(2,1)}, u32[]{:S(2)}, u32[]{:S(2)}) async-start(bf16[16,32,4096]{2,1,0:T(8,128)(2,1)} %send_near.1), calls=%async_computation.1 | async-start | bytes 8388608 | tf_op jit(solution)/shard_map/all_to_all | solution.py:388
  60.1 26.3 %collective-permute-start = (bf16[128,4224]{1,0:T(8,128)(2,1)S(1)}, bf16[128,4224]{1,0:T(8,128)(2,1)S(1)}, u32[]{:S(2)}, u32[]{:S(2)}) collective-permute-start(bf16[128,4224]{1,0:T(8,128)(2,1)S(1)} %copy-done.2), channel_id=1, source_target_pairs={{0,64},{32,96},{64,0},{96,32},{1,65},{33,97},{65,1},{97,33},{2,66}... | collective-permute-start | bytes 3244040 | tf_op jit(solution)/shard_map/ppermute | solution.py:385
  86.5 1.0 copy-start.4
  121.5 39.4 %all-to-all-start.2 = ((bf16[16,16,4096]{2,1,0:T(8,128)(2,1)}), bf16[16,16,4096]{2,1,0:T(8,128)(2,1)S(1)}, u32[]{:S(2)}, u32[]{:S(2)}) async-start(bf16[16,16,4096]{2,1,0:T(8,128)(2,1)} %send_far.1), calls=%async_computation.2 | async-start | bytes 4194304 | tf_op jit(solution)/shard_map/all_to_all | solution.py:388
  127.2 10.0 %slice-start = ((s8[6291456]{0:T(1024)(128)(4,1)}), s8[4194304]{0:T(1024)(128)(4,1)S(1)}, s32[]{:S(2)}) async-start(s8[6291456]{0:T(1024)(128)(4,1)} %bitcast.54), calls=%async_computation.4 | async-start | bytes 8388608
  132.2 5.0 %slice-start.1 = ((s8[6291456]{0:T(1024)(128)(4,1)}), s8[2097152]{0:T(1024)(128)(4,1)S(1)}, s32[]{:S(2)}) async-start(s8[6291456]{0:T(1024)(128)(4,1)} %bitcast.54), calls=%async_computation.5 | async-start | bytes 4194304
  160.9 1.3 copy-start.1
  181.0 27.0 %collective-permute-start.9 = (bf16[4,256,2304]{2,1,0:T(8,128)(2,1)}, bf16[4,256,2304]{2,1,0:T(8,128)(2,1)}, u32[]{:S(2)}, u32[]{:S(2)}) collective-permute-start(bf16[4,256,2304]{2,1,0:T(8,128)(2,1)} %theirs.1), channel_id=1, source_target_pairs={{0,1},{1,0},{2,3},{3,2},{4,5},{5,4},{6,7},{7,6},{8,9},{9,8},{10,11... | collective-permute-start | bytes 14155784 | tf_op jit(solution)/shard_map/ppermute | solution.py:429
  200.8 219.8 %all-to-all-start.3 = ((bf16[16,64,2176]{2,1,0:T(8,128)(2,1)}), bf16[16,64,2176]{2,1,0:T(8,128)(2,1)}, u32[]{:S(2)}, u32[]{:S(2)}) async-start(bf16[16,64,2176]{2,1,0:T(8,128)(2,1)} %dx_far.1), calls=%async_computation.3 | async-start | bytes 8912896 | tf_op jit(solution)/shard_map/all_to_all | solution.py:388
  213.6 54.8 %collective-permute-start.10 = (bf16[1,256,2304]{2,1,0:T(8,128)(2,1)}, bf16[1,256,2304]{2,1,0:T(8,128)(2,1)S(1)}, u32[]{:S(2)}, u32[]{:S(2)}) collective-permute-start(bf16[1,256,2304]{2,1,0:T(8,128)(2,1)} %mine_1.1), channel_id=1, source_target_pairs={{0,32},{32,64},{64,96},{96,0},{1,33},{33,65},{65,97},{97,1},{2,34}... | collective-permute-start | bytes 3538952 | tf_op jit(solution)/shard_map/ppermute | solution.py:385
  219.1 49.3 %collective-permute-start.11 = (bf16[1,256,2304]{2,1,0:T(8,128)(2,1)}, bf16[1,256,2304]{2,1,0:T(8,128)(2,1)S(1)}, u32[]{:S(2)}, u32[]{:S(2)}) collective-permute-start(bf16[1,256,2304]{2,1,0:T(8,128)(2,1)} %mine_2.1), channel_id=1, source_target_pairs={{0,64},{32,96},{64,0},{96,32},{1,65},{33,97},{65,1},{97,33},{2,66}... | collective-permute-start | bytes 3538952 | tf_op jit(solution)/shard_map/ppermute | solution.py:385
  226.9 47.6 %collective-permute-start.12 = (bf16[1,256,2304]{2,1,0:T(8,128)(2,1)}, bf16[1,256,2304]{2,1,0:T(8,128)(2,1)S(1)}, u32[]{:S(2)}, u32[]{:S(2)}) collective-permute-start(bf16[1,256,2304]{2,1,0:T(8,128)(2,1)} %mine_3.1), channel_id=1, source_target_pairs={{0,96},{32,0},{64,32},{96,64},{1,97},{33,1},{65,33},{97,65},{2,98}... | collective-permute-start | bytes 3538952 | tf_op jit(solution)/shard_map/ppermute | solution.py:385
  268.4 6.1 %copy-start.6 = (bf16[1,256,2304]{2,1,0:T(8,128)(2,1)}, bf16[1,256,2304]{2,1,0:T(8,128)(2,1)S(1)}, u32[]{:S(2)}) copy-start(bf16[1,256,2304]{2,1,0:T(8,128)(2,1)S(1)} %collective-permute-done.10.refs_1_) | copy-start | bytes 3538948
  268.4 6.1 %copy-start.7 = (bf16[1,256,2304]{2,1,0:T(8,128)(2,1)}, bf16[1,256,2304]{2,1,0:T(8,128)(2,1)S(1)}, u32[]{:S(2)}) copy-start(bf16[1,256,2304]{2,1,0:T(8,128)(2,1)S(1)} %collective-permute-done.11.refs_2_) | copy-start | bytes 3538948
  274.5 1.1 copy-start.8
  420.3 44.0 %collective-permute-start.13 = (bf16[2,256,2304]{2,1,0:T(8,128)(2,1)}, bf16[2,256,2304]{2,1,0:T(8,128)(2,1)S(1)}, u32[]{:S(2)}, u32[]{:S(2)}) collective-permute-start(bf16[2,256,2304]{2,1,0:T(8,128)(2,1)} %get-tuple-element.55), channel_id=1, source_target_pairs={{0,1},{1,0},{2,3},{3,2},{4,5},{5,4},{6,7},{7,6},{8,9},{9,8},{10,11... | collective-permute-start | bytes 7077896 | tf_op jit(solution)/shard_map/ppermute | solution.py:455
  428.3 27.4 %collective-permute-start.6 = (bf16[128,2176]{1,0:T(8,128)(2,1)}, bf16[128,2176]{1,0:T(8,128)(2,1)S(1)}, u32[]{:S(2)}, u32[]{:S(2)}) collective-permute-start(bf16[128,2176]{1,0:T(8,128)(2,1)} %get-tuple-element.46), channel_id=1, source_target_pairs={{0,96},{32,0},{64,32},{96,64},{1,97},{33,1},{65,33},{97,65},{2,98}... | collective-permute-start | bytes 1671176 | tf_op jit(solution)/shard_map/ppermute | solution.py:385
  430.9 28.1 %collective-permute-start.7 = (bf16[128,2176]{1,0:T(8,128)(2,1)}, bf16[128,2176]{1,0:T(8,128)(2,1)S(1)}, u32[]{:S(2)}, u32[]{:S(2)}) collective-permute-start(bf16[128,2176]{1,0:T(8,128)(2,1)} %get-tuple-element.47), channel_id=1, source_target_pairs={{0,32},{32,64},{64,96},{96,0},{1,33},{33,65},{65,97},{97,1},{2,34}... | collective-permute-start | bytes 1671176 | tf_op jit(solution)/shard_map/ppermute | solution.py:385
  430.9 28.1 %collective-permute-start.8 = (bf16[128,2176]{1,0:T(8,128)(2,1)}, bf16[128,2176]{1,0:T(8,128)(2,1)S(1)}, u32[]{:S(2)}, u32[]{:S(2)}) collective-permute-start(bf16[128,2176]{1,0:T(8,128)(2,1)} %get-tuple-element.48), channel_id=1, source_target_pairs={{0,64},{32,96},{64,0},{96,32},{1,65},{33,97},{65,1},{97,33},{2,66}... | collective-permute-start | bytes 1671176 | tf_op jit(solution)/shard_map/ppermute | solution.py:385
  455.7 3.3 copy-start.9
  459.0 0.8 copy-start.10
  459.0 1.0 copy-start.11
  464.3 1.4 copy-start.5

commit v3 on v2

--- a/solution.py
+++ b/solution.py
@@ -88,7 +88,8 @@
     )(plane, *packed)
 
 
-def hidden_kernel(x_ref, do_ref, wg_ref, wu_ref, wd_ref, hid_ref, da_ref, db_ref, s_ref):
+def hidden_kernel(x_ref, do_ref, wg_ref, wu_ref, wd_ref, hid_ref, da_ref, db_ref, s_ref, sum_ref):
+    step = pl.program_id(0)
     gate = dot(x_ref[...], wg_ref[...], NN)
     upper = dot(x_ref[...], wu_ref[...], NN)
     sig = jax.nn.sigmoid(gate)
@@ -96,30 +97,46 @@
     hid = (act * upper).astype(BF16)
     hid_ref[...] = hid
     dhid = dot(do_ref[...], wd_ref[...], NN)
-    total = jnp.sum(hid.astype(F32) * dhid, axis=1, keepdims=True)
-    high = total.astype(BF16).astype(F32)
-    lane = iota(s_ref.shape, 1)
-    s_ref[...] = jnp.where(lane == 0, high, jnp.where(lane == 1, total - high, 0.0)).astype(BF16)
+    part = jnp.sum(hid.astype(F32) * dhid, axis=1, keepdims=True)
     da_ref[...] = (dhid * upper * sig * (1.0 + gate * (1.0 - sig))).astype(BF16)
     db_ref[...] = (dhid * act).astype(BF16)
+
+    @pl.when(step == 0)
+    def _():
+        sum_ref[...] = jnp.broadcast_to(part, sum_ref.shape)
+
+    @pl.when(step > 0)
+    def _():
+        sum_ref[...] = sum_ref[...] + part
+
+    @pl.when(step == pl.num_programs(0) - 1)
+    def _():
+        total = sum_ref[...]
+        high = total.astype(BF16).astype(F32)
+        lane = iota(s_ref.shape, 1)
+        s_ref[...] = jnp.where(lane == 0, high, jnp.where(lane == 1, total - high, 0.0)).astype(BF16)
 
 
 def hidden_grads(name, rows, wg, wu, wd):
     n_rows, width = rows.shape[0], rows.shape[1] // 2
     hidden = wg.shape[1]
+    block = 2 * LANES
+    weight = pl.BlockSpec((width, block), lambda i: (0, i))
+    result = pl.BlockSpec((n_rows, block), lambda i: (0, i))
     return pl.pallas_call(
         hidden_kernel,
-        grid=(1,),
+        grid=(hidden // block,),
         in_specs=[
             pl.BlockSpec((n_rows, width), lambda i: (0, 0), pipeline_mode=pl.Buffered(1)),
             pl.BlockSpec((n_rows, width), lambda i: (0, 1), pipeline_mode=pl.Buffered(1)),
-            whole((width, hidden)),
-            whole((width, hidden)),
-            whole((width, hidden)),
+            weight,
+            weight,
+            weight,
         ],
-        out_specs=[whole((n_rows, hidden))] * 3 + [whole((n_rows, LANES))],
+        out_specs=[result] * 3 + [whole((n_rows, LANES))],
         out_shape=[jax.ShapeDtypeStruct((n_rows, hidden), BF16)] * 3
         + [jax.ShapeDtypeStruct((n_rows, LANES), BF16)],
+        scratch_shapes=[pltpu.VMEM((n_rows, LANES), F32)],
         compiler_params=params(32),
         cost_estimate=cost(6 * n_rows * width * hidden, 6 * width * hidden + n_rows * (4 * width + 6 * hidden)),
         name=name,
@@ -168,7 +185,7 @@
     )(split(da), split(db), split(s), wg, wu, *extra)
 
 
-def weight_kernel(n_chunk, with_sum, where_ref, *refs):
+def weight_kernel(n_chunk, where_ref, *refs):
     xs, dos = refs[:n_chunk], refs[n_chunk : 2 * n_chunk]
     hids, das, dbs = (refs[(2 + i) * n_chunk : (3 + i) * n_chunk] for i in range(3))
     rest = refs[5 * n_chunk :]
@@ -184,12 +201,12 @@
     for m, (lefts, rights) in enumerate(((xs, das), (xs, dbs), (dos, hids))):
         part = total(lefts, rights)
         lanes = slice(m * hidden, (m + 1) * hidden)
-        if with_sum:
-            part = part + rest[0][0, :, lanes].astype(F32)
+        for addend in rest[:-1]:
+            part = part + addend[0, :, lanes].astype(F32)
         out_ref[0, :, lanes] = part.astype(BF16)
 
 
-def weight_grads(name, where, steps, rows, hids, das, dbs, add=None, add_at=0):
+def weight_grads(name, where, steps, rows, hids, das, dbs, add=()):
     n_chunk = len(rows)
     width, hidden = rows[0].shape[1] // 2, hids[0].shape[1]
     half = width // 8
@@ -201,12 +218,12 @@
     in_specs = [columns(r, 0) for r in rows] + [columns(r, lefts) for r in rows]
     in_specs += [whole(a.shape) for a in hids + das + dbs]
     args = rows + rows + hids + das + dbs
-    if add is not None:
-        in_specs.append(pl.BlockSpec((1, half, 3 * hidden), lambda i, at: (i + add_at, 0, 0)))
-        args.append(add)
+    for addend, first in add:
+        in_specs.append(pl.BlockSpec((1, half, 3 * hidden), lambda i, at, first=first: (i + first, 0, 0)))
+        args.append(addend)
     total = sum(r.shape[0] for r in rows)
     return pl.pallas_call(
-        functools.partial(weight_kernel, n_chunk, add is not None),
+        functools.partial(weight_kernel, n_chunk),
         grid_spec=pltpu.PrefetchScalarGridSpec(
             num_scalar_prefetch=1,
             grid=(steps,),
@@ -220,58 +237,64 @@
     )(where, *args)
 
 
-def pick_kernel(n_out, index_ref, *refs):
-    sources, out_refs, sems = refs[: -n_out - 1], refs[-n_out - 1 : -1], refs[-1]
-    per = out_refs[0].shape[0]
-    for o in range(n_out * per):
-        for s, source in enumerate(sources):
-
-            @pl.when(index_ref[o] == s)
-            def _():
-                pltpu.make_async_copy(source.at[0], out_refs[o // per].at[o % per], sems.at[o]).start()
-
-    for o in range(n_out * per):
-        pltpu.make_async_copy(sources[0].at[0], out_refs[o // per].at[o % per], sems.at[o]).wait()
-
-
-def pick(index, sources, n_out, per):
-    shape = (per,) + sources[0].shape[1:]
-    return pl.pallas_call(
-        functools.partial(pick_kernel, n_out),
-        in_specs=[SMEM] + [ANY] * len(sources),
-        out_specs=[ANY] * n_out,
-        out_shape=[jax.ShapeDtypeStruct(shape, BF16)] * n_out,
-        scratch_shapes=[pltpu.SemaphoreType.DMA((n_out * per,))],
+def fetch(index, sources, target, sem):
+    for i, source in enumerate(sources):
+
+        @pl.when(index == i)
+        def _():
+            pltpu.make_async_copy(source.at[0], target, sem).start()
+
+    pltpu.make_async_copy(sources[0].at[0], target, sem).wait()
+
+
+def pick_kernel(index_ref, *refs):
+    fetch(index_ref[pl.program_id(0)], refs[:-2], refs[-2].at[0], refs[-1])
+
+
+def pick(index, sources, count):
+    _, half, lanes = sources[0].shape
+    return pl.pallas_call(
+        pick_kernel,
+        grid_spec=pltpu.PrefetchScalarGridSpec(
+            num_scalar_prefetch=1,
+            grid=(count,),
+            in_specs=[ANY] * len(sources),
+            out_specs=pl.BlockSpec((1, half, lanes), lambda j, w: (j, 0, 0)),
+            scratch_shapes=[pltpu.SemaphoreType.DMA],
+        ),
+        out_shape=jax.ShapeDtypeStruct((count, half, lanes), BF16),
         compiler_params=params(16),
         name="pick",
     )(index, *sources)
 
 
-def update_kernel(where_ref, mask_ref, own_ref, other_ref, *refs):
-    weights, outs = refs[:3], refs[3:]
+def update_kernel(n_source, where_ref, mask_ref, *refs):
+    sources, other_ref = refs[:n_source], refs[n_source]
+    weights, outs = refs[n_source + 1 : n_source + 4], refs[n_source + 4 : n_source + 7]
+    own_ref, sem = refs[-2:]
     hidden = weights[0].shape[2]
     j = pl.program_id(1)
 
-    def write(grad_ref):
+    def write(grad_ref, *lead):
         for m in range(3):
             rate = mask_ref[j, m].astype(F32)
             weight = weights[m][0].astype(F32)
-            grad = grad_ref[0, :, m * hidden : (m + 1) * hidden].astype(F32)
+            grad = grad_ref[(*lead, slice(None), slice(m * hidden, (m + 1) * hidden))].astype(F32)
             outs[m][0] = (weight - step_size * grad - shrink_rate * rate * weight).astype(BF16)
 
     @pl.when(pl.program_id(0) == 0)
     def _():
+        fetch(where_ref[2 + j], sources, own_ref, sem)
         write(own_ref)
 
     @pl.when(pl.program_id(0) == 1)
     def _():
-        write(other_ref)
-
-
-def update(where, mask, own, other, weights, shard_rows):
-    local, half, _ = own.shape
+        write(other_ref, 0)
+
+
+def update(where, mask, sources, other, weights, shard_rows):
+    local, half, _ = other.shape
     hidden = weights[0].shape[2]
-    last = local - 1
 
     def at(h, w):
         return w[0] * (1 - h) + (1 - w[0]) * h
@@ -279,22 +302,21 @@
     weight = pl.BlockSpec((1, half, hidden), lambda h, j, w: (j, CORES * w[1] + at(h, w), 0))
     result = pl.BlockSpec((1, half, hidden), lambda h, j, w: (j, at(h, w), 0))
     return pl.pallas_call(
-        update_kernel,
+        functools.partial(update_kernel, len(sources)),
         grid_spec=pltpu.PrefetchScalarGridSpec(
             num_scalar_prefetch=1,
             grid=(CORES, local),
-            in_specs=[
-                SMEM,
-                pl.BlockSpec((1, half, 3 * hidden), lambda h, j, w: (j * (1 - h) + last * h, 0, 0)),
-                pl.BlockSpec((1, half, 3 * hidden), lambda h, j, w: (j * h, 0, 0)),
-            ]
+            in_specs=[SMEM]
+            + [ANY] * len(sources)
+            + [pl.BlockSpec((1, half, 3 * hidden), lambda h, j, w: (j * h, 0, 0))]
             + [weight] * 3,
             out_specs=[result] * 3,
+            scratch_shapes=[pltpu.VMEM((half, 3 * hidden), BF16), pltpu.SemaphoreType.DMA],
         ),
         out_shape=[jax.ShapeDtypeStruct((local, shard_rows, hidden), BF16)] * 3,
         compiler_params=params(32),
         name="update",
-    )(where, mask, own, other, *weights)
+    )(where, mask, *sources, other, *weights)
 
 
 def combine_kernel(topk, capacity, stride, plane_ref, back_ref, *refs):
@@ -391,9 +413,9 @@
         [expert_ids.astype(BF16), route_probs, jnp.zeros((tok_rows, LANES - 2 * topk), BF16)], axis=1
     )
     packed = jnp.concatenate([tokens, out_grad, meta], axis=1)
-    near, far = (1, n_group - 1), (2,)
-    from_near = [across(packed, r) for r in near]
-    from_far = [across(packed, r) for r in far]
+    shifts = (1, n_group - 1, 2)
+    moved = [across(packed, r) for r in shifts]
+    from_near, from_far = moved[:2], moved[2:]
 
     mine = core == p // local_exp
     weights = []
@@ -401,60 +423,61 @@
         other = lax.ppermute(w, "expert", other_core)
         pick_of = functools.partial(lax.dynamic_index_in_dim, index=p % local_exp, axis=0, keepdims=False)
         weights.append(jnp.where(mine, pick_of(w), pick_of(other)))
-    wg, wu, wd = weights
-
-    got = []
-    for name, chunk in (("own", [packed]), ("near", from_near), ("far", from_far)):
-        if got:
-            chunk = list(chunk)
-            chunk[0], got[-1] = lax.optimization_barrier((chunk[0], got[-1])) if False else (chunk[0], got[-1])
-        rows = dispatch("send_" + name, plane, chunk, n_chip, topk, capacity, stride, width)
-        if got:
-            rows, got[-1] = lax.optimization_barrier((rows, got[-1]))
-        got.append(exchange(rows))
-
-    rows, hids, das, dbs, sums = [], [], [], [], []
-    for name, part in zip(("own", "near", "far"), got):
-        part = part.reshape(-1, 2 * width)
-        hid, da, db, s = hidden_grads("hidden_" + name, part, wg, wu, wd)
-        rows.append(part)
-        hids.append(hid)
-        das.append(da)
-        dbs.append(db)
-        sums.append(s)
-
+
+    def send(name, chunk):
+        return dispatch("send_" + name, plane, chunk, n_chip, topk, capacity, stride, width)
+
+    def flat(part):
+        return part.reshape(-1, 2 * width)
+
+    def hidden_of(name, part):
+        return hidden_grads("hidden_" + name, part, *weights)
+
+    def dx_of(name, grads, first, into):
+        _, da, db, s = grads
+        return input_grads("dx_" + name, da, db, s, weights[0], weights[1], n_chip, capacity, n_group, first, into)
+
+    got_own = exchange(send("own", [packed]))
+    to_near, got_own = lax.optimization_barrier((send("near", from_near), got_own))
+    got_near = exchange(to_near)
+    own = flat(got_own)
+    own_grads = hidden_of("own", own)
+    dx = dx_of("own", own_grads, 0, None)
+    to_far, got_near, dx, *own_grads = lax.optimization_barrier((send("far", from_far), got_near, dx, *own_grads))
+    got_far = exchange(to_far)
+    near = flat(got_near)
+    near_grads = hidden_of("near", near)
+    dx = dx_of("near", near_grads, 1, dx)
     order = (2, 1, n_group - 1, 0)
     blocks = jnp.stack([CORES * ((p + r) % n_group) for r in order]).astype(jnp.int32)
-    theirs = weight_grads("theirs", blocks + (1 - core), n_group, rows, hids, das, dbs)
+    both = jnp.concatenate([blocks + (1 - core), blocks + core])
+    hids, das, dbs = ([own_grads[i], near_grads[i]] for i in range(3))
+    partial = weight_grads("partial", both, CORES * n_group, [own, near], hids, das, dbs)
+    got_far, partial, dx = lax.optimization_barrier((got_far, partial, dx))
+    last = flat(got_far)
+    far_grads = hidden_of("far", last)
+    hids, das, dbs = ([a] for a in far_grads[:3])
+    theirs = weight_grads("theirs", blocks + (1 - core), n_group, [last], hids, das, dbs, [(partial, 0)])
     added = lax.ppermute(theirs, "expert", other_core)
-
-    dx, first = None, 0
-    for i, name in enumerate(("own", "near", "far")):
-        dx = input_grads("dx_" + name, das[i], dbs[i], sums[i], wg, wu, n_chip, capacity, n_group, first, dx)
-        first += rows[i].shape[0] // (n_chip * capacity)
-    back = exchange(dx)
+    back = exchange(dx_of("far", far_grads, 3, dx))
 
     landed = [None] * n_group
     for i, r in enumerate(order):
-        block = weight_grads(
-            f"mine_{r}", blocks[i : i + 1] + core, 1, rows, hids, das, dbs, added, i
-        )
+        add = [(partial, n_group + i), (added, i)]
+        block = weight_grads(f"mine_{r}", blocks[i : i + 1] + core, 1, [last], hids, das, dbs, add)
         landed[r] = across(block, r) if r else block
 
     parts = combine(plane, back, [packed] + from_near + from_far, topk, capacity, stride)
-    home = [parts[0]] + [across(a, n_group - r) for a, r in zip(parts[1:], near + far)]
+    home = [parts[0]] + [across(a, n_group - r) for a, r in zip(parts[1:], shifts)]
     grad_tokens, grad_probs = finish(route_probs, home, width)
 
     def source(owner, j):
         return (p - (local_exp * owner + j)) % n_group
 
-    index = jnp.stack(
-        [source(1 - core, j) for j in range(local_exp)] + [source(core, j) for j in range(local_exp)]
-    ).astype(jnp.int32)
-    outgoing, own = pick(index, landed, 2, local_exp)
-    other = lax.ppermute(outgoing, "expert", other_core)
-    where = jnp.stack([core, p]).astype(jnp.int32)
-    new = update(where, decay_mask, own, other, (w_gate, w_up, w_down), shard_rows)
+    index = jnp.stack([source(1 - core, j) for j in range(local_exp)]).astype(jnp.int32)
+    other = lax.ppermute(pick(index, landed, local_exp), "expert", other_core)
+    where = jnp.stack([core, p] + [source(core, j) for j in range(local_exp)]).astype(jnp.int32)
+    new = update(where, decay_mask, landed, other, (w_gate, w_up, w_down), shard_rows)
     return (grad_tokens, grad_probs, *new)
 
 

time: 474 us -> 316 us (0.67)
  Pallas kernels: 256 us -> 122 us
  waiting for transfers between devices: 144 us -> 123 us
    pallas_call x10 -> x11, Pallas kernels: 213 us -> 78.8 us  [the longest x6 36.9 us: weight_grads(): pl.pallas_call(functools.partial(weight_kernel, n_chunk), grid_spec=pltpu...]
    all_to_all x4, waiting for transfers between devices: 30.5 us -> 2.19 us  [exchange(): lax.all_to_all(a, 'expert', 0, 0, axis_index_groups=same_core, tiled=True)]
    ppermute x9, waiting for transfers between devices: 113 us -> 121 us  [across(): lax.ppermute(a, 'dp', [(i, (i + r) % n_group) for i in range(n_group)])]
    unnamed x32 -> x36, local copies, waits for them, and re-layouts: 10.3 us -> 10.3 us
  transfers between devices with their start and end apart: 18 -> 18, of which waited for: 7 -> 9; matrix products, arithmetic and copies ran while one was open for 5% -> 7% of each run, Pallas kernels for 49% -> 31%
where the time goes in v3:
time: 316 us; the launch traced here: 315 us
  waiting for transfers between devices  123 us (39%)
  Pallas kernels  122 us (39%)
  starting transfers between devices  39.2 us (12%)
  other arithmetic  16.1 us (5%)
  local copies, waits for them, and re-layouts  13.5 us (4%)
    ppermute x9, waiting for transfers between devices, across(): lax.ppermute(a, 'dp', [(i, (i + r) % n_group) for i in range(n_group)])  121 us
    pallas_call x6, Pallas kernels, weight_grads(): pl.pallas_call(functools.partial(weight_kernel, n_chunk), grid_spec=pltpu...  36.9 us
    all_to_all x4, starting transfers between devices, exchange(): lax.all_to_all(a, 'expert', 0, 0, axis_index_groups=same_core, tiled=True)  27 us
    pallas_call x3, Pallas kernels, hidden_grads(): pl.pallas_call(hidden_kernel, grid=(hidden // block,), in_specs=[pl.Block...  26.4 us
    pallas_call x3, Pallas kernels, input_grads(): pl.pallas_call(dx_kernel, grid=(count,), in_specs=[group(hidden, 0), grou...  19.8 us
    select_n x3, other arithmetic, body(): weights.append(jnp.where(mine, pick_of(w), pick_of(other)))  13.4 us
    pallas_call x3, Pallas kernels, dispatch(): pl.pallas_call(functools.partial(dispatch_kernel, topk, capacity, stride)...  13.2 us
    ppermute x9, starting transfers between devices, across(): lax.ppermute(a, 'dp', [(i, (i + r) % n_group) for i in range(n_group)])  11.2 us
  transfers between devices with their start and end apart: 18, of which 9 were waited for; matrix products, arithmetic and copies ran while one was open for 7% of the time, Pallas kernels for 31%

profile of v3, /device:TPU:0, one launch (start us, length us, event | category | flops | bytes accessed | tf_op | source)
XLA Modules:
  0.0 315.0 jit_solution(10528862964833487065)
XLA Ops:
  0.6 0.1 collective-permute-start.3
  0.7 0.5 collective-permute-start.4
  1.2 0.1 collective-permute-start.5
  1.3 0.7 convert_element_type.3
  2.0 0.1 copy.15
  2.1 0.8 copy.17.probs_ref
  3.0 3.1 concatenate.6.refs_0_
  6.1 3.8 %send_own.1 = bf16[16,16,4096]{2,1,0:T(8,128)(2,1)} custom-call(s32[1]{0:T(128)} %bitcast.plane_ref, bf16[128,4224]{1,0:T(8,128)(2,1)} %concatenate.6.refs_0_), custom_call_target="tpu_custom_call" | custom-call | flops 268435456 | bytes 4194304 | tf_op jit(solution)/shard_map/send_own/pallas_call | solution.py:81
  9.8 8.1 %all-to-all-start = ((bf16[16,16,4096]{2,1,0:T(8,128)(2,1)}), bf16[16,16,4096]{2,1,0:T(8,128)(2,1)S(1)}, u32[]{:S(2)}, u32[]{:S(2)}) async-start(bf16[16,16,4096]{2,1,0:T(8,128)(2,1)} %send_own.1), calls=%async_computation | async-start | bytes 4194304 | tf_op jit(solution)/shard_map/all_to_all | solution.py:410
  18.0 2.8 collective-permute-start.2
  20.8 23.4 %collective-permute-done.2.refs_1_.refs_2_ = bf16[128,4224]{1,0:T(8,128)(2,1)S(1)} collective-permute-done((bf16[128,4224]{1,0:T(8,128)(2,1)S(1)}, bf16[128,4224]{1,0:T(8,128)(2,1)S(1)}, u32[]{:S(2)}, u32[]{:S(2)}) %collective-permute-start.2) | collective-permute-done | bytes 1081376 | tf_op jit(solution)/shard_map/ppermute | solution.py:407
  44.2 1.0 copy-done.6
  45.2 2.5 collective-permute-done.1.refs_0_.refs_1_
  47.7 5.6 %send_near.1 = bf16[16,32,4096]{2,1,0:T(8,128)(2,1)} custom-call(s32[1]{0:T(128)} %bitcast.plane_ref, bf16[128,4224]{1,0:T(8,128)(2,1)} %collective-permute-done.1.refs_0_.refs_1_, bf16[128,4224]{1,0:T(8,128)(2,1)} %copy-done.6), custom_call_target="tpu_custom_call" | custom-call | flops 536870912 | bytes 8388608 | tf_op jit(solution)/shard_map/send_near/pallas_call | solution.py:81
  53.4 1.4 copy-done.1
  54.7 7.0 %all-to-all-start.1 = ((bf16[16,32,4096]{2,1,0:T(8,128)(2,1)}), bf16[16,32,4096]{2,1,0:T(8,128)(2,1)}, u32[]{:S(2)}, u32[]{:S(2)}) async-start(bf16[16,32,4096]{2,1,0:T(8,128)(2,1)} %send_near.1), calls=%async_computation.1 | async-start | bytes 8388608 | tf_op jit(solution)/shard_map/all_to_all | solution.py:410
  61.7 0.3 collective-permute-start
  62.0 25.4 %collective-permute-done.refs_0_.refs_3_ = bf16[128,4224]{1,0:T(8,128)(2,1)S(1)} collective-permute-done((bf16[128,4224]{1,0:T(8,128)(2,1)S(1)}, bf16[128,4224]{1,0:T(8,128)(2,1)S(1)}, u32[]{:S(2)}, u32[]{:S(2)}) %collective-permute-start) | collective-permute-done | bytes 1081376 | tf_op jit(solution)/shard_map/ppermute | solution.py:407
  87.5 1.0 copy-done.7
  88.5 3.8 %send_far.1 = bf16[16,16,4096]{2,1,0:T(8,128)(2,1)} custom-call(s32[1]{0:T(128)} %bitcast.plane_ref, bf16[128,4224]{1,0:T(8,128)(2,1)} %copy-done.7), custom_call_target="tpu_custom_call" | custom-call | flops 268435456 | bytes 4194304 | tf_op jit(solution)/shard_map/send_far/pallas_call | solution.py:81
  92.3 4.9 %select_bitcast_fusion.2.wg_ref = bf16[2048,768]{1,0:T(8,128)(2,1)} fusion(bf16[2,2048,768]{2,1,0:T(8,128)(2,1)} %collective-permute-done.3, s32[]{:T(128)S(6)} %select_n.86, bf16[2,2048,768]{2,1,0:T(8,128)(2,1)} %refs_5_.1, pred[]{:T(512)S(6)} %eq.16), kind=kLoop, calls=%fused_computation.2 | loop fusion | flops 1572864 | bytes 9437189 | tf_op jit(solution)/shard_map/jit(_where)/select_n | solution.py:425
  97.2 0.0 collective-permute-done.4
  97.2 4.5 %select_bitcast_fusion.1.wu_ref = bf16[2048,768]{1,0:T(8,128)(2,1)} fusion(bf16[2,2048,768]{2,1,0:T(8,128)(2,1)} %collective-permute-done.4, s32[]{:T(128)S(6)} %select_n.86, bf16[2,2048,768]{2,1,0:T(8,128)(2,1)S(1)} %bitcast.45, pred[]{:T(512)S(6)} %eq.16), kind=kLoop, calls=%fused_computation.1 | loop fusion | flops 1572864 | bytes 9437189 | tf_op jit(solution)/shard_map/jit(_where)/select_n | solution.py:425
  101.7 0.0 collective-permute-done.5
  101.7 4.0 %select_bitcast_fusion.wd_ref = bf16[2048,768]{1,0:T(8,128)(2,1)} fusion(bf16[2,2048,768]{2,1,0:T(8,128)(2,1)} %collective-permute-done.5, s32[]{:T(128)S(6)} %select_n.86, bf16[2,2048,768]{2,1,0:T(8,128)(2,1)S(1)} %bitcast.47, pred[]{:T(512)S(6)} %eq.16), kind=kLoop, calls=%fused_computation | loop fusion | flops 1572864 | bytes 9437189 | tf_op jit(solution)/shard_map/jit(_where)/select_n | solution.py:425
  105.7 7.9 %hidden_own.1 = (bf16[256,768]{1,0:T(8,128)(2,1)}, bf16[256,768]{1,0:T(8,128)(2,1)}, bf16[256,768]{1,0:T(8,128)(2,1)}, bf16[256,128]{1,0:T(8,128)(2,1)}) custom-call(bf16[256,4096]{1,0:T(8,128)(2,1)} %bitcast.40, bf16[256,4096]{1,0:T(8,128)(2,1)} %bitcast.41, bf16[2048,768]{1,0:T(8,128)(2,1)} %select_bitcast_fusion.2.wg_ref, ...), custom_call_target="tpu_custom_call" | custom-call | flops 2415919104 | bytes 12713984 | tf_op jit(solution)/shard_map/hidden_own/pallas_call | solution.py:126
  113.7 6.0 %dx_own.1.refs_0_ = bf16[16,64,2176]{2,1,0:T(8,128)(2,1)} custom-call(bf16[16,16,768]{2,1,0:T(8,128)(2,1)} %bitcast.52, bf16[16,16,768]{2,1,0:T(8,128)(2,1)} %bitcast.53, bf16[16,16,128]{2,1,0:T(8,128)(2,1)} %bitcast.56, bf16[2048,768]{1,0:T(8,128)(2,1)} %select_bitcast_fusion.2.wg_ref, bf16[2048,768]{1,0:T(8,128)(2,1)} %select_bitcast_fusion.1.wu_ref), custom_call_target="tpu_custom_call" | custom-call | flops 1610612736 | bytes 7340032 | tf_op jit(solution)/shard_map/dx_own/pallas_call | solution.py:168
  119.6 2.2 all-to-all-done.1
  121.8 4.6 %all-to-all-start.2 = ((bf16[16,16,4096]{2,1,0:T(8,128)(2,1)}), bf16[16,16,4096]{2,1,0:T(8,128)(2,1)S(1)}, u32[]{:S(2)}, u32[]{:S(2)}) async-start(bf16[16,16,4096]{2,1,0:T(8,128)(2,1)} %send_far.1), calls=%async_computation.2 | async-start | bytes 4194304 | tf_op jit(solution)/shard_map/all_to_all | solution.py:410
  126.5 0.1 broadcast_add_fusion.1
  126.6 0.6 pad_add_fusion.1.where_ref
  127.2 10.6 %hidden_near.1 = (bf16[512,768]{1,0:T(8,128)(2,1)}, bf16[512,768]{1,0:T(8,128)(2,1)}, bf16[512,768]{1,0:T(8,128)(2,1)}, bf16[512,128]{1,0:T(8,128)(2,1)}) custom-call(bf16[512,4096]{1,0:T(8,128)(2,1)} %bitcast.12.x_ref.do_ref.refs_1_.refs_3_, bf16[512,4096]{1,0:T(8,128)(2,1)} %bitcast.12.x_ref.do_ref.refs_1_.refs_3_, ...), custom_call_target="tpu_custom_call" | custom-call | flops 4831838208 | bytes 15990784 | tf_op jit(solution)/shard_map/hidden_near/pallas_call | solution.py:126
  137.9 7.9 %dx_near.1.refs_0_ = bf16[16,64,2176]{2,1,0:T(8,128)(2,1)} custom-call(bf16[16,32,768]{2,1,0:T(8,128)(2,1)} %bitcast.50, bf16[16,32,768]{2,1,0:T(8,128)(2,1)} %bitcast.51, bf16[16,32,128]{2,1,0:T(8,128)(2,1)} %bitcast.54, bf16[2048,768]{1,0:T(8,128)(2,1)} %select_bitcast_fusion.2.wg_ref, ...), custom_call_target="tpu_custom_call", output_to_operand_aliasing={{}: (5, {})} | custom-call | flops 3221225472 | bytes 8388608 | tf_op jit(solution)/shard_map/dx_near/pallas_call | solution.py:168
  145.8 14.6 %partial.1.refs_5_ = bf16[8,256,2304]{2,1,0:T(8,128)(2,1)} custom-call(s32[8]{0:T(128)} %pad_add_fusion.1.where_ref, bf16[256,4096]{1,0:T(8,128)(2,1)} %bitcast.42, bf16[512,4096]{1,0:T(8,128)(2,1)} %bitcast.12.x_ref.do_ref.refs_1_.refs_3_, bf16[256,4096]{1,0:T(8,128)(2,1)} %bitcast.43, bf16[512,4096]{1,0:T(8,128)(2,1)} %bitcast.12.x_ref.do_ref.refs_1_.refs_3_, ...), custom_call_target="tpu_custom_call" | custom-call | flops 7247757312 | bytes 12976128 | tf_op jit(solution)/shard_map/partial/pallas_call | solution.py:225
  160.4 0.0 all-to-all-done.2
  160.4 1.4 copy-done
  161.9 7.9 %hidden_far.1 = (bf16[256,768]{1,0:T(8,128)(2,1)}, bf16[256,768]{1,0:T(8,128)(2,1)}, bf16[256,768]{1,0:T(8,128)(2,1)}, bf16[256,128]{1,0:T(8,128)(2,1)}) custom-call(bf16[256,4096]{1,0:T(8,128)(2,1)} %bitcast.28, bf16[256,4096]{1,0:T(8,128)(2,1)} %bitcast.29, bf16[2048,768]{1,0:T(8,128)(2,1)} %select_bitcast_fusion.2.wg_ref, ...), custom_call_target="tpu_custom_call" | custom-call | flops 2415919104 | bytes 12713984 | tf_op jit(solution)/shard_map/hidden_far/pallas_call | solution.py:126
  169.8 7.3 %theirs.1 = bf16[4,256,2304]{2,1,0:T(8,128)(2,1)} custom-call(s32[4]{0:T(128)} %copy-done.12, bf16[256,4096]{1,0:T(8,128)(2,1)} %bitcast.30, bf16[256,4096]{1,0:T(8,128)(2,1)} %bitcast.31, bf16[256,768]{1,0:T(8,128)(2,1)} %get-tuple-element.64.refs_2_, bf16[256,768]{1,0:T(8,128)(2,1)} %get-tuple-element.54.refs_3_, ...), custom_call_target="tpu_custom_call" | custom-call | flops 1207959552 | bytes 5898240 | tf_op jit(solution)/shard_map/theirs/pallas_call | solution.py:225
  177.1 6.0 %dx_far.1 = bf16[16,64,2176]{2,1,0:T(8,128)(2,1)} custom-call(bf16[16,16,768]{2,1,0:T(8,128)(2,1)} %bitcast.48, bf16[16,16,768]{2,1,0:T(8,128)(2,1)} %bitcast.49, bf16[16,16,128]{2,1,0:T(8,128)(2,1)} %bitcast.55, bf16[2048,768]{1,0:T(8,128)(2,1)} %select_bitcast_fusion.2.wg_ref, ...), custom_call_target="tpu_custom_call", output_to_operand_aliasing={{}: (5, {})} | custom-call | flops 1610612736 | bytes 7340032 | tf_op jit(solution)/shard_map/dx_far/pallas_call | solution.py:168
  183.1 7.2 %all-to-all-start.3 = ((bf16[16,64,2176]{2,1,0:T(8,128)(2,1)}), bf16[16,64,2176]{2,1,0:T(8,128)(2,1)}, u32[]{:S(2)}, u32[]{:S(2)}) async-start(bf16[16,64,2176]{2,1,0:T(8,128)(2,1)} %dx_far.1), calls=%async_computation.3 | async-start | bytes 8912896 | tf_op jit(solution)/shard_map/all_to_all | solution.py:410
  190.3 3.7 %mine_1.1 = bf16[1,256,2304]{2,1,0:T(8,128)(2,1)} custom-call(s32[1]{0:T(128)S(6)} %add.106.where_ref, bf16[256,4096]{1,0:T(8,128)(2,1)} %bitcast.32, bf16[256,4096]{1,0:T(8,128)(2,1)} %bitcast.33, bf16[256,768]{1,0:T(8,128)(2,1)} %get-tuple-element.64.refs_2_, bf16[256,768]{1,0:T(8,128)(2,1)} %get-tuple-element.54.refs_3_, ...), custom_call_target="tpu_custom_call" | custom-call | flops 301989888 | bytes 2359296 | tf_op jit(solution)/shard_map/mine_1/pallas_call | solution.py:225
  194.1 3.7 %mine_2.1 = bf16[1,256,2304]{2,1,0:T(8,128)(2,1)} custom-call(s32[1]{0:T(128)S(6)} %add.107.where_ref, bf16[256,4096]{1,0:T(8,128)(2,1)} %bitcast.34, bf16[256,4096]{1,0:T(8,128)(2,1)} %bitcast.35, bf16[256,768]{1,0:T(8,128)(2,1)} %get-tuple-element.64.refs_2_, bf16[256,768]{1,0:T(8,128)(2,1)} %get-tuple-element.54.refs_3_, ...), custom_call_target="tpu_custom_call" | custom-call | flops 301989888 | bytes 2359296 | tf_op jit(solution)/shard_map/mine_2/pallas_call | solution.py:225
  197.8 3.2 %collective-permute-start.11 = (bf16[1,256,2304]{2,1,0:T(8,128)(2,1)}, bf16[1,256,2304]{2,1,0:T(8,128)(2,1)S(1)}, u32[]{:S(2)}, u32[]{:S(2)}) collective-permute-start(bf16[1,256,2304]{2,1,0:T(8,128)(2,1)} %mine_2.1), channel_id=1, source_target_pairs={{0,64},{32,96},{64,0},{96,32},{1,65},{33,97},{65,1},{97,33},{2,66}... | collective-permute-start | bytes 3538952 | tf_op jit(solution)/shard_map/ppermute | solution.py:407
  201.0 3.7 %mine_3.1 = bf16[1,256,2304]{2,1,0:T(8,128)(2,1)} custom-call(s32[1]{0:T(128)S(6)} %add.108.where_ref, bf16[256,4096]{1,0:T(8,128)(2,1)} %bitcast.36, bf16[256,4096]{1,0:T(8,128)(2,1)} %bitcast.37, bf16[256,768]{1,0:T(8,128)(2,1)} %get-tuple-element.64.refs_2_, bf16[256,768]{1,0:T(8,128)(2,1)} %get-tuple-element.54.refs_3_, ...), custom_call_target="tpu_custom_call" | custom-call | flops 301989888 | bytes 2359296 | tf_op jit(solution)/shard_map/mine_3/pallas_call | solution.py:225
  204.7 0.7 collective-permute-start.12
  205.4 0.7 pad_add_fusion.3.index_ref
  206.0 3.8 %mine_0.1.refs_0_ = bf16[1,256,2304]{2,1,0:T(8,128)(2,1)} custom-call(s32[1]{0:T(128)S(6)} %add.105.where_ref, bf16[256,4096]{1,0:T(8,128)(2,1)} %bitcast.38, bf16[256,4096]{1,0:T(8,128)(2,1)} %bitcast.39, bf16[256,768]{1,0:T(8,128)(2,1)} %get-tuple-element.64.refs_2_, bf16[256,768]{1,0:T(8,128)(2,1)} %get-tuple-element.54.refs_3_, ...), custom_call_target="tpu_custom_call" | custom-call | flops 301989888 | bytes 2359296 | tf_op jit(solution)/shard_map/mine_0/pallas_call | solution.py:225
  209.8 14.5 %collective-permute-done.10.refs_1_ = bf16[1,256,2304]{2,1,0:T(8,128)(2,1)S(1)} collective-permute-done((bf16[1,256,2304]{2,1,0:T(8,128)(2,1)}, bf16[1,256,2304]{2,1,0:T(8,128)(2,1)S(1)}, u32[]{:S(2)}, u32[]{:S(2)}) %collective-permute-start.10) | collective-permute-done | bytes 1179680 | tf_op jit(solution)/shard_map/ppermute | solution.py:407
  224.3 24.6 %collective-permute-done.11.refs_2_ = bf16[1,256,2304]{2,1,0:T(8,128)(2,1)S(1)} collective-permute-done((bf16[1,256,2304]{2,1,0:T(8,128)(2,1)}, bf16[1,256,2304]{2,1,0:T(8,128)(2,1)S(1)}, u32[]{:S(2)}, u32[]{:S(2)}) %collective-permute-start.11) | collective-permute-done | bytes 1179680 | tf_op jit(solution)/shard_map/ppermute | solution.py:407
  248.8 4.3 %collective-permute-done.12.refs_3_ = bf16[1,256,2304]{2,1,0:T(8,128)(2,1)S(1)} collective-permute-done((bf16[1,256,2304]{2,1,0:T(8,128)(2,1)}, bf16[1,256,2304]{2,1,0:T(8,128)(2,1)S(1)}, u32[]{:S(2)}, u32[]{:S(2)}) %collective-permute-start.12) | collective-permute-done | bytes 1179680 | tf_op jit(solution)/shard_map/ppermute | solution.py:407
  253.2 1.0 copy-done.5
  254.2 4.7 %pick.1 = bf16[2,256,2304]{2,1,0:T(8,128)(2,1)} custom-call(s32[2]{0:T(128)} %pad_add_fusion.3.index_ref, bf16[1,256,2304]{2,1,0:T(8,128)(2,1)} %mine_0.1.refs_0_, bf16[1,256,2304]{2,1,0:T(8,128)(2,1)} %copy-done.3, bf16[1,256,2304]{2,1,0:T(8,128)(2,1)} %copy-done.4, bf16[1,256,2304]{2,1,0:T(8,128)(2,1)} %copy-done.5), custom_call_target="tpu_custom_call" | custom-call | tf_op jit(solution)/shard_map/pick/pallas_call | solution.py:256
  258.9 0.3 collective-permute-start.13
  259.2 7.6 %combine.1 = (bf16[128,2176]{1,0:T(8,128)(2,1)}, bf16[128,2176]{1,0:T(8,128)(2,1)}, bf16[128,2176]{1,0:T(8,128)(2,1)}, bf16[128,2176]{1,0:T(8,128)(2,1)}) custom-call(s32[1]{0:T(128)} %bitcast.plane_ref, bf16[16,64,2176]{2,1,0:T(8,128)(2,1)} %all-to-all-done.3.back_ref, bf16[128,4224]{1,0:T(8,128)(2,1)} %concatenate.6.refs_0_, ...), custom_call_target="tpu_custom_call" | custom-call | flops 570425344 | bytes 8912896 | tf_op jit(solution)/shard_map/combine/pallas_call | solution.py:358
  266.8 2.8 collective-permute-start.6
  269.6 1.5 collective-permute-start.8
  271.0 0.6 pad_add_fusion.2.where_ref
  271.7 22.6 %collective-permute-done.6.refs_1_ = bf16[128,2176]{1,0:T(8,128)(2,1)S(1)} collective-permute-done((bf16[128,2176]{1,0:T(8,128)(2,1)}, bf16[128,2176]{1,0:T(8,128)(2,1)S(1)}, u32[]{:S(2)}, u32[]{:S(2)}) %collective-permute-start.6) | collective-permute-done | bytes 557088 | tf_op jit(solution)/shard_map/ppermute | solution.py:407
  294.3 3.3 %collective-permute-done.7.refs_2_ = bf16[128,2176]{1,0:T(8,128)(2,1)S(1)} collective-permute-done((bf16[128,2176]{1,0:T(8,128)(2,1)}, bf16[128,2176]{1,0:T(8,128)(2,1)S(1)}, u32[]{:S(2)}, u32[]{:S(2)}) %collective-permute-start.7) | collective-permute-done | bytes 557088 | tf_op jit(solution)/shard_map/ppermute | solution.py:407
  297.5 0.8 copy-done.10
  298.3 2.9 finish.1
  301.2 1.4 copy.18
  302.6 1.4 copy-done.8
  304.0 10.7 %update.1 = (bf16[2,512,768]{2,1,0:T(8,128)(2,1)}, bf16[2,512,768]{2,1,0:T(8,128)(2,1)}, bf16[2,512,768]{2,1,0:T(8,128)(2,1)}) custom-call(s32[4]{0:T(128)} %pad_add_fusion.2.where_ref, s32[2,3]{1,0:T(2,128)} %mask_ref.1, bf16[1,256,2304]{2,1,0:T(8,128)(2,1)} %mine_0.1.refs_0_, bf16[1,256,2304]{2,1,0:T(8,128)(2,1)} %copy-done.3, ...), custom_call_target="tpu_custom_call" | custom-call | tf_op jit(solution)/shard_map/update/pallas_call | solution.py:304
  (41 shorter events, 0.1 us)
Async XLA Ops:
  0.6 91.6 %collective-permute-start.3 = (bf16[2,2048,768]{2,1,0:T(8,128)(2,1)}, bf16[2,2048,768]{2,1,0:T(8,128)(2,1)}, u32[]{:S(2)}, u32[]{:S(2)}) collective-permute-start(bf16[2,2048,768]{2,1,0:T(8,128)(2,1)} %refs_5_.1), channel_id=1, source_target_pairs={{0,1},{1,0},{2,3},{3,2},{4,5},{5,4},{6,7},{7,6},{8,9},{9,8},{10,11... | collective-permute-start | bytes 18874376 | tf_op jit(solution)/shard_map/ppermute | solution.py:423
  0.7 96.5 %collective-permute-start.4 = (bf16[2,2048,768]{2,1,0:T(8,128)(2,1)}, bf16[2,2048,768]{2,1,0:T(8,128)(2,1)}, u32[]{:S(2)}, u32[]{:S(2)}) collective-permute-start(bf16[2,2048,768]{2,1,0:T(8,128)(2,1)} %refs_6_.1), channel_id=1, source_target_pairs={{0,1},{1,0},{2,3},{3,2},{4,5},{5,4},{6,7},{7,6},{8,9},{9,8},{10,11... | collective-permute-start | bytes 18874376 | tf_op jit(solution)/shard_map/ppermute | solution.py:423
  1.2 100.5 %collective-permute-start.5 = (bf16[2,2048,768]{2,1,0:T(8,128)(2,1)}, bf16[2,2048,768]{2,1,0:T(8,128)(2,1)}, u32[]{:S(2)}, u32[]{:S(2)}) collective-permute-start(bf16[2,2048,768]{2,1,0:T(8,128)(2,1)} %refs_7_.1), channel_id=1, source_target_pairs={{0,1},{1,0},{2,3},{3,2},{4,5},{5,4},{6,7},{7,6},{8,9},{9,8},{10,11... | collective-permute-start | bytes 18874376 | tf_op jit(solution)/shard_map/ppermute | solution.py:423
  2.9 3.1 copy-start.11
  6.1 11.9 %copy-start.2 = (bf16[128,4224]{1,0:T(8,128)(2,1)S(1)}, bf16[128,4224]{1,0:T(8,128)(2,1)}, u32[]{:S(2)}) copy-start(bf16[128,4224]{1,0:T(8,128)(2,1)} %concatenate.6.refs_0_) | copy-start | bytes 3244036
  9.8 43.6 %all-to-all-start = ((bf16[16,16,4096]{2,1,0:T(8,128)(2,1)}), bf16[16,16,4096]{2,1,0:T(8,128)(2,1)S(1)}, u32[]{:S(2)}, u32[]{:S(2)}) async-start(bf16[16,16,4096]{2,1,0:T(8,128)(2,1)} %send_own.1), calls=%async_computation | async-start | bytes 4194304 | tf_op jit(solution)/shard_map/all_to_all | solution.py:410
  18.0 26.3 %collective-permute-start.2 = (bf16[128,4224]{1,0:T(8,128)(2,1)S(1)}, bf16[128,4224]{1,0:T(8,128)(2,1)S(1)}, u32[]{:S(2)}, u32[]{:S(2)}) collective-permute-start(bf16[128,4224]{1,0:T(8,128)(2,1)S(1)} %copy-done.2), channel_id=1, source_target_pairs={{0,96},{32,0},{64,32},{96,64},{1,97},{33,1},{65,33},{97,65},{2,98}... | collective-permute-start | bytes 3244040 | tf_op jit(solution)/shard_map/ppermute | solution.py:407
  20.8 27.0 %collective-permute-start.1 = (bf16[128,4224]{1,0:T(8,128)(2,1)S(1)}, bf16[128,4224]{1,0:T(8,128)(2,1)}, u32[]{:S(2)}, u32[]{:S(2)}) collective-permute-start(bf16[128,4224]{1,0:T(8,128)(2,1)S(1)} %copy-done.2), channel_id=1, source_target_pairs={{0,32},{32,64},{64,96},{96,0},{1,33},{33,65},{65,97},{97,1},{2,34}... | collective-permute-start | bytes 3244040 | tf_op jit(solution)/shard_map/ppermute | solution.py:407
  44.2 1.0 copy-start.6
  53.4 1.4 copy-start.1
  54.7 67.1 %all-to-all-start.1 = ((bf16[16,32,4096]{2,1,0:T(8,128)(2,1)}), bf16[16,32,4096]{2,1,0:T(8,128)(2,1)}, u32[]{:S(2)}, u32[]{:S(2)}) async-start(bf16[16,32,4096]{2,1,0:T(8,128)(2,1)} %send_near.1), calls=%async_computation.1 | async-start | bytes 8388608 | tf_op jit(solution)/shard_map/all_to_all | solution.py:410
  61.7 25.8 %collective-permute-start = (bf16[128,4224]{1,0:T(8,128)(2,1)S(1)}, bf16[128,4224]{1,0:T(8,128)(2,1)S(1)}, u32[]{:S(2)}, u32[]{:S(2)}) collective-permute-start(bf16[128,4224]{1,0:T(8,128)(2,1)S(1)} %copy-done.2), channel_id=1, source_target_pairs={{0,64},{32,96},{64,0},{96,32},{1,65},{33,97},{65,1},{97,33},{2,66}... | collective-permute-start | bytes 3244040 | tf_op jit(solution)/shard_map/ppermute | solution.py:407
  87.5 1.0 copy-start.7
  88.5 8.7 %slice-start = ((s8[6291456]{0:T(1024)(128)(4,1)}), s8[2097152]{0:T(1024)(128)(4,1)S(1)}, s32[]{:S(2)}) async-start(s8[6291456]{0:T(1024)(128)(4,1)} %bitcast.44), calls=%async_computation.4 | async-start | bytes 4194304
  92.3 5.0 %slice-start.1 = ((s8[6291456]{0:T(1024)(128)(4,1)}), s8[4194304]{0:T(1024)(128)(4,1)S(1)}, s32[]{:S(2)}) async-start(s8[6291456]{0:T(1024)(128)(4,1)} %bitcast.44), calls=%async_computation.5 | async-start | bytes 8388608
  92.3 9.4 %slice-start.2 = ((s8[6291456]{0:T(1024)(128)(4,1)}), s8[4194304]{0:T(1024)(128)(4,1)S(1)}, s32[]{:S(2)}) async-start(s8[6291456]{0:T(1024)(128)(4,1)} %bitcast.46), calls=%async_computation.6 | async-start | bytes 8388608
  97.2 4.5 %slice-start.3 = ((s8[6291456]{0:T(1024)(128)(4,1)}), s8[2097152]{0:T(1024)(128)(4,1)S(1)}, s32[]{:S(2)}) async-start(s8[6291456]{0:T(1024)(128)(4,1)} %bitcast.46), calls=%async_computation.7 | async-start | bytes 4194304
  121.8 38.6 %all-to-all-start.2 = ((bf16[16,16,4096]{2,1,0:T(8,128)(2,1)}), bf16[16,16,4096]{2,1,0:T(8,128)(2,1)S(1)}, u32[]{:S(2)}, u32[]{:S(2)}) async-start(bf16[16,16,4096]{2,1,0:T(8,128)(2,1)} %send_far.1), calls=%async_computation.2 | async-start | bytes 4194304 | tf_op jit(solution)/shard_map/all_to_all | solution.py:410
  126.6 11.3 %copy-start.12 = (s32[4]{0:T(128)}, s32[4]{0:T(128)S(1)}, u32[]{:S(2)}) copy-start(s32[4]{0:T(128)S(1)} %get-tuple-element.74.where_ref) | copy-start | bytes 52
  160.4 1.4 copy-start
  177.1 13.2 %collective-permute-start.9 = (bf16[4,256,2304]{2,1,0:T(8,128)(2,1)}, bf16[4,256,2304]{2,1,0:T(8,128)(2,1)}, u32[]{:S(2)}, u32[]{:S(2)}) collective-permute-start(bf16[4,256,2304]{2,1,0:T(8,128)(2,1)} %theirs.1), channel_id=1, source_target_pairs={{0,1},{1,0},{2,3},{3,2},{4,5},{5,4},{6,7},{7,6},{8,9},{9,8},{10,11... | collective-permute-start | bytes 14155784 | tf_op jit(solution)/shard_map/ppermute | solution.py:461
  183.1 76.2 %all-to-all-start.3 = ((bf16[16,64,2176]{2,1,0:T(8,128)(2,1)}), bf16[16,64,2176]{2,1,0:T(8,128)(2,1)}, u32[]{:S(2)}, u32[]{:S(2)}) async-start(bf16[16,64,2176]{2,1,0:T(8,128)(2,1)} %dx_far.1), calls=%async_computation.3 | async-start | bytes 8912896 | tf_op jit(solution)/shard_map/all_to_all | solution.py:410
  194.0 30.2 %collective-permute-start.10 = (bf16[1,256,2304]{2,1,0:T(8,128)(2,1)}, bf16[1,256,2304]{2,1,0:T(8,128)(2,1)S(1)}, u32[]{:S(2)}, u32[]{:S(2)}) collective-permute-start(bf16[1,256,2304]{2,1,0:T(8,128)(2,1)} %mine_1.1), channel_id=1, source_target_pairs={{0,32},{32,64},{64,96},{96,0},{1,33},{33,65},{65,97},{97,1},{2,34}... | collective-permute-start | bytes 3538952 | tf_op jit(solution)/shard_map/ppermute | solution.py:407
  197.8 51.1 %collective-permute-start.11 = (bf16[1,256,2304]{2,1,0:T(8,128)(2,1)}, bf16[1,256,2304]{2,1,0:T(8,128)(2,1)S(1)}, u32[]{:S(2)}, u32[]{:S(2)}) collective-permute-start(bf16[1,256,2304]{2,1,0:T(8,128)(2,1)} %mine_2.1), channel_id=1, source_target_pairs={{0,64},{32,96},{64,0},{96,32},{1,65},{33,97},{65,1},{97,33},{2,66}... | collective-permute-start | bytes 3538952 | tf_op jit(solution)/shard_map/ppermute | solution.py:407
  204.7 48.5 %collective-permute-start.12 = (bf16[1,256,2304]{2,1,0:T(8,128)(2,1)}, bf16[1,256,2304]{2,1,0:T(8,128)(2,1)S(1)}, u32[]{:S(2)}, u32[]{:S(2)}) collective-permute-start(bf16[1,256,2304]{2,1,0:T(8,128)(2,1)} %mine_3.1), channel_id=1, source_target_pairs={{0,96},{32,0},{64,32},{96,64},{1,97},{33,1},{65,33},{97,65},{2,98}... | collective-permute-start | bytes 3538952 | tf_op jit(solution)/shard_map/ppermute | solution.py:407
  224.3 28.9 %copy-start.3 = (bf16[1,256,2304]{2,1,0:T(8,128)(2,1)}, bf16[1,256,2304]{2,1,0:T(8,128)(2,1)S(1)}, u32[]{:S(2)}) copy-start(bf16[1,256,2304]{2,1,0:T(8,128)(2,1)S(1)} %collective-permute-done.10.refs_1_) | copy-start | bytes 3538948
  248.8 4.3 %copy-start.4 = (bf16[1,256,2304]{2,1,0:T(8,128)(2,1)}, bf16[1,256,2304]{2,1,0:T(8,128)(2,1)S(1)}, u32[]{:S(2)}) copy-start(bf16[1,256,2304]{2,1,0:T(8,128)(2,1)S(1)} %collective-permute-done.11.refs_2_) | copy-start | bytes 3538948
  253.2 1.0 copy-start.5
  258.9 43.7 %collective-permute-start.13 = (bf16[2,256,2304]{2,1,0:T(8,128)(2,1)}, bf16[2,256,2304]{2,1,0:T(8,128)(2,1)S(1)}, u32[]{:S(2)}, u32[]{:S(2)}) collective-permute-start(bf16[2,256,2304]{2,1,0:T(8,128)(2,1)} %pick.1), channel_id=1, source_target_pairs={{0,1},{1,0},{2,3},{3,2},{4,5},{5,4},{6,7},{7,6},{8,9},{9,8},{10,11... | collective-permute-start | bytes 7077896 | tf_op jit(solution)/shard_map/ppermute | solution.py:478
  266.8 27.5 %collective-permute-start.6 = (bf16[128,2176]{1,0:T(8,128)(2,1)}, bf16[128,2176]{1,0:T(8,128)(2,1)S(1)}, u32[]{:S(2)}, u32[]{:S(2)}) collective-permute-start(bf16[128,2176]{1,0:T(8,128)(2,1)} %get-tuple-element.59), channel_id=1, source_target_pairs={{0,96},{32,0},{64,32},{96,64},{1,97},{33,1},{65,33},{97,65},{2,98}... | collective-permute-start | bytes 1671176 | tf_op jit(solution)/shard_map/ppermute | solution.py:407
  269.6 28.0 %collective-permute-start.7 = (bf16[128,2176]{1,0:T(8,128)(2,1)}, bf16[128,2176]{1,0:T(8,128)(2,1)S(1)}, u32[]{:S(2)}, u32[]{:S(2)}) collective-permute-start(bf16[128,2176]{1,0:T(8,128)(2,1)} %get-tuple-element.60), channel_id=1, source_target_pairs={{0,32},{32,64},{64,96},{96,0},{1,33},{33,65},{65,97},{97,1},{2,34}... | collective-permute-start | bytes 1671176 | tf_op jit(solution)/shard_map/ppermute | solution.py:407
  269.6 28.0 %collective-permute-start.8 = (bf16[128,2176]{1,0:T(8,128)(2,1)}, bf16[128,2176]{1,0:T(8,128)(2,1)}, u32[]{:S(2)}, u32[]{:S(2)}) collective-permute-start(bf16[128,2176]{1,0:T(8,128)(2,1)} %get-tuple-element.61), channel_id=1, source_target_pairs={{0,64},{32,96},{64,0},{96,32},{1,65},{33,97},{65,1},{97,33},{2,66}... | collective-permute-start | bytes 1671176 | tf_op jit(solution)/shard_map/ppermute | solution.py:407
  294.3 3.3 %copy-start.9 = (bf16[128,2176]{1,0:T(8,128)(2,1)}, bf16[128,2176]{1,0:T(8,128)(2,1)S(1)}, u32[]{:S(2)}) copy-start(bf16[128,2176]{1,0:T(8,128)(2,1)S(1)} %collective-permute-done.6.refs_1_) | copy-start | bytes 1671172
  297.5 0.8 copy-start.10
  302.6 1.4 copy-start.8

commit v4 on v1

--- a/solution.py
+++ b/solution.py
@@ -53,71 +53,78 @@
     return at == place, spread
 
 
-def dispatch_kernel(local_exp, capacity, ids_ref, probs_ref, tok_ref, grad_ref, *out_refs):
+def dispatch_kernel(chunk, local_exp, capacity, ids_ref, probs_ref, tok_ref, grad_ref, out_ref):
     ids_t = ids_ref[...]
     topk, tok = ids_t.shape
-    n_experts = out_refs[0].shape[0] // capacity * local_exp
+    n_experts = out_ref.shape[0] // capacity * local_exp
     width = tok_ref.shape[1]
     values = slot_values(ids_t, n_experts, capacity)
     rows = lax.broadcasted_iota(jnp.int32, (n_experts, tok), 0)
     prob = jnp.zeros((n_experts, tok), F32)
     for k in range(topk):
         prob = prob + jnp.where(ids_t[k : k + 1, :] == rows, probs_ref[k : k + 1, :].astype(F32), 0.0)
-    for chunk, out_ref in enumerate(out_refs):
-        onehot, spread = slot_rows(values, chunk, local_exp, capacity)
-        prob_rows = dot(spread, prob.astype(BF16), NN)
-        pick = jnp.where(onehot, 1.0, 0.0).astype(BF16)
-        weighted = jnp.where(onehot, prob_rows, 0.0).astype(BF16)
-        out_ref[:, :width] = dot(pick, tok_ref[...], NN).astype(BF16)
-        out_ref[:, width:] = dot(weighted, grad_ref[...], NN).astype(BF16)
-
-
-def dispatch(local_exp, capacity, n_experts, ids_t, probs_t, tokens, out_grad):
+    onehot, spread = slot_rows(values, chunk, local_exp, capacity)
+    prob_rows = dot(spread, prob.astype(BF16), NN)
+    pick = jnp.where(onehot, 1.0, 0.0).astype(BF16)
+    weighted = jnp.where(onehot, prob_rows, 0.0).astype(BF16)
+    out_ref[:, :width] = dot(pick, tok_ref[...], NN).astype(BF16)
+    out_ref[:, width:] = dot(weighted, grad_ref[...], NN).astype(BF16)
+
+
+def dispatch(chunk, local_exp, capacity, n_experts, ids_t, probs_t, tokens, out_grad):
     tok, width = tokens.shape
     n_rows = n_experts // local_exp * capacity
     return pl.pallas_call(
-        functools.partial(dispatch_kernel, local_exp, capacity),
-        out_shape=[jax.ShapeDtypeStruct((n_rows, 2 * width), BF16)] * local_exp,
-        compiler_params=pltpu.CompilerParams(vmem_limit_bytes=VMEM_LIMIT),
-        cost_estimate=cost(4 * local_exp * n_rows * tok * width, 4 * width * (tok + local_exp * n_rows)),
-        name="dispatch",
+        functools.partial(dispatch_kernel, chunk, local_exp, capacity),
+        out_shape=jax.ShapeDtypeStruct((n_rows, 2 * width), BF16),
+        compiler_params=pltpu.CompilerParams(vmem_limit_bytes=VMEM_LIMIT),
+        cost_estimate=cost(4 * n_rows * tok * width, 4 * width * (tok + n_rows)),
+        name=f"dispatch{chunk}",
     )(ids_t, probs_t, tokens, out_grad)
 
 
-def grads_kernel(x_ref, do_ref, wg_ref, wu_ref, wd_ref, g_ref, da_ref, db_ref, s_ref):
-    x = x_ref[...]
-    do = do_ref[...]
-    gate = dot(x, wg_ref[0], NN)
-    upper = dot(x, wu_ref[0], NN)
+def hidden_kernel(x_ref, do_ref, wg_ref, wu_ref, wd_ref, hid_ref, da_ref, db_ref, s_ref, sum_ref):
+    step = pl.program_id(0)
+    gate = dot(x_ref[...], wg_ref[0], NN)
+    upper = dot(x_ref[...], wu_ref[0], NN)
     sig = jax.nn.sigmoid(gate)
     act = gate * sig
     hid = (act * upper).astype(BF16)
-    dhid = dot(do, wd_ref[0], NN)
-    total = jnp.sum(hid.astype(F32) * dhid, axis=1, keepdims=True)
-    high = total.astype(BF16).astype(F32)
-    lane = lax.broadcasted_iota(jnp.int32, s_ref.shape, 1)
-    s_ref[...] = jnp.where(lane == 0, high, jnp.where(lane == 1, total - high, 0.0)).astype(BF16)
-    hidden = hid.shape[1]
-    g_ref[:, 2 * hidden :] = dot(do, hid, TN).astype(BF16)
-    dgate = (dhid * upper * sig * (1.0 + gate * (1.0 - sig))).astype(BF16)
-    da_ref[...] = dgate
-    g_ref[:, :hidden] = dot(x, dgate, TN).astype(BF16)
-    dup = (dhid * act).astype(BF16)
-    db_ref[...] = dup
-    g_ref[:, hidden : 2 * hidden] = dot(x, dup, TN).astype(BF16)
-
-
-def expert_grads(chunk, rows, wg, wu, wd):
+    hid_ref[...] = hid
+    dhid = dot(do_ref[...], wd_ref[0], NN)
+    part = jnp.sum(hid.astype(F32) * dhid, axis=1, keepdims=True)
+    da_ref[...] = (dhid * upper * sig * (1.0 + gate * (1.0 - sig))).astype(BF16)
+    db_ref[...] = (dhid * act).astype(BF16)
+
+    @pl.when(step == 0)
+    def _():
+        sum_ref[...] = jnp.broadcast_to(part, sum_ref.shape)
+
+    @pl.when(step > 0)
+    def _():
+        sum_ref[...] = sum_ref[...] + part
+
+    @pl.when(step == pl.num_programs(0) - 1)
+    def _():
+        total = sum_ref[...]
+        high = total.astype(BF16).astype(F32)
+        lane = lax.broadcasted_iota(jnp.int32, s_ref.shape, 1)
+        s_ref[...] = jnp.where(lane == 0, high, jnp.where(lane == 1, total - high, 0.0)).astype(BF16)
+
+
+def whole(shape):
+    return pl.BlockSpec(shape, lambda *_: (0,) * len(shape), pipeline_mode=pl.Buffered(1))
+
+
+def hidden_grads(chunk, rows, wg, wu, wd):
     n_rows, width = rows.shape[0], rows.shape[1] // 2
     hidden = wg.shape[2]
-    weight = pl.BlockSpec((1, width, hidden), lambda i: (chunk, 0, 0), pipeline_mode=pl.Buffered(1))
-
-    def whole(shape):
-        return pl.BlockSpec(shape, lambda i: (0, 0), pipeline_mode=pl.Buffered(1))
-
-    return pl.pallas_call(
-        grads_kernel,
-        grid=(1,),
+    block = 2 * LANES
+    weight = pl.BlockSpec((1, width, block), lambda i: (chunk, 0, i))
+    result = pl.BlockSpec((n_rows, block), lambda i: (0, i))
+    return pl.pallas_call(
+        hidden_kernel,
+        grid=(hidden // block,),
         in_specs=[
             pl.BlockSpec((n_rows, width), lambda i: (0, 0), pipeline_mode=pl.Buffered(1)),
             pl.BlockSpec((n_rows, width), lambda i: (0, 1), pipeline_mode=pl.Buffered(1)),
@@ -125,22 +132,95 @@
             weight,
             weight,
         ],
-        out_specs=[
-            whole((width, 3 * hidden)),
-            whole((n_rows, hidden)),
-            whole((n_rows, hidden)),
-            whole((n_rows, LANES)),
-        ],
-        out_shape=[
-            jax.ShapeDtypeStruct((width, 3 * hidden), BF16),
-            jax.ShapeDtypeStruct((n_rows, hidden), BF16),
-            jax.ShapeDtypeStruct((n_rows, hidden), BF16),
-            jax.ShapeDtypeStruct((n_rows, LANES), BF16),
-        ],
-        compiler_params=pltpu.CompilerParams(vmem_limit_bytes=VMEM_LIMIT),
-        cost_estimate=cost(12000 * n_rows * width * hidden, 12 * width * hidden + 4 * n_rows * (width + hidden)),
-        name=f"grads{chunk}",
+        out_specs=[result] * 3 + [whole((n_rows, LANES))],
+        out_shape=[jax.ShapeDtypeStruct((n_rows, hidden), BF16)] * 3
+        + [jax.ShapeDtypeStruct((n_rows, LANES), BF16)],
+        scratch_shapes=[pltpu.VMEM((n_rows, LANES), F32)],
+        compiler_params=pltpu.CompilerParams(vmem_limit_bytes=VMEM_LIMIT),
+        cost_estimate=cost(6 * n_rows * width * hidden, 6 * width * hidden + n_rows * (4 * width + 6 * hidden)),
+        name=f"hidden{chunk}",
     )(rows, rows, wg, wu, wd)
+
+
+def weight_kernel(n_add, where_ref, x_ref, do_ref, hid_ref, da_ref, db_ref, *refs):
+    adds, outs = refs[:n_add], refs[n_add:]
+    hidden = hid_ref.shape[1]
+    for m, (left, right) in enumerate(((x_ref, da_ref), (x_ref, db_ref), (do_ref, hid_ref))):
+        part = dot(left[...], right[...], TN)
+        lanes = slice(m * hidden, (m + 1) * hidden)
+        for addend in adds:
+            part = part + addend[:, lanes].astype(F32)
+        for i, out_ref in enumerate(outs):
+
+            @pl.when(pl.program_id(0) == i)
+            def _():
+                out_ref[:, lanes] = part.astype(BF16)
+
+
+def weight_grads(name, where, count, half, rows, hid, da, db, *adds):
+    n_rows, width = rows.shape[0], rows.shape[1] // 2
+    hidden = hid.shape[1]
+    lefts = width // half
+    shape = (half, 3 * hidden)
+    return pl.pallas_call(
+        functools.partial(weight_kernel, len(adds)),
+        grid_spec=pltpu.PrefetchScalarGridSpec(
+            num_scalar_prefetch=1,
+            grid=(count,),
+            in_specs=[
+                pl.BlockSpec((n_rows, half), lambda i, at: (0, at[i])),
+                pl.BlockSpec((n_rows, half), lambda i, at: (0, at[i] + lefts)),
+            ]
+            + [whole(a.shape) for a in (hid, da, db, *adds)],
+            out_specs=[whole(shape)] * count,
+        ),
+        out_shape=[jax.ShapeDtypeStruct(shape, BF16)] * count,
+        compiler_params=pltpu.CompilerParams(vmem_limit_bytes=VMEM_LIMIT),
+        cost_estimate=cost(6 * count * n_rows * half * hidden, 6 * n_rows * hidden + 6 * count * half * hidden),
+        name=name,
+    )(where, rows, rows, hid, da, db, *adds)
+
+
+def update_kernel(chunk, where_ref, mask_ref, *refs):
+    grads, weights = refs[:6], refs[6:9]
+    outs = refs[-3:]
+    hidden = weights[0].shape[2]
+    for half in range(2):
+
+        @pl.when(pl.program_id(0) == half)
+        def _():
+            for m in range(3):
+                lanes = slice(m * hidden, (m + 1) * hidden)
+                grad = sum(g[:, lanes].astype(F32) for g in grads[3 * half : 3 * half + 3])
+                weight = weights[m][0].astype(F32)
+                rate = mask_ref[chunk, m].astype(F32)
+                outs[m][0] = (weight - step_size * grad - shrink_rate * rate * weight).astype(BF16)
+
+
+def update(chunk, where, mask, grads, weights, into):
+    half, lanes = grads[0].shape
+    local, _, hidden = weights[0].shape
+    grad = pl.BlockSpec((half, lanes), lambda h, w: (0, 0), pipeline_mode=pl.Buffered(1))
+    weight = pl.BlockSpec((1, half, hidden), lambda h, w: (chunk, 2 * w[0] + h, 0))
+    result = pl.BlockSpec((1, half, hidden), lambda h, w: (chunk, h, 0))
+    extra = list(into or [])
+    return pl.pallas_call(
+        functools.partial(update_kernel, chunk),
+        grid_spec=pltpu.PrefetchScalarGridSpec(
+            num_scalar_prefetch=1,
+            grid=(2,),
+            in_specs=[pl.BlockSpec(memory_space=pltpu.SMEM)]
+            + [grad] * 6
+            + [weight] * 3
+            + [pl.BlockSpec(memory_space=pl.ANY)] * len(extra),
+            out_specs=[result] * 3,
+        ),
+        out_shape=[jax.ShapeDtypeStruct((local, 2 * half, hidden), BF16)] * 3,
+        input_output_aliases={11 + i: i for i in range(len(extra))},
+        compiler_params=pltpu.CompilerParams(vmem_limit_bytes=VMEM_LIMIT),
+        cost_estimate=cost(10 * half * lanes, 20 * half * lanes),
+        name=f"update{chunk}",
+    )(where, mask, *grads, *weights, *extra)
 
 
 def dx_kernel(da_ref, db_ref, s_ref, wg_ref, wu_ref, out_ref):
@@ -206,7 +286,7 @@
             jax.ShapeDtypeStruct((topk, tok), F32),
         ],
         compiler_params=pltpu.CompilerParams(vmem_limit_bytes=VMEM_LIMIT),
-        cost_estimate=cost(2000 * n_rows * tok * width, 2 * width * (n_rows + tok)),
+        cost_estimate=cost(2 * n_rows * tok * width, 2 * width * (n_rows + tok)),
         name="combine",
     )(ids_t, *backs)
 
@@ -216,44 +296,72 @@
     n_group = lax.axis_size("dp")
     local_exp = w_gate.shape[0]
     width = tokens.shape[1]
-    hidden = w_gate.shape[2]
     tok_rows, topk = expert_ids.shape
     n_experts = n_owner * local_exp
     capacity = tok_rows * topk // n_experts
     ids_t = expert_ids.T
     probs_t = route_probs.T
-    shard_rows = width // n_group
-    first_row = lax.axis_index("dp") * shard_rows
-
-    sends = dispatch(local_exp, capacity, n_experts, ids_t, probs_t, tokens, out_grad)
+    half = width // n_group // 2
+    plane = lax.axis_index("dp").astype(jnp.int32)
+    where = plane.reshape(1)
+
+    def half_shard(ahead, second):
+        return 2 * ((plane + ahead) % n_group) + second
+
+    def blocks(*pairs):
+        return jnp.stack([half_shard(*pair) for pair in pairs]).astype(jnp.int32)
+
+    def up(a):
+        return lax.ppermute(a, "dp", [(i, (i + 1) % n_group) for i in range(n_group)])
+
+    def down(a):
+        return lax.ppermute(a, "dp", [(i, (i - 1) % n_group) for i in range(n_group)])
+
     got = []
-    for rows in sends:
+    for chunk in range(local_exp):
+        rows = dispatch(chunk, local_exp, capacity, n_experts, ids_t, probs_t, tokens, out_grad)
         if got:
             rows, got[-1] = lax.optimization_barrier((rows, got[-1]))
         rows = rows.reshape(n_owner, capacity, 2 * width)
         got.append(lax.all_to_all(rows, "expert", split_axis=0, concat_axis=0, tiled=True))
-    summed, backs = [], []
+    def swap(a):
+        a = a.reshape(n_owner, capacity, width + LANES)
+        back = lax.all_to_all(a, "expert", split_axis=0, concat_axis=0, tiled=True)
+        return back.reshape(n_owner * capacity, width + LANES)
+
+    weights = (w_gate, w_up, w_down)
+    near_pairs = ((1, 1), (n_group - 1, 0), (0, 0), (0, 1))
+    new, backs, sent = None, [], None
     for chunk in range(local_exp):
         rows = got[chunk].reshape(n_owner * capacity, 2 * width)
-        g, da, db, s = expert_grads(chunk, rows, w_gate, w_up, w_down)
-        summed.append(lax.psum_scatter(g, "dp", scatter_dimension=0, tiled=True))
-        if chunk + 1 < local_exp:
-            da, got[chunk + 1] = lax.optimization_barrier((da, got[chunk + 1]))
-        dx = input_grads(chunk, da, db, s, w_gate, w_up).reshape(n_owner, capacity, width + LANES)
-        back = lax.all_to_all(dx, "expert", split_axis=0, concat_axis=0, tiled=True)
-        backs.append(back.reshape(n_owner * capacity, width + LANES))
+        if sent:
+            rows, near_up, near_down, dx = lax.optimization_barrier((rows, near_up, near_down, dx))
+            backs.append(swap(dx))
+        hid, da, db, s = hidden_grads(chunk, rows, *weights)
+        first = weight_grads(f"first{chunk}", blocks((2, 0), (2, 1)), 2, half, rows, hid, da, db)
+        far_up, far_down = up(first[0]), down(first[1])
+        if sent:
+            dx = input_grads(chunk, da, db, s, w_gate, w_up)
+            rows, _, dx, *sent = lax.optimization_barrier((rows, first[0], dx, *sent))
+            grads = (second[2], sent[0], near_down, second[3], near_up, sent[1])
+            new = update(chunk - 1, where, decay_mask, grads, weights, new)
+        second = weight_grads(f"second{chunk}", blocks(*near_pairs), 4, half, rows, hid, da, db)
+        near_up, near_down = up(second[0]), down(second[1])
+        far_up, far_down, _ = lax.optimization_barrier((far_up, far_down, second[0]))
+        sum_up = weight_grads(f"up{chunk}", blocks((1, 0)), 1, half, rows, hid, da, db, far_up)[0]
+        sum_down = weight_grads(f"down{chunk}", blocks((n_group - 1, 1)), 1, half, rows, hid, da, db, far_down)[0]
+        sent = [up(sum_up), down(sum_down)]
+        if chunk == 0:
+            da, got[1], _, _ = lax.optimization_barrier((da, got[1], sum_up, sum_down))
+            dx = input_grads(chunk, da, db, s, w_gate, w_up)
+    backs.append(swap(dx))
+    *backs, near_up, near_down = lax.optimization_barrier((*backs, near_up, near_down))
+    grads = (second[2], sent[0], near_down, second[3], near_up, sent[1])
+    new = update(local_exp - 1, where, decay_mask, grads, weights, new)
     grad_tokens, scores = combine(local_exp, capacity, ids_t, backs, width)
     grad_probs = (scores / probs_t.astype(F32)).astype(BF16).T
 
-    rates = decay_mask.astype(F32)
-
-    def update(weight, column):
-        weight_f = lax.dynamic_slice_in_dim(weight, first_row, shard_rows, 1).astype(F32)
-        grad_w = jnp.stack([s[:, column * hidden : (column + 1) * hidden] for s in summed]).astype(F32)
-        factor = rates[:, column][:, None, None]
-        return (weight_f - step_size * grad_w - shrink_rate * factor * weight_f).astype(BF16)
-
-    return (grad_tokens, grad_probs, update(w_gate, 0), update(w_up, 1), update(w_down, 2))
+    return (grad_tokens, grad_probs, *new)
 
 
 def solution(mesh):

time: 296 us -> 270 us (0.912)
  blocking collectives: 59.6 us -> 0 us
  Pallas kernels: 65.4 us -> 115 us
  starting transfers between devices: 14.5 us -> 44.1 us
  waiting for transfers between devices: 127 us -> 104 us
  between operations: 14.1 us -> 0.77 us
  other arithmetic: 9.34 us -> 2.48 us
    all_to_all x1 -> x0, blocking collectives: 59.6 us -> none  [body(): lax.all_to_all(rows, 'expert', split_axis=0, concat_axis=0, tiled=True)]
    reduce_scatter x2 -> x0, waiting for transfers between devices: 58.2 us -> none  [body(): summed.append(lax.psum_scatter(g, 'dp', scatter_dimension=0, tiled=True))]
    ppermute x0 -> x12, waiting for transfers between devices: none -> 55.4 us  [the longest x6 31.1 us: down(): lax.ppermute(a, 'dp', [(i, (i - 1) % n_group) for i in range(n_group)])]
    pallas_call x3 -> x14, Pallas kernels: 44.4 us -> 94.1 us  [the longest x8 50.6 us: weight_grads(): pl.pallas_call(functools.partial(weight_kernel, len(adds)), grid_spec=plt...]
    all_to_all x2, waiting for transfers between devices: 34.2 us -> 0.01 us  [swap(): back = lax.all_to_all(a, 'expert', split_axis=0, concat_axis=0, tiled=True)]
    ppermute x0 -> x12, starting transfers between devices: none -> 15.6 us  [the longest x6 12.3 us: down(): lax.ppermute(a, 'dp', [(i, (i - 1) % n_group) for i in range(n_group)])]
    all_to_all x1 -> x2, waiting for transfers between devices: 34.3 us -> 48.6 us  [body(): lax.all_to_all(rows, 'expert', split_axis=0, concat_axis=0, tiled=True)]
    all_to_all x1 -> x2, starting transfers between devices: 4.86 us -> 13.4 us  [body(): lax.all_to_all(rows, 'expert', split_axis=0, concat_axis=0, tiled=True)]
  transfers between devices with their start and end apart: 5 -> 16, of which waited for: 4 -> 10; matrix products, arithmetic and copies ran while one was open for 1% -> 1% of each run, Pallas kernels for 20% -> 39%
where the time goes in v4:
time: 270 us
  Pallas kernels  115 us (43%)
  waiting for transfers between devices  104 us (39%)
  starting transfers between devices  44.1 us (16%)
  local copies, waits for them, and re-layouts  2.81 us (1%)
    pallas_call x8, Pallas kernels, weight_grads(): pl.pallas_call(functools.partial(weight_kernel, len(adds)), grid_spec=plt...  50.6 us
    all_to_all x2, waiting for transfers between devices, body(): lax.all_to_all(rows, 'expert', split_axis=0, concat_axis=0, tiled=True)  48.6 us
    ppermute x6, waiting for transfers between devices, down(): lax.ppermute(a, 'dp', [(i, (i - 1) % n_group) for i in range(n_group)])  31.1 us
    ppermute x6, waiting for transfers between devices, up(): lax.ppermute(a, 'dp', [(i, (i + 1) % n_group) for i in range(n_group)])  24.4 us
    pallas_call x2, Pallas kernels, hidden_grads(): pl.pallas_call(hidden_kernel, grid=(hidden // block,), in_specs=[pl.Block...  21.4 us
    pallas_call x2, Pallas kernels, input_grads(): pl.pallas_call(dx_kernel, grid=(1,), in_specs=[whole((n_rows, hidden)), w...  16.4 us
    all_to_all x2, starting transfers between devices, swap(): back = lax.all_to_all(a, 'expert', split_axis=0, concat_axis=0, tiled=True)  15.1 us
    all_to_all x2, starting transfers between devices, body(): lax.all_to_all(rows, 'expert', split_axis=0, concat_axis=0, tiled=True)  13.4 us
  transfers between devices with their start and end apart: 16, of which 10 were waited for; matrix products, arithmetic and copies ran while one was open for 1% of the time, Pallas kernels for 39%

profile of v4, /device:TPU:0, one launch (start us, length us, event | category | flops | bytes accessed | tf_op | source)
XLA Modules:
  0.0 269.6 jit_solution(13299476469701434329)
XLA Ops:
  0.6 4.7 %dispatch0.1 = bf16[512,4096]{1,0:T(8,128)(2,1)} custom-call(s32[8,128]{1,0:T(8,128)} %bitcast.27, bf16[8,128]{1,0:T(8,128)(2,1)} %bitcast.30, bf16[128,2048]{1,0:T(8,128)(2,1)} %tok_ref.3, bf16[128,2048]{1,0:T(8,128)(2,1)} %grad_ref.3), custom_call_target="tpu_custom_call" | custom-call | flops 536870912 | bytes 5242880 | tf_op jit(solution)/shard_map/dispatch0/pallas_call | solution.py:77
  5.4 8.5 %all-to-all-start = ((bf16[32,16,4096]{2,1,0:T(8,128)(2,1)}), bf16[32,16,4096]{2,1,0:T(8,128)(2,1)}, u32[]{:S(2)}, u32[]{:S(2)}) async-start(bf16[32,16,4096]{2,1,0:T(8,128)(2,1)} %bitcast.23), calls=%async_computation | async-start | bytes 8388608 | tf_op jit(solution)/shard_map/all_to_all | solution.py:326
  13.9 4.8 %dispatch1.1 = bf16[512,4096]{1,0:T(8,128)(2,1)} custom-call(s32[8,128]{1,0:T(8,128)} %bitcast.28, bf16[8,128]{1,0:T(8,128)(2,1)} %bitcast.31, bf16[128,2048]{1,0:T(8,128)(2,1)} %tok_ref.3, bf16[128,2048]{1,0:T(8,128)(2,1)} %grad_ref.3), custom_call_target="tpu_custom_call" | custom-call | flops 536870912 | bytes 5242880 | tf_op jit(solution)/shard_map/dispatch1/pallas_call | solution.py:77
  18.7 48.6 %all-to-all-done = bf16[32,16,4096]{2,1,0:T(8,128)(2,1)} async-done(((bf16[32,16,4096]{2,1,0:T(8,128)(2,1)}), bf16[32,16,4096]{2,1,0:T(8,128)(2,1)}, u32[]{:S(2)}, u32[]{:S(2)}) %all-to-all-start) | async-done | bytes 4194336 | tf_op jit(solution)/shard_map/all_to_all | solution.py:326
  67.4 4.9 %all-to-all-start.1 = ((bf16[32,16,4096]{2,1,0:T(8,128)(2,1)}), bf16[32,16,4096]{2,1,0:T(8,128)(2,1)}, u32[]{:S(2)}, u32[]{:S(2)}) async-start(bf16[32,16,4096]{2,1,0:T(8,128)(2,1)} %bitcast.22), calls=%async_computation.1 | async-start | bytes 8388608 | tf_op jit(solution)/shard_map/all_to_all | solution.py:326
  72.3 0.6 pad_add_fusion.where_ref
  72.8 10.7 %hidden0.1 = (bf16[512,768]{1,0:T(8,128)(2,1)}, bf16[512,768]{1,0:T(8,128)(2,1)}, bf16[512,768]{1,0:T(8,128)(2,1)}, bf16[512,128]{1,0:T(8,128)(2,1)}) custom-call(bf16[512,4096]{1,0:T(8,128)(2,1)} %bitcast.3.x_ref.do_ref, bf16[512,4096]{1,0:T(8,128)(2,1)} %bitcast.3.x_ref.do_ref, bf16[2,2048,768]{2,1,0:T(8,128)(2,1)} %refs_6_.3, ...), custom_call_target="tpu_custom_call" | custom-call | flops 4831838208 | bytes 15990784 | tf_op jit(solution)/shard_map/hidden0/pallas_call | solution.py:125
  83.5 6.8 %first0.1 = (bf16[256,2304]{1,0:T(8,128)(2,1)}, bf16[256,2304]{1,0:T(8,128)(2,1)}) custom-call(s32[2]{0:T(128)} %pad_add_fusion.where_ref, bf16[512,4096]{1,0:T(8,128)(2,1)} %bitcast.3.x_ref.do_ref, bf16[512,4096]{1,0:T(8,128)(2,1)} %bitcast.3.x_ref.do_ref, bf16[512,768]{1,0:T(8,128)(2,1)} %get-tuple-element.56.hid_ref, ...), custom_call_target="tpu_custom_call" | custom-call | flops 1207959552 | bytes 4718592 | tf_op jit(solution)/shard_map/first0/pallas_call | solution.py:165
  90.3 1.5 collective-permute-start
  91.8 1.7 collective-permute-start.1
  93.5 0.7 pad_add_fusion.1.where_ref
  94.2 10.6 %second0.1 = (bf16[256,2304]{1,0:T(8,128)(2,1)}, bf16[256,2304]{1,0:T(8,128)(2,1)}, bf16[256,2304]{1,0:T(8,128)(2,1)}, bf16[256,2304]{1,0:T(8,128)(2,1)}) custom-call(s32[4]{0:T(128)} %pad_add_fusion.1.where_ref, bf16[512,4096]{1,0:T(8,128)(2,1)} %bitcast.3.x_ref.do_ref, bf16[512,4096]{1,0:T(8,128)(2,1)} %bitcast.3.x_ref.do_ref, ...), custom_call_target="tpu_custom_call" | custom-call | flops 2415919104 | bytes 7077888 | tf_op jit(solution)/shard_map/second0/pallas_call | solution.py:165
  104.8 1.5 collective-permute-start.3
  106.3 0.5 collective-permute-start.2
  106.8 13.9 %collective-permute-done.refs_0_ = bf16[256,2304]{1,0:T(8,128)(2,1)} collective-permute-done((bf16[256,2304]{1,0:T(8,128)(2,1)}, bf16[256,2304]{1,0:T(8,128)(2,1)}, u32[]{:S(2)}, u32[]{:S(2)}) %collective-permute-start) | collective-permute-done | bytes 1179680 | tf_op jit(solution)/shard_map/ppermute | solution.py:315
  120.7 0.3 collective-permute-done.1.refs_0_
  121.0 4.0 %up0.1 = bf16[256,2304]{1,0:T(8,128)(2,1)} custom-call(s32[1]{0:T(128)} %bitcast.5.where_ref, bf16[512,4096]{1,0:T(8,128)(2,1)} %bitcast.3.x_ref.do_ref, bf16[512,4096]{1,0:T(8,128)(2,1)} %bitcast.3.x_ref.do_ref, bf16[512,768]{1,0:T(8,128)(2,1)} %get-tuple-element.56.hid_ref, bf16[512,768]{1,0:T(8,128)(2,1)} %get-tuple-element.65.da_ref, ...), custom_call_target="tpu_custom_call" | custom-call | flops 603979776 | bytes 3538944 | tf_op jit(solution)/shard_map/up0/pallas_call | solution.py:165
  125.0 4.0 %down0.1 = bf16[256,2304]{1,0:T(8,128)(2,1)} custom-call(s32[1]{0:T(128)} %bitcast.12.where_ref, bf16[512,4096]{1,0:T(8,128)(2,1)} %bitcast.3.x_ref.do_ref, bf16[512,4096]{1,0:T(8,128)(2,1)} %bitcast.3.x_ref.do_ref, bf16[512,768]{1,0:T(8,128)(2,1)} %get-tuple-element.56.hid_ref, bf16[512,768]{1,0:T(8,128)(2,1)} %get-tuple-element.65.da_ref, ...), custom_call_target="tpu_custom_call" | custom-call | flops 603979776 | bytes 3538944 | tf_op jit(solution)/shard_map/down0/pallas_call | solution.py:165
  129.0 0.0 all-to-all-done.1
  129.0 8.2 %dx0.1 = bf16[512,2176]{1,0:T(8,128)(2,1)} custom-call(bf16[512,768]{1,0:T(8,128)(2,1)} %get-tuple-element.65.da_ref, bf16[512,768]{1,0:T(8,128)(2,1)} %get-tuple-element.57.db_ref, bf16[512,128]{1,0:T(8,128)(2,1)} %get-tuple-element.66.s_ref, bf16[2,2048,768]{2,1,0:T(8,128)(2,1)} %refs_6_.3, bf16[2,2048,768]{2,1,0:T(8,128)(2,1)} %refs_7_.3), custom_call_target="tpu_custom_call" | custom-call | flops 3221225472 | bytes 9961472 | tf_op jit(solution)/shard_map/dx0/pallas_call | solution.py:240
  137.2 7.8 %collective-permute-done.3.refs_2_ = bf16[256,2304]{1,0:T(8,128)(2,1)S(1)} collective-permute-done((bf16[256,2304]{1,0:T(8,128)(2,1)}, bf16[256,2304]{1,0:T(8,128)(2,1)S(1)}, u32[]{:S(2)}, u32[]{:S(2)}) %collective-permute-start.3) | collective-permute-done | bytes 1179680 | tf_op jit(solution)/shard_map/ppermute | solution.py:318
  145.0 0.0 copy-start.1
  145.0 0.0 collective-permute-done.2.refs_4_
  145.0 0.0 copy-start.2
  145.0 1.1 copy-done.2
  146.0 0.3 copy-done.1
  146.4 7.4 %all-to-all-start.2 = ((bf16[32,16,2176]{2,1,0:T(8,128)(2,1)}), bf16[32,16,2176]{2,1,0:T(8,128)(2,1)S(1)}, u32[]{:S(2)}, u32[]{:S(2)}) async-start(bf16[32,16,2176]{2,1,0:T(8,128)(2,1)} %bitcast.26), calls=%async_computation.2 | async-start | bytes 4456448 | tf_op jit(solution)/shard_map/all_to_all | solution.py:329
  153.8 3.0 %collective-permute-start.5 = (bf16[256,2304]{1,0:T(8,128)(2,1)}, bf16[256,2304]{1,0:T(8,128)(2,1)S(1)}, u32[]{:S(2)}, u32[]{:S(2)}) collective-permute-start(bf16[256,2304]{1,0:T(8,128)(2,1)} %down0.1), channel_id=1, source_target_pairs={{0,96},{32,0},{64,32},{96,64},{1,97},{33,1},{65,33},{97,65},{2,98}... | collective-permute-start | bytes 3538952 | tf_op jit(solution)/shard_map/ppermute | solution.py:318
  156.8 0.0 collective-permute-start.4
  156.8 10.7 %hidden1.1 = (bf16[512,768]{1,0:T(8,128)(2,1)}, bf16[512,768]{1,0:T(8,128)(2,1)}, bf16[512,768]{1,0:T(8,128)(2,1)}, bf16[512,128]{1,0:T(8,128)(2,1)}) custom-call(bf16[512,4096]{1,0:T(8,128)(2,1)} %bitcast.13.x_ref.do_ref, bf16[512,4096]{1,0:T(8,128)(2,1)} %bitcast.13.x_ref.do_ref, bf16[2,2048,768]{2,1,0:T(8,128)(2,1)} %refs_6_.3, ...), custom_call_target="tpu_custom_call" | custom-call | flops 4831838208 | bytes 15990784 | tf_op jit(solution)/shard_map/hidden1/pallas_call | solution.py:125
  167.5 6.8 %first1.1 = (bf16[256,2304]{1,0:T(8,128)(2,1)}, bf16[256,2304]{1,0:T(8,128)(2,1)}) custom-call(s32[2]{0:T(128)} %pad_add_fusion.where_ref, bf16[512,4096]{1,0:T(8,128)(2,1)} %bitcast.13.x_ref.do_ref, bf16[512,4096]{1,0:T(8,128)(2,1)} %bitcast.13.x_ref.do_ref, bf16[512,768]{1,0:T(8,128)(2,1)} %get-tuple-element.69.hid_ref, ...), custom_call_target="tpu_custom_call" | custom-call | flops 1207959552 | bytes 4718592 | tf_op jit(solution)/shard_map/first1/pallas_call | solution.py:165
  174.3 3.2 %collective-permute-start.9 = (bf16[256,2304]{1,0:T(8,128)(2,1)}, bf16[256,2304]{1,0:T(8,128)(2,1)}, u32[]{:S(2)}, u32[]{:S(2)}) collective-permute-start(bf16[256,2304]{1,0:T(8,128)(2,1)} %get-tuple-element.83), channel_id=1, source_target_pairs={{0,96},{32,0},{64,32},{96,64},{1,97},{33,1},{65,33},{97,65},{2,98}... | collective-permute-start | bytes 3538952 | tf_op jit(solution)/shard_map/ppermute | solution.py:318
  177.5 0.0 collective-permute-start.8
  177.5 8.2 %dx1.1 = bf16[512,2176]{1,0:T(8,128)(2,1)} custom-call(bf16[512,768]{1,0:T(8,128)(2,1)} %get-tuple-element.70.da_ref, bf16[512,768]{1,0:T(8,128)(2,1)} %get-tuple-element.71.db_ref, bf16[512,128]{1,0:T(8,128)(2,1)} %get-tuple-element.73.s_ref, bf16[2,2048,768]{2,1,0:T(8,128)(2,1)} %refs_6_.3, bf16[2,2048,768]{2,1,0:T(8,128)(2,1)} %refs_7_.3), custom_call_target="tpu_custom_call" | custom-call | flops 3221225472 | bytes 9961472 | tf_op jit(solution)/shard_map/dx1/pallas_call | solution.py:240
  185.7 0.0 collective-permute-done.5.refs_5_
  185.7 0.0 copy-start.3
  185.7 1.5 collective-permute-done.4.refs_1_
  187.2 0.0 all-to-all-done.2
  187.2 0.0 copy-start
  187.2 0.0 copy-done.3
  187.2 1.4 copy-done
  188.5 7.7 %all-to-all-start.3 = ((bf16[32,16,2176]{2,1,0:T(8,128)(2,1)}), bf16[32,16,2176]{2,1,0:T(8,128)(2,1)}, u32[]{:S(2)}, u32[]{:S(2)}) async-start(bf16[32,16,2176]{2,1,0:T(8,128)(2,1)} %bitcast.25), calls=%async_computation.3 | async-start | bytes 4456448 | tf_op jit(solution)/shard_map/all_to_all | solution.py:329
  196.3 10.5 %second1.1 = (bf16[256,2304]{1,0:T(8,128)(2,1)}, bf16[256,2304]{1,0:T(8,128)(2,1)}, bf16[256,2304]{1,0:T(8,128)(2,1)}, bf16[256,2304]{1,0:T(8,128)(2,1)}) custom-call(s32[4]{0:T(128)} %pad_add_fusion.1.where_ref, bf16[512,4096]{1,0:T(8,128)(2,1)} %bitcast.13.x_ref.do_ref, bf16[512,4096]{1,0:T(8,128)(2,1)} %bitcast.13.x_ref.do_ref, ...), custom_call_target="tpu_custom_call" | custom-call | flops 2415919104 | bytes 7077888 | tf_op jit(solution)/shard_map/second1/pallas_call | solution.py:165
  206.8 2.1 collective-permute-start.7
  208.9 0.0 collective-permute-start.6
  208.9 0.0 collective-permute-done.9.refs_0_
  208.9 2.5 collective-permute-done.8.refs_0_
  211.5 4.0 %up1.1 = bf16[256,2304]{1,0:T(8,128)(2,1)} custom-call(s32[1]{0:T(128)} %bitcast.5.where_ref, bf16[512,4096]{1,0:T(8,128)(2,1)} %bitcast.13.x_ref.do_ref, bf16[512,4096]{1,0:T(8,128)(2,1)} %bitcast.13.x_ref.do_ref, bf16[512,768]{1,0:T(8,128)(2,1)} %get-tuple-element.69.hid_ref, bf16[512,768]{1,0:T(8,128)(2,1)} %get-tuple-element.70.da_ref, ...), custom_call_target="tpu_custom_call" | custom-call | flops 603979776 | bytes 3538944 | tf_op jit(solution)/shard_map/up1/pallas_call | solution.py:165
  215.5 4.0 %down1.1 = bf16[256,2304]{1,0:T(8,128)(2,1)} custom-call(s32[1]{0:T(128)} %bitcast.12.where_ref, bf16[512,4096]{1,0:T(8,128)(2,1)} %bitcast.13.x_ref.do_ref, bf16[512,4096]{1,0:T(8,128)(2,1)} %bitcast.13.x_ref.do_ref, bf16[512,768]{1,0:T(8,128)(2,1)} %get-tuple-element.69.hid_ref, bf16[512,768]{1,0:T(8,128)(2,1)} %get-tuple-element.70.da_ref, ...), custom_call_target="tpu_custom_call" | custom-call | flops 603979776 | bytes 3538944 | tf_op jit(solution)/shard_map/down1/pallas_call | solution.py:165
  219.5 0.7 collective-permute-start.11
  220.2 1.3 collective-permute-start.10
  221.5 6.2 %update0.1 = (bf16[2,512,768]{2,1,0:T(8,128)(2,1)}, bf16[2,512,768]{2,1,0:T(8,128)(2,1)}, bf16[2,512,768]{2,1,0:T(8,128)(2,1)}) custom-call(s32[1]{0:T(128)} %bitcast.19.where_ref, s32[2,3]{1,0:T(2,128)} %mask_ref.3, bf16[256,2304]{1,0:T(8,128)(2,1)} %get-tuple-element.89.refs_0_, bf16[256,2304]{1,0:T(8,128)(2,1)} %collective-permute-done.4.refs_1_, ...), custom_call_target="tpu_custom_call" | custom-call | flops 5898240 | bytes 11796480 | tf_op jit(solution)/shard_map/update0/pallas_call | solution.py:207
  227.7 8.1 %collective-permute-done.7.refs_2_ = bf16[256,2304]{1,0:T(8,128)(2,1)S(1)} collective-permute-done((bf16[256,2304]{1,0:T(8,128)(2,1)}, bf16[256,2304]{1,0:T(8,128)(2,1)S(1)}, u32[]{:S(2)}, u32[]{:S(2)}) %collective-permute-start.7) | collective-permute-done | bytes 1179680 | tf_op jit(solution)/shard_map/ppermute | solution.py:318
  235.9 3.3 %collective-permute-done.6.refs_4_ = bf16[256,2304]{1,0:T(8,128)(2,1)S(1)} collective-permute-done((bf16[256,2304]{1,0:T(8,128)(2,1)}, bf16[256,2304]{1,0:T(8,128)(2,1)S(1)}, u32[]{:S(2)}, u32[]{:S(2)}) %collective-permute-start.6) | collective-permute-done | bytes 1179680 | tf_op jit(solution)/shard_map/ppermute | solution.py:315
  239.2 0.0 all-to-all-done.3
  239.2 4.8 %combine.1 = (bf16[128,2048]{1,0:T(8,128)(2,1)}, f32[8,128]{1,0:T(8,128)}) custom-call(s32[8,128]{1,0:T(8,128)} %bitcast.29, bf16[512,2176]{1,0:T(8,128)(2,1)} %bitcast.24, bf16[512,2176]{1,0:T(8,128)(2,1)} %bitcast.17.refs_1_), custom_call_target="tpu_custom_call" | custom-call | flops 536870912 | bytes 4718592 | tf_op jit(solution)/shard_map/combine/pallas_call | solution.py:282
  244.1 0.0 copy-done.4
  244.1 0.0 copy-done.5
  244.1 0.0 copy-done.7
  244.1 1.3 fusion
  245.4 14.8 %collective-permute-done.11.refs_5_ = bf16[256,2304]{1,0:T(8,128)(2,1)S(1)} collective-permute-done((bf16[256,2304]{1,0:T(8,128)(2,1)}, bf16[256,2304]{1,0:T(8,128)(2,1)S(1)}, u32[]{:S(2)}, u32[]{:S(2)}) %collective-permute-start.11) | collective-permute-done | bytes 1179680 | tf_op jit(solution)/shard_map/ppermute | solution.py:318
  260.2 3.1 %collective-permute-done.10.refs_1_ = bf16[256,2304]{1,0:T(8,128)(2,1)} collective-permute-done((bf16[256,2304]{1,0:T(8,128)(2,1)}, bf16[256,2304]{1,0:T(8,128)(2,1)}, u32[]{:S(2)}, u32[]{:S(2)}) %collective-permute-start.10) | collective-permute-done | bytes 1179680 | tf_op jit(solution)/shard_map/ppermute | solution.py:315
  263.3 0.0 copy-done.6
  263.3 6.3 %update1.1 = (bf16[2,512,768]{2,1,0:T(8,128)(2,1)}, bf16[2,512,768]{2,1,0:T(8,128)(2,1)}, bf16[2,512,768]{2,1,0:T(8,128)(2,1)}) custom-call(s32[1]{0:T(128)} %bitcast.19.where_ref, s32[2,3]{1,0:T(2,128)} %mask_ref.3, bf16[256,2304]{1,0:T(8,128)(2,1)} %get-tuple-element.82.refs_0_, ...), custom_call_target="tpu_custom_call", output_to_operand_aliasing={{0}: (11, {}), {1}: (12, {}), {2}: (13, {})} | custom-call | flops 5898240 | bytes 11796480 | tf_op jit(solution)/shard_map/update1/pallas_call | solution.py:207
  (4 shorter events, 0.0 us)
Async XLA Ops:
  5.4 62.0 %all-to-all-start = ((bf16[32,16,4096]{2,1,0:T(8,128)(2,1)}), bf16[32,16,4096]{2,1,0:T(8,128)(2,1)}, u32[]{:S(2)}, u32[]{:S(2)}) async-start(bf16[32,16,4096]{2,1,0:T(8,128)(2,1)} %bitcast.23), calls=%async_computation | async-start | bytes 8388608 | tf_op jit(solution)/shard_map/all_to_all | solution.py:326
  67.4 61.6 %all-to-all-start.1 = ((bf16[32,16,4096]{2,1,0:T(8,128)(2,1)}), bf16[32,16,4096]{2,1,0:T(8,128)(2,1)}, u32[]{:S(2)}, u32[]{:S(2)}) async-start(bf16[32,16,4096]{2,1,0:T(8,128)(2,1)} %bitcast.22), calls=%async_computation.1 | async-start | bytes 8388608 | tf_op jit(solution)/shard_map/all_to_all | solution.py:326
  90.3 30.4 %collective-permute-start = (bf16[256,2304]{1,0:T(8,128)(2,1)}, bf16[256,2304]{1,0:T(8,128)(2,1)}, u32[]{:S(2)}, u32[]{:S(2)}) collective-permute-start(bf16[256,2304]{1,0:T(8,128)(2,1)} %get-tuple-element.58), channel_id=1, source_target_pairs={{0,32},{32,64},{64,96},{96,0},{1,33},{33,65},{65,97},{97,1},{2,34}... | collective-permute-start | bytes 3538952 | tf_op jit(solution)/shard_map/ppermute | solution.py:315
  91.8 29.2 %collective-permute-start.1 = (bf16[256,2304]{1,0:T(8,128)(2,1)}, bf16[256,2304]{1,0:T(8,128)(2,1)}, u32[]{:S(2)}, u32[]{:S(2)}) collective-permute-start(bf16[256,2304]{1,0:T(8,128)(2,1)} %get-tuple-element.59), channel_id=1, source_target_pairs={{0,96},{32,0},{64,32},{96,64},{1,97},{33,1},{65,33},{97,65},{2,98}... | collective-permute-start | bytes 3538952 | tf_op jit(solution)/shard_map/ppermute | solution.py:318
  104.8 40.2 %collective-permute-start.3 = (bf16[256,2304]{1,0:T(8,128)(2,1)}, bf16[256,2304]{1,0:T(8,128)(2,1)S(1)}, u32[]{:S(2)}, u32[]{:S(2)}) collective-permute-start(bf16[256,2304]{1,0:T(8,128)(2,1)} %get-tuple-element.64), channel_id=1, source_target_pairs={{0,96},{32,0},{64,32},{96,64},{1,97},{33,1},{65,33},{97,65},{2,98}... | collective-permute-start | bytes 3538952 | tf_op jit(solution)/shard_map/ppermute | solution.py:318
  106.3 38.7 %collective-permute-start.2 = (bf16[256,2304]{1,0:T(8,128)(2,1)}, bf16[256,2304]{1,0:T(8,128)(2,1)S(1)}, u32[]{:S(2)}, u32[]{:S(2)}) collective-permute-start(bf16[256,2304]{1,0:T(8,128)(2,1)} %get-tuple-element.60), channel_id=1, source_target_pairs={{0,32},{32,64},{64,96},{96,0},{1,33},{33,65},{65,97},{97,1},{2,34}... | collective-permute-start | bytes 3538952 | tf_op jit(solution)/shard_map/ppermute | solution.py:315
  145.0 1.4 copy-start.1
  145.0 1.1 copy-start.2
  146.4 40.8 %all-to-all-start.2 = ((bf16[32,16,2176]{2,1,0:T(8,128)(2,1)}), bf16[32,16,2176]{2,1,0:T(8,128)(2,1)S(1)}, u32[]{:S(2)}, u32[]{:S(2)}) async-start(bf16[32,16,2176]{2,1,0:T(8,128)(2,1)} %bitcast.26), calls=%async_computation.2 | async-start | bytes 4456448 | tf_op jit(solution)/shard_map/all_to_all | solution.py:329
  153.8 31.9 %collective-permute-start.5 = (bf16[256,2304]{1,0:T(8,128)(2,1)}, bf16[256,2304]{1,0:T(8,128)(2,1)S(1)}, u32[]{:S(2)}, u32[]{:S(2)}) collective-permute-start(bf16[256,2304]{1,0:T(8,128)(2,1)} %down0.1), channel_id=1, source_target_pairs={{0,96},{32,0},{64,32},{96,64},{1,97},{33,1},{65,33},{97,65},{2,98}... | collective-permute-start | bytes 3538952 | tf_op jit(solution)/shard_map/ppermute | solution.py:318
  156.8 30.4 %collective-permute-start.4 = (bf16[256,2304]{1,0:T(8,128)(2,1)}, bf16[256,2304]{1,0:T(8,128)(2,1)}, u32[]{:S(2)}, u32[]{:S(2)}) collective-permute-start(bf16[256,2304]{1,0:T(8,128)(2,1)} %up0.1), channel_id=1, source_target_pairs={{0,32},{32,64},{64,96},{96,0},{1,33},{33,65},{65,97},{97,1},{2,34}... | collective-permute-start | bytes 3538952 | tf_op jit(solution)/shard_map/ppermute | solution.py:315
  174.3 34.7 %collective-permute-start.9 = (bf16[256,2304]{1,0:T(8,128)(2,1)}, bf16[256,2304]{1,0:T(8,128)(2,1)}, u32[]{:S(2)}, u32[]{:S(2)}) collective-permute-start(bf16[256,2304]{1,0:T(8,128)(2,1)} %get-tuple-element.83), channel_id=1, source_target_pairs={{0,96},{32,0},{64,32},{96,64},{1,97},{33,1},{65,33},{97,65},{2,98}... | collective-permute-start | bytes 3538952 | tf_op jit(solution)/shard_map/ppermute | solution.py:318
  177.5 34.0 %collective-permute-start.8 = (bf16[256,2304]{1,0:T(8,128)(2,1)}, bf16[256,2304]{1,0:T(8,128)(2,1)}, u32[]{:S(2)}, u32[]{:S(2)}) collective-permute-start(bf16[256,2304]{1,0:T(8,128)(2,1)} %get-tuple-element.72), channel_id=1, source_target_pairs={{0,32},{32,64},{64,96},{96,0},{1,33},{33,65},{65,97},{97,1},{2,34}... | collective-permute-start | bytes 3538952 | tf_op jit(solution)/shard_map/ppermute | solution.py:315
  185.7 1.5 copy-start.3
  187.2 1.4 copy-start
  188.5 50.7 %all-to-all-start.3 = ((bf16[32,16,2176]{2,1,0:T(8,128)(2,1)}), bf16[32,16,2176]{2,1,0:T(8,128)(2,1)}, u32[]{:S(2)}, u32[]{:S(2)}) async-start(bf16[32,16,2176]{2,1,0:T(8,128)(2,1)} %bitcast.25), calls=%async_computation.3 | async-start | bytes 4456448 | tf_op jit(solution)/shard_map/all_to_all | solution.py:329
  206.8 29.0 %collective-permute-start.7 = (bf16[256,2304]{1,0:T(8,128)(2,1)}, bf16[256,2304]{1,0:T(8,128)(2,1)S(1)}, u32[]{:S(2)}, u32[]{:S(2)}) collective-permute-start(bf16[256,2304]{1,0:T(8,128)(2,1)} %get-tuple-element.77), channel_id=1, source_target_pairs={{0,96},{32,0},{64,32},{96,64},{1,97},{33,1},{65,33},{97,65},{2,98}... | collective-permute-start | bytes 3538952 | tf_op jit(solution)/shard_map/ppermute | solution.py:318
  208.9 30.3 %collective-permute-start.6 = (bf16[256,2304]{1,0:T(8,128)(2,1)}, bf16[256,2304]{1,0:T(8,128)(2,1)S(1)}, u32[]{:S(2)}, u32[]{:S(2)}) collective-permute-start(bf16[256,2304]{1,0:T(8,128)(2,1)} %get-tuple-element.76), channel_id=1, source_target_pairs={{0,32},{32,64},{64,96},{96,0},{1,33},{33,65},{65,97},{97,1},{2,34}... | collective-permute-start | bytes 3538952 | tf_op jit(solution)/shard_map/ppermute | solution.py:315
  219.5 40.7 %collective-permute-start.11 = (bf16[256,2304]{1,0:T(8,128)(2,1)}, bf16[256,2304]{1,0:T(8,128)(2,1)S(1)}, u32[]{:S(2)}, u32[]{:S(2)}) collective-permute-start(bf16[256,2304]{1,0:T(8,128)(2,1)} %down1.1), channel_id=1, source_target_pairs={{0,96},{32,0},{64,32},{96,64},{1,97},{33,1},{65,33},{97,65},{2,98}... | collective-permute-start | bytes 3538952 | tf_op jit(solution)/shard_map/ppermute | solution.py:318
  220.2 43.2 %collective-permute-start.10 = (bf16[256,2304]{1,0:T(8,128)(2,1)}, bf16[256,2304]{1,0:T(8,128)(2,1)}, u32[]{:S(2)}, u32[]{:S(2)}) collective-permute-start(bf16[256,2304]{1,0:T(8,128)(2,1)} %up1.1), channel_id=1, source_target_pairs={{0,32},{32,64},{64,96},{96,0},{1,33},{33,65},{65,97},{97,1},{2,34}... | collective-permute-start | bytes 3538952 | tf_op jit(solution)/shard_map/ppermute | solution.py:315
  235.9 8.2 %copy-start.4 = (bf16[256,2304]{1,0:T(8,128)(2,1)}, bf16[256,2304]{1,0:T(8,128)(2,1)S(1)}, u32[]{:S(2)}) copy-start(bf16[256,2304]{1,0:T(8,128)(2,1)S(1)} %collective-permute-done.7.refs_2_) | copy-start | bytes 3538948
  239.2 4.9 %copy-start.5 = (bf16[256,2304]{1,0:T(8,128)(2,1)}, bf16[256,2304]{1,0:T(8,128)(2,1)S(1)}, u32[]{:S(2)}) copy-start(bf16[256,2304]{1,0:T(8,128)(2,1)S(1)} %collective-permute-done.6.refs_4_) | copy-start | bytes 3538948
  239.2 4.9 %copy-start.7 = (bf16[128,8]{0,1:T(8,128)(2,1)S(1)}, bf16[128,8]{0,1:T(8,128)(2,1)}, u32[]{:S(2)}) copy-start(bf16[128,8]{0,1:T(8,128)(2,1)} %param.11) | copy-start | bytes 6148
  260.2 3.1 %copy-start.6 = (bf16[256,2304]{1,0:T(8,128)(2,1)}, bf16[256,2304]{1,0:T(8,128)(2,1)S(1)}, u32[]{:S(2)}) copy-start(bf16[256,2304]{1,0:T(8,128)(2,1)S(1)} %collective-permute-done.11.refs_5_) | copy-start | bytes 3538948

commit v5 on v4

v5 whole, which is shorter than its diff:
```python
import functools

import jax
import jax.numpy as jnp
from jax import lax
from jax.experimental import pallas as pl
from jax.experimental.pallas import tpu as pltpu
from jax.sharding import PartitionSpec as P

step_size = 0.004
shrink_rate = 0.1
LANES = 128
F32 = jnp.float32
BF16 = jnp.bfloat16
VMEM_LIMIT = 60 * 1024 * 1024


def dot(a, b, dims):
    return lax.dot_general(a, b, (dims, ((), ())), preferred_element_type=F32)


def cost(flops, moved, chunk=1):
    scale = (10, 18)[min(chunk, 1)]
    return pl.CostEstimate(flops=scale * flops, transcendentals=0, bytes_accessed=scale * moved)


NN = ((1,), (0,))
NT = ((1,), (1,))
TN = ((0,), (0,))


def slot_values(ids_t, n_experts, capacity):
    topk, tok = ids_t.shape
    rows = lax.broadcasted_iota(jnp.int32, (n_experts, tok), 0)
    hit = ids_t[0:1, :] == rows
    for k in range(1, topk):
        hit = jnp.logical_or(hit, ids_t[k : k + 1, :] == rows)
    hit_f = jnp.where(hit, 1.0, 0.0)
    earlier = lax.broadcasted_iota(jnp.int32, (tok, tok), 0) < lax.broadcasted_iota(
        jnp.int32, (tok, tok), 1
    )
    count = dot(hit_f.astype(BF16), jnp.where(earlier, 1.0, 0.0).astype(BF16), NN)
    return jnp.where(jnp.logical_and(hit, count < capacity), count, -1.0)


def slot_rows(values, chunk, local_exp, capacity):
    n_experts, tok = values.shape
    n_rows = n_experts // local_exp * capacity
    expert_of = lax.broadcasted_iota(jnp.int32, (n_rows, n_experts), 0) // capacity * local_exp + chunk
    spread = jnp.where(expert_of == lax.broadcasted_iota(jnp.int32, (n_rows, n_experts), 1), 1.0, 0.0)
    spread = spread.astype(BF16)
    at = dot(spread, values.astype(BF16), NN)
    place = (lax.broadcasted_iota(jnp.int32, (n_rows, tok), 0) % capacity).astype(F32)
    return at == place, spread


def dispatch_kernel(chunk, local_exp, capacity, ids_ref, probs_ref, tok_ref, grad_ref, out_ref):
    ids_t = ids_ref[...]
    topk, tok = ids_t.shape
    n_experts = out_ref.shape[0] // capacity * local_exp
    width = tok_ref.shape[1]
    values = slot_values(ids_t, n_experts, capacity)
    rows = lax.broadcasted_iota(jnp.int32, (n_experts, tok), 0)
    prob = jnp.zeros((n_experts, tok), F32)
    for k in range(topk):
        prob = prob + jnp.where(ids_t[k : k + 1, :] == rows, probs_ref[k : k + 1, :].astype(F32), 0.0)
    onehot, spread = slot_rows(values, chunk, local_exp, capacity)
    prob_rows = dot(spread, prob.astype(BF16), NN)
    pick = jnp.where(onehot, 1.0, 0.0).astype(BF16)
    weighted = jnp.where(onehot, prob_rows, 0.0).astype(BF16)
    out_ref[:, :width] = dot(pick, tok_ref[...], NN).astype(BF16)
    out_ref[:, width:] = dot(weighted, grad_ref[...], NN).astype(BF16)


def dispatch(chunk, local_exp, capacity, n_experts, ids_t, probs_t, tokens, out_grad):
    tok, width = tokens.shape
    n_rows = n_experts // local_exp * capacity
    return pl.pallas_call(
        functools.partial(dispatch_kernel, chunk, local_exp, capacity),
        out_shape=jax.ShapeDtypeStruct((n_rows, 2 * width), BF16),
        compiler_params=pltpu.CompilerParams(vmem_limit_bytes=VMEM_LIMIT),
        cost_estimate=cost(4 * n_rows * tok * width, 4 * width * (tok + n_rows), 0),
        name=f"dispatch{chunk}",
    )(ids_t, probs_t, tokens, out_grad)


def hidden_kernel(
    where_ref, x_ref, do_ref, xa_ref, xb_ref, da_col_ref, db_col_ref, wg_ref, wu_ref, wd_ref,
    hid_ref, da_ref, db_ref, s_ref, a_ref, b_ref, sum_ref,
):
    step = pl.program_id(0)
    gate = dot(x_ref[...], wg_ref[0], NN)
    upper = dot(x_ref[...], wu_ref[0], NN)
    sig = jax.nn.sigmoid(gate)
    act = gate * sig
    hid = (act * upper).astype(BF16)
    hid_ref[...] = hid
    dhid = dot(do_ref[...], wd_ref[0], NN)
    part = jnp.sum(hid.astype(F32) * dhid, axis=1, keepdims=True)
    dgate = (dhid * upper * sig * (1.0 + gate * (1.0 - sig))).astype(BF16)
    dup = (dhid * act).astype(BF16)
    da_ref[...] = dgate
    db_ref[...] = dup
    for out_ref, x_col, do_col in ((a_ref, xa_ref, da_col_ref), (b_ref, xb_ref, db_col_ref)):
        out_ref[0] = dot(x_col[...], dgate, TN).astype(BF16)
        out_ref[1] = dot(x_col[...], dup, TN).astype(BF16)
        out_ref[2] = dot(do_col[...], hid, TN).astype(BF16)

    @pl.when(step == 0)
    def _():
        sum_ref[...] = jnp.broadcast_to(part, sum_ref.shape)

    @pl.when(step > 0)
    def _():
        sum_ref[...] = sum_ref[...] + part

    @pl.when(step == pl.num_programs(0) - 1)
    def _():
        total = sum_ref[...]
        high = total.astype(BF16).astype(F32)
        lane = lax.broadcasted_iota(jnp.int32, s_ref.shape, 1)
        s_ref[...] = jnp.where(lane == 0, high, jnp.where(lane == 1, total - high, 0.0)).astype(BF16)


def whole(shape):
    return pl.BlockSpec(shape, lambda *_: (0,) * len(shape), pipeline_mode=pl.Buffered(1))


def hidden_grads(chunk, where, half, rows, wg, wu, wd):
    n_rows, width = rows.shape[0], rows.shape[1] // 2
    hidden = wg.shape[2]
    block = 2 * LANES
    lefts = width // half
    once = pl.Buffered(1)
    weight = pl.BlockSpec((1, width, block), lambda i, at: (chunk, 0, i))
    result = pl.BlockSpec((n_rows, block), lambda i, at: (0, i))
    shard = pl.BlockSpec((3, half, block), lambda i, at: (0, 0, i))
    return pl.pallas_call(
        hidden_kernel,
        grid_spec=pltpu.PrefetchScalarGridSpec(
            num_scalar_prefetch=1,
            grid=(hidden // block,),
            in_specs=[
                pl.BlockSpec((n_rows, width), lambda i, at: (0, 0), pipeline_mode=once),
                pl.BlockSpec((n_rows, width), lambda i, at: (0, 1), pipeline_mode=once),
                pl.BlockSpec((n_rows, half), lambda i, at: (0, at[0]), pipeline_mode=once),
                pl.BlockSpec((n_rows, half), lambda i, at: (0, at[1]), pipeline_mode=once),
                pl.BlockSpec((n_rows, half), lambda i, at: (0, at[0] + lefts), pipeline_mode=once),
                pl.BlockSpec((n_rows, half), lambda i, at: (0, at[1] + lefts), pipeline_mode=once),
                weight,
                weight,
                weight,
            ],
            out_specs=[result] * 3 + [whole((n_rows, LANES)), shard, shard],
            scratch_shapes=[pltpu.VMEM((n_rows, LANES), F32)],
        ),
        out_shape=[jax.ShapeDtypeStruct((n_rows, hidden), BF16)] * 3
        + [jax.ShapeDtypeStruct((n_rows, LANES), BF16)]
        + [jax.ShapeDtypeStruct((3, half, hidden), BF16)] * 2,
        compiler_params=pltpu.CompilerParams(vmem_limit_bytes=VMEM_LIMIT),
        cost_estimate=cost(8 * n_rows * width * hidden, 6 * width * hidden + n_rows * (4 * width + 6 * hidden), chunk),
        name=f"hidden{chunk}",
    )(where, *[rows] * 6, wg, wu, wd)


def weight_kernel(n_add, where_ref, x_ref, do_ref, hid_ref, da_ref, db_ref, *refs):
    adds, outs = refs[:n_add], refs[n_add:]
    for m, (left, right) in enumerate(((x_ref, da_ref), (x_ref, db_ref), (do_ref, hid_ref))):
        part = dot(left[...], right[...], TN)
        for addend in adds:
            part = part + addend[m].astype(F32)
        for i, out_ref in enumerate(outs):

            @pl.when(pl.program_id(0) == i)
            def _():
                out_ref[m] = part.astype(BF16)


def weight_grads(name, chunk, where, count, half, rows, hid, da, db, *adds):
    n_rows, width = rows.shape[0], rows.shape[1] // 2
    hidden = hid.shape[1]
    lefts = width // half
    shape = (3, half, hidden)
    return pl.pallas_call(
        functools.partial(weight_kernel, len(adds)),
        grid_spec=pltpu.PrefetchScalarGridSpec(
            num_scalar_prefetch=1,
            grid=(count,),
            in_specs=[
                pl.BlockSpec((n_rows, half), lambda i, at: (0, at[i])),
                pl.BlockSpec((n_rows, half), lambda i, at: (0, at[i] + lefts)),
            ]
            + [whole(a.shape) for a in (hid, da, db, *adds)],
            out_specs=[whole(shape)] * count,
        ),
        out_shape=[jax.ShapeDtypeStruct(shape, BF16)] * count,
        compiler_params=pltpu.CompilerParams(vmem_limit_bytes=VMEM_LIMIT),
        cost_estimate=cost(6 * count * n_rows * half * hidden, 6 * n_rows * hidden + 6 * count * half * hidden, chunk),
        name=name,
    )(where, rows, rows, hid, da, db, *adds)


def update_kernel(chunk, where_ref, mask_ref, *refs):
    grads, weights = refs[:6], refs[6:9]
    outs = refs[-3:]
    for second in range(2):

        @pl.when(pl.program_id(0) == second)
        def _():
            for m in range(3):
                grad = sum(g[m].astype(F32) for g in grads[3 * second : 3 * second + 3])
                weight = weights[m][0].astype(F32)
                rate = mask_ref[chunk, m].astype(F32)
                outs[m][0] = (weight - step_size * grad - shrink_rate * rate * weight).astype(BF16)


def update(chunk, where, mask, grads, weights, into):
    _, half, hidden = grads[0].shape
    local = weights[0].shape[0]
    steps = 4
    block = half // steps
    early = pl.BlockSpec((3, block, hidden), lambda h, r, w: (0, r * (1 - h) + (steps - 1) * h, 0))
    late = pl.BlockSpec((3, block, hidden), lambda h, r, w: (0, r * h, 0))
    weight = pl.BlockSpec((1, block, hidden), lambda h, r, w: (chunk, (2 * w[0] + h) * steps + r, 0))
    result = pl.BlockSpec((1, block, hidden), lambda h, r, w: (chunk, h * steps + r, 0))
    extra = list(into or [])
    return pl.pallas_call(
        functools.partial(update_kernel, chunk),
        grid_spec=pltpu.PrefetchScalarGridSpec(
            num_scalar_prefetch=1,
            grid=(2, steps),
            in_specs=[pl.BlockSpec(memory_space=pltpu.SMEM)]
            + [early] * 3
            + [late] * 3
            + [weight] * 3
            + [pl.BlockSpec(memory_space=pl.ANY)] * len(extra),
            out_specs=[result] * 3,
        ),
        out_shape=[jax.ShapeDtypeStruct((local, 2 * half, hidden), BF16)] * 3,
        input_output_aliases={11 + i: i for i in range(len(extra))},
        compiler_params=pltpu.CompilerParams(vmem_limit_bytes=VMEM_LIMIT),
        cost_estimate=cost(10 * half * hidden, 60 * half * hidden),
        name=f"update{chunk}",
    )(where, mask, *grads, *weights, *extra)


def dx_kernel(da_ref, db_ref, s_ref, wg_ref, wu_ref, *refs):
    out_ref = refs[-1]
    n_owner, capacity, lanes = out_ref.shape
    width = wg_ref.shape[1]
    dx = (dot(da_ref[...], wg_ref[0], NT) + dot(db_ref[...], wu_ref[0], NT)).astype(BF16)
    out_ref[:, :, :width] = dx.reshape(n_owner, capacity, width)
    out_ref[:, :, width:] = s_ref[...].reshape(n_owner, capacity, lanes - width)


def input_grads(chunk, local_exp, capacity, da, db, s, wg, wu, into):
    n_rows, hidden = da.shape
    width = wg.shape[1]
    n_owner = n_rows // capacity
    weight = pl.BlockSpec((1, width, hidden), lambda i: (chunk, 0, 0), pipeline_mode=pl.Buffered(1))
    extra = [] if into is None else [into]
    return pl.pallas_call(
        dx_kernel,
        grid=(1,),
        in_specs=[whole((n_rows, hidden)), whole((n_rows, hidden)), whole((n_rows, LANES)), weight, weight]
        + [pl.BlockSpec(memory_space=pl.ANY)] * len(extra),
        out_specs=pl.BlockSpec(
            (n_owner, capacity, width + LANES), lambda i: (0, chunk, 0), pipeline_mode=pl.Buffered(1)
        ),
        out_shape=jax.ShapeDtypeStruct((n_owner, local_exp * capacity, width + LANES), BF16),
        input_output_aliases={5: 0} if extra else {},
        compiler_params=pltpu.CompilerParams(vmem_limit_bytes=VMEM_LIMIT),
        cost_estimate=cost(4 * n_rows * width * hidden, 4 * width * hidden + 2 * n_rows * (width + 2 * hidden), chunk),
        name=f"dx{chunk}",
    )(da, db, s, wg, wu, *extra)


def combine_kernel(local_exp, capacity, ids_ref, back_ref, tok_ref, prob_ref):
    ids_t = ids_ref[...]
    topk, tok = ids_t.shape
    n_rows = back_ref.shape[0] * capacity
    n_experts = back_ref.shape[0] * local_exp
    width = tok_ref.shape[1]
    values = slot_values(ids_t, n_experts, capacity)
    total = jnp.zeros((tok, width), F32)
    by_expert = jnp.zeros((n_experts, tok), F32)
    for chunk in range(local_exp):
        onehot, spread = slot_rows(values, chunk, local_exp, capacity)
        pick = jnp.where(onehot, 1.0, 0.0)
        slots = slice(chunk * capacity, (chunk + 1) * capacity)
        dx = back_ref[:, slots, :width].reshape(n_rows, width)
        total = total + dot(pick.astype(BF16), dx, TN)
        s = back_ref[:, slots, width:].reshape(n_rows, LANES).astype(F32)
        placed = pick * (s[:, 0:1] + s[:, 1:2])
        high = placed.astype(BF16)
        low = (placed - high.astype(F32)).astype(BF16)
        by_expert = by_expert + dot(spread, high, TN) + dot(spread, low, TN)
    tok_ref[...] = total.astype(BF16)
    rows = lax.broadcasted_iota(jnp.int32, (n_experts, tok), 0)
    for k in range(topk):
        mine = jnp.where(ids_t[k : k + 1, :] == rows, by_expert, 0.0)
        prob_ref[k : k + 1, :] = jnp.sum(mine, axis=0, keepdims=True)


def combine(local_exp, capacity, ids_t, back, width):
    topk, tok = ids_t.shape
    return pl.pallas_call(
        functools.partial(combine_kernel, local_exp, capacity),
        out_shape=[
            jax.ShapeDtypeStruct((tok, width), BF16),
            jax.ShapeDtypeStruct((topk, tok), F32),
        ],
        compiler_params=pltpu.CompilerParams(vmem_limit_bytes=VMEM_LIMIT),
        cost_estimate=cost(2 * back.shape[0] * back.shape[1] * tok * width, 2 * back.size),
        name="combine",
    )(ids_t, back)


def body(tokens, out_grad, expert_ids, route_probs, w_gate, w_up, w_down, decay_mask):
    n_owner = lax.axis_size("expert")
    n_group = lax.axis_size("dp")
    local_exp = w_gate.shape[0]
    width = tokens.shape[1]
    tok_rows, topk = expert_ids.shape
    n_experts = n_owner * local_exp
    capacity = tok_rows * topk // n_experts
    ids_t = expert_ids.T
    probs_t = route_probs.T
    half = width // n_group // 2
    plane = lax.axis_index("dp").astype(jnp.int32)
    where = plane.reshape(1)

    def half_shard(ahead, second):
        return 2 * ((plane + ahead) % n_group) + second

    def blocks(*pairs):
        return jnp.stack([half_shard(*pair) for pair in pairs]).astype(jnp.int32)

    def up(a):
        return lax.ppermute(a, "dp", [(i, (i + 1) % n_group) for i in range(n_group)])

    def down(a):
        return lax.ppermute(a, "dp", [(i, (i - 1) % n_group) for i in range(n_group)])

    def send(chunk):
        return dispatch(chunk, local_exp, capacity, n_experts, ids_t, probs_t, tokens, out_grad)

    def swap(a):
        return lax.all_to_all(a, "expert", split_axis=0, concat_axis=0, tiled=True)

    def swap_rows(a):
        a = a.reshape(n_owner, capacity, a.shape[1])
        return swap(a).reshape(n_owner * capacity, a.shape[2])

    def order(value, *after):
        return lax.optimization_barrier((value, *after))[0]

    weights = (w_gate, w_up, w_down)
    far_pairs = ((2, 0), (2, 1))
    near_pairs = ((1, 1), (n_group - 1, 0))
    own_pairs = ((0, 0), (0, 1))
    new, dx, before = None, None, None
    sends = [send(chunk) for chunk in range(local_exp)]
    rows = order(swap_rows(sends[0]), *sends[1:])
    for chunk in range(local_exp):
        hid, da, db, s, *far = hidden_grads(chunk, blocks(*far_pairs), half, rows, *weights)
        far_up, far_down = up(far[0]), down(far[1])
        grads = (rows, hid, da, db)
        if before:
            rows, _, *last = lax.optimization_barrier((rows, far[0], *before[1]))
            own, (near_up, near_down) = before[0], before[2]
            new = update(chunk - 1, where, decay_mask, (own[0], last[0], near_down, own[1], near_up, last[1]), weights, new)
            grads = (rows, hid, da, db)
        near = weight_grads(f"near{chunk}", chunk, blocks(*near_pairs), 2, half, *grads)
        near_up, near_down = up(near[0]), down(near[1])
        if chunk + 1 < local_exp:
            following = swap_rows(order(sends[chunk + 1], near[0]))
        if before:
            dx = input_grads(chunk, local_exp, capacity, da, db, s, w_gate, w_up, order(dx, near[0]))
            far_up, far_down = order(far_up, dx), order(far_down, dx)
            back = swap(dx)
        far_up, far_down, _ = lax.optimization_barrier((far_up, far_down, near[0]))
        sum_up = weight_grads(f"up{chunk}", chunk, blocks((1, 0)), 1, half, *grads, far_up)[0]
        sum_down = weight_grads(f"down{chunk}", chunk, blocks((n_group - 1, 1)), 1, half, *grads, far_down)[0]
        own = list(weight_grads(f"own{chunk}", chunk, blocks(*own_pairs), 2, half, *grads))
        sent = [up(sum_up), down(sum_down)]
        if chunk + 1 < local_exp:
            dx = input_grads(chunk, local_exp, capacity, order(da, sum_up, sum_down), db, s, w_gate, w_up, dx)
            rows, dx, own[0], near_up, near_down, *_ = lax.optimization_barrier(
                (following, dx, own[0], near_up, near_down, sum_up, sum_down)
            )
        before = (own, sent, (near_up, near_down))
    back, near_up, near_down = lax.optimization_barrier((back, near_up, near_down))
    new = update(
        local_exp - 1, where, decay_mask, (own[0], sent[0], near_down, own[1], near_up, sent[1]), weights, new
    )
    grad_tokens, scores = combine(local_exp, capacity, ids_t, back, width)
    grad_probs = (scores / probs_t.astype(F32)).astype(BF16).T

    return (grad_tokens, grad_probs, *new)


def solution(mesh):
    placed = (
        P(("dp", "expert"), None),
        P(("dp", "expert"), None),
        P(("dp", "expert"), None),
        P(("dp", "expert"), None),
        P("expert", None, None),
        P("expert", None, None),
        P("expert", None, None),
        P("expert", None),
    )
    return jax.shard_map(
        body,
        mesh=mesh,
        in_specs=placed,
        out_specs=(
            P(("dp", "expert"), None),
            P(("dp", "expert"), None),
            P("expert", "dp", None),
            P("expert", "dp", None),
            P("expert", "dp", None),
        ),
        check_vma=False,
    )
```

time: 270 us -> 265 us (0.981)
  starting transfers between devices: 44.1 us -> 38 us
  Pallas kernels: 115 us -> 120 us
  waiting for transfers between devices: 104 us -> 100 us
    all_to_all x4 -> x3, waiting for transfers between devices: 48.6 us -> 78 us  [swap(): return lax.all_to_all(a, 'expert', split_axis=0, concat_axis=0, tiled=True)]
    ppermute x6, waiting for transfers between devices: 31.1 us -> 10.9 us  [down(): lax.ppermute(a, 'dp', [(i, (i - 1) % n_group) for i in range(n_group)])]
    ppermute x6, waiting for transfers between devices: 24.4 us -> 11.1 us  [up(): lax.ppermute(a, 'dp', [(i, (i + 1) % n_group) for i in range(n_group)])]
    all_to_all x4 -> x3, starting transfers between devices: 28.5 us -> 18.3 us  [swap(): return lax.all_to_all(a, 'expert', split_axis=0, concat_axis=0, tiled=True)]
    pallas_call x2, Pallas kernels: 21.4 us -> 30.5 us  [hidden_grads(): pl.pallas_call(hidden_kernel, grid_spec=pltpu.PrefetchScalarGridSpec(num_...]
    pallas_call x8, Pallas kernels: 50.6 us -> 43.3 us  [weight_grads(): pl.pallas_call(functools.partial(weight_kernel, len(adds)), grid_spec=plt...]
    ppermute x6, starting transfers between devices: 12.3 us -> 17.9 us  [down(): lax.ppermute(a, 'dp', [(i, (i - 1) % n_group) for i in range(n_group)])]
    pallas_call x2, Pallas kernels: 12.5 us -> 16 us  [update(): pl.pallas_call(functools.partial(update_kernel, chunk), grid_spec=pltpu.P...]
  transfers between devices with their start and end apart: 16 -> 15, of which waited for: 10 -> 8; matrix products, arithmetic and copies ran while one was open for 1% -> 1% of each run, Pallas kernels for 39% -> 35%
where the time goes in v5:
time: 265 us; the launch traced here: 264 us
  Pallas kernels  120 us (45%)
  waiting for transfers between devices  100 us (38%)
  starting transfers between devices  38 us (14%)
  other arithmetic  3.16 us (1%)
    all_to_all x3, waiting for transfers between devices, swap(): return lax.all_to_all(a, 'expert', split_axis=0, concat_axis=0, tiled=True)  78 us
    pallas_call x8, Pallas kernels, weight_grads(): pl.pallas_call(functools.partial(weight_kernel, len(adds)), grid_spec=plt...  43.3 us
    pallas_call x2, Pallas kernels, hidden_grads(): pl.pallas_call(hidden_kernel, grid_spec=pltpu.PrefetchScalarGridSpec(num_...  30.5 us
    all_to_all x3, starting transfers between devices, swap(): return lax.all_to_all(a, 'expert', split_axis=0, concat_axis=0, tiled=True)  18.3 us
    ppermute x6, starting transfers between devices, down(): lax.ppermute(a, 'dp', [(i, (i - 1) % n_group) for i in range(n_group)])  17.9 us
    pallas_call x2, Pallas kernels, input_grads(): pl.pallas_call(dx_kernel, grid=(1,), in_specs=[whole((n_rows, hidden)), w...  16.5 us
    pallas_call x2, Pallas kernels, update(): pl.pallas_call(functools.partial(update_kernel, chunk), grid_spec=pltpu.P...  16 us
    ppermute x6, waiting for transfers between devices, up(): lax.ppermute(a, 'dp', [(i, (i + 1) % n_group) for i in range(n_group)])  11.1 us
  transfers between devices with their start and end apart: 15, of which 8 were waited for; matrix products, arithmetic and copies ran while one was open for 1% of the time, Pallas kernels for 35%

profile of v5, /device:TPU:0, one launch (start us, length us, event | category | flops | bytes accessed | tf_op | source)
XLA Modules:
  0.0 264.4 jit_solution(3996300566333616382)
XLA Ops:
  0.6 4.8 %dispatch0.1 = bf16[512,4096]{1,0:T(8,128)(2,1)} custom-call(s32[8,128]{1,0:T(8,128)} %bitcast.22, bf16[8,128]{1,0:T(8,128)(2,1)} %bitcast.20, bf16[128,2048]{1,0:T(8,128)(2,1)} %tok_ref.3, bf16[128,2048]{1,0:T(8,128)(2,1)} %grad_ref.3), custom_call_target="tpu_custom_call" | custom-call | flops 5368709120 | bytes 52428800 | tf_op jit(solution)/shard_map/dispatch0/pallas_call | solution.py:78
  5.4 8.5 %all-to-all-start = ((bf16[32,16,4096]{2,1,0:T(8,128)(2,1)}), bf16[32,16,4096]{2,1,0:T(8,128)(2,1)}, u32[]{:S(2)}, u32[]{:S(2)}) async-start(bf16[32,16,4096]{2,1,0:T(8,128)(2,1)} %bitcast.18), calls=%async_computation | async-start | bytes 8388608 | tf_op jit(solution)/shard_map/all_to_all | solution.py:349
  14.0 0.7 pad_add_fusion.where_ref
  14.7 0.6 pad_add_fusion.2.where_ref
  15.2 0.6 pad_add_fusion.1.where_ref
  15.9 4.7 %dispatch1.1 = bf16[512,4096]{1,0:T(8,128)(2,1)} custom-call(s32[8,128]{1,0:T(8,128)} %bitcast.23, bf16[8,128]{1,0:T(8,128)(2,1)} %bitcast.21, bf16[128,2048]{1,0:T(8,128)(2,1)} %tok_ref.3, bf16[128,2048]{1,0:T(8,128)(2,1)} %grad_ref.3), custom_call_target="tpu_custom_call" | custom-call | flops 5368709120 | bytes 52428800 | tf_op jit(solution)/shard_map/dispatch1/pallas_call | solution.py:78
  20.6 46.8 %all-to-all-done = bf16[32,16,4096]{2,1,0:T(8,128)(2,1)} async-done(((bf16[32,16,4096]{2,1,0:T(8,128)(2,1)}), bf16[32,16,4096]{2,1,0:T(8,128)(2,1)}, u32[]{:S(2)}, u32[]{:S(2)}) %all-to-all-start) | async-done | bytes 4194336 | tf_op jit(solution)/shard_map/all_to_all | solution.py:349
  67.4 15.3 %hidden0.1 = (bf16[512,768]{1,0:T(8,128)(2,1)}, bf16[512,768]{1,0:T(8,128)(2,1)}, bf16[512,768]{1,0:T(8,128)(2,1)}, bf16[512,128]{1,0:T(8,128)(2,1)}, bf16[3,256...) custom-call(s32[2]{0:T(128)} %pad_add_fusion.where_ref, ...), custom_call_target="tpu_custom_call" | custom-call | flops 64424509440 | bytes 159907840 | tf_op jit(solution)/shard_map/hidden0/pallas_call | solution.py:138
  82.7 1.4 collective-permute-start
  84.2 1.8 collective-permute-start.1
  86.0 6.8 %near0.1 = (bf16[3,256,768]{2,1,0:T(8,128)(2,1)}, bf16[3,256,768]{2,1,0:T(8,128)(2,1)}) custom-call(s32[2]{0:T(128)} %pad_add_fusion.1.where_ref, bf16[512,4096]{1,0:T(8,128)(2,1)} %bitcast.7.x_ref.do_ref.xa_ref.xb_ref.da_col_ref.db_col_ref, bf16[512,4096]{1,0:T(8,128)(2,1)} %bitcast.7.x_ref.do_ref.xa_ref.xb_ref.da_col_ref.db_col_ref, ...), custom_call_target="tpu_custom_call" | custom-call | flops 12079595520 | bytes 47185920 | tf_op jit(solution)/shard_map/near0/pallas_call | solution.py:184
  92.8 0.2 collective-permute-start.2
  93.0 3.0 %collective-permute-start.3 = (bf16[3,256,768]{2,1,0:T(8,128)(2,1)}, bf16[3,256,768]{2,1,0:T(8,128)(2,1)S(1)}, u32[]{:S(2)}, u32[]{:S(2)}) collective-permute-start(bf16[3,256,768]{2,1,0:T(8,128)(2,1)} %get-tuple-element.67), channel_id=1, source_target_pairs={{0,96},{32,0},{64,32},{96,64},{1,97},{33,1},{65,33},{97,65},{2,98}... | collective-permute-start | bytes 3538952 | tf_op jit(solution)/shard_map/ppermute | solution.py:343
  96.0 4.9 %all-to-all-start.1 = ((bf16[32,16,4096]{2,1,0:T(8,128)(2,1)}), bf16[32,16,4096]{2,1,0:T(8,128)(2,1)}, u32[]{:S(2)}, u32[]{:S(2)}) async-start(bf16[32,16,4096]{2,1,0:T(8,128)(2,1)} %bitcast.19), calls=%async_computation.1 | async-start | bytes 8388608 | tf_op jit(solution)/shard_map/all_to_all | solution.py:349
  100.9 6.8 %own0.1 = (bf16[3,256,768]{2,1,0:T(8,128)(2,1)}, bf16[3,256,768]{2,1,0:T(8,128)(2,1)}) custom-call(s32[2]{0:T(128)} %pad_add_fusion.2.where_ref, bf16[512,4096]{1,0:T(8,128)(2,1)} %bitcast.7.x_ref.do_ref.xa_ref.xb_ref.da_col_ref.db_col_ref, bf16[512,4096]{1,0:T(8,128)(2,1)} %bitcast.7.x_ref.do_ref.xa_ref.xb_ref.da_col_ref.db_col_ref, ...), custom_call_target="tpu_custom_call" | custom-call | flops 12079595520 | bytes 47185920 | tf_op jit(solution)/shard_map/own0/pallas_call | solution.py:184
  107.6 5.4 %collective-permute-done.refs_0_ = bf16[3,256,768]{2,1,0:T(8,128)(2,1)S(1)} collective-permute-done((bf16[3,256,768]{2,1,0:T(8,128)(2,1)}, bf16[3,256,768]{2,1,0:T(8,128)(2,1)S(1)}, u32[]{:S(2)}, u32[]{:S(2)}) %collective-permute-start) | collective-permute-done | bytes 1179680 | tf_op jit(solution)/shard_map/ppermute | solution.py:340
  113.1 0.0 copy-start.7
  113.1 0.3 collective-permute-done.1.refs_0_
  113.4 4.1 %down0.1 = bf16[3,256,768]{2,1,0:T(8,128)(2,1)} custom-call(s32[1]{0:T(128)} %bitcast.11.where_ref, bf16[512,4096]{1,0:T(8,128)(2,1)} %bitcast.7.x_ref.do_ref.xa_ref.xb_ref.da_col_ref.db_col_ref, bf16[512,4096]{1,0:T(8,128)(2,1)} %bitcast.7.x_ref.do_ref.xa_ref.xb_ref.da_col_ref.db_col_ref, bf16[512,768]{1,0:T(8,128)(2,1)} %get-tuple-element.55.hid_ref, ...), custom_call_target="tpu_custom_call" | custom-call | flops 6039797760 | bytes 35389440 | tf_op jit(solution)/shard_map/down0/pallas_call | solution.py:184
  117.5 0.0 copy-done.7
  117.5 2.9 %collective-permute-start.5 = (bf16[3,256,768]{2,1,0:T(8,128)(2,1)}, bf16[3,256,768]{2,1,0:T(8,128)(2,1)}, u32[]{:S(2)}, u32[]{:S(2)}) collective-permute-start(bf16[3,256,768]{2,1,0:T(8,128)(2,1)} %down0.1), channel_id=1, source_target_pairs={{0,96},{32,0},{64,32},{96,64},{1,97},{33,1},{65,33},{97,65},{2,98}... | collective-permute-start | bytes 3538952 | tf_op jit(solution)/shard_map/ppermute | solution.py:343
  120.4 4.0 %up0.1 = bf16[3,256,768]{2,1,0:T(8,128)(2,1)} custom-call(s32[1]{0:T(128)} %bitcast.10.where_ref, bf16[512,4096]{1,0:T(8,128)(2,1)} %bitcast.7.x_ref.do_ref.xa_ref.xb_ref.da_col_ref.db_col_ref, bf16[512,4096]{1,0:T(8,128)(2,1)} %bitcast.7.x_ref.do_ref.xa_ref.xb_ref.da_col_ref.db_col_ref, bf16[512,768]{1,0:T(8,128)(2,1)} %get-tuple-element.55.hid_ref, ...), custom_call_target="tpu_custom_call" | custom-call | flops 6039797760 | bytes 35389440 | tf_op jit(solution)/shard_map/up0/pallas_call | solution.py:184
  124.4 0.0 collective-permute-start.4
  124.4 8.3 %dx0.1.refs_0_ = bf16[32,32,2176]{2,1,0:T(8,128)(2,1)} custom-call(bf16[512,768]{1,0:T(8,128)(2,1)} %get-tuple-element.64.da_ref, bf16[512,768]{1,0:T(8,128)(2,1)} %get-tuple-element.57.db_ref, bf16[512,128]{1,0:T(8,128)(2,1)} %get-tuple-element.65.s_ref, bf16[2,2048,768]{2,1,0:T(8,128)(2,1)} %refs_6_.3, bf16[2,2048,768]{2,1,0:T(8,128)(2,1)} %refs_7_.3), custom_call_target="tpu_custom_call" | custom-call | flops 32212254720 | bytes 99614720 | tf_op jit(solution)/shard_map/dx0/pallas_call | solution.py:262
  132.7 5.7 %collective-permute-done.2.refs_4_ = bf16[3,256,768]{2,1,0:T(8,128)(2,1)S(1)} collective-permute-done((bf16[3,256,768]{2,1,0:T(8,128)(2,1)}, bf16[3,256,768]{2,1,0:T(8,128)(2,1)S(1)}, u32[]{:S(2)}, u32[]{:S(2)}) %collective-permute-start.2) | collective-permute-done | bytes 1179680 | tf_op jit(solution)/shard_map/ppermute | solution.py:340
  138.4 0.0 copy-start
  138.4 0.2 collective-permute-done.3.refs_2_
  138.6 0.0 copy-start.1
  138.6 15.8 %all-to-all-done.1 = bf16[32,16,4096]{2,1,0:T(8,128)(2,1)} async-done(((bf16[32,16,4096]{2,1,0:T(8,128)(2,1)}), bf16[32,16,4096]{2,1,0:T(8,128)(2,1)}, u32[]{:S(2)}, u32[]{:S(2)}) %all-to-all-start.1) | async-done | bytes 4194336 | tf_op jit(solution)/shard_map/all_to_all | solution.py:349
  154.4 15.2 %hidden1.1 = (bf16[512,768]{1,0:T(8,128)(2,1)}, bf16[512,768]{1,0:T(8,128)(2,1)}, bf16[512,768]{1,0:T(8,128)(2,1)}, bf16[512,128]{1,0:T(8,128)(2,1)}, bf16[3,256...) custom-call(s32[2]{0:T(128)} %pad_add_fusion.where_ref, ...), custom_call_target="tpu_custom_call" | custom-call | flops 115964116992 | bytes 287834112 | tf_op jit(solution)/shard_map/hidden1/pallas_call | solution.py:138
  169.6 0.0 copy-done
  169.6 0.0 copy-done.1
  169.6 0.1 collective-permute-start.8
  169.7 0.0 collective-permute-done.5.refs_5_
  169.7 0.0 collective-permute-done.4.refs_1_
  169.7 6.8 %near1.1 = (bf16[3,256,768]{2,1,0:T(8,128)(2,1)}, bf16[3,256,768]{2,1,0:T(8,128)(2,1)}) custom-call(s32[2]{0:T(128)} %pad_add_fusion.1.where_ref, bf16[512,4096]{1,0:T(8,128)(2,1)} %bitcast.9.x_ref.do_ref.xa_ref.xb_ref.da_col_ref.db_col_ref, bf16[512,4096]{1,0:T(8,128)(2,1)} %bitcast.9.x_ref.do_ref.xa_ref.xb_ref.da_col_ref.db_col_ref, ...), custom_call_target="tpu_custom_call" | custom-call | flops 21743271936 | bytes 84934656 | tf_op jit(solution)/shard_map/near1/pallas_call | solution.py:184
  176.5 3.2 %collective-permute-start.9 = (bf16[3,256,768]{2,1,0:T(8,128)(2,1)}, bf16[3,256,768]{2,1,0:T(8,128)(2,1)}, u32[]{:S(2)}, u32[]{:S(2)}) collective-permute-start(bf16[3,256,768]{2,1,0:T(8,128)(2,1)} %get-tuple-element.84), channel_id=1, source_target_pairs={{0,96},{32,0},{64,32},{96,64},{1,97},{33,1},{65,33},{97,65},{2,98}... | collective-permute-start | bytes 3538952 | tf_op jit(solution)/shard_map/ppermute | solution.py:343
  179.7 8.2 %dx1.1 = bf16[32,32,2176]{2,1,0:T(8,128)(2,1)} custom-call(bf16[512,768]{1,0:T(8,128)(2,1)} %get-tuple-element.69.da_ref, bf16[512,768]{1,0:T(8,128)(2,1)} %get-tuple-element.70.db_ref, bf16[512,128]{1,0:T(8,128)(2,1)} %get-tuple-element.71.s_ref, bf16[2,2048,768]{2,1,0:T(8,128)(2,1)} %refs_6_.3, ...), custom_call_target="tpu_custom_call", output_to_operand_aliasing={{}: (5, {})} | custom-call | flops 57982058496 | bytes 179306496 | tf_op jit(solution)/shard_map/dx1/pallas_call | solution.py:262
  188.0 4.9 %all-to-all-start.2 = ((bf16[32,32,2176]{2,1,0:T(8,128)(2,1)}), bf16[32,32,2176]{2,1,0:T(8,128)(2,1)}, u32[]{:S(2)}, u32[]{:S(2)}) async-start(bf16[32,32,2176]{2,1,0:T(8,128)(2,1)} %dx1.1), calls=%async_computation.2 | async-start | bytes 8912896 | tf_op jit(solution)/shard_map/all_to_all | solution.py:349
  192.8 0.1 collective-permute-start.6
  192.9 3.2 %collective-permute-start.7 = (bf16[3,256,768]{2,1,0:T(8,128)(2,1)}, bf16[3,256,768]{2,1,0:T(8,128)(2,1)S(1)}, u32[]{:S(2)}, u32[]{:S(2)}) collective-permute-start(bf16[3,256,768]{2,1,0:T(8,128)(2,1)} %get-tuple-element.78), channel_id=1, source_target_pairs={{0,96},{32,0},{64,32},{96,64},{1,97},{33,1},{65,33},{97,65},{2,98}... | collective-permute-start | bytes 3538952 | tf_op jit(solution)/shard_map/ppermute | solution.py:343
  196.1 10.3 %collective-permute-done.9.refs_0_ = bf16[3,256,768]{2,1,0:T(8,128)(2,1)} collective-permute-done((bf16[3,256,768]{2,1,0:T(8,128)(2,1)}, bf16[3,256,768]{2,1,0:T(8,128)(2,1)}, u32[]{:S(2)}, u32[]{:S(2)}) %collective-permute-start.9) | collective-permute-done | bytes 1179680 | tf_op jit(solution)/shard_map/ppermute | solution.py:343
  206.5 0.0 collective-permute-done.8.refs_0_
  206.5 1.0 copy-done.6
  207.5 4.0 %down1.1 = bf16[3,256,768]{2,1,0:T(8,128)(2,1)} custom-call(s32[1]{0:T(128)} %bitcast.11.where_ref, bf16[512,4096]{1,0:T(8,128)(2,1)} %bitcast.9.x_ref.do_ref.xa_ref.xb_ref.da_col_ref.db_col_ref, bf16[512,4096]{1,0:T(8,128)(2,1)} %bitcast.9.x_ref.do_ref.xa_ref.xb_ref.da_col_ref.db_col_ref, bf16[512,768]{1,0:T(8,128)(2,1)} %get-tuple-element.75.hid_ref, ...), custom_call_target="tpu_custom_call" | custom-call | flops 10871635968 | bytes 63700992 | tf_op jit(solution)/shard_map/down1/pallas_call | solution.py:184
  211.5 3.7 %collective-permute-start.11 = (bf16[3,256,768]{2,1,0:T(8,128)(2,1)}, bf16[3,256,768]{2,1,0:T(8,128)(2,1)S(1)}, u32[]{:S(2)}, u32[]{:S(2)}) collective-permute-start(bf16[3,256,768]{2,1,0:T(8,128)(2,1)} %down1.1), channel_id=1, source_target_pairs={{0,96},{32,0},{64,32},{96,64},{1,97},{33,1},{65,33},{97,65},{2,98}... | collective-permute-start | bytes 3538952 | tf_op jit(solution)/shard_map/ppermute | solution.py:343
  215.2 4.1 %up1.1 = bf16[3,256,768]{2,1,0:T(8,128)(2,1)} custom-call(s32[1]{0:T(128)} %bitcast.10.where_ref, bf16[512,4096]{1,0:T(8,128)(2,1)} %bitcast.9.x_ref.do_ref.xa_ref.xb_ref.da_col_ref.db_col_ref, bf16[512,4096]{1,0:T(8,128)(2,1)} %bitcast.9.x_ref.do_ref.xa_ref.xb_ref.da_col_ref.db_col_ref, bf16[512,768]{1,0:T(8,128)(2,1)} %get-tuple-element.75.hid_ref, ...), custom_call_target="tpu_custom_call" | custom-call | flops 10871635968 | bytes 63700992 | tf_op jit(solution)/shard_map/up1/pallas_call | solution.py:184
  219.3 0.0 collective-permute-start.10
  219.3 6.8 %own1.1 = (bf16[3,256,768]{2,1,0:T(8,128)(2,1)}, bf16[3,256,768]{2,1,0:T(8,128)(2,1)}) custom-call(s32[2]{0:T(128)} %pad_add_fusion.2.where_ref, bf16[512,4096]{1,0:T(8,128)(2,1)} %bitcast.9.x_ref.do_ref.xa_ref.xb_ref.da_col_ref.db_col_ref, bf16[512,4096]{1,0:T(8,128)(2,1)} %bitcast.9.x_ref.do_ref.xa_ref.xb_ref.da_col_ref.db_col_ref, ...), custom_call_target="tpu_custom_call" | custom-call | flops 21743271936 | bytes 84934656 | tf_op jit(solution)/shard_map/own1/pallas_call | solution.py:184
  226.1 8.0 %update0.1 = (bf16[2,512,768]{2,1,0:T(8,128)(2,1)}, bf16[2,512,768]{2,1,0:T(8,128)(2,1)}, bf16[2,512,768]{2,1,0:T(8,128)(2,1)}) custom-call(s32[1]{0:T(128)} %bitcast.15.where_ref, s32[2,3]{1,0:T(2,128)} %mask_ref.3, bf16[3,256,768]{2,1,0:T(8,128)(2,1)} %get-tuple-element.91.refs_0_, bf16[3,256,768]{2,1,0:T(8,128)(2,1)} %collective-permute-done.4.refs_1_, ...), custom_call_target="tpu_custom_call" | custom-call | flops 35389440 | bytes 212336640 | tf_op jit(solution)/shard_map/update0/pallas_call | solution.py:227
  234.1 0.0 collective-permute-done.6.refs_4_
  234.1 0.0 copy-start.2
  234.1 0.0 collective-permute-done.7.refs_2_
  234.1 0.0 copy-start.3
  234.2 15.4 %all-to-all-done.2.back_ref = bf16[32,32,2176]{2,1,0:T(8,128)(2,1)} async-done(((bf16[32,32,2176]{2,1,0:T(8,128)(2,1)}), bf16[32,32,2176]{2,1,0:T(8,128)(2,1)}, u32[]{:S(2)}, u32[]{:S(2)}) %all-to-all-start.2) | async-done | bytes 4456480 | tf_op jit(solution)/shard_map/all_to_all | solution.py:349
  249.5 4.4 %combine.1 = (bf16[128,2048]{1,0:T(8,128)(2,1)}, f32[8,128]{1,0:T(8,128)}) custom-call(s32[8,128]{1,0:T(8,128)} %bitcast.24, bf16[32,32,2176]{2,1,0:T(8,128)(2,1)} %all-to-all-done.2.back_ref), custom_call_target="tpu_custom_call" | custom-call | flops 9663676416 | bytes 80216064 | tf_op jit(solution)/shard_map/combine/pallas_call | solution.py:307
  253.9 0.0 copy-done.2
  253.9 0.0 copy-done.3
  253.9 0.0 copy-done.5
  253.9 1.3 fusion
  255.2 0.0 collective-permute-done.11.refs_5_
  255.2 0.0 collective-permute-done.10.refs_1_
  255.2 1.0 copy-done.4
  256.2 8.0 %update1.1 = (bf16[2,512,768]{2,1,0:T(8,128)(2,1)}, bf16[2,512,768]{2,1,0:T(8,128)(2,1)}, bf16[2,512,768]{2,1,0:T(8,128)(2,1)}) custom-call(s32[1]{0:T(128)} %bitcast.15.where_ref, s32[2,3]{1,0:T(2,128)} %mask_ref.3, bf16[3,256,768]{2,1,0:T(8,128)(2,1)} %get-tuple-element.82.refs_0_, ...), custom_call_target="tpu_custom_call", output_to_operand_aliasing={{0}: (11, {}), {1}: (12, {}), {2}: (13, {})} | custom-call | flops 35389440 | bytes 212336640 | tf_op jit(solution)/shard_map/update1/pallas_call | solution.py:227
  (3 shorter events, 0.0 us)
Async XLA Ops:
  5.4 62.0 %all-to-all-start = ((bf16[32,16,4096]{2,1,0:T(8,128)(2,1)}), bf16[32,16,4096]{2,1,0:T(8,128)(2,1)}, u32[]{:S(2)}, u32[]{:S(2)}) async-start(bf16[32,16,4096]{2,1,0:T(8,128)(2,1)} %bitcast.18), calls=%async_computation | async-start | bytes 8388608 | tf_op jit(solution)/shard_map/all_to_all | solution.py:349
  82.7 30.4 %collective-permute-start = (bf16[3,256,768]{2,1,0:T(8,128)(2,1)}, bf16[3,256,768]{2,1,0:T(8,128)(2,1)S(1)}, u32[]{:S(2)}, u32[]{:S(2)}) collective-permute-start(bf16[3,256,768]{2,1,0:T(8,128)(2,1)} %get-tuple-element.60), channel_id=1, source_target_pairs={{0,32},{32,64},{64,96},{96,0},{1,33},{33,65},{65,97},{97,1},{2,34}... | collective-permute-start | bytes 3538952 | tf_op jit(solution)/shard_map/ppermute | solution.py:340
  84.2 29.2 %collective-permute-start.1 = (bf16[3,256,768]{2,1,0:T(8,128)(2,1)}, bf16[3,256,768]{2,1,0:T(8,128)(2,1)}, u32[]{:S(2)}, u32[]{:S(2)}) collective-permute-start(bf16[3,256,768]{2,1,0:T(8,128)(2,1)} %get-tuple-element.61), channel_id=1, source_target_pairs={{0,96},{32,0},{64,32},{96,64},{1,97},{33,1},{65,33},{97,65},{2,98}... | collective-permute-start | bytes 3538952 | tf_op jit(solution)/shard_map/ppermute | solution.py:343
  92.8 45.6 %collective-permute-start.2 = (bf16[3,256,768]{2,1,0:T(8,128)(2,1)}, bf16[3,256,768]{2,1,0:T(8,128)(2,1)S(1)}, u32[]{:S(2)}, u32[]{:S(2)}) collective-permute-start(bf16[3,256,768]{2,1,0:T(8,128)(2,1)} %get-tuple-element.58), channel_id=1, source_target_pairs={{0,32},{32,64},{64,96},{96,0},{1,33},{33,65},{65,97},{97,1},{2,34}... | collective-permute-start | bytes 3538952 | tf_op jit(solution)/shard_map/ppermute | solution.py:340
  93.0 45.6 %collective-permute-start.3 = (bf16[3,256,768]{2,1,0:T(8,128)(2,1)}, bf16[3,256,768]{2,1,0:T(8,128)(2,1)S(1)}, u32[]{:S(2)}, u32[]{:S(2)}) collective-permute-start(bf16[3,256,768]{2,1,0:T(8,128)(2,1)} %get-tuple-element.67), channel_id=1, source_target_pairs={{0,96},{32,0},{64,32},{96,64},{1,97},{33,1},{65,33},{97,65},{2,98}... | collective-permute-start | bytes 3538952 | tf_op jit(solution)/shard_map/ppermute | solution.py:343
  96.0 58.4 %all-to-all-start.1 = ((bf16[32,16,4096]{2,1,0:T(8,128)(2,1)}), bf16[32,16,4096]{2,1,0:T(8,128)(2,1)}, u32[]{:S(2)}, u32[]{:S(2)}) async-start(bf16[32,16,4096]{2,1,0:T(8,128)(2,1)} %bitcast.19), calls=%async_computation.1 | async-start | bytes 8388608 | tf_op jit(solution)/shard_map/all_to_all | solution.py:349
  113.1 4.4 %copy-start.7 = (bf16[3,256,768]{2,1,0:T(8,128)(2,1)}, bf16[3,256,768]{2,1,0:T(8,128)(2,1)S(1)}, u32[]{:S(2)}) copy-start(bf16[3,256,768]{2,1,0:T(8,128)(2,1)S(1)} %collective-permute-done.refs_0_) | copy-start | bytes 3538948
  117.5 52.2 %collective-permute-start.5 = (bf16[3,256,768]{2,1,0:T(8,128)(2,1)}, bf16[3,256,768]{2,1,0:T(8,128)(2,1)}, u32[]{:S(2)}, u32[]{:S(2)}) collective-permute-start(bf16[3,256,768]{2,1,0:T(8,128)(2,1)} %down0.1), channel_id=1, source_target_pairs={{0,96},{32,0},{64,32},{96,64},{1,97},{33,1},{65,33},{97,65},{2,98}... | collective-permute-start | bytes 3538952 | tf_op jit(solution)/shard_map/ppermute | solution.py:343
  124.4 45.3 %collective-permute-start.4 = (bf16[3,256,768]{2,1,0:T(8,128)(2,1)}, bf16[3,256,768]{2,1,0:T(8,128)(2,1)}, u32[]{:S(2)}, u32[]{:S(2)}) collective-permute-start(bf16[3,256,768]{2,1,0:T(8,128)(2,1)} %up0.1), channel_id=1, source_target_pairs={{0,32},{32,64},{64,96},{96,0},{1,33},{33,65},{65,97},{97,1},{2,34}... | collective-permute-start | bytes 3538952 | tf_op jit(solution)/shard_map/ppermute | solution.py:340
  138.4 31.2 %copy-start = (bf16[3,256,768]{2,1,0:T(8,128)(2,1)}, bf16[3,256,768]{2,1,0:T(8,128)(2,1)S(1)}, u32[]{:S(2)}) copy-start(bf16[3,256,768]{2,1,0:T(8,128)(2,1)S(1)} %collective-permute-done.2.refs_4_) | copy-start | bytes 3538948
  138.6 31.0 %copy-start.1 = (bf16[3,256,768]{2,1,0:T(8,128)(2,1)}, bf16[3,256,768]{2,1,0:T(8,128)(2,1)S(1)}, u32[]{:S(2)}) copy-start(bf16[3,256,768]{2,1,0:T(8,128)(2,1)S(1)} %collective-permute-done.3.refs_2_) | copy-start | bytes 3538948
  169.6 36.9 %collective-permute-start.8 = (bf16[3,256,768]{2,1,0:T(8,128)(2,1)}, bf16[3,256,768]{2,1,0:T(8,128)(2,1)S(1)}, u32[]{:S(2)}, u32[]{:S(2)}) collective-permute-start(bf16[3,256,768]{2,1,0:T(8,128)(2,1)} %get-tuple-element.73), channel_id=1, source_target_pairs={{0,32},{32,64},{64,96},{96,0},{1,33},{33,65},{65,97},{97,1},{2,34}... | collective-permute-start | bytes 3538952 | tf_op jit(solution)/shard_map/ppermute | solution.py:340
  176.5 29.9 %collective-permute-start.9 = (bf16[3,256,768]{2,1,0:T(8,128)(2,1)}, bf16[3,256,768]{2,1,0:T(8,128)(2,1)}, u32[]{:S(2)}, u32[]{:S(2)}) collective-permute-start(bf16[3,256,768]{2,1,0:T(8,128)(2,1)} %get-tuple-element.84), channel_id=1, source_target_pairs={{0,96},{32,0},{64,32},{96,64},{1,97},{33,1},{65,33},{97,65},{2,98}... | collective-permute-start | bytes 3538952 | tf_op jit(solution)/shard_map/ppermute | solution.py:343
  188.0 61.6 %all-to-all-start.2 = ((bf16[32,32,2176]{2,1,0:T(8,128)(2,1)}), bf16[32,32,2176]{2,1,0:T(8,128)(2,1)}, u32[]{:S(2)}, u32[]{:S(2)}) async-start(bf16[32,32,2176]{2,1,0:T(8,128)(2,1)} %dx1.1), calls=%async_computation.2 | async-start | bytes 8912896 | tf_op jit(solution)/shard_map/all_to_all | solution.py:349
  192.8 41.3 %collective-permute-start.6 = (bf16[3,256,768]{2,1,0:T(8,128)(2,1)}, bf16[3,256,768]{2,1,0:T(8,128)(2,1)S(1)}, u32[]{:S(2)}, u32[]{:S(2)}) collective-permute-start(bf16[3,256,768]{2,1,0:T(8,128)(2,1)} %get-tuple-element.76), channel_id=1, source_target_pairs={{0,32},{32,64},{64,96},{96,0},{1,33},{33,65},{65,97},{97,1},{2,34}... | collective-permute-start | bytes 3538952 | tf_op jit(solution)/shard_map/ppermute | solution.py:340
  192.9 41.2 %collective-permute-start.7 = (bf16[3,256,768]{2,1,0:T(8,128)(2,1)}, bf16[3,256,768]{2,1,0:T(8,128)(2,1)S(1)}, u32[]{:S(2)}, u32[]{:S(2)}) collective-permute-start(bf16[3,256,768]{2,1,0:T(8,128)(2,1)} %get-tuple-element.78), channel_id=1, source_target_pairs={{0,96},{32,0},{64,32},{96,64},{1,97},{33,1},{65,33},{97,65},{2,98}... | collective-permute-start | bytes 3538952 | tf_op jit(solution)/shard_map/ppermute | solution.py:343
  206.5 1.0 copy-start.6
  211.5 43.7 %collective-permute-start.11 = (bf16[3,256,768]{2,1,0:T(8,128)(2,1)}, bf16[3,256,768]{2,1,0:T(8,128)(2,1)S(1)}, u32[]{:S(2)}, u32[]{:S(2)}) collective-permute-start(bf16[3,256,768]{2,1,0:T(8,128)(2,1)} %down1.1), channel_id=1, source_target_pairs={{0,96},{32,0},{64,32},{96,64},{1,97},{33,1},{65,33},{97,65},{2,98}... | collective-permute-start | bytes 3538952 | tf_op jit(solution)/shard_map/ppermute | solution.py:343
  219.3 35.9 %collective-permute-start.10 = (bf16[3,256,768]{2,1,0:T(8,128)(2,1)}, bf16[3,256,768]{2,1,0:T(8,128)(2,1)}, u32[]{:S(2)}, u32[]{:S(2)}) collective-permute-start(bf16[3,256,768]{2,1,0:T(8,128)(2,1)} %up1.1), channel_id=1, source_target_pairs={{0,32},{32,64},{64,96},{96,0},{1,33},{33,65},{65,97},{97,1},{2,34}... | collective-permute-start | bytes 3538952 | tf_op jit(solution)/shard_map/ppermute | solution.py:340
  234.1 19.8 %copy-start.5 = (bf16[128,8]{0,1:T(8,128)(2,1)S(1)}, bf16[128,8]{0,1:T(8,128)(2,1)}, u32[]{:S(2)}) copy-start(bf16[128,8]{0,1:T(8,128)(2,1)} %param.11) | copy-start | bytes 6148
  234.1 19.8 %copy-start.2 = (bf16[3,256,768]{2,1,0:T(8,128)(2,1)}, bf16[3,256,768]{2,1,0:T(8,128)(2,1)S(1)}, u32[]{:S(2)}) copy-start(bf16[3,256,768]{2,1,0:T(8,128)(2,1)S(1)} %collective-permute-done.6.refs_4_) | copy-start | bytes 3538948
  234.1 19.8 %copy-start.3 = (bf16[3,256,768]{2,1,0:T(8,128)(2,1)}, bf16[3,256,768]{2,1,0:T(8,128)(2,1)S(1)}, u32[]{:S(2)}) copy-start(bf16[3,256,768]{2,1,0:T(8,128)(2,1)S(1)} %collective-permute-done.7.refs_2_) | copy-start | bytes 3538948
  255.2 1.0 copy-start.4

commit v6 on v5

--- a/solution.py
+++ b/solution.py
@@ -163,8 +163,8 @@
     )(where, *[rows] * 6, wg, wu, wd)
 
 
-def weight_kernel(n_add, where_ref, x_ref, do_ref, hid_ref, da_ref, db_ref, *refs):
-    adds, outs = refs[:n_add], refs[n_add:]
+def weight_kernel(n_add, n_after, where_ref, x_ref, do_ref, hid_ref, da_ref, db_ref, *refs):
+    adds, outs = refs[:n_add], refs[n_add + n_after :]
     for m, (left, right) in enumerate(((x_ref, da_ref), (x_ref, db_ref), (do_ref, hid_ref))):
         part = dot(left[...], right[...], TN)
         for addend in adds:
@@ -176,13 +176,13 @@
                 out_ref[m] = part.astype(BF16)
 
 
-def weight_grads(name, chunk, where, count, half, rows, hid, da, db, *adds):
+def weight_grads(name, chunk, where, count, half, rows, hid, da, db, *adds, after=()):
     n_rows, width = rows.shape[0], rows.shape[1] // 2
     hidden = hid.shape[1]
     lefts = width // half
     shape = (3, half, hidden)
     return pl.pallas_call(
-        functools.partial(weight_kernel, len(adds)),
+        functools.partial(weight_kernel, len(adds), len(after)),
         grid_spec=pltpu.PrefetchScalarGridSpec(
             num_scalar_prefetch=1,
             grid=(count,),
@@ -190,14 +190,32 @@
                 pl.BlockSpec((n_rows, half), lambda i, at: (0, at[i])),
                 pl.BlockSpec((n_rows, half), lambda i, at: (0, at[i] + lefts)),
             ]
-            + [whole(a.shape) for a in (hid, da, db, *adds)],
+            + [whole(a.shape) for a in (hid, da, db, *adds)]
+            + [pl.BlockSpec(memory_space=pl.ANY)] * len(after),
             out_specs=[whole(shape)] * count,
         ),
         out_shape=[jax.ShapeDtypeStruct(shape, BF16)] * count,
         compiler_params=pltpu.CompilerParams(vmem_limit_bytes=VMEM_LIMIT),
         cost_estimate=cost(6 * count * n_rows * half * hidden, 6 * n_rows * hidden + 6 * count * half * hidden, chunk),
         name=name,
-    )(where, rows, rows, hid, da, db, *adds)
+    )(where, rows, rows, hid, da, db, *adds, *after)
+
+
+def mark_kernel(a_ref, b_ref, out_ref):
+    out_ref[...] = a_ref[0] + b_ref[0]
+
+
+def mark(chunk, first, second):
+    corner = pl.BlockSpec((1, 16, LANES), lambda i: (0, 0, 0))
+    return pl.pallas_call(
+        mark_kernel,
+        grid=(1,),
+        in_specs=[corner, corner],
+        out_specs=pl.BlockSpec((16, LANES), lambda i: (0, 0)),
+        out_shape=jax.ShapeDtypeStruct((16, LANES), BF16),
+        cost_estimate=cost(5 * 3 * first.size, 5 * 3 * first.size, chunk),
+        name=f"mark{chunk}",
+    )(first, second)
 
 
 def update_kernel(chunk, where_ref, mask_ref, *refs):
@@ -217,7 +235,7 @@
 def update(chunk, where, mask, grads, weights, into):
     _, half, hidden = grads[0].shape
     local = weights[0].shape[0]
-    steps = 4
+    steps = 2
     block = half // steps
     early = pl.BlockSpec((3, block, hidden), lambda h, r, w: (0, r * (1 - h) + (steps - 1) * h, 0))
     late = pl.BlockSpec((3, block, hidden), lambda h, r, w: (0, r * h, 0))
@@ -365,20 +383,21 @@
     for chunk in range(local_exp):
         hid, da, db, s, *far = hidden_grads(chunk, blocks(*far_pairs), half, rows, *weights)
         far_up, far_down = up(far[0]), down(far[1])
-        grads = (rows, hid, da, db)
+        grads, after = (rows, hid, da, db), ()
         if before:
-            rows, _, *last = lax.optimization_barrier((rows, far[0], *before[1]))
+            dx, left = lax.optimization_barrier((dx, mark(chunk, *far)))
+            after = [left]
+            dx = input_grads(chunk, local_exp, capacity, da, db, s, w_gate, w_up, dx)
+            back = swap(dx)
+            rows, _, *last = lax.optimization_barrier((rows, dx, *before[1]))
             own, (near_up, near_down) = before[0], before[2]
             new = update(chunk - 1, where, decay_mask, (own[0], last[0], near_down, own[1], near_up, last[1]), weights, new)
             grads = (rows, hid, da, db)
-        near = weight_grads(f"near{chunk}", chunk, blocks(*near_pairs), 2, half, *grads)
+        if chunk + 1 < local_exp:
+            following, *after = lax.optimization_barrier((sends[chunk + 1], mark(chunk, *far)))
+            following = swap_rows(following)
+        near = weight_grads(f"near{chunk}", chunk, blocks(*near_pairs), 2, half, *grads, after=after)
         near_up, near_down = up(near[0]), down(near[1])
-        if chunk + 1 < local_exp:
-            following = swap_rows(order(sends[chunk + 1], near[0]))
-        if before:
-            dx = input_grads(chunk, local_exp, capacity, da, db, s, w_gate, w_up, order(dx, near[0]))
-            far_up, far_down = order(far_up, dx), order(far_down, dx)
-            back = swap(dx)
         far_up, far_down, _ = lax.optimization_barrier((far_up, far_down, near[0]))
         sum_up = weight_grads(f"up{chunk}", chunk, blocks((1, 0)), 1, half, *grads, far_up)[0]
         sum_down = weight_grads(f"down{chunk}", chunk, blocks((n_group - 1, 1)), 1, half, *grads, far_down)[0]

time: 265 us -> 249 us (0.940)
  waiting for transfers between devices: 100 us -> 87.4 us
    all_to_all x3, waiting for transfers between devices: 78 us -> 72 us  [swap(): return lax.all_to_all(a, 'expert', split_axis=0, concat_axis=0, tiled=True)]
    ppermute x6, starting transfers between devices: 17.9 us -> 13.3 us  [down(): lax.ppermute(a, 'dp', [(i, (i - 1) % n_group) for i in range(n_group)])]
    ppermute x6, waiting for transfers between devices: 11.1 us -> 6.84 us  [up(): lax.ppermute(a, 'dp', [(i, (i + 1) % n_group) for i in range(n_group)])]
    pallas_call x2, Pallas kernels: 16 us -> 12.8 us  [update(): pl.pallas_call(functools.partial(update_kernel, chunk), grid_spec=pltpu.P...]
    pallas_call x8 -> x10, Pallas kernels: 43.3 us -> 46 us  [the longest x8 43.2 us: weight_grads(): pl.pallas_call(functools.partial(weight_kernel, len(adds), len(after)), g...]
  transfers between devices with their start and end apart: 15 -> 15, of which waited for: 8 -> 9; matrix products, arithmetic and copies ran while one was open for 1% -> 1% of each run, Pallas kernels for 35% -> 37%
where the time goes in v6:
time: 249 us
  Pallas kernels  120 us (48%)
  waiting for transfers between devices  87.4 us (35%)
  starting transfers between devices  35.6 us (14%)
  other arithmetic  3.05 us (1%)
    all_to_all x3, waiting for transfers between devices, swap(): return lax.all_to_all(a, 'expert', split_axis=0, concat_axis=0, tiled=True)  72 us
    pallas_call x8, Pallas kernels, weight_grads(): pl.pallas_call(functools.partial(weight_kernel, len(adds), len(after)), g...  43.2 us
    pallas_call x2, Pallas kernels, hidden_grads(): pl.pallas_call(hidden_kernel, grid_spec=pltpu.PrefetchScalarGridSpec(num_...  30.4 us
    all_to_all x3, starting transfers between devices, swap(): return lax.all_to_all(a, 'expert', split_axis=0, concat_axis=0, tiled=True)  18.3 us
    pallas_call x2, Pallas kernels, input_grads(): pl.pallas_call(dx_kernel, grid=(1,), in_specs=[whole((n_rows, hidden)), w...  16.5 us
    ppermute x6, starting transfers between devices, down(): lax.ppermute(a, 'dp', [(i, (i - 1) % n_group) for i in range(n_group)])  13.3 us
    pallas_call x2, Pallas kernels, update(): pl.pallas_call(functools.partial(update_kernel, chunk), grid_spec=pltpu.P...  12.8 us
    pallas_call x2, Pallas kernels, dispatch(): pl.pallas_call(functools.partial(dispatch_kernel, chunk, local_exp, capac...  9.47 us
  transfers between devices with their start and end apart: 15, of which 9 were waited for; matrix products, arithmetic and copies ran while one was open for 1% of the time, Pallas kernels for 37%

profile of v6, /device:TPU:0, one launch (start us, length us, event | category | flops | bytes accessed | tf_op | source)
XLA Modules:
  0.0 248.6 jit_solution(3529391939071362250)
XLA Ops:
  0.6 4.8 %dispatch0.1 = bf16[512,4096]{1,0:T(8,128)(2,1)} custom-call(s32[8,128]{1,0:T(8,128)} %bitcast.22, bf16[8,128]{1,0:T(8,128)(2,1)} %bitcast.20, bf16[128,2048]{1,0:T(8,128)(2,1)} %tok_ref.3, bf16[128,2048]{1,0:T(8,128)(2,1)} %grad_ref.3), custom_call_target="tpu_custom_call" | custom-call | flops 5368709120 | bytes 52428800 | tf_op jit(solution)/shard_map/dispatch0/pallas_call | solution.py:78
  5.4 8.5 %all-to-all-start = ((bf16[32,16,4096]{2,1,0:T(8,128)(2,1)}), bf16[32,16,4096]{2,1,0:T(8,128)(2,1)}, u32[]{:S(2)}, u32[]{:S(2)}) async-start(bf16[32,16,4096]{2,1,0:T(8,128)(2,1)} %bitcast.18), calls=%async_computation | async-start | bytes 8388608 | tf_op jit(solution)/shard_map/all_to_all | solution.py:367
  14.0 0.6 pad_add_fusion.where_ref
  14.6 0.6 pad_add_fusion.1.where_ref
  15.2 0.6 pad_add_fusion.2.where_ref
  15.8 4.7 %dispatch1.1 = bf16[512,4096]{1,0:T(8,128)(2,1)} custom-call(s32[8,128]{1,0:T(8,128)} %bitcast.23, bf16[8,128]{1,0:T(8,128)(2,1)} %bitcast.21, bf16[128,2048]{1,0:T(8,128)(2,1)} %tok_ref.3, bf16[128,2048]{1,0:T(8,128)(2,1)} %grad_ref.3), custom_call_target="tpu_custom_call" | custom-call | flops 5368709120 | bytes 52428800 | tf_op jit(solution)/shard_map/dispatch1/pallas_call | solution.py:78
  20.5 47.0 %all-to-all-done = bf16[32,16,4096]{2,1,0:T(8,128)(2,1)} async-done(((bf16[32,16,4096]{2,1,0:T(8,128)(2,1)}), bf16[32,16,4096]{2,1,0:T(8,128)(2,1)}, u32[]{:S(2)}, u32[]{:S(2)}) %all-to-all-start) | async-done | bytes 4194336 | tf_op jit(solution)/shard_map/all_to_all | solution.py:367
  67.4 15.2 %hidden0.1 = (bf16[512,768]{1,0:T(8,128)(2,1)}, bf16[512,768]{1,0:T(8,128)(2,1)}, bf16[512,768]{1,0:T(8,128)(2,1)}, bf16[512,128]{1,0:T(8,128)(2,1)}, bf16[3,256...) custom-call(s32[2]{0:T(128)} %pad_add_fusion.where_ref, ...), custom_call_target="tpu_custom_call" | custom-call | flops 64424509440 | bytes 159907840 | tf_op jit(solution)/shard_map/hidden0/pallas_call | solution.py:138
  82.7 1.5 collective-permute-start
  84.2 0.0 copy-start.4
  84.2 1.4 mark0.1.refs_0_
  85.6 0.0 copy-done.4
  85.6 1.7 collective-permute-start.1
  87.3 4.9 %all-to-all-start.1 = ((bf16[32,16,4096]{2,1,0:T(8,128)(2,1)}), bf16[32,16,4096]{2,1,0:T(8,128)(2,1)}, u32[]{:S(2)}, u32[]{:S(2)}) async-start(bf16[32,16,4096]{2,1,0:T(8,128)(2,1)} %bitcast.19), calls=%async_computation.1 | async-start | bytes 8388608 | tf_op jit(solution)/shard_map/all_to_all | solution.py:367
  92.2 6.8 %near0.1 = (bf16[3,256,768]{2,1,0:T(8,128)(2,1)}, bf16[3,256,768]{2,1,0:T(8,128)(2,1)}) custom-call(s32[2]{0:T(128)} %pad_add_fusion.1.where_ref, bf16[512,4096]{1,0:T(8,128)(2,1)} %bitcast.5.x_ref.do_ref.xa_ref.xb_ref.da_col_ref.db_col_ref, bf16[512,4096]{1,0:T(8,128)(2,1)} %bitcast.5.x_ref.do_ref.xa_ref.xb_ref.da_col_ref.db_col_ref, ...), custom_call_target="tpu_custom_call" | custom-call | flops 12079595520 | bytes 47185920 | tf_op jit(solution)/shard_map/near0/pallas_call | solution.py:184
  99.0 1.5 collective-permute-start.3
  100.5 0.5 collective-permute-start.2
  101.0 6.8 %own0.1 = (bf16[3,256,768]{2,1,0:T(8,128)(2,1)}, bf16[3,256,768]{2,1,0:T(8,128)(2,1)}) custom-call(s32[2]{0:T(128)} %pad_add_fusion.2.where_ref, bf16[512,4096]{1,0:T(8,128)(2,1)} %bitcast.5.x_ref.do_ref.xa_ref.xb_ref.da_col_ref.db_col_ref, bf16[512,4096]{1,0:T(8,128)(2,1)} %bitcast.5.x_ref.do_ref.xa_ref.xb_ref.da_col_ref.db_col_ref, ...), custom_call_target="tpu_custom_call" | custom-call | flops 12079595520 | bytes 47185920 | tf_op jit(solution)/shard_map/own0/pallas_call | solution.py:184
  107.8 5.2 %collective-permute-done.refs_0_ = bf16[3,256,768]{2,1,0:T(8,128)(2,1)S(1)} collective-permute-done((bf16[3,256,768]{2,1,0:T(8,128)(2,1)}, bf16[3,256,768]{2,1,0:T(8,128)(2,1)S(1)}, u32[]{:S(2)}, u32[]{:S(2)}) %collective-permute-start) | collective-permute-done | bytes 1179680 | tf_op jit(solution)/shard_map/ppermute | solution.py:358
  113.0 0.0 copy-start.6
  113.0 1.5 collective-permute-done.1.refs_0_
  114.5 0.0 copy-start.7
  114.5 1.0 copy-done.7
  115.5 4.0 %down0.1 = bf16[3,256,768]{2,1,0:T(8,128)(2,1)} custom-call(s32[1]{0:T(128)} %bitcast.11.where_ref, bf16[512,4096]{1,0:T(8,128)(2,1)} %bitcast.5.x_ref.do_ref.xa_ref.xb_ref.da_col_ref.db_col_ref, bf16[512,4096]{1,0:T(8,128)(2,1)} %bitcast.5.x_ref.do_ref.xa_ref.xb_ref.da_col_ref.db_col_ref, bf16[512,768]{1,0:T(8,128)(2,1)} %get-tuple-element.59.hid_ref, ...), custom_call_target="tpu_custom_call" | custom-call | flops 6039797760 | bytes 35389440 | tf_op jit(solution)/shard_map/down0/pallas_call | solution.py:184
  119.5 0.0 copy-done.6
  119.5 2.9 %collective-permute-start.5 = (bf16[3,256,768]{2,1,0:T(8,128)(2,1)}, bf16[3,256,768]{2,1,0:T(8,128)(2,1)}, u32[]{:S(2)}, u32[]{:S(2)}) collective-permute-start(bf16[3,256,768]{2,1,0:T(8,128)(2,1)} %down0.1), channel_id=1, source_target_pairs={{0,96},{32,0},{64,32},{96,64},{1,97},{33,1},{65,33},{97,65},{2,98}... | collective-permute-start | bytes 3538952 | tf_op jit(solution)/shard_map/ppermute | solution.py:361
  122.5 4.0 %up0.1 = bf16[3,256,768]{2,1,0:T(8,128)(2,1)} custom-call(s32[1]{0:T(128)} %bitcast.8.where_ref, bf16[512,4096]{1,0:T(8,128)(2,1)} %bitcast.5.x_ref.do_ref.xa_ref.xb_ref.da_col_ref.db_col_ref, bf16[512,4096]{1,0:T(8,128)(2,1)} %bitcast.5.x_ref.do_ref.xa_ref.xb_ref.da_col_ref.db_col_ref, bf16[512,768]{1,0:T(8,128)(2,1)} %get-tuple-element.59.hid_ref, ...), custom_call_target="tpu_custom_call" | custom-call | flops 6039797760 | bytes 35389440 | tf_op jit(solution)/shard_map/up0/pallas_call | solution.py:184
  126.5 0.0 collective-permute-start.4
  126.5 8.2 %dx0.1.refs_0_ = bf16[32,32,2176]{2,1,0:T(8,128)(2,1)} custom-call(bf16[512,768]{1,0:T(8,128)(2,1)} %get-tuple-element.65.da_ref, bf16[512,768]{1,0:T(8,128)(2,1)} %get-tuple-element.60.db_ref, bf16[512,128]{1,0:T(8,128)(2,1)} %get-tuple-element.66.s_ref, bf16[2,2048,768]{2,1,0:T(8,128)(2,1)} %refs_6_.3, bf16[2,2048,768]{2,1,0:T(8,128)(2,1)} %refs_7_.3), custom_call_target="tpu_custom_call" | custom-call | flops 32212254720 | bytes 99614720 | tf_op jit(solution)/shard_map/dx0/pallas_call | solution.py:280
  134.7 5.2 %collective-permute-done.3.refs_2_ = bf16[3,256,768]{2,1,0:T(8,128)(2,1)} collective-permute-done((bf16[3,256,768]{2,1,0:T(8,128)(2,1)}, bf16[3,256,768]{2,1,0:T(8,128)(2,1)}, u32[]{:S(2)}, u32[]{:S(2)}) %collective-permute-start.3) | collective-permute-done | bytes 1179680 | tf_op jit(solution)/shard_map/ppermute | solution.py:361
  139.9 0.0 collective-permute-done.2.refs_4_
  139.9 5.8 %all-to-all-done.1 = bf16[32,16,4096]{2,1,0:T(8,128)(2,1)} async-done(((bf16[32,16,4096]{2,1,0:T(8,128)(2,1)}), bf16[32,16,4096]{2,1,0:T(8,128)(2,1)}, u32[]{:S(2)}, u32[]{:S(2)}) %all-to-all-start.1) | async-done | bytes 4194336 | tf_op jit(solution)/shard_map/all_to_all | solution.py:367
  145.7 15.2 %hidden1.1 = (bf16[512,768]{1,0:T(8,128)(2,1)}, bf16[512,768]{1,0:T(8,128)(2,1)}, bf16[512,768]{1,0:T(8,128)(2,1)}, bf16[512,128]{1,0:T(8,128)(2,1)}, bf16[3,256...) custom-call(s32[2]{0:T(128)} %pad_add_fusion.where_ref, ...), custom_call_target="tpu_custom_call" | custom-call | flops 115964116992 | bytes 287834112 | tf_op jit(solution)/shard_map/hidden1/pallas_call | solution.py:138
  160.9 0.4 collective-permute-start.8
  161.3 1.4 mark1.1.refs_0_
  162.7 0.0 copy-done.3
  162.7 2.9 %collective-permute-start.9 = (bf16[3,256,768]{2,1,0:T(8,128)(2,1)S(1)}, bf16[3,256,768]{2,1,0:T(8,128)(2,1)}, u32[]{:S(2)}, u32[]{:S(2)}) collective-permute-start(bf16[3,256,768]{2,1,0:T(8,128)(2,1)S(1)} %copy-done.3), channel_id=1, source_target_pairs={{0,96},{32,0},{64,32},{96,64},{1,97},{33,1},{65,33},{97,65},{2,98}... | collective-permute-start | bytes 3538952 | tf_op jit(solution)/shard_map/ppermute | solution.py:361
  165.6 8.2 %dx1.1 = bf16[32,32,2176]{2,1,0:T(8,128)(2,1)} custom-call(bf16[512,768]{1,0:T(8,128)(2,1)} %get-tuple-element.70.da_ref, bf16[512,768]{1,0:T(8,128)(2,1)} %get-tuple-element.71.db_ref, bf16[512,128]{1,0:T(8,128)(2,1)} %get-tuple-element.72.s_ref, bf16[2,2048,768]{2,1,0:T(8,128)(2,1)} %refs_6_.3, ...), custom_call_target="tpu_custom_call", output_to_operand_aliasing={{}: (5, {})} | custom-call | flops 57982058496 | bytes 179306496 | tf_op jit(solution)/shard_map/dx1/pallas_call | solution.py:280
  173.8 4.9 %all-to-all-start.2 = ((bf16[32,32,2176]{2,1,0:T(8,128)(2,1)}), bf16[32,32,2176]{2,1,0:T(8,128)(2,1)}, u32[]{:S(2)}, u32[]{:S(2)}) async-start(bf16[32,32,2176]{2,1,0:T(8,128)(2,1)} %dx1.1), calls=%async_computation.2 | async-start | bytes 8912896 | tf_op jit(solution)/shard_map/all_to_all | solution.py:367
  178.7 0.0 collective-permute-done.5.refs_5_
  178.7 0.0 collective-permute-done.4.refs_1_
  178.7 6.8 %near1.1 = (bf16[3,256,768]{2,1,0:T(8,128)(2,1)}, bf16[3,256,768]{2,1,0:T(8,128)(2,1)}) custom-call(s32[2]{0:T(128)} %pad_add_fusion.1.where_ref, bf16[512,4096]{1,0:T(8,128)(2,1)} %bitcast.7.x_ref.do_ref.xa_ref.xb_ref.da_col_ref.db_col_ref, bf16[512,4096]{1,0:T(8,128)(2,1)} %bitcast.7.x_ref.do_ref.xa_ref.xb_ref.da_col_ref.db_col_ref, ...), custom_call_target="tpu_custom_call" | custom-call | flops 21743271936 | bytes 84934656 | tf_op jit(solution)/shard_map/near1/pallas_call | solution.py:184
  185.5 0.4 collective-permute-start.7
  185.9 1.7 collective-permute-start.6
  187.5 0.0 collective-permute-done.8.refs_0_
  187.5 1.4 collective-permute-done.9.refs_0_
  189.0 4.0 %down1.1 = bf16[3,256,768]{2,1,0:T(8,128)(2,1)} custom-call(s32[1]{0:T(128)} %bitcast.11.where_ref, bf16[512,4096]{1,0:T(8,128)(2,1)} %bitcast.7.x_ref.do_ref.xa_ref.xb_ref.da_col_ref.db_col_ref, bf16[512,4096]{1,0:T(8,128)(2,1)} %bitcast.7.x_ref.do_ref.xa_ref.xb_ref.da_col_ref.db_col_ref, bf16[512,768]{1,0:T(8,128)(2,1)} %get-tuple-element.78.hid_ref, ...), custom_call_target="tpu_custom_call" | custom-call | flops 10871635968 | bytes 63700992 | tf_op jit(solution)/shard_map/down1/pallas_call | solution.py:184
  193.0 3.8 %collective-permute-start.11 = (bf16[3,256,768]{2,1,0:T(8,128)(2,1)}, bf16[3,256,768]{2,1,0:T(8,128)(2,1)S(1)}, u32[]{:S(2)}, u32[]{:S(2)}) collective-permute-start(bf16[3,256,768]{2,1,0:T(8,128)(2,1)} %down1.1), channel_id=1, source_target_pairs={{0,96},{32,0},{64,32},{96,64},{1,97},{33,1},{65,33},{97,65},{2,98}... | collective-permute-start | bytes 3538952 | tf_op jit(solution)/shard_map/ppermute | solution.py:361
  196.8 4.0 %up1.1 = bf16[3,256,768]{2,1,0:T(8,128)(2,1)} custom-call(s32[1]{0:T(128)} %bitcast.8.where_ref, bf16[512,4096]{1,0:T(8,128)(2,1)} %bitcast.7.x_ref.do_ref.xa_ref.xb_ref.da_col_ref.db_col_ref, bf16[512,4096]{1,0:T(8,128)(2,1)} %bitcast.7.x_ref.do_ref.xa_ref.xb_ref.da_col_ref.db_col_ref, bf16[512,768]{1,0:T(8,128)(2,1)} %get-tuple-element.78.hid_ref, ...), custom_call_target="tpu_custom_call" | custom-call | flops 10871635968 | bytes 63700992 | tf_op jit(solution)/shard_map/up1/pallas_call | solution.py:184
  200.8 0.0 collective-permute-start.10
  200.8 6.8 %own1.1 = (bf16[3,256,768]{2,1,0:T(8,128)(2,1)}, bf16[3,256,768]{2,1,0:T(8,128)(2,1)}) custom-call(s32[2]{0:T(128)} %pad_add_fusion.2.where_ref, bf16[512,4096]{1,0:T(8,128)(2,1)} %bitcast.7.x_ref.do_ref.xa_ref.xb_ref.da_col_ref.db_col_ref, bf16[512,4096]{1,0:T(8,128)(2,1)} %bitcast.7.x_ref.do_ref.xa_ref.xb_ref.da_col_ref.db_col_ref, ...), custom_call_target="tpu_custom_call" | custom-call | flops 21743271936 | bytes 84934656 | tf_op jit(solution)/shard_map/own1/pallas_call | solution.py:184
  207.6 6.4 %update0.1 = (bf16[2,512,768]{2,1,0:T(8,128)(2,1)}, bf16[2,512,768]{2,1,0:T(8,128)(2,1)}, bf16[2,512,768]{2,1,0:T(8,128)(2,1)}) custom-call(s32[1]{0:T(128)} %bitcast.15.where_ref, s32[2,3]{1,0:T(2,128)} %mask_ref.3, bf16[3,256,768]{2,1,0:T(8,128)(2,1)} %get-tuple-element.91.refs_0_, bf16[3,256,768]{2,1,0:T(8,128)(2,1)} %collective-permute-done.4.refs_1_, ...), custom_call_target="tpu_custom_call" | custom-call | flops 35389440 | bytes 212336640 | tf_op jit(solution)/shard_map/update0/pallas_call | solution.py:245
  214.1 0.5 collective-permute-done.7.refs_2_
  214.5 1.6 collective-permute-done.6.refs_4_
  216.2 19.2 %all-to-all-done.2.back_ref = bf16[32,32,2176]{2,1,0:T(8,128)(2,1)} async-done(((bf16[32,32,2176]{2,1,0:T(8,128)(2,1)}), bf16[32,32,2176]{2,1,0:T(8,128)(2,1)}, u32[]{:S(2)}, u32[]{:S(2)}) %all-to-all-start.2) | async-done | bytes 4456480 | tf_op jit(solution)/shard_map/all_to_all | solution.py:367
  235.4 4.4 %combine.1 = (bf16[128,2048]{1,0:T(8,128)(2,1)}, f32[8,128]{1,0:T(8,128)}) custom-call(s32[8,128]{1,0:T(8,128)} %bitcast.24, bf16[32,32,2176]{2,1,0:T(8,128)(2,1)} %all-to-all-done.2.back_ref), custom_call_target="tpu_custom_call" | custom-call | flops 9663676416 | bytes 80216064 | tf_op jit(solution)/shard_map/combine/pallas_call | solution.py:325
  239.8 0.0 copy-done
  239.8 0.0 copy-done.1
  239.8 0.0 copy-done.5
  239.8 1.3 fusion
  241.0 0.0 collective-permute-done.11.refs_5_
  241.0 0.0 collective-permute-done.10.refs_1_
  241.1 1.0 copy-done.2
  242.1 6.4 %update1.1 = (bf16[2,512,768]{2,1,0:T(8,128)(2,1)}, bf16[2,512,768]{2,1,0:T(8,128)(2,1)}, bf16[2,512,768]{2,1,0:T(8,128)(2,1)}) custom-call(s32[1]{0:T(128)} %bitcast.15.where_ref, s32[2,3]{1,0:T(2,128)} %mask_ref.3, bf16[3,256,768]{2,1,0:T(8,128)(2,1)} %get-tuple-element.85.refs_0_, ...), custom_call_target="tpu_custom_call", output_to_operand_aliasing={{0}: (11, {}), {1}: (12, {}), {2}: (13, {})} | custom-call | flops 35389440 | bytes 212336640 | tf_op jit(solution)/shard_map/update1/pallas_call | solution.py:245
  (5 shorter events, 0.0 us)
Async XLA Ops:
  5.4 62.0 %all-to-all-start = ((bf16[32,16,4096]{2,1,0:T(8,128)(2,1)}), bf16[32,16,4096]{2,1,0:T(8,128)(2,1)}, u32[]{:S(2)}, u32[]{:S(2)}) async-start(bf16[32,16,4096]{2,1,0:T(8,128)(2,1)} %bitcast.18), calls=%async_computation | async-start | bytes 8388608 | tf_op jit(solution)/shard_map/all_to_all | solution.py:367
  82.7 30.4 %collective-permute-start = (bf16[3,256,768]{2,1,0:T(8,128)(2,1)}, bf16[3,256,768]{2,1,0:T(8,128)(2,1)S(1)}, u32[]{:S(2)}, u32[]{:S(2)}) collective-permute-start(bf16[3,256,768]{2,1,0:T(8,128)(2,1)} %get-tuple-element.55.a_ref), channel_id=1, source_target_pairs={{0,32},{32,64},{64,96},{96,0},{1,33},{33,65},{65,97},{97,1},{2,34}... | collective-permute-start | bytes 3538952 | tf_op jit(solution)/shard_map/ppermute | solution.py:358
  84.2 1.4 copy-start.4
  85.6 28.9 %collective-permute-start.1 = (bf16[3,256,768]{2,1,0:T(8,128)(2,1)S(1)}, bf16[3,256,768]{2,1,0:T(8,128)(2,1)S(1)}, u32[]{:S(2)}, u32[]{:S(2)}) collective-permute-start(bf16[3,256,768]{2,1,0:T(8,128)(2,1)S(1)} %copy-done.4), channel_id=1, source_target_pairs={{0,96},{32,0},{64,32},{96,64},{1,97},{33,1},{65,33},{97,65},{2,98}... | collective-permute-start | bytes 3538952 | tf_op jit(solution)/shard_map/ppermute | solution.py:361
  87.3 58.3 %all-to-all-start.1 = ((bf16[32,16,4096]{2,1,0:T(8,128)(2,1)}), bf16[32,16,4096]{2,1,0:T(8,128)(2,1)}, u32[]{:S(2)}, u32[]{:S(2)}) async-start(bf16[32,16,4096]{2,1,0:T(8,128)(2,1)} %bitcast.19), calls=%async_computation.1 | async-start | bytes 8388608 | tf_op jit(solution)/shard_map/all_to_all | solution.py:367
  99.0 40.9 %collective-permute-start.3 = (bf16[3,256,768]{2,1,0:T(8,128)(2,1)}, bf16[3,256,768]{2,1,0:T(8,128)(2,1)}, u32[]{:S(2)}, u32[]{:S(2)}) collective-permute-start(bf16[3,256,768]{2,1,0:T(8,128)(2,1)} %get-tuple-element.68), channel_id=1, source_target_pairs={{0,96},{32,0},{64,32},{96,64},{1,97},{33,1},{65,33},{97,65},{2,98}... | collective-permute-start | bytes 3538952 | tf_op jit(solution)/shard_map/ppermute | solution.py:361
  100.5 39.4 %collective-permute-start.2 = (bf16[3,256,768]{2,1,0:T(8,128)(2,1)}, bf16[3,256,768]{2,1,0:T(8,128)(2,1)}, u32[]{:S(2)}, u32[]{:S(2)}) collective-permute-start(bf16[3,256,768]{2,1,0:T(8,128)(2,1)} %get-tuple-element.62), channel_id=1, source_target_pairs={{0,32},{32,64},{64,96},{96,0},{1,33},{33,65},{65,97},{97,1},{2,34}... | collective-permute-start | bytes 3538952 | tf_op jit(solution)/shard_map/ppermute | solution.py:358
  113.0 6.5 %copy-start.6 = (bf16[3,256,768]{2,1,0:T(8,128)(2,1)}, bf16[3,256,768]{2,1,0:T(8,128)(2,1)S(1)}, u32[]{:S(2)}) copy-start(bf16[3,256,768]{2,1,0:T(8,128)(2,1)S(1)} %collective-permute-done.refs_0_) | copy-start | bytes 3538948
  114.5 1.0 copy-start.7
  119.5 59.1 %collective-permute-start.5 = (bf16[3,256,768]{2,1,0:T(8,128)(2,1)}, bf16[3,256,768]{2,1,0:T(8,128)(2,1)}, u32[]{:S(2)}, u32[]{:S(2)}) collective-permute-start(bf16[3,256,768]{2,1,0:T(8,128)(2,1)} %down0.1), channel_id=1, source_target_pairs={{0,96},{32,0},{64,32},{96,64},{1,97},{33,1},{65,33},{97,65},{2,98}... | collective-permute-start | bytes 3538952 | tf_op jit(solution)/shard_map/ppermute | solution.py:361
  126.5 52.2 %collective-permute-start.4 = (bf16[3,256,768]{2,1,0:T(8,128)(2,1)}, bf16[3,256,768]{2,1,0:T(8,128)(2,1)}, u32[]{:S(2)}, u32[]{:S(2)}) collective-permute-start(bf16[3,256,768]{2,1,0:T(8,128)(2,1)} %up0.1), channel_id=1, source_target_pairs={{0,32},{32,64},{64,96},{96,0},{1,33},{33,65},{65,97},{97,1},{2,34}... | collective-permute-start | bytes 3538952 | tf_op jit(solution)/shard_map/ppermute | solution.py:358
  160.9 26.6 %collective-permute-start.8 = (bf16[3,256,768]{2,1,0:T(8,128)(2,1)}, bf16[3,256,768]{2,1,0:T(8,128)(2,1)}, u32[]{:S(2)}, u32[]{:S(2)}) collective-permute-start(bf16[3,256,768]{2,1,0:T(8,128)(2,1)} %get-tuple-element.74.a_ref), channel_id=1, source_target_pairs={{0,32},{32,64},{64,96},{96,0},{1,33},{33,65},{65,97},{97,1},{2,34}... | collective-permute-start | bytes 3538952 | tf_op jit(solution)/shard_map/ppermute | solution.py:358
  161.3 1.4 copy-start.3
  162.7 26.3 %collective-permute-start.9 = (bf16[3,256,768]{2,1,0:T(8,128)(2,1)S(1)}, bf16[3,256,768]{2,1,0:T(8,128)(2,1)}, u32[]{:S(2)}, u32[]{:S(2)}) collective-permute-start(bf16[3,256,768]{2,1,0:T(8,128)(2,1)S(1)} %copy-done.3), channel_id=1, source_target_pairs={{0,96},{32,0},{64,32},{96,64},{1,97},{33,1},{65,33},{97,65},{2,98}... | collective-permute-start | bytes 3538952 | tf_op jit(solution)/shard_map/ppermute | solution.py:361
  173.8 61.6 %all-to-all-start.2 = ((bf16[32,32,2176]{2,1,0:T(8,128)(2,1)}), bf16[32,32,2176]{2,1,0:T(8,128)(2,1)}, u32[]{:S(2)}, u32[]{:S(2)}) async-start(bf16[32,32,2176]{2,1,0:T(8,128)(2,1)} %dx1.1), calls=%async_computation.2 | async-start | bytes 8912896 | tf_op jit(solution)/shard_map/all_to_all | solution.py:367
  185.5 29.0 %collective-permute-start.7 = (bf16[3,256,768]{2,1,0:T(8,128)(2,1)}, bf16[3,256,768]{2,1,0:T(8,128)(2,1)S(1)}, u32[]{:S(2)}, u32[]{:S(2)}) collective-permute-start(bf16[3,256,768]{2,1,0:T(8,128)(2,1)} %get-tuple-element.81), channel_id=1, source_target_pairs={{0,96},{32,0},{64,32},{96,64},{1,97},{33,1},{65,33},{97,65},{2,98}... | collective-permute-start | bytes 3538952 | tf_op jit(solution)/shard_map/ppermute | solution.py:361
  185.9 30.3 %collective-permute-start.6 = (bf16[3,256,768]{2,1,0:T(8,128)(2,1)}, bf16[3,256,768]{2,1,0:T(8,128)(2,1)S(1)}, u32[]{:S(2)}, u32[]{:S(2)}) collective-permute-start(bf16[3,256,768]{2,1,0:T(8,128)(2,1)} %get-tuple-element.80), channel_id=1, source_target_pairs={{0,32},{32,64},{64,96},{96,0},{1,33},{33,65},{65,97},{97,1},{2,34}... | collective-permute-start | bytes 3538952 | tf_op jit(solution)/shard_map/ppermute | solution.py:358
  193.0 48.0 %collective-permute-start.11 = (bf16[3,256,768]{2,1,0:T(8,128)(2,1)}, bf16[3,256,768]{2,1,0:T(8,128)(2,1)S(1)}, u32[]{:S(2)}, u32[]{:S(2)}) collective-permute-start(bf16[3,256,768]{2,1,0:T(8,128)(2,1)} %down1.1), channel_id=1, source_target_pairs={{0,96},{32,0},{64,32},{96,64},{1,97},{33,1},{65,33},{97,65},{2,98}... | collective-permute-start | bytes 3538952 | tf_op jit(solution)/shard_map/ppermute | solution.py:361
  200.8 40.2 %collective-permute-start.10 = (bf16[3,256,768]{2,1,0:T(8,128)(2,1)}, bf16[3,256,768]{2,1,0:T(8,128)(2,1)}, u32[]{:S(2)}, u32[]{:S(2)}) collective-permute-start(bf16[3,256,768]{2,1,0:T(8,128)(2,1)} %up1.1), channel_id=1, source_target_pairs={{0,32},{32,64},{64,96},{96,0},{1,33},{33,65},{65,97},{97,1},{2,34}... | collective-permute-start | bytes 3538952 | tf_op jit(solution)/shard_map/ppermute | solution.py:358
  214.1 25.7 %copy-start.5 = (bf16[128,8]{0,1:T(8,128)(2,1)S(1)}, bf16[128,8]{0,1:T(8,128)(2,1)}, u32[]{:S(2)}) copy-start(bf16[128,8]{0,1:T(8,128)(2,1)} %param.11) | copy-start | bytes 6148
  214.5 25.2 %copy-start = (bf16[3,256,768]{2,1,0:T(8,128)(2,1)}, bf16[3,256,768]{2,1,0:T(8,128)(2,1)S(1)}, u32[]{:S(2)}) copy-start(bf16[3,256,768]{2,1,0:T(8,128)(2,1)S(1)} %collective-permute-done.7.refs_2_) | copy-start | bytes 3538948
  216.2 23.6 %copy-start.1 = (bf16[3,256,768]{2,1,0:T(8,128)(2,1)}, bf16[3,256,768]{2,1,0:T(8,128)(2,1)S(1)}, u32[]{:S(2)}) copy-start(bf16[3,256,768]{2,1,0:T(8,128)(2,1)S(1)} %collective-permute-done.6.refs_4_) | copy-start | bytes 3538948
  241.0 1.0 copy-start.2

commit v7 on v6

--- a/solution.py
+++ b/solution.py
@@ -20,7 +20,7 @@
 
 
 def cost(flops, moved, chunk=1):
-    scale = (10, 18)[min(chunk, 1)]
+    scale = (7, 24)[min(chunk, 1)]
     return pl.CostEstimate(flops=scale * flops, transcendentals=0, bytes_accessed=scale * moved)
 
 
@@ -43,10 +43,11 @@
     return jnp.where(jnp.logical_and(hit, count < capacity), count, -1.0)
 
 
-def slot_rows(values, chunk, local_exp, capacity):
+def slot_rows(values, chunk, local_exp, capacity, first=0, n_rows=None):
     n_experts, tok = values.shape
-    n_rows = n_experts // local_exp * capacity
-    expert_of = lax.broadcasted_iota(jnp.int32, (n_rows, n_experts), 0) // capacity * local_exp + chunk
+    n_rows = n_rows or n_experts // local_exp * capacity
+    row = lax.broadcasted_iota(jnp.int32, (n_rows, n_experts), 0) + first
+    expert_of = row // capacity * local_exp + chunk
     spread = jnp.where(expert_of == lax.broadcasted_iota(jnp.int32, (n_rows, n_experts), 1), 1.0, 0.0)
     spread = spread.astype(BF16)
     at = dot(spread, values.astype(BF16), NN)
@@ -54,18 +55,26 @@
     return at == place, spread
 
 
-def dispatch_kernel(chunk, local_exp, capacity, ids_ref, probs_ref, tok_ref, grad_ref, out_ref):
-    ids_t = ids_ref[...]
-    topk, tok = ids_t.shape
-    n_experts = out_ref.shape[0] // capacity * local_exp
+def dispatch_kernel(
+    chunk, local_exp, capacity, ids_ref, probs_ref, tok_ref, grad_ref, out_ref, values_ref, prob_ref
+):
+    n_experts, tok = values_ref.shape
+    n_rows = out_ref.shape[0]
     width = tok_ref.shape[1]
-    values = slot_values(ids_t, n_experts, capacity)
-    rows = lax.broadcasted_iota(jnp.int32, (n_experts, tok), 0)
-    prob = jnp.zeros((n_experts, tok), F32)
-    for k in range(topk):
-        prob = prob + jnp.where(ids_t[k : k + 1, :] == rows, probs_ref[k : k + 1, :].astype(F32), 0.0)
-    onehot, spread = slot_rows(values, chunk, local_exp, capacity)
-    prob_rows = dot(spread, prob.astype(BF16), NN)
+    step = pl.program_id(0)
+
+    @pl.when(step == 0)
+    def _():
+        ids_t = ids_ref[...]
+        rows = lax.broadcasted_iota(jnp.int32, (n_experts, tok), 0)
+        prob = jnp.zeros((n_experts, tok), F32)
+        for k in range(ids_t.shape[0]):
+            prob = prob + jnp.where(ids_t[k : k + 1, :] == rows, probs_ref[k : k + 1, :].astype(F32), 0.0)
+        values_ref[...] = slot_values(ids_t, n_experts, capacity)
+        prob_ref[...] = prob
+
+    onehot, spread = slot_rows(values_ref[...], chunk, local_exp, capacity, step * n_rows, n_rows)
+    prob_rows = dot(spread, prob_ref[...].astype(BF16), NN)
     pick = jnp.where(onehot, 1.0, 0.0).astype(BF16)
     weighted = jnp.where(onehot, prob_rows, 0.0).astype(BF16)
     out_ref[:, :width] = dot(pick, tok_ref[...], NN).astype(BF16)
@@ -75,9 +84,14 @@
 def dispatch(chunk, local_exp, capacity, n_experts, ids_t, probs_t, tokens, out_grad):
     tok, width = tokens.shape
     n_rows = n_experts // local_exp * capacity
+    steps = 4
     return pl.pallas_call(
         functools.partial(dispatch_kernel, chunk, local_exp, capacity),
+        grid=(steps,),
+        in_specs=[whole(a.shape) for a in (ids_t, probs_t, tokens, out_grad)],
+        out_specs=pl.BlockSpec((n_rows // steps, 2 * width), lambda i: (i, 0)),
         out_shape=jax.ShapeDtypeStruct((n_rows, 2 * width), BF16),
+        scratch_shapes=[pltpu.VMEM((n_experts, tok), F32), pltpu.VMEM((n_experts, tok), F32)],
         compiler_params=pltpu.CompilerParams(vmem_limit_bytes=VMEM_LIMIT),
         cost_estimate=cost(4 * n_rows * tok * width, 4 * width * (tok + n_rows), 0),
         name=f"dispatch{chunk}",
@@ -85,26 +99,40 @@
 
 
 def hidden_kernel(
-    where_ref, x_ref, do_ref, xa_ref, xb_ref, da_col_ref, db_col_ref, wg_ref, wu_ref, wd_ref,
-    hid_ref, da_ref, db_ref, s_ref, a_ref, b_ref, sum_ref,
+    where_ref, x_ref, rows_ref, wg_ref, wu_ref, wd_ref,
+    hid_ref, da_ref, db_ref, s_ref, a_ref, b_ref, sum_ref, do_ref, sem,
 ):
     step = pl.program_id(0)
+    width = x_ref.shape[1]
+    fetch = pltpu.make_async_copy(rows_ref.at[:, pl.ds(width, width)], do_ref, sem)
+
+    @pl.when(step == 0)
+    def _():
+        fetch.start()
+
     gate = dot(x_ref[...], wg_ref[0], NN)
     upper = dot(x_ref[...], wu_ref[0], NN)
     sig = jax.nn.sigmoid(gate)
     act = gate * sig
     hid = (act * upper).astype(BF16)
     hid_ref[...] = hid
+
+    @pl.when(step == 0)
+    def _():
+        fetch.wait()
+
     dhid = dot(do_ref[...], wd_ref[0], NN)
     part = jnp.sum(hid.astype(F32) * dhid, axis=1, keepdims=True)
     dgate = (dhid * upper * sig * (1.0 + gate * (1.0 - sig))).astype(BF16)
     dup = (dhid * act).astype(BF16)
     da_ref[...] = dgate
     db_ref[...] = dup
-    for out_ref, x_col, do_col in ((a_ref, xa_ref, da_col_ref), (b_ref, xb_ref, db_col_ref)):
-        out_ref[0] = dot(x_col[...], dgate, TN).astype(BF16)
-        out_ref[1] = dot(x_col[...], dup, TN).astype(BF16)
-        out_ref[2] = dot(do_col[...], hid, TN).astype(BF16)
+    half = a_ref.shape[1]
+    for i, out_ref in enumerate((a_ref, b_ref)):
+        columns = pl.ds(pl.multiple_of(where_ref[i] * half, half), half)
+        out_ref[0] = dot(x_ref[:, columns], dgate, TN).astype(BF16)
+        out_ref[1] = dot(x_ref[:, columns], dup, TN).astype(BF16)
+        out_ref[2] = dot(do_ref[:, columns], hid, TN).astype(BF16)
 
     @pl.when(step == 0)
     def _():
@@ -130,7 +158,6 @@
     n_rows, width = rows.shape[0], rows.shape[1] // 2
     hidden = wg.shape[2]
     block = 2 * LANES
-    lefts = width // half
     once = pl.Buffered(1)
     weight = pl.BlockSpec((1, width, block), lambda i, at: (chunk, 0, i))
     result = pl.BlockSpec((n_rows, block), lambda i, at: (0, i))
@@ -142,17 +169,17 @@
             grid=(hidden // block,),
             in_specs=[
                 pl.BlockSpec((n_rows, width), lambda i, at: (0, 0), pipeline_mode=once),
-                pl.BlockSpec((n_rows, width), lambda i, at: (0, 1), pipeline_mode=once),
-                pl.BlockSpec((n_rows, half), lambda i, at: (0, at[0]), pipeline_mode=once),
-                pl.BlockSpec((n_rows, half), lambda i, at: (0, at[1]), pipeline_mode=once),
-                pl.BlockSpec((n_rows, half), lambda i, at: (0, at[0] + lefts), pipeline_mode=once),
-                pl.BlockSpec((n_rows, half), lambda i, at: (0, at[1] + lefts), pipeline_mode=once),
+                pl.BlockSpec(memory_space=pl.ANY),
                 weight,
                 weight,
                 weight,
             ],
             out_specs=[result] * 3 + [whole((n_rows, LANES)), shard, shard],
-            scratch_shapes=[pltpu.VMEM((n_rows, LANES), F32)],
+            scratch_shapes=[
+                pltpu.VMEM((n_rows, LANES), F32),
+                pltpu.VMEM((n_rows, width), BF16),
+                pltpu.SemaphoreType.DMA,
+            ],
         ),
         out_shape=[jax.ShapeDtypeStruct((n_rows, hidden), BF16)] * 3
         + [jax.ShapeDtypeStruct((n_rows, LANES), BF16)]
@@ -160,7 +187,7 @@
         compiler_params=pltpu.CompilerParams(vmem_limit_bytes=VMEM_LIMIT),
         cost_estimate=cost(8 * n_rows * width * hidden, 6 * width * hidden + n_rows * (4 * width + 6 * hidden), chunk),
         name=f"hidden{chunk}",
-    )(where, *[rows] * 6, wg, wu, wd)
+    )(where, rows, rows, wg, wu, wd)
 
 
 def weight_kernel(n_add, n_after, where_ref, x_ref, do_ref, hid_ref, da_ref, db_ref, *refs):
@@ -219,14 +246,14 @@
 
 
 def update_kernel(chunk, where_ref, mask_ref, *refs):
-    grads, weights = refs[:6], refs[6:9]
+    grads, weights = refs[:4], refs[4:7]
     outs = refs[-3:]
     for second in range(2):
 
         @pl.when(pl.program_id(0) == second)
         def _():
             for m in range(3):
-                grad = sum(g[m].astype(F32) for g in grads[3 * second : 3 * second + 3])
+                grad = sum(g[m].astype(F32) for g in grads[2 * second : 2 * second + 2])
                 weight = weights[m][0].astype(F32)
                 rate = mask_ref[chunk, m].astype(F32)
                 outs[m][0] = (weight - step_size * grad - shrink_rate * rate * weight).astype(BF16)
@@ -248,14 +275,14 @@
             num_scalar_prefetch=1,
             grid=(2, steps),
             in_specs=[pl.BlockSpec(memory_space=pltpu.SMEM)]
-            + [early] * 3
-            + [late] * 3
+            + [early] * 2
+            + [late] * 2
             + [weight] * 3
             + [pl.BlockSpec(memory_space=pl.ANY)] * len(extra),
             out_specs=[result] * 3,
         ),
         out_shape=[jax.ShapeDtypeStruct((local, 2 * half, hidden), BF16)] * 3,
-        input_output_aliases={11 + i: i for i in range(len(extra))},
+        input_output_aliases={9 + i: i for i in range(len(extra))},
         compiler_params=pltpu.CompilerParams(vmem_limit_bytes=VMEM_LIMIT),
         cost_estimate=cost(10 * half * hidden, 60 * half * hidden),
         name=f"update{chunk}",
@@ -264,27 +291,32 @@
 
 def dx_kernel(da_ref, db_ref, s_ref, wg_ref, wu_ref, *refs):
     out_ref = refs[-1]
-    n_owner, capacity, lanes = out_ref.shape
-    width = wg_ref.shape[1]
-    dx = (dot(da_ref[...], wg_ref[0], NT) + dot(db_ref[...], wu_ref[0], NT)).astype(BF16)
-    out_ref[:, :, :width] = dx.reshape(n_owner, capacity, width)
-    out_ref[:, :, width:] = s_ref[...].reshape(n_owner, capacity, lanes - width)
+    n_owner, capacity, block = out_ref.shape
+    last = pl.num_programs(0) - 1
+
+    @pl.when(pl.program_id(0) < last)
+    def _():
+        dx = dot(da_ref[...], wg_ref[0], NT) + dot(db_ref[...], wu_ref[0], NT)
+        out_ref[...] = dx.astype(BF16).reshape(n_owner, capacity, block)
+
+    @pl.when(pl.program_id(0) == last)
+    def _():
+        out_ref[:, :, :LANES] = s_ref[...].reshape(n_owner, capacity, LANES)
 
 
 def input_grads(chunk, local_exp, capacity, da, db, s, wg, wu, into):
     n_rows, hidden = da.shape
     width = wg.shape[1]
     n_owner = n_rows // capacity
-    weight = pl.BlockSpec((1, width, hidden), lambda i: (chunk, 0, 0), pipeline_mode=pl.Buffered(1))
+    block = width // 4
+    weight = pl.BlockSpec((1, block, hidden), lambda i: (chunk, jnp.minimum(i, 3), 0))
     extra = [] if into is None else [into]
     return pl.pallas_call(
         dx_kernel,
-        grid=(1,),
+        grid=(5,),
         in_specs=[whole((n_rows, hidden)), whole((n_rows, hidden)), whole((n_rows, LANES)), weight, weight]
         + [pl.BlockSpec(memory_space=pl.ANY)] * len(extra),
-        out_specs=pl.BlockSpec(
-            (n_owner, capacity, width + LANES), lambda i: (0, chunk, 0), pipeline_mode=pl.Buffered(1)
-        ),
+        out_specs=pl.BlockSpec((n_owner, capacity, block), lambda i: (0, chunk, i)),
         out_shape=jax.ShapeDtypeStruct((n_owner, local_exp * capacity, width + LANES), BF16),
         input_output_aliases={5: 0} if extra else {},
         compiler_params=pltpu.CompilerParams(vmem_limit_bytes=VMEM_LIMIT),
@@ -293,7 +325,7 @@
     )(da, db, s, wg, wu, *extra)
 
 
-def combine_kernel(local_exp, capacity, ids_ref, back_ref, tok_ref, prob_ref):
+def combine_kernel(local_exp, capacity, ids_ref, probs_ref, back_ref, tok_ref, prob_ref):
     ids_t = ids_ref[...]
     topk, tok = ids_t.shape
     n_rows = back_ref.shape[0] * capacity
@@ -317,21 +349,22 @@
     rows = lax.broadcasted_iota(jnp.int32, (n_experts, tok), 0)
     for k in range(topk):
         mine = jnp.where(ids_t[k : k + 1, :] == rows, by_expert, 0.0)
-        prob_ref[k : k + 1, :] = jnp.sum(mine, axis=0, keepdims=True)
-
-
-def combine(local_exp, capacity, ids_t, back, width):
+        score = jnp.sum(mine, axis=0, keepdims=True)
+        prob_ref[k : k + 1, :] = (score / probs_ref[k : k + 1, :].astype(F32)).astype(BF16)
+
+
+def combine(local_exp, capacity, ids_t, probs_t, back, width):
     topk, tok = ids_t.shape
     return pl.pallas_call(
         functools.partial(combine_kernel, local_exp, capacity),
         out_shape=[
             jax.ShapeDtypeStruct((tok, width), BF16),
-            jax.ShapeDtypeStruct((topk, tok), F32),
+            jax.ShapeDtypeStruct((topk, tok), BF16),
         ],
         compiler_params=pltpu.CompilerParams(vmem_limit_bytes=VMEM_LIMIT),
         cost_estimate=cost(2 * back.shape[0] * back.shape[1] * tok * width, 2 * back.size),
         name="combine",
-    )(ids_t, back)
+    )(ids_t, probs_t, back)
 
 
 def body(tokens, out_grad, expert_ids, route_probs, w_gate, w_up, w_down, decay_mask):
@@ -373,10 +406,15 @@
     def order(value, *after):
         return lax.optimization_barrier((value, *after))[0]
 
+    def own_sum(chunk, grads, near_up, near_down):
+        return [
+            weight_grads(f"own{chunk}{second}", chunk, blocks((0, second)), 1, half, *grads, landed)[0]
+            for second, landed in enumerate((near_down, near_up))
+        ]
+
     weights = (w_gate, w_up, w_down)
     far_pairs = ((2, 0), (2, 1))
     near_pairs = ((1, 1), (n_group - 1, 0))
-    own_pairs = ((0, 0), (0, 1))
     new, dx, before = None, None, None
     sends = [send(chunk) for chunk in range(local_exp)]
     rows = order(swap_rows(sends[0]), *sends[1:])
@@ -389,9 +427,7 @@
             after = [left]
             dx = input_grads(chunk, local_exp, capacity, da, db, s, w_gate, w_up, dx)
             back = swap(dx)
-            rows, _, *last = lax.optimization_barrier((rows, dx, *before[1]))
-            own, (near_up, near_down) = before[0], before[2]
-            new = update(chunk - 1, where, decay_mask, (own[0], last[0], near_down, own[1], near_up, last[1]), weights, new)
+            rows, _, *last = lax.optimization_barrier((rows, dx, *before[-1]))
             grads = (rows, hid, da, db)
         if chunk + 1 < local_exp:
             following, *after = lax.optimization_barrier((sends[chunk + 1], mark(chunk, *far)))
@@ -401,21 +437,23 @@
         far_up, far_down, _ = lax.optimization_barrier((far_up, far_down, near[0]))
         sum_up = weight_grads(f"up{chunk}", chunk, blocks((1, 0)), 1, half, *grads, far_up)[0]
         sum_down = weight_grads(f"down{chunk}", chunk, blocks((n_group - 1, 1)), 1, half, *grads, far_down)[0]
-        own = list(weight_grads(f"own{chunk}", chunk, blocks(*own_pairs), 2, half, *grads))
+        if before:
+            landed = before[1]
+            *landed, sum_up, sum_down = lax.optimization_barrier((*landed, sum_up, sum_down))
+            own = own_sum(chunk - 1, before[0], *landed)
+            new = update(chunk - 1, where, decay_mask, (own[0], last[0], own[1], last[1]), weights, new)
         sent = [up(sum_up), down(sum_down)]
         if chunk + 1 < local_exp:
             dx = input_grads(chunk, local_exp, capacity, order(da, sum_up, sum_down), db, s, w_gate, w_up, dx)
-            rows, dx, own[0], near_up, near_down, *_ = lax.optimization_barrier(
-                (following, dx, own[0], near_up, near_down, sum_up, sum_down)
-            )
-        before = (own, sent, (near_up, near_down))
-    back, near_up, near_down = lax.optimization_barrier((back, near_up, near_down))
+            rows, dx, near_up, near_down = lax.optimization_barrier((following, dx, near_up, near_down))
+            before = (grads, (near_up, near_down), sent)
+    own = own_sum(local_exp - 1, grads, near_up, near_down)
+    back, *own = lax.optimization_barrier((back, *own))
     new = update(
-        local_exp - 1, where, decay_mask, (own[0], sent[0], near_down, own[1], near_up, sent[1]), weights, new
+        local_exp - 1, where, decay_mask, (own[0], sent[0], own[1], sent[1]), weights, new
     )
-    grad_tokens, scores = combine(local_exp, capacity, ids_t, back, width)
-    grad_probs = (scores / probs_t.astype(F32)).astype(BF16).T
-
+    grad_tokens, grad_probs = combine(local_exp, capacity, ids_t, probs_t, back, width)
+    grad_probs = grad_probs.T
     return (grad_tokens, grad_probs, *new)
 
 

time: 249 us -> 250 us (level)
  waiting for transfers between devices: 87.4 us -> 83.6 us
    ppermute x6, waiting for transfers between devices: 6.84 us -> 16.8 us  [up(): lax.ppermute(a, 'dp', [(i, (i + 1) % n_group) for i in range(n_group)])]
    ppermute x6, waiting for transfers between devices: 8.61 us -> 0.61 us  [down(): lax.ppermute(a, 'dp', [(i, (i - 1) % n_group) for i in range(n_group)])]
    all_to_all x3, waiting for transfers between devices: 72 us -> 66.2 us  [swap(): return lax.all_to_all(a, 'expert', split_axis=0, concat_axis=0, tiled=True)]
    pallas_call x8 -> x10, Pallas kernels: 43.2 us -> 45.8 us  [weight_grads(): pl.pallas_call(functools.partial(weight_kernel, len(adds), len(after)), g...]
    ppermute x6, starting transfers between devices: 13.3 us -> 15.8 us  [down(): lax.ppermute(a, 'dp', [(i, (i - 1) % n_group) for i in range(n_group)])]
  transfers between devices with their start and end apart: 15 -> 15, of which waited for: 9 -> 9; matrix products, arithmetic and copies ran while one was open for 1% -> 1% of each run, Pallas kernels for 37% -> 38%
where the time goes in v7:
time: 250 us; the launch traced here: 249 us
  Pallas kernels  122 us (49%)
  waiting for transfers between devices  83.6 us (33%)
  starting transfers between devices  37.8 us (15%)
  local copies, waits for them, and re-layouts  3.5 us (1%)
    all_to_all x3, waiting for transfers between devices, swap(): return lax.all_to_all(a, 'expert', split_axis=0, concat_axis=0, tiled=True)  66.2 us
    pallas_call x10, Pallas kernels, weight_grads(): pl.pallas_call(functools.partial(weight_kernel, len(adds), len(after)), g...  45.8 us
    pallas_call x2, Pallas kernels, hidden_grads(): pl.pallas_call(hidden_kernel, grid_spec=pltpu.PrefetchScalarGridSpec(num_...  32.6 us
    all_to_all x3, starting transfers between devices, swap(): return lax.all_to_all(a, 'expert', split_axis=0, concat_axis=0, tiled=True)  18.3 us
    ppermute x6, waiting for transfers between devices, up(): lax.ppermute(a, 'dp', [(i, (i + 1) % n_group) for i in range(n_group)])  16.8 us
    ppermute x6, starting transfers between devices, down(): lax.ppermute(a, 'dp', [(i, (i - 1) % n_group) for i in range(n_group)])  15.8 us
    pallas_call x2, Pallas kernels, input_grads(): pl.pallas_call(dx_kernel, grid=(5,), in_specs=[whole((n_rows, hidden)), w...  15.1 us
    pallas_call x2, Pallas kernels, update(): pl.pallas_call(functools.partial(update_kernel, chunk), grid_spec=pltpu.P...  11.1 us
  transfers between devices with their start and end apart: 15, of which 9 were waited for; matrix products, arithmetic and copies ran while one was open for 1% of the time, Pallas kernels for 38%

profile of v7, /device:TPU:0, one launch (start us, length us, event | category | flops | bytes accessed | tf_op | source)
XLA Modules:
  0.0 249.2 jit_solution(16601296943614401671)
XLA Ops:
  0.6 5.2 %dispatch0.1 = bf16[512,4096]{1,0:T(8,128)(2,1)} custom-call(s32[8,128]{1,0:T(8,128)} %bitcast.18, bf16[8,128]{1,0:T(8,128)(2,1)} %bitcast.21, bf16[128,2048]{1,0:T(8,128)(2,1)} %tok_ref.3, bf16[128,2048]{1,0:T(8,128)(2,1)} %grad_ref.3), custom_call_target="tpu_custom_call" | custom-call | flops 3758096384 | bytes 36700160 | tf_op jit(solution)/shard_map/dispatch0/pallas_call | solution.py:88
  5.9 8.5 %all-to-all-start = ((bf16[32,16,4096]{2,1,0:T(8,128)(2,1)}), bf16[32,16,4096]{2,1,0:T(8,128)(2,1)}, u32[]{:S(2)}, u32[]{:S(2)}) async-start(bf16[32,16,4096]{2,1,0:T(8,128)(2,1)} %bitcast.17), calls=%async_computation | async-start | bytes 8388608 | tf_op jit(solution)/shard_map/all_to_all | solution.py:400
  14.4 0.7 pad_add_fusion.where_ref
  15.1 5.1 %dispatch1.1 = bf16[512,4096]{1,0:T(8,128)(2,1)} custom-call(s32[8,128]{1,0:T(8,128)} %bitcast.19, bf16[8,128]{1,0:T(8,128)(2,1)} %bitcast.22, bf16[128,2048]{1,0:T(8,128)(2,1)} %tok_ref.3, bf16[128,2048]{1,0:T(8,128)(2,1)} %grad_ref.3), custom_call_target="tpu_custom_call" | custom-call | flops 3758096384 | bytes 36700160 | tf_op jit(solution)/shard_map/dispatch1/pallas_call | solution.py:88
  20.2 47.7 %all-to-all-done = bf16[32,16,4096]{2,1,0:T(8,128)(2,1)} async-done(((bf16[32,16,4096]{2,1,0:T(8,128)(2,1)}), bf16[32,16,4096]{2,1,0:T(8,128)(2,1)}, u32[]{:S(2)}, u32[]{:S(2)}) %all-to-all-start) | async-done | bytes 4194336 | tf_op jit(solution)/shard_map/all_to_all | solution.py:400
  67.9 16.3 %hidden0.1 = (bf16[512,768]{1,0:T(8,128)(2,1)}, bf16[512,768]{1,0:T(8,128)(2,1)}, bf16[512,768]{1,0:T(8,128)(2,1)}, bf16[512,128]{1,0:T(8,128)(2,1)}, bf16[3,256...) custom-call(s32[2]{0:T(128)} %pad_add_fusion.where_ref, bf16[512,4096]{1,0:T(8,128)(2,1)} %bitcast.5.x_ref.rows_ref.do_ref, ...), custom_call_target="tpu_custom_call" | custom-call | flops 45097156608 | bytes 111935488 | tf_op jit(solution)/shard_map/hidden0/pallas_call | solution.py:165
  84.2 1.6 collective-permute-start
  85.8 1.7 collective-permute-start.1
  87.5 1.3 mark0.1.refs_0_
  88.8 4.9 %all-to-all-start.1 = ((bf16[32,16,4096]{2,1,0:T(8,128)(2,1)}), bf16[32,16,4096]{2,1,0:T(8,128)(2,1)}, u32[]{:S(2)}, u32[]{:S(2)}) async-start(bf16[32,16,4096]{2,1,0:T(8,128)(2,1)} %bitcast.16), calls=%async_computation.1 | async-start | bytes 8388608 | tf_op jit(solution)/shard_map/all_to_all | solution.py:400
  93.7 0.7 pad_add_fusion.1.where_ref
  94.4 6.8 %near0.1 = (bf16[3,256,768]{2,1,0:T(8,128)(2,1)}, bf16[3,256,768]{2,1,0:T(8,128)(2,1)}) custom-call(s32[2]{0:T(128)} %pad_add_fusion.1.where_ref, bf16[512,4096]{1,0:T(8,128)(2,1)} %bitcast.5.x_ref.rows_ref.do_ref, bf16[512,4096]{1,0:T(8,128)(2,1)} %bitcast.5.x_ref.rows_ref.do_ref, bf16[512,768]{1,0:T(8,128)(2,1)} %get-tuple-element.58.hid_ref, ...), custom_call_target="tpu_custom_call" | custom-call | flops 8455716864 | bytes 33030144 | tf_op jit(solution)/shard_map/near0/pallas_call | solution.py:211
  101.2 0.4 collective-permute-start.2
  101.5 2.9 %collective-permute-start.3 = (bf16[3,256,768]{2,1,0:T(8,128)(2,1)}, bf16[3,256,768]{2,1,0:T(8,128)(2,1)S(1)}, u32[]{:S(2)}, u32[]{:S(2)}) collective-permute-start(bf16[3,256,768]{2,1,0:T(8,128)(2,1)} %get-tuple-element.66), channel_id=1, source_target_pairs={{0,96},{32,0},{64,32},{96,64},{1,97},{33,1},{65,33},{97,65},{2,98}... | collective-permute-start | bytes 3538952 | tf_op jit(solution)/shard_map/ppermute | solution.py:394
  104.4 10.2 %collective-permute-done.refs_0_ = bf16[3,256,768]{2,1,0:T(8,128)(2,1)S(1)} collective-permute-done((bf16[3,256,768]{2,1,0:T(8,128)(2,1)}, bf16[3,256,768]{2,1,0:T(8,128)(2,1)S(1)}, u32[]{:S(2)}, u32[]{:S(2)}) %collective-permute-start) | collective-permute-done | bytes 1179680 | tf_op jit(solution)/shard_map/ppermute | solution.py:391
  114.6 0.0 copy-start.3
  114.6 0.3 collective-permute-done.1.refs_0_
  115.0 1.0 copy-done.5
  116.0 4.0 %down0.1 = bf16[3,256,768]{2,1,0:T(8,128)(2,1)} custom-call(s32[1]{0:T(128)} %bitcast.11.where_ref, bf16[512,4096]{1,0:T(8,128)(2,1)} %bitcast.5.x_ref.rows_ref.do_ref, bf16[512,4096]{1,0:T(8,128)(2,1)} %bitcast.5.x_ref.rows_ref.do_ref, bf16[512,768]{1,0:T(8,128)(2,1)} %get-tuple-element.58.hid_ref, bf16[512,768]{1,0:T(8,128)(2,1)} %get-tuple-element.64.da_ref, ...), custom_call_target="tpu_custom_call" | custom-call | flops 4227858432 | bytes 24772608 | tf_op jit(solution)/shard_map/down0/pallas_call | solution.py:211
  120.0 0.0 copy-done.3
  120.0 2.8 %collective-permute-start.5 = (bf16[3,256,768]{2,1,0:T(8,128)(2,1)}, bf16[3,256,768]{2,1,0:T(8,128)(2,1)}, u32[]{:S(2)}, u32[]{:S(2)}) collective-permute-start(bf16[3,256,768]{2,1,0:T(8,128)(2,1)} %down0.1), channel_id=1, source_target_pairs={{0,96},{32,0},{64,32},{96,64},{1,97},{33,1},{65,33},{97,65},{2,98}... | collective-permute-start | bytes 3538952 | tf_op jit(solution)/shard_map/ppermute | solution.py:394
  122.9 4.0 %up0.1 = bf16[3,256,768]{2,1,0:T(8,128)(2,1)} custom-call(s32[1]{0:T(128)} %bitcast.8.where_ref, bf16[512,4096]{1,0:T(8,128)(2,1)} %bitcast.5.x_ref.rows_ref.do_ref, bf16[512,4096]{1,0:T(8,128)(2,1)} %bitcast.5.x_ref.rows_ref.do_ref, bf16[512,768]{1,0:T(8,128)(2,1)} %get-tuple-element.58.hid_ref, bf16[512,768]{1,0:T(8,128)(2,1)} %get-tuple-element.64.da_ref, ...), custom_call_target="tpu_custom_call" | custom-call | flops 4227858432 | bytes 24772608 | tf_op jit(solution)/shard_map/up0/pallas_call | solution.py:211
  126.9 0.0 collective-permute-start.4
  126.9 7.6 %dx0.1.refs_0_ = bf16[32,32,2176]{2,1,0:T(8,128)(2,1)} custom-call(bf16[512,768]{1,0:T(8,128)(2,1)} %get-tuple-element.64.da_ref, bf16[512,768]{1,0:T(8,128)(2,1)} %get-tuple-element.59.db_ref, bf16[512,128]{1,0:T(8,128)(2,1)} %get-tuple-element.65.s_ref, bf16[2,2048,768]{2,1,0:T(8,128)(2,1)} %refs_4_.3, bf16[2,2048,768]{2,1,0:T(8,128)(2,1)} %refs_5_.3), custom_call_target="tpu_custom_call" | custom-call | flops 22548578304 | bytes 69730304 | tf_op jit(solution)/shard_map/dx0/pallas_call | solution.py:314
  134.5 5.5 %collective-permute-done.2.refs_0_ = bf16[3,256,768]{2,1,0:T(8,128)(2,1)} collective-permute-done((bf16[3,256,768]{2,1,0:T(8,128)(2,1)}, bf16[3,256,768]{2,1,0:T(8,128)(2,1)}, u32[]{:S(2)}, u32[]{:S(2)}) %collective-permute-start.2) | collective-permute-done | bytes 1179680 | tf_op jit(solution)/shard_map/ppermute | solution.py:391
  140.0 0.2 collective-permute-done.3.refs_0_
  140.2 6.9 %all-to-all-done.1 = bf16[32,16,4096]{2,1,0:T(8,128)(2,1)} async-done(((bf16[32,16,4096]{2,1,0:T(8,128)(2,1)}), bf16[32,16,4096]{2,1,0:T(8,128)(2,1)}, u32[]{:S(2)}, u32[]{:S(2)}) %all-to-all-start.1) | async-done | bytes 4194336 | tf_op jit(solution)/shard_map/all_to_all | solution.py:400
  147.2 16.3 %hidden1.1 = (bf16[512,768]{1,0:T(8,128)(2,1)}, bf16[512,768]{1,0:T(8,128)(2,1)}, bf16[512,768]{1,0:T(8,128)(2,1)}, bf16[512,128]{1,0:T(8,128)(2,1)}, bf16[3,256...) custom-call(s32[2]{0:T(128)} %pad_add_fusion.where_ref, bf16[512,4096]{1,0:T(8,128)(2,1)} %bitcast.7.x_ref.rows_ref.do_ref, ...), custom_call_target="tpu_custom_call" | custom-call | flops 154618822656 | bytes 383778816 | tf_op jit(solution)/shard_map/hidden1/pallas_call | solution.py:165
  163.5 0.0 copy-done.4
  163.5 0.5 collective-permute-start.8
  164.0 1.4 mark1.1.refs_0_
  165.4 0.0 copy-done.2
  165.4 2.8 %collective-permute-start.9 = (bf16[3,256,768]{2,1,0:T(8,128)(2,1)S(1)}, bf16[3,256,768]{2,1,0:T(8,128)(2,1)S(1)}, u32[]{:S(2)}, u32[]{:S(2)}) collective-permute-start(bf16[3,256,768]{2,1,0:T(8,128)(2,1)S(1)} %copy-done.2), channel_id=1, source_target_pairs={{0,96},{32,0},{64,32},{96,64},{1,97},{33,1},{65,33},{97,65},{2,98}... | collective-permute-start | bytes 3538952 | tf_op jit(solution)/shard_map/ppermute | solution.py:394
  168.2 7.5 %dx1.1 = bf16[32,32,2176]{2,1,0:T(8,128)(2,1)} custom-call(bf16[512,768]{1,0:T(8,128)(2,1)} %get-tuple-element.68.da_ref, bf16[512,768]{1,0:T(8,128)(2,1)} %get-tuple-element.69.db_ref, bf16[512,128]{1,0:T(8,128)(2,1)} %get-tuple-element.70.s_ref, bf16[2,2048,768]{2,1,0:T(8,128)(2,1)} %refs_4_.3, ...), custom_call_target="tpu_custom_call", output_to_operand_aliasing={{}: (5, {})} | custom-call | flops 77309411328 | bytes 239075328 | tf_op jit(solution)/shard_map/dx1/pallas_call | solution.py:314
  175.7 4.9 %all-to-all-start.2 = ((bf16[32,32,2176]{2,1,0:T(8,128)(2,1)}), bf16[32,32,2176]{2,1,0:T(8,128)(2,1)}, u32[]{:S(2)}, u32[]{:S(2)}) async-start(bf16[32,32,2176]{2,1,0:T(8,128)(2,1)} %dx1.1), calls=%async_computation.2 | async-start | bytes 8912896 | tf_op jit(solution)/shard_map/all_to_all | solution.py:400
  180.6 0.0 collective-permute-done.5.refs_3_
  180.6 0.0 collective-permute-done.4.refs_1_
  180.6 6.8 %near1.1 = (bf16[3,256,768]{2,1,0:T(8,128)(2,1)}, bf16[3,256,768]{2,1,0:T(8,128)(2,1)}) custom-call(s32[2]{0:T(128)} %pad_add_fusion.1.where_ref, bf16[512,4096]{1,0:T(8,128)(2,1)} %bitcast.7.x_ref.rows_ref.do_ref, bf16[512,4096]{1,0:T(8,128)(2,1)} %bitcast.7.x_ref.rows_ref.do_ref, bf16[512,768]{1,0:T(8,128)(2,1)} %get-tuple-element.76.hid_ref, ...), custom_call_target="tpu_custom_call" | custom-call | flops 28991029248 | bytes 113246208 | tf_op jit(solution)/shard_map/near1/pallas_call | solution.py:211
  187.4 0.0 collective-permute-start.7
  187.4 3.2 %collective-permute-start.6 = (bf16[3,256,768]{2,1,0:T(8,128)(2,1)}, bf16[3,256,768]{2,1,0:T(8,128)(2,1)}, u32[]{:S(2)}, u32[]{:S(2)}) collective-permute-start(bf16[3,256,768]{2,1,0:T(8,128)(2,1)} %get-tuple-element.78), channel_id=1, source_target_pairs={{0,96},{32,0},{64,32},{96,64},{1,97},{33,1},{65,33},{97,65},{2,98}... | collective-permute-start | bytes 3538952 | tf_op jit(solution)/shard_map/ppermute | solution.py:394
  190.7 0.0 collective-permute-done.8.refs_0_
  190.7 0.0 collective-permute-done.9.refs_0_
  190.7 0.0 copy-start.8
  190.7 1.0 copy-done.8
  191.7 4.0 %down1.1 = bf16[3,256,768]{2,1,0:T(8,128)(2,1)} custom-call(s32[1]{0:T(128)} %bitcast.11.where_ref, bf16[512,4096]{1,0:T(8,128)(2,1)} %bitcast.7.x_ref.rows_ref.do_ref, bf16[512,4096]{1,0:T(8,128)(2,1)} %bitcast.7.x_ref.rows_ref.do_ref, bf16[512,768]{1,0:T(8,128)(2,1)} %get-tuple-element.76.hid_ref, bf16[512,768]{1,0:T(8,128)(2,1)} %get-tuple-element.68.da_ref, ...), custom_call_target="tpu_custom_call" | custom-call | flops 14495514624 | bytes 84934656 | tf_op jit(solution)/shard_map/down1/pallas_call | solution.py:211
  195.7 0.0 copy-done.7
  195.7 4.1 %up1.1 = bf16[3,256,768]{2,1,0:T(8,128)(2,1)} custom-call(s32[1]{0:T(128)} %bitcast.8.where_ref, bf16[512,4096]{1,0:T(8,128)(2,1)} %bitcast.7.x_ref.rows_ref.do_ref, bf16[512,4096]{1,0:T(8,128)(2,1)} %bitcast.7.x_ref.rows_ref.do_ref, bf16[512,768]{1,0:T(8,128)(2,1)} %get-tuple-element.76.hid_ref, bf16[512,768]{1,0:T(8,128)(2,1)} %get-tuple-element.68.da_ref, ...), custom_call_target="tpu_custom_call" | custom-call | flops 14495514624 | bytes 84934656 | tf_op jit(solution)/shard_map/up1/pallas_call | solution.py:211
  199.8 1.2 collective-permute-start.10
  201.1 0.0 copy-done.6
  201.1 2.3 collective-permute-start.11
  203.4 4.0 %own01.1.refs_2_ = bf16[3,256,768]{2,1,0:T(8,128)(2,1)} custom-call(s32[1]{0:T(128)} %bitcast.13.where_ref, bf16[512,4096]{1,0:T(8,128)(2,1)} %bitcast.5.x_ref.rows_ref.do_ref, bf16[512,4096]{1,0:T(8,128)(2,1)} %bitcast.5.x_ref.rows_ref.do_ref, bf16[512,768]{1,0:T(8,128)(2,1)} %get-tuple-element.58.hid_ref, bf16[512,768]{1,0:T(8,128)(2,1)} %get-tuple-element.64.da_ref, ...), custom_call_target="tpu_custom_call" | custom-call | flops 4227858432 | bytes 24772608 | tf_op jit(solution)/shard_map/own01/pallas_call | solution.py:211
  207.4 4.0 %own00.1.refs_0_ = bf16[3,256,768]{2,1,0:T(8,128)(2,1)} custom-call(s32[1]{0:T(128)} %bitcast.12.where_ref, bf16[512,4096]{1,0:T(8,128)(2,1)} %bitcast.5.x_ref.rows_ref.do_ref, bf16[512,4096]{1,0:T(8,128)(2,1)} %bitcast.5.x_ref.rows_ref.do_ref, bf16[512,768]{1,0:T(8,128)(2,1)} %get-tuple-element.58.hid_ref, bf16[512,768]{1,0:T(8,128)(2,1)} %get-tuple-element.64.da_ref, ...), custom_call_target="tpu_custom_call" | custom-call | flops 4227858432 | bytes 24772608 | tf_op jit(solution)/shard_map/own00/pallas_call | solution.py:211
  211.5 5.6 %update0.1 = (bf16[2,512,768]{2,1,0:T(8,128)(2,1)}, bf16[2,512,768]{2,1,0:T(8,128)(2,1)}, bf16[2,512,768]{2,1,0:T(8,128)(2,1)}) custom-call(s32[1]{0:T(128)} %bitcast.15.where_ref, s32[2,3]{1,0:T(2,128)} %mask_ref.3, bf16[3,256,768]{2,1,0:T(8,128)(2,1)} %own00.1.refs_0_, bf16[3,256,768]{2,1,0:T(8,128)(2,1)} %collective-permute-done.4.refs_1_, ...), custom_call_target="tpu_custom_call" | custom-call | flops 47185920 | bytes 283115520 | tf_op jit(solution)/shard_map/update0/pallas_call | solution.py:272
  217.1 0.7 collective-permute-done.7.refs_0_
  217.8 4.0 %own11.1.refs_2_ = bf16[3,256,768]{2,1,0:T(8,128)(2,1)} custom-call(s32[1]{0:T(128)} %bitcast.13.where_ref, bf16[512,4096]{1,0:T(8,128)(2,1)} %bitcast.7.x_ref.rows_ref.do_ref, bf16[512,4096]{1,0:T(8,128)(2,1)} %bitcast.7.x_ref.rows_ref.do_ref, bf16[512,768]{1,0:T(8,128)(2,1)} %get-tuple-element.76.hid_ref, bf16[512,768]{1,0:T(8,128)(2,1)} %get-tuple-element.68.da_ref, ...), custom_call_target="tpu_custom_call" | custom-call | flops 14495514624 | bytes 84934656 | tf_op jit(solution)/shard_map/own11/pallas_call | solution.py:211
  221.8 0.0 collective-permute-done.6.refs_0_
  221.8 4.0 %own10.1.refs_0_ = bf16[3,256,768]{2,1,0:T(8,128)(2,1)} custom-call(s32[1]{0:T(128)} %bitcast.12.where_ref, bf16[512,4096]{1,0:T(8,128)(2,1)} %bitcast.7.x_ref.rows_ref.do_ref, bf16[512,4096]{1,0:T(8,128)(2,1)} %bitcast.7.x_ref.rows_ref.do_ref, bf16[512,768]{1,0:T(8,128)(2,1)} %get-tuple-element.76.hid_ref, bf16[512,768]{1,0:T(8,128)(2,1)} %get-tuple-element.68.da_ref, ...), custom_call_target="tpu_custom_call" | custom-call | flops 14495514624 | bytes 84934656 | tf_op jit(solution)/shard_map/own10/pallas_call | solution.py:211
  225.8 11.5 %all-to-all-done.2.back_ref = bf16[32,32,2176]{2,1,0:T(8,128)(2,1)} async-done(((bf16[32,32,2176]{2,1,0:T(8,128)(2,1)}), bf16[32,32,2176]{2,1,0:T(8,128)(2,1)}, u32[]{:S(2)}, u32[]{:S(2)}) %all-to-all-start.2) | async-done | bytes 4456480 | tf_op jit(solution)/shard_map/all_to_all | solution.py:400
  237.3 4.4 %combine.1 = (bf16[128,2048]{1,0:T(8,128)(2,1)}, bf16[8,128]{1,0:T(8,128)(2,1)}) custom-call(s32[8,128]{1,0:T(8,128)} %bitcast.20, bf16[8,128]{1,0:T(8,128)(2,1)} %bitcast.23, bf16[32,32,2176]{2,1,0:T(8,128)(2,1)} %all-to-all-done.2.back_ref), custom_call_target="tpu_custom_call" | custom-call | flops 12884901888 | bytes 106954752 | tf_op jit(solution)/shard_map/combine/pallas_call | solution.py:358
  241.7 0.4 collective-permute-done.10.refs_1_
  242.1 0.0 collective-permute-done.11.refs_3_
  242.1 1.0 copy-done
  243.2 0.4 copy-done.1
  243.5 5.5 %update1.1 = (bf16[2,512,768]{2,1,0:T(8,128)(2,1)}, bf16[2,512,768]{2,1,0:T(8,128)(2,1)}, bf16[2,512,768]{2,1,0:T(8,128)(2,1)}) custom-call(s32[1]{0:T(128)} %bitcast.15.where_ref, s32[2,3]{1,0:T(2,128)} %mask_ref.3, bf16[3,256,768]{2,1,0:T(8,128)(2,1)} %own10.1.refs_0_, ...), custom_call_target="tpu_custom_call", output_to_operand_aliasing={{0}: (9, {}), {1}: (10, {}), {2}: (11, {})} | custom-call | flops 47185920 | bytes 283115520 | tf_op jit(solution)/shard_map/update1/pallas_call | solution.py:272
  (7 shorter events, 0.0 us)
Async XLA Ops:
  5.9 62.0 %all-to-all-start = ((bf16[32,16,4096]{2,1,0:T(8,128)(2,1)}), bf16[32,16,4096]{2,1,0:T(8,128)(2,1)}, u32[]{:S(2)}, u32[]{:S(2)}) async-start(bf16[32,16,4096]{2,1,0:T(8,128)(2,1)} %bitcast.17), calls=%async_computation | async-start | bytes 8388608 | tf_op jit(solution)/shard_map/all_to_all | solution.py:400
  84.2 30.4 %collective-permute-start = (bf16[3,256,768]{2,1,0:T(8,128)(2,1)}, bf16[3,256,768]{2,1,0:T(8,128)(2,1)S(1)}, u32[]{:S(2)}, u32[]{:S(2)}) collective-permute-start(bf16[3,256,768]{2,1,0:T(8,128)(2,1)} %get-tuple-element.54.a_ref), channel_id=1, source_target_pairs={{0,32},{32,64},{64,96},{96,0},{1,33},{33,65},{65,97},{97,1},{2,34}... | collective-permute-start | bytes 3538952 | tf_op jit(solution)/shard_map/ppermute | solution.py:391
  85.8 29.1 %collective-permute-start.1 = (bf16[3,256,768]{2,1,0:T(8,128)(2,1)}, bf16[3,256,768]{2,1,0:T(8,128)(2,1)S(1)}, u32[]{:S(2)}, u32[]{:S(2)}) collective-permute-start(bf16[3,256,768]{2,1,0:T(8,128)(2,1)} %get-tuple-element.55.b_ref), channel_id=1, source_target_pairs={{0,96},{32,0},{64,32},{96,64},{1,97},{33,1},{65,33},{97,65},{2,98}... | collective-permute-start | bytes 3538952 | tf_op jit(solution)/shard_map/ppermute | solution.py:394
  88.8 58.3 %all-to-all-start.1 = ((bf16[32,16,4096]{2,1,0:T(8,128)(2,1)}), bf16[32,16,4096]{2,1,0:T(8,128)(2,1)}, u32[]{:S(2)}, u32[]{:S(2)}) async-start(bf16[32,16,4096]{2,1,0:T(8,128)(2,1)} %bitcast.16), calls=%async_computation.1 | async-start | bytes 8388608 | tf_op jit(solution)/shard_map/all_to_all | solution.py:400
  101.2 38.8 %collective-permute-start.2 = (bf16[3,256,768]{2,1,0:T(8,128)(2,1)}, bf16[3,256,768]{2,1,0:T(8,128)(2,1)}, u32[]{:S(2)}, u32[]{:S(2)}) collective-permute-start(bf16[3,256,768]{2,1,0:T(8,128)(2,1)} %get-tuple-element.61), channel_id=1, source_target_pairs={{0,32},{32,64},{64,96},{96,0},{1,33},{33,65},{65,97},{97,1},{2,34}... | collective-permute-start | bytes 3538952 | tf_op jit(solution)/shard_map/ppermute | solution.py:391
  101.5 38.7 %collective-permute-start.3 = (bf16[3,256,768]{2,1,0:T(8,128)(2,1)}, bf16[3,256,768]{2,1,0:T(8,128)(2,1)S(1)}, u32[]{:S(2)}, u32[]{:S(2)}) collective-permute-start(bf16[3,256,768]{2,1,0:T(8,128)(2,1)} %get-tuple-element.66), channel_id=1, source_target_pairs={{0,96},{32,0},{64,32},{96,64},{1,97},{33,1},{65,33},{97,65},{2,98}... | collective-permute-start | bytes 3538952 | tf_op jit(solution)/shard_map/ppermute | solution.py:394
  114.6 5.4 %copy-start.3 = (bf16[3,256,768]{2,1,0:T(8,128)(2,1)}, bf16[3,256,768]{2,1,0:T(8,128)(2,1)S(1)}, u32[]{:S(2)}) copy-start(bf16[3,256,768]{2,1,0:T(8,128)(2,1)S(1)} %collective-permute-done.refs_0_) | copy-start | bytes 3538948
  115.0 1.0 copy-start.5
  120.0 60.6 %collective-permute-start.5 = (bf16[3,256,768]{2,1,0:T(8,128)(2,1)}, bf16[3,256,768]{2,1,0:T(8,128)(2,1)}, u32[]{:S(2)}, u32[]{:S(2)}) collective-permute-start(bf16[3,256,768]{2,1,0:T(8,128)(2,1)} %down0.1), channel_id=1, source_target_pairs={{0,96},{32,0},{64,32},{96,64},{1,97},{33,1},{65,33},{97,65},{2,98}... | collective-permute-start | bytes 3538952 | tf_op jit(solution)/shard_map/ppermute | solution.py:394
  126.9 53.7 %collective-permute-start.4 = (bf16[3,256,768]{2,1,0:T(8,128)(2,1)}, bf16[3,256,768]{2,1,0:T(8,128)(2,1)}, u32[]{:S(2)}, u32[]{:S(2)}) collective-permute-start(bf16[3,256,768]{2,1,0:T(8,128)(2,1)} %up0.1), channel_id=1, source_target_pairs={{0,32},{32,64},{64,96},{96,0},{1,33},{33,65},{65,97},{97,1},{2,34}... | collective-permute-start | bytes 3538952 | tf_op jit(solution)/shard_map/ppermute | solution.py:391
  140.2 23.2 %copy-start.4 = (bf16[3,256,768]{2,1,0:T(8,128)(2,1)}, bf16[3,256,768]{2,1,0:T(8,128)(2,1)S(1)}, u32[]{:S(2)}) copy-start(bf16[3,256,768]{2,1,0:T(8,128)(2,1)S(1)} %collective-permute-done.3.refs_0_) | copy-start | bytes 3538948
  163.5 27.2 %collective-permute-start.8 = (bf16[3,256,768]{2,1,0:T(8,128)(2,1)}, bf16[3,256,768]{2,1,0:T(8,128)(2,1)S(1)}, u32[]{:S(2)}, u32[]{:S(2)}) collective-permute-start(bf16[3,256,768]{2,1,0:T(8,128)(2,1)} %get-tuple-element.72.a_ref), channel_id=1, source_target_pairs={{0,32},{32,64},{64,96},{96,0},{1,33},{33,65},{65,97},{97,1},{2,34}... | collective-permute-start | bytes 3538952 | tf_op jit(solution)/shard_map/ppermute | solution.py:391
  164.0 1.4 copy-start.2
  165.4 25.3 %collective-permute-start.9 = (bf16[3,256,768]{2,1,0:T(8,128)(2,1)S(1)}, bf16[3,256,768]{2,1,0:T(8,128)(2,1)S(1)}, u32[]{:S(2)}, u32[]{:S(2)}) collective-permute-start(bf16[3,256,768]{2,1,0:T(8,128)(2,1)S(1)} %copy-done.2), channel_id=1, source_target_pairs={{0,96},{32,0},{64,32},{96,64},{1,97},{33,1},{65,33},{97,65},{2,98}... | collective-permute-start | bytes 3538952 | tf_op jit(solution)/shard_map/ppermute | solution.py:394
  175.7 61.6 %all-to-all-start.2 = ((bf16[32,32,2176]{2,1,0:T(8,128)(2,1)}), bf16[32,32,2176]{2,1,0:T(8,128)(2,1)}, u32[]{:S(2)}, u32[]{:S(2)}) async-start(bf16[32,32,2176]{2,1,0:T(8,128)(2,1)} %dx1.1), calls=%async_computation.2 | async-start | bytes 8912896 | tf_op jit(solution)/shard_map/all_to_all | solution.py:400
  187.4 30.3 %collective-permute-start.7 = (bf16[3,256,768]{2,1,0:T(8,128)(2,1)}, bf16[3,256,768]{2,1,0:T(8,128)(2,1)}, u32[]{:S(2)}, u32[]{:S(2)}) collective-permute-start(bf16[3,256,768]{2,1,0:T(8,128)(2,1)} %get-tuple-element.79), channel_id=1, source_target_pairs={{0,32},{32,64},{64,96},{96,0},{1,33},{33,65},{65,97},{97,1},{2,34}... | collective-permute-start | bytes 3538952 | tf_op jit(solution)/shard_map/ppermute | solution.py:391
  187.4 34.4 %collective-permute-start.6 = (bf16[3,256,768]{2,1,0:T(8,128)(2,1)}, bf16[3,256,768]{2,1,0:T(8,128)(2,1)}, u32[]{:S(2)}, u32[]{:S(2)}) collective-permute-start(bf16[3,256,768]{2,1,0:T(8,128)(2,1)} %get-tuple-element.78), channel_id=1, source_target_pairs={{0,96},{32,0},{64,32},{96,64},{1,97},{33,1},{65,33},{97,65},{2,98}... | collective-permute-start | bytes 3538952 | tf_op jit(solution)/shard_map/ppermute | solution.py:394
  190.7 5.1 %copy-start.7 = (bf16[3,256,768]{2,1,0:T(8,128)(2,1)}, bf16[3,256,768]{2,1,0:T(8,128)(2,1)S(1)}, u32[]{:S(2)}) copy-start(bf16[3,256,768]{2,1,0:T(8,128)(2,1)S(1)} %collective-permute-done.8.refs_0_) | copy-start | bytes 3538948
  190.7 1.0 copy-start.8
  195.7 5.3 %copy-start.6 = (bf16[3,256,768]{2,1,0:T(8,128)(2,1)S(1)}, bf16[3,256,768]{2,1,0:T(8,128)(2,1)}, u32[]{:S(2)}) copy-start(bf16[3,256,768]{2,1,0:T(8,128)(2,1)} %down1.1) | copy-start | bytes 3538948
  199.8 42.3 %collective-permute-start.10 = (bf16[3,256,768]{2,1,0:T(8,128)(2,1)}, bf16[3,256,768]{2,1,0:T(8,128)(2,1)S(1)}, u32[]{:S(2)}, u32[]{:S(2)}) collective-permute-start(bf16[3,256,768]{2,1,0:T(8,128)(2,1)} %up1.1), channel_id=1, source_target_pairs={{0,32},{32,64},{64,96},{96,0},{1,33},{33,65},{65,97},{97,1},{2,34}... | collective-permute-start | bytes 3538952 | tf_op jit(solution)/shard_map/ppermute | solution.py:391
  201.1 41.0 %collective-permute-start.11 = (bf16[3,256,768]{2,1,0:T(8,128)(2,1)S(1)}, bf16[3,256,768]{2,1,0:T(8,128)(2,1)S(1)}, u32[]{:S(2)}, u32[]{:S(2)}) collective-permute-start(bf16[3,256,768]{2,1,0:T(8,128)(2,1)S(1)} %copy-done.6), channel_id=1, source_target_pairs={{0,96},{32,0},{64,32},{96,64},{1,97},{33,1},{65,33},{97,65},{2,98}... | collective-permute-start | bytes 3538952 | tf_op jit(solution)/shard_map/ppermute | solution.py:394
  242.1 1.0 copy-start
  242.1 1.4 copy-start.1

commit v8 on v7

--- a/solution.py
+++ b/solution.py
@@ -43,11 +43,10 @@
     return jnp.where(jnp.logical_and(hit, count < capacity), count, -1.0)
 
 
-def slot_rows(values, chunk, local_exp, capacity, first=0, n_rows=None):
+def slot_rows(values, chunk, local_exp, capacity):
     n_experts, tok = values.shape
-    n_rows = n_rows or n_experts // local_exp * capacity
-    row = lax.broadcasted_iota(jnp.int32, (n_rows, n_experts), 0) + first
-    expert_of = row // capacity * local_exp + chunk
+    n_rows = n_experts // local_exp * capacity
+    expert_of = lax.broadcasted_iota(jnp.int32, (n_rows, n_experts), 0) // capacity * local_exp + chunk
     spread = jnp.where(expert_of == lax.broadcasted_iota(jnp.int32, (n_rows, n_experts), 1), 1.0, 0.0)
     spread = spread.astype(BF16)
     at = dot(spread, values.astype(BF16), NN)
@@ -55,26 +54,18 @@
     return at == place, spread
 
 
-def dispatch_kernel(
-    chunk, local_exp, capacity, ids_ref, probs_ref, tok_ref, grad_ref, out_ref, values_ref, prob_ref
-):
-    n_experts, tok = values_ref.shape
-    n_rows = out_ref.shape[0]
+def dispatch_kernel(chunk, local_exp, capacity, ids_ref, probs_ref, tok_ref, grad_ref, out_ref):
+    ids_t = ids_ref[...]
+    topk, tok = ids_t.shape
+    n_experts = out_ref.shape[0] // capacity * local_exp
     width = tok_ref.shape[1]
-    step = pl.program_id(0)
-
-    @pl.when(step == 0)
-    def _():
-        ids_t = ids_ref[...]
-        rows = lax.broadcasted_iota(jnp.int32, (n_experts, tok), 0)
-        prob = jnp.zeros((n_experts, tok), F32)
-        for k in range(ids_t.shape[0]):
-            prob = prob + jnp.where(ids_t[k : k + 1, :] == rows, probs_ref[k : k + 1, :].astype(F32), 0.0)
-        values_ref[...] = slot_values(ids_t, n_experts, capacity)
-        prob_ref[...] = prob
-
-    onehot, spread = slot_rows(values_ref[...], chunk, local_exp, capacity, step * n_rows, n_rows)
-    prob_rows = dot(spread, prob_ref[...].astype(BF16), NN)
+    values = slot_values(ids_t, n_experts, capacity)
+    rows = lax.broadcasted_iota(jnp.int32, (n_experts, tok), 0)
+    prob = jnp.zeros((n_experts, tok), F32)
+    for k in range(topk):
+        prob = prob + jnp.where(ids_t[k : k + 1, :] == rows, probs_ref[k : k + 1, :].astype(F32), 0.0)
+    onehot, spread = slot_rows(values, chunk, local_exp, capacity)
+    prob_rows = dot(spread, prob.astype(BF16), NN)
     pick = jnp.where(onehot, 1.0, 0.0).astype(BF16)
     weighted = jnp.where(onehot, prob_rows, 0.0).astype(BF16)
     out_ref[:, :width] = dot(pick, tok_ref[...], NN).astype(BF16)
@@ -84,14 +75,9 @@
 def dispatch(chunk, local_exp, capacity, n_experts, ids_t, probs_t, tokens, out_grad):
     tok, width = tokens.shape
     n_rows = n_experts // local_exp * capacity
-    steps = 4
     return pl.pallas_call(
         functools.partial(dispatch_kernel, chunk, local_exp, capacity),
-        grid=(steps,),
-        in_specs=[whole(a.shape) for a in (ids_t, probs_t, tokens, out_grad)],
-        out_specs=pl.BlockSpec((n_rows // steps, 2 * width), lambda i: (i, 0)),
         out_shape=jax.ShapeDtypeStruct((n_rows, 2 * width), BF16),
-        scratch_shapes=[pltpu.VMEM((n_experts, tok), F32), pltpu.VMEM((n_experts, tok), F32)],
         compiler_params=pltpu.CompilerParams(vmem_limit_bytes=VMEM_LIMIT),
         cost_estimate=cost(4 * n_rows * tok * width, 4 * width * (tok + n_rows), 0),
         name=f"dispatch{chunk}",
@@ -99,40 +85,26 @@
 
 
 def hidden_kernel(
-    where_ref, x_ref, rows_ref, wg_ref, wu_ref, wd_ref,
-    hid_ref, da_ref, db_ref, s_ref, a_ref, b_ref, sum_ref, do_ref, sem,
+    where_ref, x_ref, do_ref, xa_ref, xb_ref, da_col_ref, db_col_ref, wg_ref, wu_ref, wd_ref,
+    hid_ref, da_ref, db_ref, s_ref, a_ref, b_ref, sum_ref,
 ):
     step = pl.program_id(0)
-    width = x_ref.shape[1]
-    fetch = pltpu.make_async_copy(rows_ref.at[:, pl.ds(width, width)], do_ref, sem)
-
-    @pl.when(step == 0)
-    def _():
-        fetch.start()
-
     gate = dot(x_ref[...], wg_ref[0], NN)
     upper = dot(x_ref[...], wu_ref[0], NN)
     sig = jax.nn.sigmoid(gate)
     act = gate * sig
     hid = (act * upper).astype(BF16)
     hid_ref[...] = hid
-
-    @pl.when(step == 0)
-    def _():
-        fetch.wait()
-
     dhid = dot(do_ref[...], wd_ref[0], NN)
     part = jnp.sum(hid.astype(F32) * dhid, axis=1, keepdims=True)
     dgate = (dhid * upper * sig * (1.0 + gate * (1.0 - sig))).astype(BF16)
     dup = (dhid * act).astype(BF16)
     da_ref[...] = dgate
     db_ref[...] = dup
-    half = a_ref.shape[1]
-    for i, out_ref in enumerate((a_ref, b_ref)):
-        columns = pl.ds(pl.multiple_of(where_ref[i] * half, half), half)
-        out_ref[0] = dot(x_ref[:, columns], dgate, TN).astype(BF16)
-        out_ref[1] = dot(x_ref[:, columns], dup, TN).astype(BF16)
-        out_ref[2] = dot(do_ref[:, columns], hid, TN).astype(BF16)
+    for out_ref, x_col, do_col in ((a_ref, xa_ref, da_col_ref), (b_ref, xb_ref, db_col_ref)):
+        out_ref[0] = dot(x_col[...], dgate, TN).astype(BF16)
+        out_ref[1] = dot(x_col[...], dup, TN).astype(BF16)
+        out_ref[2] = dot(do_col[...], hid, TN).astype(BF16)
 
     @pl.when(step == 0)
     def _():
@@ -158,6 +130,7 @@
     n_rows, width = rows.shape[0], rows.shape[1] // 2
     hidden = wg.shape[2]
     block = 2 * LANES
+    lefts = width // half
     once = pl.Buffered(1)
     weight = pl.BlockSpec((1, width, block), lambda i, at: (chunk, 0, i))
     result = pl.BlockSpec((n_rows, block), lambda i, at: (0, i))
@@ -169,17 +142,17 @@
             grid=(hidden // block,),
             in_specs=[
                 pl.BlockSpec((n_rows, width), lambda i, at: (0, 0), pipeline_mode=once),
-                pl.BlockSpec(memory_space=pl.ANY),
+                pl.BlockSpec((n_rows, width), lambda i, at: (0, 1), pipeline_mode=once),
+                pl.BlockSpec((n_rows, half), lambda i, at: (0, at[0]), pipeline_mode=once),
+                pl.BlockSpec((n_rows, half), lambda i, at: (0, at[1]), pipeline_mode=once),
+                pl.BlockSpec((n_rows, half), lambda i, at: (0, at[0] + lefts), pipeline_mode=once),
+                pl.BlockSpec((n_rows, half), lambda i, at: (0, at[1] + lefts), pipeline_mode=once),
                 weight,
                 weight,
                 weight,
             ],
             out_specs=[result] * 3 + [whole((n_rows, LANES)), shard, shard],
-            scratch_shapes=[
-                pltpu.VMEM((n_rows, LANES), F32),
-                pltpu.VMEM((n_rows, width), BF16),
-                pltpu.SemaphoreType.DMA,
-            ],
+            scratch_shapes=[pltpu.VMEM((n_rows, LANES), F32)],
         ),
         out_shape=[jax.ShapeDtypeStruct((n_rows, hidden), BF16)] * 3
         + [jax.ShapeDtypeStruct((n_rows, LANES), BF16)]
@@ -187,7 +160,7 @@
         compiler_params=pltpu.CompilerParams(vmem_limit_bytes=VMEM_LIMIT),
         cost_estimate=cost(8 * n_rows * width * hidden, 6 * width * hidden + n_rows * (4 * width + 6 * hidden), chunk),
         name=f"hidden{chunk}",
-    )(where, rows, rows, wg, wu, wd)
+    )(where, *[rows] * 6, wg, wu, wd)
 
 
 def weight_kernel(n_add, n_after, where_ref, x_ref, do_ref, hid_ref, da_ref, db_ref, *refs):

time: 250 us -> 248 us (level)
  Pallas kernels: 122 us -> 119 us
where the time goes in v8:
time: 248 us; the launch traced here: 247 us
  Pallas kernels  119 us (48%)
  waiting for transfers between devices  83.9 us (34%)
  starting transfers between devices  37.7 us (15%)
  local copies, waits for them, and re-layouts  3.6 us (1%)
    all_to_all x3, waiting for transfers between devices, swap(): return lax.all_to_all(a, 'expert', split_axis=0, concat_axis=0, tiled=True)  66.6 us
    pallas_call x10, Pallas kernels, weight_grads(): pl.pallas_call(functools.partial(weight_kernel, len(adds), len(after)), g...  45.8 us
    pallas_call x2, Pallas kernels, hidden_grads(): pl.pallas_call(hidden_kernel, grid_spec=pltpu.PrefetchScalarGridSpec(num_...  30.5 us
    all_to_all x3, starting transfers between devices, swap(): return lax.all_to_all(a, 'expert', split_axis=0, concat_axis=0, tiled=True)  18.3 us
    ppermute x6, waiting for transfers between devices, up(): lax.ppermute(a, 'dp', [(i, (i + 1) % n_group) for i in range(n_group)])  16.9 us
    ppermute x6, starting transfers between devices, down(): lax.ppermute(a, 'dp', [(i, (i - 1) % n_group) for i in range(n_group)])  16.2 us
    pallas_call x2, Pallas kernels, input_grads(): pl.pallas_call(dx_kernel, grid=(5,), in_specs=[whole((n_rows, hidden)), w...  15.1 us
    pallas_call x2, Pallas kernels, update(): pl.pallas_call(functools.partial(update_kernel, chunk), grid_spec=pltpu.P...  11.1 us
  transfers between devices with their start and end apart: 15, of which 9 were waited for; matrix products, arithmetic and copies ran while one was open for 1% of the time, Pallas kernels for 38%

profile of v8, /device:TPU:0, one launch (start us, length us, event | category | flops | bytes accessed | tf_op | source)
XLA Modules:
  0.0 246.5 jit_solution(8421459063192711687)
XLA Ops:
  0.6 4.8 %dispatch0.1 = bf16[512,4096]{1,0:T(8,128)(2,1)} custom-call(s32[8,128]{1,0:T(8,128)} %bitcast.18, bf16[8,128]{1,0:T(8,128)(2,1)} %bitcast.21, bf16[128,2048]{1,0:T(8,128)(2,1)} %tok_ref.3, bf16[128,2048]{1,0:T(8,128)(2,1)} %grad_ref.3), custom_call_target="tpu_custom_call" | custom-call | flops 3758096384 | bytes 36700160 | tf_op jit(solution)/shard_map/dispatch0/pallas_call | solution.py:78
  5.4 8.5 %all-to-all-start = ((bf16[32,16,4096]{2,1,0:T(8,128)(2,1)}), bf16[32,16,4096]{2,1,0:T(8,128)(2,1)}, u32[]{:S(2)}, u32[]{:S(2)}) async-start(bf16[32,16,4096]{2,1,0:T(8,128)(2,1)} %bitcast.17), calls=%async_computation | async-start | bytes 8388608 | tf_op jit(solution)/shard_map/all_to_all | solution.py:373
  14.0 0.7 pad_add_fusion.where_ref
  14.6 4.7 %dispatch1.1 = bf16[512,4096]{1,0:T(8,128)(2,1)} custom-call(s32[8,128]{1,0:T(8,128)} %bitcast.19, bf16[8,128]{1,0:T(8,128)(2,1)} %bitcast.22, bf16[128,2048]{1,0:T(8,128)(2,1)} %tok_ref.3, bf16[128,2048]{1,0:T(8,128)(2,1)} %grad_ref.3), custom_call_target="tpu_custom_call" | custom-call | flops 3758096384 | bytes 36700160 | tf_op jit(solution)/shard_map/dispatch1/pallas_call | solution.py:78
  19.3 48.1 %all-to-all-done = bf16[32,16,4096]{2,1,0:T(8,128)(2,1)} async-done(((bf16[32,16,4096]{2,1,0:T(8,128)(2,1)}), bf16[32,16,4096]{2,1,0:T(8,128)(2,1)}, u32[]{:S(2)}, u32[]{:S(2)}) %all-to-all-start) | async-done | bytes 4194336 | tf_op jit(solution)/shard_map/all_to_all | solution.py:373
  67.4 15.3 %hidden0.1 = (bf16[512,768]{1,0:T(8,128)(2,1)}, bf16[512,768]{1,0:T(8,128)(2,1)}, bf16[512,768]{1,0:T(8,128)(2,1)}, bf16[512,128]{1,0:T(8,128)(2,1)}, bf16[3,256...) custom-call(s32[2]{0:T(128)} %pad_add_fusion.where_ref, ...), custom_call_target="tpu_custom_call" | custom-call | flops 45097156608 | bytes 111935488 | tf_op jit(solution)/shard_map/hidden0/pallas_call | solution.py:138
  82.7 1.5 collective-permute-start
  84.2 1.8 collective-permute-start.1
  86.0 1.3 mark0.1.refs_0_
  87.3 4.9 %all-to-all-start.1 = ((bf16[32,16,4096]{2,1,0:T(8,128)(2,1)}), bf16[32,16,4096]{2,1,0:T(8,128)(2,1)}, u32[]{:S(2)}, u32[]{:S(2)}) async-start(bf16[32,16,4096]{2,1,0:T(8,128)(2,1)} %bitcast.16), calls=%async_computation.1 | async-start | bytes 8388608 | tf_op jit(solution)/shard_map/all_to_all | solution.py:373
  92.2 0.7 pad_add_fusion.1.where_ref
  92.9 6.8 %near0.1 = (bf16[3,256,768]{2,1,0:T(8,128)(2,1)}, bf16[3,256,768]{2,1,0:T(8,128)(2,1)}) custom-call(s32[2]{0:T(128)} %pad_add_fusion.1.where_ref, bf16[512,4096]{1,0:T(8,128)(2,1)} %bitcast.5.x_ref.do_ref.xa_ref.xb_ref.da_col_ref.db_col_ref, bf16[512,4096]{1,0:T(8,128)(2,1)} %bitcast.5.x_ref.do_ref.xa_ref.xb_ref.da_col_ref.db_col_ref, ...), custom_call_target="tpu_custom_call" | custom-call | flops 8455716864 | bytes 33030144 | tf_op jit(solution)/shard_map/near0/pallas_call | solution.py:184
  99.7 0.3 collective-permute-start.2
  99.9 3.0 %collective-permute-start.3 = (bf16[3,256,768]{2,1,0:T(8,128)(2,1)}, bf16[3,256,768]{2,1,0:T(8,128)(2,1)S(1)}, u32[]{:S(2)}, u32[]{:S(2)}) collective-permute-start(bf16[3,256,768]{2,1,0:T(8,128)(2,1)} %get-tuple-element.66), channel_id=1, source_target_pairs={{0,96},{32,0},{64,32},{96,64},{1,97},{33,1},{65,33},{97,65},{2,98}... | collective-permute-start | bytes 3538952 | tf_op jit(solution)/shard_map/ppermute | solution.py:367
  102.9 10.2 %collective-permute-done.refs_0_ = bf16[3,256,768]{2,1,0:T(8,128)(2,1)S(1)} collective-permute-done((bf16[3,256,768]{2,1,0:T(8,128)(2,1)}, bf16[3,256,768]{2,1,0:T(8,128)(2,1)S(1)}, u32[]{:S(2)}, u32[]{:S(2)}) %collective-permute-start) | collective-permute-done | bytes 1179680 | tf_op jit(solution)/shard_map/ppermute | solution.py:364
  113.1 0.0 copy-start.3
  113.1 0.2 collective-permute-done.1.refs_0_
  113.3 1.1 copy-done.5
  114.5 4.0 %down0.1 = bf16[3,256,768]{2,1,0:T(8,128)(2,1)} custom-call(s32[1]{0:T(128)} %bitcast.11.where_ref, bf16[512,4096]{1,0:T(8,128)(2,1)} %bitcast.5.x_ref.do_ref.xa_ref.xb_ref.da_col_ref.db_col_ref, bf16[512,4096]{1,0:T(8,128)(2,1)} %bitcast.5.x_ref.do_ref.xa_ref.xb_ref.da_col_ref.db_col_ref, bf16[512,768]{1,0:T(8,128)(2,1)} %get-tuple-element.58.hid_ref, ...), custom_call_target="tpu_custom_call" | custom-call | flops 4227858432 | bytes 24772608 | tf_op jit(solution)/shard_map/down0/pallas_call | solution.py:184
  118.5 0.0 copy-done.3
  118.5 2.8 %collective-permute-start.5 = (bf16[3,256,768]{2,1,0:T(8,128)(2,1)}, bf16[3,256,768]{2,1,0:T(8,128)(2,1)}, u32[]{:S(2)}, u32[]{:S(2)}) collective-permute-start(bf16[3,256,768]{2,1,0:T(8,128)(2,1)} %down0.1), channel_id=1, source_target_pairs={{0,96},{32,0},{64,32},{96,64},{1,97},{33,1},{65,33},{97,65},{2,98}... | collective-permute-start | bytes 3538952 | tf_op jit(solution)/shard_map/ppermute | solution.py:367
  121.4 4.0 %up0.1 = bf16[3,256,768]{2,1,0:T(8,128)(2,1)} custom-call(s32[1]{0:T(128)} %bitcast.8.where_ref, bf16[512,4096]{1,0:T(8,128)(2,1)} %bitcast.5.x_ref.do_ref.xa_ref.xb_ref.da_col_ref.db_col_ref, bf16[512,4096]{1,0:T(8,128)(2,1)} %bitcast.5.x_ref.do_ref.xa_ref.xb_ref.da_col_ref.db_col_ref, bf16[512,768]{1,0:T(8,128)(2,1)} %get-tuple-element.58.hid_ref, ...), custom_call_target="tpu_custom_call" | custom-call | flops 4227858432 | bytes 24772608 | tf_op jit(solution)/shard_map/up0/pallas_call | solution.py:184
  125.4 0.0 collective-permute-start.4
  125.4 7.6 %dx0.1.refs_0_ = bf16[32,32,2176]{2,1,0:T(8,128)(2,1)} custom-call(bf16[512,768]{1,0:T(8,128)(2,1)} %get-tuple-element.64.da_ref, bf16[512,768]{1,0:T(8,128)(2,1)} %get-tuple-element.59.db_ref, bf16[512,128]{1,0:T(8,128)(2,1)} %get-tuple-element.65.s_ref, bf16[2,2048,768]{2,1,0:T(8,128)(2,1)} %refs_4_.3, bf16[2,2048,768]{2,1,0:T(8,128)(2,1)} %refs_5_.3), custom_call_target="tpu_custom_call" | custom-call | flops 22548578304 | bytes 69730304 | tf_op jit(solution)/shard_map/dx0/pallas_call | solution.py:287
  133.0 5.5 %collective-permute-done.2.refs_0_ = bf16[3,256,768]{2,1,0:T(8,128)(2,1)} collective-permute-done((bf16[3,256,768]{2,1,0:T(8,128)(2,1)}, bf16[3,256,768]{2,1,0:T(8,128)(2,1)}, u32[]{:S(2)}, u32[]{:S(2)}) %collective-permute-start.2) | collective-permute-done | bytes 1179680 | tf_op jit(solution)/shard_map/ppermute | solution.py:364
  138.5 0.1 collective-permute-done.3.refs_0_
  138.6 7.0 %all-to-all-done.1 = bf16[32,16,4096]{2,1,0:T(8,128)(2,1)} async-done(((bf16[32,16,4096]{2,1,0:T(8,128)(2,1)}), bf16[32,16,4096]{2,1,0:T(8,128)(2,1)}, u32[]{:S(2)}, u32[]{:S(2)}) %all-to-all-start.1) | async-done | bytes 4194336 | tf_op jit(solution)/shard_map/all_to_all | solution.py:373
  145.7 15.2 %hidden1.1 = (bf16[512,768]{1,0:T(8,128)(2,1)}, bf16[512,768]{1,0:T(8,128)(2,1)}, bf16[512,768]{1,0:T(8,128)(2,1)}, bf16[512,128]{1,0:T(8,128)(2,1)}, bf16[3,256...) custom-call(s32[2]{0:T(128)} %pad_add_fusion.where_ref, ...), custom_call_target="tpu_custom_call" | custom-call | flops 154618822656 | bytes 383778816 | tf_op jit(solution)/shard_map/hidden1/pallas_call | solution.py:138
  160.9 0.0 copy-done.4
  160.9 0.3 collective-permute-start.8
  161.2 1.4 mark1.1.refs_0_
  162.6 0.0 copy-done.2
  162.6 3.0 %collective-permute-start.9 = (bf16[3,256,768]{2,1,0:T(8,128)(2,1)S(1)}, bf16[3,256,768]{2,1,0:T(8,128)(2,1)S(1)}, u32[]{:S(2)}, u32[]{:S(2)}) collective-permute-start(bf16[3,256,768]{2,1,0:T(8,128)(2,1)S(1)} %copy-done.2), channel_id=1, source_target_pairs={{0,96},{32,0},{64,32},{96,64},{1,97},{33,1},{65,33},{97,65},{2,98}... | collective-permute-start | bytes 3538952 | tf_op jit(solution)/shard_map/ppermute | solution.py:367
  165.6 7.5 %dx1.1 = bf16[32,32,2176]{2,1,0:T(8,128)(2,1)} custom-call(bf16[512,768]{1,0:T(8,128)(2,1)} %get-tuple-element.68.da_ref, bf16[512,768]{1,0:T(8,128)(2,1)} %get-tuple-element.69.db_ref, bf16[512,128]{1,0:T(8,128)(2,1)} %get-tuple-element.70.s_ref, bf16[2,2048,768]{2,1,0:T(8,128)(2,1)} %refs_4_.3, ...), custom_call_target="tpu_custom_call", output_to_operand_aliasing={{}: (5, {})} | custom-call | flops 77309411328 | bytes 239075328 | tf_op jit(solution)/shard_map/dx1/pallas_call | solution.py:287
  173.1 4.9 %all-to-all-start.2 = ((bf16[32,32,2176]{2,1,0:T(8,128)(2,1)}), bf16[32,32,2176]{2,1,0:T(8,128)(2,1)}, u32[]{:S(2)}, u32[]{:S(2)}) async-start(bf16[32,32,2176]{2,1,0:T(8,128)(2,1)} %dx1.1), calls=%async_computation.2 | async-start | bytes 8912896 | tf_op jit(solution)/shard_map/all_to_all | solution.py:373
  178.0 0.0 collective-permute-done.5.refs_3_
  178.0 0.0 collective-permute-done.4.refs_1_
  178.0 6.8 %near1.1 = (bf16[3,256,768]{2,1,0:T(8,128)(2,1)}, bf16[3,256,768]{2,1,0:T(8,128)(2,1)}) custom-call(s32[2]{0:T(128)} %pad_add_fusion.1.where_ref, bf16[512,4096]{1,0:T(8,128)(2,1)} %bitcast.7.x_ref.do_ref.xa_ref.xb_ref.da_col_ref.db_col_ref, bf16[512,4096]{1,0:T(8,128)(2,1)} %bitcast.7.x_ref.do_ref.xa_ref.xb_ref.da_col_ref.db_col_ref, ...), custom_call_target="tpu_custom_call" | custom-call | flops 28991029248 | bytes 113246208 | tf_op jit(solution)/shard_map/near1/pallas_call | solution.py:184
  184.8 0.0 collective-permute-start.7
  184.8 3.2 %collective-permute-start.6 = (bf16[3,256,768]{2,1,0:T(8,128)(2,1)}, bf16[3,256,768]{2,1,0:T(8,128)(2,1)}, u32[]{:S(2)}, u32[]{:S(2)}) collective-permute-start(bf16[3,256,768]{2,1,0:T(8,128)(2,1)} %get-tuple-element.78), channel_id=1, source_target_pairs={{0,96},{32,0},{64,32},{96,64},{1,97},{33,1},{65,33},{97,65},{2,98}... | collective-permute-start | bytes 3538952 | tf_op jit(solution)/shard_map/ppermute | solution.py:367
  188.1 0.0 collective-permute-done.8.refs_0_
  188.1 0.0 collective-permute-done.9.refs_0_
  188.1 0.0 copy-start.8
  188.1 1.0 copy-done.8
  189.1 4.0 %down1.1 = bf16[3,256,768]{2,1,0:T(8,128)(2,1)} custom-call(s32[1]{0:T(128)} %bitcast.11.where_ref, bf16[512,4096]{1,0:T(8,128)(2,1)} %bitcast.7.x_ref.do_ref.xa_ref.xb_ref.da_col_ref.db_col_ref, bf16[512,4096]{1,0:T(8,128)(2,1)} %bitcast.7.x_ref.do_ref.xa_ref.xb_ref.da_col_ref.db_col_ref, bf16[512,768]{1,0:T(8,128)(2,1)} %get-tuple-element.76.hid_ref, ...), custom_call_target="tpu_custom_call" | custom-call | flops 14495514624 | bytes 84934656 | tf_op jit(solution)/shard_map/down1/pallas_call | solution.py:184
  193.1 0.0 copy-done.7
  193.1 4.1 %up1.1 = bf16[3,256,768]{2,1,0:T(8,128)(2,1)} custom-call(s32[1]{0:T(128)} %bitcast.8.where_ref, bf16[512,4096]{1,0:T(8,128)(2,1)} %bitcast.7.x_ref.do_ref.xa_ref.xb_ref.da_col_ref.db_col_ref, bf16[512,4096]{1,0:T(8,128)(2,1)} %bitcast.7.x_ref.do_ref.xa_ref.xb_ref.da_col_ref.db_col_ref, bf16[512,768]{1,0:T(8,128)(2,1)} %get-tuple-element.76.hid_ref, ...), custom_call_target="tpu_custom_call" | custom-call | flops 14495514624 | bytes 84934656 | tf_op jit(solution)/shard_map/up1/pallas_call | solution.py:184
  197.2 1.2 collective-permute-start.10
  198.4 0.0 copy-done.6
  198.4 2.4 collective-permute-start.11
  200.8 4.0 %own01.1.refs_2_ = bf16[3,256,768]{2,1,0:T(8,128)(2,1)} custom-call(s32[1]{0:T(128)} %bitcast.13.where_ref, bf16[512,4096]{1,0:T(8,128)(2,1)} %bitcast.5.x_ref.do_ref.xa_ref.xb_ref.da_col_ref.db_col_ref, bf16[512,4096]{1,0:T(8,128)(2,1)} %bitcast.5.x_ref.do_ref.xa_ref.xb_ref.da_col_ref.db_col_ref, bf16[512,768]{1,0:T(8,128)(2,1)} %get-tuple-element.58.hid_ref, ...), custom_call_target="tpu_custom_call" | custom-call | flops 4227858432 | bytes 24772608 | tf_op jit(solution)/shard_map/own01/pallas_call | solution.py:184
  204.8 4.0 %own00.1.refs_0_ = bf16[3,256,768]{2,1,0:T(8,128)(2,1)} custom-call(s32[1]{0:T(128)} %bitcast.12.where_ref, bf16[512,4096]{1,0:T(8,128)(2,1)} %bitcast.5.x_ref.do_ref.xa_ref.xb_ref.da_col_ref.db_col_ref, bf16[512,4096]{1,0:T(8,128)(2,1)} %bitcast.5.x_ref.do_ref.xa_ref.xb_ref.da_col_ref.db_col_ref, bf16[512,768]{1,0:T(8,128)(2,1)} %get-tuple-element.58.hid_ref, ...), custom_call_target="tpu_custom_call" | custom-call | flops 4227858432 | bytes 24772608 | tf_op jit(solution)/shard_map/own00/pallas_call | solution.py:184
  208.9 5.6 %update0.1 = (bf16[2,512,768]{2,1,0:T(8,128)(2,1)}, bf16[2,512,768]{2,1,0:T(8,128)(2,1)}, bf16[2,512,768]{2,1,0:T(8,128)(2,1)}) custom-call(s32[1]{0:T(128)} %bitcast.15.where_ref, s32[2,3]{1,0:T(2,128)} %mask_ref.3, bf16[3,256,768]{2,1,0:T(8,128)(2,1)} %own00.1.refs_0_, bf16[3,256,768]{2,1,0:T(8,128)(2,1)} %collective-permute-done.4.refs_1_, ...), custom_call_target="tpu_custom_call" | custom-call | flops 47185920 | bytes 283115520 | tf_op jit(solution)/shard_map/update0/pallas_call | solution.py:245
  214.4 0.7 collective-permute-done.7.refs_0_
  215.2 4.0 %own11.1.refs_2_ = bf16[3,256,768]{2,1,0:T(8,128)(2,1)} custom-call(s32[1]{0:T(128)} %bitcast.13.where_ref, bf16[512,4096]{1,0:T(8,128)(2,1)} %bitcast.7.x_ref.do_ref.xa_ref.xb_ref.da_col_ref.db_col_ref, bf16[512,4096]{1,0:T(8,128)(2,1)} %bitcast.7.x_ref.do_ref.xa_ref.xb_ref.da_col_ref.db_col_ref, bf16[512,768]{1,0:T(8,128)(2,1)} %get-tuple-element.76.hid_ref, ...), custom_call_target="tpu_custom_call" | custom-call | flops 14495514624 | bytes 84934656 | tf_op jit(solution)/shard_map/own11/pallas_call | solution.py:184
  219.2 0.0 collective-permute-done.6.refs_0_
  219.2 4.0 %own10.1.refs_0_ = bf16[3,256,768]{2,1,0:T(8,128)(2,1)} custom-call(s32[1]{0:T(128)} %bitcast.12.where_ref, bf16[512,4096]{1,0:T(8,128)(2,1)} %bitcast.7.x_ref.do_ref.xa_ref.xb_ref.da_col_ref.db_col_ref, bf16[512,4096]{1,0:T(8,128)(2,1)} %bitcast.7.x_ref.do_ref.xa_ref.xb_ref.da_col_ref.db_col_ref, bf16[512,768]{1,0:T(8,128)(2,1)} %get-tuple-element.76.hid_ref, ...), custom_call_target="tpu_custom_call" | custom-call | flops 14495514624 | bytes 84934656 | tf_op jit(solution)/shard_map/own10/pallas_call | solution.py:184
  223.2 11.5 %all-to-all-done.2.back_ref = bf16[32,32,2176]{2,1,0:T(8,128)(2,1)} async-done(((bf16[32,32,2176]{2,1,0:T(8,128)(2,1)}), bf16[32,32,2176]{2,1,0:T(8,128)(2,1)}, u32[]{:S(2)}, u32[]{:S(2)}) %all-to-all-start.2) | async-done | bytes 4456480 | tf_op jit(solution)/shard_map/all_to_all | solution.py:373
  234.7 4.4 %combine.1 = (bf16[128,2048]{1,0:T(8,128)(2,1)}, bf16[8,128]{1,0:T(8,128)(2,1)}) custom-call(s32[8,128]{1,0:T(8,128)} %bitcast.20, bf16[8,128]{1,0:T(8,128)(2,1)} %bitcast.23, bf16[32,32,2176]{2,1,0:T(8,128)(2,1)} %all-to-all-done.2.back_ref), custom_call_target="tpu_custom_call" | custom-call | flops 12884901888 | bytes 106954752 | tf_op jit(solution)/shard_map/combine/pallas_call | solution.py:331
  239.1 0.4 collective-permute-done.10.refs_1_
  239.5 0.0 collective-permute-done.11.refs_3_
  239.5 1.0 copy-done
  240.5 0.4 copy-done.1
  240.9 5.5 %update1.1 = (bf16[2,512,768]{2,1,0:T(8,128)(2,1)}, bf16[2,512,768]{2,1,0:T(8,128)(2,1)}, bf16[2,512,768]{2,1,0:T(8,128)(2,1)}) custom-call(s32[1]{0:T(128)} %bitcast.15.where_ref, s32[2,3]{1,0:T(2,128)} %mask_ref.3, bf16[3,256,768]{2,1,0:T(8,128)(2,1)} %own10.1.refs_0_, ...), custom_call_target="tpu_custom_call", output_to_operand_aliasing={{0}: (9, {}), {1}: (10, {}), {2}: (11, {})} | custom-call | flops 47185920 | bytes 283115520 | tf_op jit(solution)/shard_map/update1/pallas_call | solution.py:245
  (7 shorter events, 0.0 us)
Async XLA Ops:
  5.4 62.0 %all-to-all-start = ((bf16[32,16,4096]{2,1,0:T(8,128)(2,1)}), bf16[32,16,4096]{2,1,0:T(8,128)(2,1)}, u32[]{:S(2)}, u32[]{:S(2)}) async-start(bf16[32,16,4096]{2,1,0:T(8,128)(2,1)} %bitcast.17), calls=%async_computation | async-start | bytes 8388608 | tf_op jit(solution)/shard_map/all_to_all | solution.py:373
  82.7 30.4 %collective-permute-start = (bf16[3,256,768]{2,1,0:T(8,128)(2,1)}, bf16[3,256,768]{2,1,0:T(8,128)(2,1)S(1)}, u32[]{:S(2)}, u32[]{:S(2)}) collective-permute-start(bf16[3,256,768]{2,1,0:T(8,128)(2,1)} %get-tuple-element.54.a_ref), channel_id=1, source_target_pairs={{0,32},{32,64},{64,96},{96,0},{1,33},{33,65},{65,97},{97,1},{2,34}... | collective-permute-start | bytes 3538952 | tf_op jit(solution)/shard_map/ppermute | solution.py:364
  84.2 29.1 %collective-permute-start.1 = (bf16[3,256,768]{2,1,0:T(8,128)(2,1)}, bf16[3,256,768]{2,1,0:T(8,128)(2,1)S(1)}, u32[]{:S(2)}, u32[]{:S(2)}) collective-permute-start(bf16[3,256,768]{2,1,0:T(8,128)(2,1)} %get-tuple-element.55.b_ref), channel_id=1, source_target_pairs={{0,96},{32,0},{64,32},{96,64},{1,97},{33,1},{65,33},{97,65},{2,98}... | collective-permute-start | bytes 3538952 | tf_op jit(solution)/shard_map/ppermute | solution.py:367
  87.3 58.3 %all-to-all-start.1 = ((bf16[32,16,4096]{2,1,0:T(8,128)(2,1)}), bf16[32,16,4096]{2,1,0:T(8,128)(2,1)}, u32[]{:S(2)}, u32[]{:S(2)}) async-start(bf16[32,16,4096]{2,1,0:T(8,128)(2,1)} %bitcast.16), calls=%async_computation.1 | async-start | bytes 8388608 | tf_op jit(solution)/shard_map/all_to_all | solution.py:373
  99.7 38.8 %collective-permute-start.2 = (bf16[3,256,768]{2,1,0:T(8,128)(2,1)}, bf16[3,256,768]{2,1,0:T(8,128)(2,1)}, u32[]{:S(2)}, u32[]{:S(2)}) collective-permute-start(bf16[3,256,768]{2,1,0:T(8,128)(2,1)} %get-tuple-element.61), channel_id=1, source_target_pairs={{0,32},{32,64},{64,96},{96,0},{1,33},{33,65},{65,97},{97,1},{2,34}... | collective-permute-start | bytes 3538952 | tf_op jit(solution)/shard_map/ppermute | solution.py:364
  99.9 38.7 %collective-permute-start.3 = (bf16[3,256,768]{2,1,0:T(8,128)(2,1)}, bf16[3,256,768]{2,1,0:T(8,128)(2,1)S(1)}, u32[]{:S(2)}, u32[]{:S(2)}) collective-permute-start(bf16[3,256,768]{2,1,0:T(8,128)(2,1)} %get-tuple-element.66), channel_id=1, source_target_pairs={{0,96},{32,0},{64,32},{96,64},{1,97},{33,1},{65,33},{97,65},{2,98}... | collective-permute-start | bytes 3538952 | tf_op jit(solution)/shard_map/ppermute | solution.py:367
  113.1 5.4 %copy-start.3 = (bf16[3,256,768]{2,1,0:T(8,128)(2,1)}, bf16[3,256,768]{2,1,0:T(8,128)(2,1)S(1)}, u32[]{:S(2)}) copy-start(bf16[3,256,768]{2,1,0:T(8,128)(2,1)S(1)} %collective-permute-done.refs_0_) | copy-start | bytes 3538948
  113.3 1.1 copy-start.5
  118.5 59.5 %collective-permute-start.5 = (bf16[3,256,768]{2,1,0:T(8,128)(2,1)}, bf16[3,256,768]{2,1,0:T(8,128)(2,1)}, u32[]{:S(2)}, u32[]{:S(2)}) collective-permute-start(bf16[3,256,768]{2,1,0:T(8,128)(2,1)} %down0.1), channel_id=1, source_target_pairs={{0,96},{32,0},{64,32},{96,64},{1,97},{33,1},{65,33},{97,65},{2,98}... | collective-permute-start | bytes 3538952 | tf_op jit(solution)/shard_map/ppermute | solution.py:367
  125.4 52.6 %collective-permute-start.4 = (bf16[3,256,768]{2,1,0:T(8,128)(2,1)}, bf16[3,256,768]{2,1,0:T(8,128)(2,1)}, u32[]{:S(2)}, u32[]{:S(2)}) collective-permute-start(bf16[3,256,768]{2,1,0:T(8,128)(2,1)} %up0.1), channel_id=1, source_target_pairs={{0,32},{32,64},{64,96},{96,0},{1,33},{33,65},{65,97},{97,1},{2,34}... | collective-permute-start | bytes 3538952 | tf_op jit(solution)/shard_map/ppermute | solution.py:364
  138.6 22.3 %copy-start.4 = (bf16[3,256,768]{2,1,0:T(8,128)(2,1)}, bf16[3,256,768]{2,1,0:T(8,128)(2,1)S(1)}, u32[]{:S(2)}) copy-start(bf16[3,256,768]{2,1,0:T(8,128)(2,1)S(1)} %collective-permute-done.3.refs_0_) | copy-start | bytes 3538948
  160.9 27.2 %collective-permute-start.8 = (bf16[3,256,768]{2,1,0:T(8,128)(2,1)}, bf16[3,256,768]{2,1,0:T(8,128)(2,1)S(1)}, u32[]{:S(2)}, u32[]{:S(2)}) collective-permute-start(bf16[3,256,768]{2,1,0:T(8,128)(2,1)} %get-tuple-element.72.a_ref), channel_id=1, source_target_pairs={{0,32},{32,64},{64,96},{96,0},{1,33},{33,65},{65,97},{97,1},{2,34}... | collective-permute-start | bytes 3538952 | tf_op jit(solution)/shard_map/ppermute | solution.py:364
  161.2 1.4 copy-start.2
  162.6 25.5 %collective-permute-start.9 = (bf16[3,256,768]{2,1,0:T(8,128)(2,1)S(1)}, bf16[3,256,768]{2,1,0:T(8,128)(2,1)S(1)}, u32[]{:S(2)}, u32[]{:S(2)}) collective-permute-start(bf16[3,256,768]{2,1,0:T(8,128)(2,1)S(1)} %copy-done.2), channel_id=1, source_target_pairs={{0,96},{32,0},{64,32},{96,64},{1,97},{33,1},{65,33},{97,65},{2,98}... | collective-permute-start | bytes 3538952 | tf_op jit(solution)/shard_map/ppermute | solution.py:367
  173.1 61.6 %all-to-all-start.2 = ((bf16[32,32,2176]{2,1,0:T(8,128)(2,1)}), bf16[32,32,2176]{2,1,0:T(8,128)(2,1)}, u32[]{:S(2)}, u32[]{:S(2)}) async-start(bf16[32,32,2176]{2,1,0:T(8,128)(2,1)} %dx1.1), calls=%async_computation.2 | async-start | bytes 8912896 | tf_op jit(solution)/shard_map/all_to_all | solution.py:373
  184.8 30.3 %collective-permute-start.7 = (bf16[3,256,768]{2,1,0:T(8,128)(2,1)}, bf16[3,256,768]{2,1,0:T(8,128)(2,1)}, u32[]{:S(2)}, u32[]{:S(2)}) collective-permute-start(bf16[3,256,768]{2,1,0:T(8,128)(2,1)} %get-tuple-element.79), channel_id=1, source_target_pairs={{0,32},{32,64},{64,96},{96,0},{1,33},{33,65},{65,97},{97,1},{2,34}... | collective-permute-start | bytes 3538952 | tf_op jit(solution)/shard_map/ppermute | solution.py:364
  184.8 34.4 %collective-permute-start.6 = (bf16[3,256,768]{2,1,0:T(8,128)(2,1)}, bf16[3,256,768]{2,1,0:T(8,128)(2,1)}, u32[]{:S(2)}, u32[]{:S(2)}) collective-permute-start(bf16[3,256,768]{2,1,0:T(8,128)(2,1)} %get-tuple-element.78), channel_id=1, source_target_pairs={{0,96},{32,0},{64,32},{96,64},{1,97},{33,1},{65,33},{97,65},{2,98}... | collective-permute-start | bytes 3538952 | tf_op jit(solution)/shard_map/ppermute | solution.py:367
  188.1 5.1 %copy-start.7 = (bf16[3,256,768]{2,1,0:T(8,128)(2,1)}, bf16[3,256,768]{2,1,0:T(8,128)(2,1)S(1)}, u32[]{:S(2)}) copy-start(bf16[3,256,768]{2,1,0:T(8,128)(2,1)S(1)} %collective-permute-done.8.refs_0_) | copy-start | bytes 3538948
  188.1 1.0 copy-start.8
  193.1 5.3 %copy-start.6 = (bf16[3,256,768]{2,1,0:T(8,128)(2,1)S(1)}, bf16[3,256,768]{2,1,0:T(8,128)(2,1)}, u32[]{:S(2)}) copy-start(bf16[3,256,768]{2,1,0:T(8,128)(2,1)} %down1.1) | copy-start | bytes 3538948
  197.2 42.3 %collective-permute-start.10 = (bf16[3,256,768]{2,1,0:T(8,128)(2,1)}, bf16[3,256,768]{2,1,0:T(8,128)(2,1)S(1)}, u32[]{:S(2)}, u32[]{:S(2)}) collective-permute-start(bf16[3,256,768]{2,1,0:T(8,128)(2,1)} %up1.1), channel_id=1, source_target_pairs={{0,32},{32,64},{64,96},{96,0},{1,33},{33,65},{65,97},{97,1},{2,34}... | collective-permute-start | bytes 3538952 | tf_op jit(solution)/shard_map/ppermute | solution.py:364
  198.4 41.1 %collective-permute-start.11 = (bf16[3,256,768]{2,1,0:T(8,128)(2,1)S(1)}, bf16[3,256,768]{2,1,0:T(8,128)(2,1)S(1)}, u32[]{:S(2)}, u32[]{:S(2)}) collective-permute-start(bf16[3,256,768]{2,1,0:T(8,128)(2,1)S(1)} %copy-done.6), channel_id=1, source_target_pairs={{0,96},{32,0},{64,32},{96,64},{1,97},{33,1},{65,33},{97,65},{2,98}... | collective-permute-start | bytes 3538952 | tf_op jit(solution)/shard_map/ppermute | solution.py:367
  239.5 1.0 copy-start
  239.5 1.4 copy-start.1

commit v9 on v8

--- a/solution.py
+++ b/solution.py
@@ -163,11 +163,92 @@
     )(where, *[rows] * 6, wg, wu, wd)
 
 
+def hidden_part_kernel(
+    first, last, where_ref, x_ref, do_ref, xa_ref, xb_ref, da_col_ref, db_col_ref, wg_ref, wu_ref, wd_ref, *refs
+):
+    hid_ref, da_ref, db_ref, s_ref, a_ref, b_ref = refs[-6:]
+    gate = dot(x_ref[...], wg_ref[0], NN)
+    upper = dot(x_ref[...], wu_ref[0], NN)
+    sig = jax.nn.sigmoid(gate)
+    act = gate * sig
+    hid = (act * upper).astype(BF16)
+    hid_ref[...] = hid
+    dhid = dot(do_ref[...], wd_ref[0], NN)
+    total = jnp.broadcast_to(jnp.sum(hid.astype(F32) * dhid, axis=1, keepdims=True), s_ref.shape)
+    dgate = (dhid * upper * sig * (1.0 + gate * (1.0 - sig))).astype(BF16)
+    dup = (dhid * act).astype(BF16)
+    da_ref[...] = dgate
+    db_ref[...] = dup
+    for out_ref, x_col, do_col in ((a_ref, xa_ref, da_col_ref), (b_ref, xb_ref, db_col_ref)):
+        out_ref[0] = dot(x_col[...], dgate, TN).astype(BF16)
+        out_ref[1] = dot(x_col[...], dup, TN).astype(BF16)
+        out_ref[2] = dot(do_col[...], hid, TN).astype(BF16)
+    if not first:
+        total = total + refs[0][...]
+    if last:
+        high = total.astype(BF16).astype(F32)
+        lane = lax.broadcasted_iota(jnp.int32, s_ref.shape, 1)
+        total = jnp.where(lane == 0, high, jnp.where(lane == 1, total - high, 0.0))
+    s_ref[...] = total.astype(s_ref.dtype)
+
+
+def hidden_parts(chunk, where, half, rows, wg, wu, wd, sent):
+    n_rows, width = rows.shape[0], rows.shape[1] // 2
+    hidden = wg.shape[2]
+    block = 2 * LANES
+    lefts = width // half
+    parts = hidden // block
+    once = pl.Buffered(1)
+    shard = jax.ShapeDtypeStruct((3, half, block), BF16)
+    kept, total, pairs = [], None, []
+    for part in range(parts):
+        first, last = part == 0, part + 1 == parts
+        if last and len(pairs) > 1:
+            total, *pairs[0] = lax.optimization_barrier((total, *pairs[0]))
+        extra = [] if first else [total]
+        result = pl.BlockSpec((n_rows, block), lambda i, at, part=part: (0, part), pipeline_mode=once)
+        weight = pl.BlockSpec((1, width, block), lambda i, at, part=part: (chunk, 0, part), pipeline_mode=once)
+        *kept, total, a, b = pl.pallas_call(
+            functools.partial(hidden_part_kernel, first, last),
+            grid_spec=pltpu.PrefetchScalarGridSpec(
+                num_scalar_prefetch=1,
+                grid=(1,),
+                in_specs=[
+                    pl.BlockSpec((n_rows, width), lambda i, at: (0, 0), pipeline_mode=once),
+                    pl.BlockSpec((n_rows, width), lambda i, at: (0, 1), pipeline_mode=once),
+                    pl.BlockSpec((n_rows, half), lambda i, at: (0, at[0]), pipeline_mode=once),
+                    pl.BlockSpec((n_rows, half), lambda i, at: (0, at[1]), pipeline_mode=once),
+                    pl.BlockSpec((n_rows, half), lambda i, at: (0, at[0] + lefts), pipeline_mode=once),
+                    pl.BlockSpec((n_rows, half), lambda i, at: (0, at[1] + lefts), pipeline_mode=once),
+                    weight,
+                    weight,
+                    weight,
+                ]
+                + [whole((n_rows, LANES))] * len(extra)
+                + [pl.BlockSpec(memory_space=pl.ANY)] * len(kept),
+                out_specs=[result] * 3 + [whole((n_rows, LANES)), whole(shard.shape), whole(shard.shape)],
+            ),
+            out_shape=[jax.ShapeDtypeStruct((n_rows, hidden), BF16)] * 3
+            + [jax.ShapeDtypeStruct((n_rows, LANES), BF16 if last else F32), shard, shard],
+            input_output_aliases={11 + i: i for i in range(len(kept))},
+            compiler_params=pltpu.CompilerParams(vmem_limit_bytes=VMEM_LIMIT),
+            cost_estimate=cost(6 * n_rows * width * block, 6 * width * block, chunk),
+            name=f"hidden{chunk}{part}",
+        )(where, *[rows] * 6, wg, wu, wd, *extra, *kept)
+        pairs.append(sent(a, b))
+        if not last:
+            early = (a, b)
+    return (*kept, total, early, pairs)
+
+
 def weight_kernel(n_add, n_after, where_ref, x_ref, do_ref, hid_ref, da_ref, db_ref, *refs):
     adds, outs = refs[:n_add], refs[n_add + n_after :]
     for m, (left, right) in enumerate(((x_ref, da_ref), (x_ref, db_ref), (do_ref, hid_ref))):
         part = dot(left[...], right[...], TN)
-        for addend in adds:
+        pieces = [a[m] for a in adds if a.shape[2] < hid_ref.shape[1]]
+        if pieces:
+            part = part + jnp.concatenate(pieces, axis=1).astype(F32)
+        for addend in adds[len(pieces) :]:
             part = part + addend[m].astype(F32)
         for i, out_ref in enumerate(outs):
 
@@ -392,8 +473,14 @@
     sends = [send(chunk) for chunk in range(local_exp)]
     rows = order(swap_rows(sends[0]), *sends[1:])
     for chunk in range(local_exp):
-        hid, da, db, s, *far = hidden_grads(chunk, blocks(*far_pairs), half, rows, *weights)
-        far_up, far_down = up(far[0]), down(far[1])
+        if chunk:
+            hid, da, db, s, *far = hidden_grads(chunk, blocks(*far_pairs), half, rows, *weights)
+            far_up, far_down = [up(far[0])], [down(far[1])]
+        else:
+            hid, da, db, s, far, pairs = hidden_parts(
+                chunk, blocks(*far_pairs), half, rows, *weights, lambda a, b: (up(a), down(b))
+            )
+            far_up, far_down = [pair[0] for pair in pairs], [pair[1] for pair in pairs]
         grads, after = (rows, hid, da, db), ()
         if before:
             dx, left = lax.optimization_barrier((dx, mark(chunk, *far)))
@@ -408,8 +495,8 @@
         near = weight_grads(f"near{chunk}", chunk, blocks(*near_pairs), 2, half, *grads, after=after)
         near_up, near_down = up(near[0]), down(near[1])
         far_up, far_down, _ = lax.optimization_barrier((far_up, far_down, near[0]))
-        sum_up = weight_grads(f"up{chunk}", chunk, blocks((1, 0)), 1, half, *grads, far_up)[0]
-        sum_down = weight_grads(f"down{chunk}", chunk, blocks((n_group - 1, 1)), 1, half, *grads, far_down)[0]
+        sum_up = weight_grads(f"up{chunk}", chunk, blocks((1, 0)), 1, half, *grads, *far_up)[0]
+        sum_down = weight_grads(f"down{chunk}", chunk, blocks((n_group - 1, 1)), 1, half, *grads, *far_down)[0]
         if before:
             landed = before[1]
             *landed, sum_up, sum_down = lax.optimization_barrier((*landed, sum_up, sum_down))

time: 248 us -> 253 us (1.020)
  waiting for transfers between devices: 83.9 us -> 74.5 us
  Pallas kernels: 119 us -> 128 us
  starting transfers between devices: 37.7 us -> 43.5 us
    pallas_call x0 -> x3, Pallas kernels: none -> 24.1 us  [hidden_parts(): pl.pallas_call(functools.partial(hidden_part_kernel, first, last), grid_s...]
    pallas_call x2 -> x1, Pallas kernels: 30.5 us -> 15.2 us  [hidden_grads(): pl.pallas_call(hidden_kernel, grid_spec=pltpu.PrefetchScalarGridSpec(num_...]
    ppermute x6 -> x8, starting transfers between devices: 16.2 us -> 22.8 us  [down(): lax.ppermute(a, 'dp', [(i, (i - 1) % n_group) for i in range(n_group)])]
    ppermute x6 -> x8, waiting for transfers between devices: 16.9 us -> 12 us  [up(): lax.ppermute(a, 'dp', [(i, (i + 1) % n_group) for i in range(n_group)])]
    all_to_all x3, waiting for transfers between devices: 66.6 us -> 62.6 us  [swap(): return lax.all_to_all(a, 'expert', split_axis=0, concat_axis=0, tiled=True)]
  transfers between devices with their start and end apart: 15 -> 19, of which waited for: 9 -> 6; matrix products, arithmetic and copies ran while one was open for 1% -> 0% of each run, Pallas kernels for 38% -> 44%
where the time goes in v9:
time: 253 us; the launch traced here: 251 us
  Pallas kernels  128 us (51%)
  waiting for transfers between devices  74.5 us (29%)
  starting transfers between devices  43.5 us (17%)
  local copies, waits for them, and re-layouts  3.35 us (1%)
    all_to_all x3, waiting for transfers between devices, swap(): return lax.all_to_all(a, 'expert', split_axis=0, concat_axis=0, tiled=True)  62.6 us
    pallas_call x10, Pallas kernels, weight_grads(): pl.pallas_call(functools.partial(weight_kernel, len(adds), len(after)), g...  45.7 us
    pallas_call x3, Pallas kernels, hidden_parts(): pl.pallas_call(functools.partial(hidden_part_kernel, first, last), grid_s...  24.1 us
    ppermute x8, starting transfers between devices, down(): lax.ppermute(a, 'dp', [(i, (i - 1) % n_group) for i in range(n_group)])  22.8 us
    all_to_all x3, starting transfers between devices, swap(): return lax.all_to_all(a, 'expert', split_axis=0, concat_axis=0, tiled=True)  18.7 us
    pallas_call x1, Pallas kernels, hidden_grads(): pl.pallas_call(hidden_kernel, grid_spec=pltpu.PrefetchScalarGridSpec(num_...  15.2 us
    pallas_call x2, Pallas kernels, input_grads(): pl.pallas_call(dx_kernel, grid=(5,), in_specs=[whole((n_rows, hidden)), w...  15.1 us
    ppermute x8, waiting for transfers between devices, up(): lax.ppermute(a, 'dp', [(i, (i + 1) % n_group) for i in range(n_group)])  12 us
  transfers between devices with their start and end apart: 19, of which 6 were waited for; matrix products, arithmetic and copies ran while one was open for 0% of the time, Pallas kernels for 44%

profile of v9, /device:TPU:0, one launch (start us, length us, event | category | flops | bytes accessed | tf_op | source)
XLA Modules:
  0.0 251.4 jit_solution(2194199193492223398)
XLA Ops:
  0.6 4.8 %dispatch0.1 = bf16[512,4096]{1,0:T(8,128)(2,1)} custom-call(s32[8,128]{1,0:T(8,128)} %bitcast.18, bf16[8,128]{1,0:T(8,128)(2,1)} %bitcast.21, bf16[128,2048]{1,0:T(8,128)(2,1)} %tok_ref.3, bf16[128,2048]{1,0:T(8,128)(2,1)} %grad_ref.3), custom_call_target="tpu_custom_call" | custom-call | flops 3758096384 | bytes 36700160 | tf_op jit(solution)/shard_map/dispatch0/pallas_call | solution.py:78
  5.4 8.5 %all-to-all-start = ((bf16[32,16,4096]{2,1,0:T(8,128)(2,1)}), bf16[32,16,4096]{2,1,0:T(8,128)(2,1)}, u32[]{:S(2)}, u32[]{:S(2)}) async-start(bf16[32,16,4096]{2,1,0:T(8,128)(2,1)} %bitcast.17), calls=%async_computation | async-start | bytes 8388608 | tf_op jit(solution)/shard_map/all_to_all | solution.py:454
  14.0 0.6 pad_add_fusion.where_ref
  14.6 0.6 pad_add_fusion.1.where_ref
  15.2 4.7 %dispatch1.1 = bf16[512,4096]{1,0:T(8,128)(2,1)} custom-call(s32[8,128]{1,0:T(8,128)} %bitcast.19, bf16[8,128]{1,0:T(8,128)(2,1)} %bitcast.22, bf16[128,2048]{1,0:T(8,128)(2,1)} %tok_ref.3, bf16[128,2048]{1,0:T(8,128)(2,1)} %grad_ref.3), custom_call_target="tpu_custom_call" | custom-call | flops 3758096384 | bytes 36700160 | tf_op jit(solution)/shard_map/dispatch1/pallas_call | solution.py:78
  20.0 47.5 %all-to-all-done = bf16[32,16,4096]{2,1,0:T(8,128)(2,1)} async-done(((bf16[32,16,4096]{2,1,0:T(8,128)(2,1)}), bf16[32,16,4096]{2,1,0:T(8,128)(2,1)}, u32[]{:S(2)}, u32[]{:S(2)}) %all-to-all-start) | async-done | bytes 4194336 | tf_op jit(solution)/shard_map/all_to_all | solution.py:454
  67.5 8.0 %hidden00.1 = (bf16[512,768]{1,0:T(8,128)(2,1)}, bf16[512,768]{1,0:T(8,128)(2,1)}, bf16[512,768]{1,0:T(8,128)(2,1)}, f32[512,128]{1,0:T(8,128)}, bf16[3,256,256]...) custom-call(s32[2]{0:T(128)} %pad_add_fusion.where_ref, ...), custom_call_target="tpu_custom_call" | custom-call | flops 11274289152 | bytes 22020096 | tf_op jit(solution)/shard_map/hidden00/pallas_call | solution.py:211
  75.4 1.5 collective-permute-start
  76.9 1.7 collective-permute-start.1
  78.7 8.1 %hidden01.1 = (bf16[512,768]{1,0:T(8,128)(2,1)}, bf16[512,768]{1,0:T(8,128)(2,1)}, bf16[512,768]{1,0:T(8,128)(2,1)}, f32[512,128]{1,0:T(8,128)}, bf16[3,256,256]...) custom-call(s32[2]{0:T(128)} %pad_add_fusion.where_ref, ...), custom_call_target="tpu_custom_call", output_to_operand_aliasing={{0}: (11, {}), {1}: (12, {}), {2}: (13, {})} | custom-call | flops 11274289152 | bytes 22020096 | tf_op jit(solution)/shard_map/hidden01/pallas_call | solution.py:211
  86.7 0.3 collective-permute-start.2
  87.1 2.9 %collective-permute-start.4 = (bf16[3,256,256]{2,1,0:T(8,128)(2,1)}, bf16[3,256,256]{2,1,0:T(8,128)(2,1)S(1)}, u32[]{:S(2)}, u32[]{:S(2)}) collective-permute-start(bf16[3,256,256]{2,1,0:T(8,128)(2,1)} %get-tuple-element.78.b_ref), channel_id=1, source_target_pairs={{0,96},{32,0},{64,32},{96,64},{1,97},{33,1},{65,33},{97,65},{2,98}... | collective-permute-start | bytes 1179656 | tf_op jit(solution)/shard_map/ppermute | solution.py:448
  90.0 1.3 mark0.1.refs_0_
  91.3 5.1 %all-to-all-start.1 = ((bf16[32,16,4096]{2,1,0:T(8,128)(2,1)}), bf16[32,16,4096]{2,1,0:T(8,128)(2,1)}, u32[]{:S(2)}, u32[]{:S(2)}) async-start(bf16[32,16,4096]{2,1,0:T(8,128)(2,1)} %bitcast.16), calls=%async_computation.1 | async-start | bytes 8388608 | tf_op jit(solution)/shard_map/all_to_all | solution.py:454
  96.3 0.0 collective-permute-done.refs_0_
  96.4 0.0 collective-permute-done.1.refs_0_
  96.4 8.1 %hidden02.1 = (bf16[512,768]{1,0:T(8,128)(2,1)}, bf16[512,768]{1,0:T(8,128)(2,1)}, bf16[512,768]{1,0:T(8,128)(2,1)}, bf16[512,128]{1,0:T(8,128)(2,1)}, bf16[3,25...) custom-call(s32[2]{0:T(128)} %pad_add_fusion.where_ref, ...), custom_call_target="tpu_custom_call", output_to_operand_aliasing={{0}: (11, {}), {1}: (12, {}), {2}: (13, {})} | custom-call | flops 11274289152 | bytes 22020096 | tf_op jit(solution)/shard_map/hidden02/pallas_call | solution.py:211
  104.5 0.1 collective-permute-start.3
  104.6 3.2 %collective-permute-start.5 = (bf16[3,256,256]{2,1,0:T(8,128)(2,1)}, bf16[3,256,256]{2,1,0:T(8,128)(2,1)S(1)}, u32[]{:S(2)}, u32[]{:S(2)}) collective-permute-start(bf16[3,256,256]{2,1,0:T(8,128)(2,1)} %get-tuple-element.93), channel_id=1, source_target_pairs={{0,96},{32,0},{64,32},{96,64},{1,97},{33,1},{65,33},{97,65},{2,98}... | collective-permute-start | bytes 1179656 | tf_op jit(solution)/shard_map/ppermute | solution.py:448
  107.8 6.8 %near0.1 = (bf16[3,256,768]{2,1,0:T(8,128)(2,1)}, bf16[3,256,768]{2,1,0:T(8,128)(2,1)}) custom-call(s32[2]{0:T(128)} %pad_add_fusion.1.where_ref, bf16[512,4096]{1,0:T(8,128)(2,1)} %bitcast.5.x_ref.do_ref.xa_ref.xb_ref.da_col_ref.db_col_ref, bf16[512,4096]{1,0:T(8,128)(2,1)} %bitcast.5.x_ref.do_ref.xa_ref.xb_ref.da_col_ref.db_col_ref, ...), custom_call_target="tpu_custom_call" | custom-call | flops 8455716864 | bytes 33030144 | tf_op jit(solution)/shard_map/near0/pallas_call | solution.py:265
  114.6 3.2 %collective-permute-start.7 = (bf16[3,256,768]{2,1,0:T(8,128)(2,1)}, bf16[3,256,768]{2,1,0:T(8,128)(2,1)}, u32[]{:S(2)}, u32[]{:S(2)}) collective-permute-start(bf16[3,256,768]{2,1,0:T(8,128)(2,1)} %get-tuple-element.104), channel_id=1, source_target_pairs={{0,96},{32,0},{64,32},{96,64},{1,97},{33,1},{65,33},{97,65},{2,98}... | collective-permute-start | bytes 3538952 | tf_op jit(solution)/shard_map/ppermute | solution.py:448
  117.8 0.0 copy-start.10
  117.8 0.0 collective-permute-done.5.refs_2_
  117.8 0.7 copy-done.9
  118.6 0.1 copy-done.11
  118.7 4.0 %down0.1 = bf16[3,256,768]{2,1,0:T(8,128)(2,1)} custom-call(s32[1]{0:T(128)} %bitcast.11.where_ref, bf16[512,4096]{1,0:T(8,128)(2,1)} %bitcast.5.x_ref.do_ref.xa_ref.xb_ref.da_col_ref.db_col_ref, bf16[512,4096]{1,0:T(8,128)(2,1)} %bitcast.5.x_ref.do_ref.xa_ref.xb_ref.da_col_ref.db_col_ref, bf16[512,768]{1,0:T(8,128)(2,1)} %get-tuple-element.88.hid_ref, ...), custom_call_target="tpu_custom_call" | custom-call | flops 4227858432 | bytes 24772608 | tf_op jit(solution)/shard_map/down0/pallas_call | solution.py:265
  122.7 2.0 collective-permute-start.9
  124.6 3.9 %up0.1 = bf16[3,256,768]{2,1,0:T(8,128)(2,1)} custom-call(s32[1]{0:T(128)} %bitcast.8.where_ref, bf16[512,4096]{1,0:T(8,128)(2,1)} %bitcast.5.x_ref.do_ref.xa_ref.xb_ref.da_col_ref.db_col_ref, bf16[512,4096]{1,0:T(8,128)(2,1)} %bitcast.5.x_ref.do_ref.xa_ref.xb_ref.da_col_ref.db_col_ref, bf16[512,768]{1,0:T(8,128)(2,1)} %get-tuple-element.88.hid_ref, ...), custom_call_target="tpu_custom_call" | custom-call | flops 4227858432 | bytes 24772608 | tf_op jit(solution)/shard_map/up0/pallas_call | solution.py:265
  128.6 0.1 collective-permute-start.8
  128.7 7.5 %dx0.1.refs_0_ = bf16[32,32,2176]{2,1,0:T(8,128)(2,1)} custom-call(bf16[512,768]{1,0:T(8,128)(2,1)} %get-tuple-element.102.da_ref, bf16[512,768]{1,0:T(8,128)(2,1)} %get-tuple-element.89.db_ref, bf16[512,128]{1,0:T(8,128)(2,1)} %get-tuple-element.103.s_ref, bf16[2,2048,768]{2,1,0:T(8,128)(2,1)} %refs_4_.3, bf16[2,2048,768]{2,1,0:T(8,128)(2,1)} %refs_5_.3), custom_call_target="tpu_custom_call" | custom-call | flops 22548578304 | bytes 69730304 | tf_op jit(solution)/shard_map/dx0/pallas_call | solution.py:368
  136.2 8.8 %collective-permute-done.6.refs_0_ = bf16[3,256,768]{2,1,0:T(8,128)(2,1)} collective-permute-done((bf16[3,256,768]{2,1,0:T(8,128)(2,1)}, bf16[3,256,768]{2,1,0:T(8,128)(2,1)}, u32[]{:S(2)}, u32[]{:S(2)}) %collective-permute-start.6) | collective-permute-done | bytes 1179680 | tf_op jit(solution)/shard_map/ppermute | solution.py:445
  145.0 0.0 collective-permute-done.7.refs_0_
  145.0 4.6 %all-to-all-done.1 = bf16[32,16,4096]{2,1,0:T(8,128)(2,1)} async-done(((bf16[32,16,4096]{2,1,0:T(8,128)(2,1)}), bf16[32,16,4096]{2,1,0:T(8,128)(2,1)}, u32[]{:S(2)}, u32[]{:S(2)}) %all-to-all-start.1) | async-done | bytes 4194336 | tf_op jit(solution)/shard_map/all_to_all | solution.py:454
  149.6 15.2 %hidden1.1 = (bf16[512,768]{1,0:T(8,128)(2,1)}, bf16[512,768]{1,0:T(8,128)(2,1)}, bf16[512,768]{1,0:T(8,128)(2,1)}, bf16[512,128]{1,0:T(8,128)(2,1)}, bf16[3,256...) custom-call(s32[2]{0:T(128)} %pad_add_fusion.where_ref, ...), custom_call_target="tpu_custom_call" | custom-call | flops 154618822656 | bytes 383778816 | tf_op jit(solution)/shard_map/hidden1/pallas_call | solution.py:138
  164.9 0.0 collective-permute-start.12
  164.9 0.0 copy-start.2
  164.9 1.4 mark1.1.refs_0_
  166.3 3.2 %collective-permute-start.13 = (bf16[3,256,768]{2,1,0:T(8,128)(2,1)S(1)}, bf16[3,256,768]{2,1,0:T(8,128)(2,1)S(1)}, u32[]{:S(2)}, u32[]{:S(2)}) collective-permute-start(bf16[3,256,768]{2,1,0:T(8,128)(2,1)S(1)} %copy-done.2), channel_id=1, source_target_pairs={{0,96},{32,0},{64,32},{96,64},{1,97},{33,1},{65,33},{97,65},{2,98}... | collective-permute-start | bytes 3538952 | tf_op jit(solution)/shard_map/ppermute | solution.py:448
  169.5 7.5 %dx1.1 = bf16[32,32,2176]{2,1,0:T(8,128)(2,1)} custom-call(bf16[512,768]{1,0:T(8,128)(2,1)} %get-tuple-element.106.da_ref, bf16[512,768]{1,0:T(8,128)(2,1)} %get-tuple-element.107.db_ref, bf16[512,128]{1,0:T(8,128)(2,1)} %get-tuple-element.108.s_ref, bf16[2,2048,768]{2,1,0:T(8,128)(2,1)} %refs_4_.3, ...), custom_call_target="tpu_custom_call", output_to_operand_aliasing={{}: (5, {})} | custom-call | flops 77309411328 | bytes 239075328 | tf_op jit(solution)/shard_map/dx1/pallas_call | solution.py:368
  177.1 5.1 %all-to-all-start.2 = ((bf16[32,32,2176]{2,1,0:T(8,128)(2,1)}), bf16[32,32,2176]{2,1,0:T(8,128)(2,1)}, u32[]{:S(2)}, u32[]{:S(2)}) async-start(bf16[32,32,2176]{2,1,0:T(8,128)(2,1)} %dx1.1), calls=%async_computation.2 | async-start | bytes 8912896 | tf_op jit(solution)/shard_map/all_to_all | solution.py:454
  182.1 0.0 collective-permute-done.9.refs_3_
  182.1 0.0 collective-permute-done.8.refs_1_
  182.2 6.9 %near1.1 = (bf16[3,256,768]{2,1,0:T(8,128)(2,1)}, bf16[3,256,768]{2,1,0:T(8,128)(2,1)}) custom-call(s32[2]{0:T(128)} %pad_add_fusion.1.where_ref, bf16[512,4096]{1,0:T(8,128)(2,1)} %bitcast.7.x_ref.do_ref.xa_ref.xb_ref.da_col_ref.db_col_ref, bf16[512,4096]{1,0:T(8,128)(2,1)} %bitcast.7.x_ref.do_ref.xa_ref.xb_ref.da_col_ref.db_col_ref, ...), custom_call_target="tpu_custom_call" | custom-call | flops 28991029248 | bytes 113246208 | tf_op jit(solution)/shard_map/near1/pallas_call | solution.py:265
  189.0 0.0 collective-permute-start.11
  189.0 3.2 %collective-permute-start.10 = (bf16[3,256,768]{2,1,0:T(8,128)(2,1)}, bf16[3,256,768]{2,1,0:T(8,128)(2,1)}, u32[]{:S(2)}, u32[]{:S(2)}) collective-permute-start(bf16[3,256,768]{2,1,0:T(8,128)(2,1)} %get-tuple-element.116), channel_id=1, source_target_pairs={{0,96},{32,0},{64,32},{96,64},{1,97},{33,1},{65,33},{97,65},{2,98}... | collective-permute-start | bytes 3538952 | tf_op jit(solution)/shard_map/ppermute | solution.py:448
  192.2 2.1 collective-permute-done.12.refs_0_
  194.4 1.1 copy-done.5
  195.4 4.0 %down1.1 = bf16[3,256,768]{2,1,0:T(8,128)(2,1)} custom-call(s32[1]{0:T(128)} %bitcast.11.where_ref, bf16[512,4096]{1,0:T(8,128)(2,1)} %bitcast.7.x_ref.do_ref.xa_ref.xb_ref.da_col_ref.db_col_ref, bf16[512,4096]{1,0:T(8,128)(2,1)} %bitcast.7.x_ref.do_ref.xa_ref.xb_ref.da_col_ref.db_col_ref, bf16[512,768]{1,0:T(8,128)(2,1)} %get-tuple-element.114.hid_ref, ...), custom_call_target="tpu_custom_call" | custom-call | flops 14495514624 | bytes 84934656 | tf_op jit(solution)/shard_map/down1/pallas_call | solution.py:265
  199.4 4.1 %up1.1 = bf16[3,256,768]{2,1,0:T(8,128)(2,1)} custom-call(s32[1]{0:T(128)} %bitcast.8.where_ref, bf16[512,4096]{1,0:T(8,128)(2,1)} %bitcast.7.x_ref.do_ref.xa_ref.xb_ref.da_col_ref.db_col_ref, bf16[512,4096]{1,0:T(8,128)(2,1)} %bitcast.7.x_ref.do_ref.xa_ref.xb_ref.da_col_ref.db_col_ref, bf16[512,768]{1,0:T(8,128)(2,1)} %get-tuple-element.114.hid_ref, ...), custom_call_target="tpu_custom_call" | custom-call | flops 14495514624 | bytes 84934656 | tf_op jit(solution)/shard_map/up1/pallas_call | solution.py:265
  203.5 3.2 %collective-permute-start.15 = (bf16[3,256,768]{2,1,0:T(8,128)(2,1)S(1)}, bf16[3,256,768]{2,1,0:T(8,128)(2,1)S(1)}, u32[]{:S(2)}, u32[]{:S(2)}) collective-permute-start(bf16[3,256,768]{2,1,0:T(8,128)(2,1)S(1)} %copy-done.3), channel_id=1, source_target_pairs={{0,96},{32,0},{64,32},{96,64},{1,97},{33,1},{65,33},{97,65},{2,98}... | collective-permute-start | bytes 3538952 | tf_op jit(solution)/shard_map/ppermute | solution.py:448
  206.7 4.0 %own01.1.refs_2_ = bf16[3,256,768]{2,1,0:T(8,128)(2,1)} custom-call(s32[1]{0:T(128)} %bitcast.13.where_ref, bf16[512,4096]{1,0:T(8,128)(2,1)} %bitcast.5.x_ref.do_ref.xa_ref.xb_ref.da_col_ref.db_col_ref, bf16[512,4096]{1,0:T(8,128)(2,1)} %bitcast.5.x_ref.do_ref.xa_ref.xb_ref.da_col_ref.db_col_ref, bf16[512,768]{1,0:T(8,128)(2,1)} %get-tuple-element.88.hid_ref, ...), custom_call_target="tpu_custom_call" | custom-call | flops 4227858432 | bytes 24772608 | tf_op jit(solution)/shard_map/own01/pallas_call | solution.py:265
  210.8 4.0 %own00.1.refs_0_ = bf16[3,256,768]{2,1,0:T(8,128)(2,1)} custom-call(s32[1]{0:T(128)} %bitcast.12.where_ref, bf16[512,4096]{1,0:T(8,128)(2,1)} %bitcast.5.x_ref.do_ref.xa_ref.xb_ref.da_col_ref.db_col_ref, bf16[512,4096]{1,0:T(8,128)(2,1)} %bitcast.5.x_ref.do_ref.xa_ref.xb_ref.da_col_ref.db_col_ref, bf16[512,768]{1,0:T(8,128)(2,1)} %get-tuple-element.88.hid_ref, ...), custom_call_target="tpu_custom_call" | custom-call | flops 4227858432 | bytes 24772608 | tf_op jit(solution)/shard_map/own00/pallas_call | solution.py:265
  214.8 5.6 %update0.1 = (bf16[2,512,768]{2,1,0:T(8,128)(2,1)}, bf16[2,512,768]{2,1,0:T(8,128)(2,1)}, bf16[2,512,768]{2,1,0:T(8,128)(2,1)}) custom-call(s32[1]{0:T(128)} %bitcast.15.where_ref, s32[2,3]{1,0:T(2,128)} %mask_ref.3, bf16[3,256,768]{2,1,0:T(8,128)(2,1)} %own00.1.refs_0_, bf16[3,256,768]{2,1,0:T(8,128)(2,1)} %collective-permute-done.8.refs_1_, ...), custom_call_target="tpu_custom_call" | custom-call | flops 47185920 | bytes 283115520 | tf_op jit(solution)/shard_map/update0/pallas_call | solution.py:326
  220.4 0.0 collective-permute-done.11.refs_0_
  220.4 4.0 %own11.1.refs_2_ = bf16[3,256,768]{2,1,0:T(8,128)(2,1)} custom-call(s32[1]{0:T(128)} %bitcast.13.where_ref, bf16[512,4096]{1,0:T(8,128)(2,1)} %bitcast.7.x_ref.do_ref.xa_ref.xb_ref.da_col_ref.db_col_ref, bf16[512,4096]{1,0:T(8,128)(2,1)} %bitcast.7.x_ref.do_ref.xa_ref.xb_ref.da_col_ref.db_col_ref, bf16[512,768]{1,0:T(8,128)(2,1)} %get-tuple-element.114.hid_ref, ...), custom_call_target="tpu_custom_call" | custom-call | flops 14495514624 | bytes 84934656 | tf_op jit(solution)/shard_map/own11/pallas_call | solution.py:265
  224.3 0.0 collective-permute-done.10.refs_0_
  224.4 4.1 %own10.1.refs_0_ = bf16[3,256,768]{2,1,0:T(8,128)(2,1)} custom-call(s32[1]{0:T(128)} %bitcast.12.where_ref, bf16[512,4096]{1,0:T(8,128)(2,1)} %bitcast.7.x_ref.do_ref.xa_ref.xb_ref.da_col_ref.db_col_ref, bf16[512,4096]{1,0:T(8,128)(2,1)} %bitcast.7.x_ref.do_ref.xa_ref.xb_ref.da_col_ref.db_col_ref, bf16[512,768]{1,0:T(8,128)(2,1)} %get-tuple-element.114.hid_ref, ...), custom_call_target="tpu_custom_call" | custom-call | flops 14495514624 | bytes 84934656 | tf_op jit(solution)/shard_map/own10/pallas_call | solution.py:265
  228.4 10.4 %all-to-all-done.2.back_ref = bf16[32,32,2176]{2,1,0:T(8,128)(2,1)} async-done(((bf16[32,32,2176]{2,1,0:T(8,128)(2,1)}), bf16[32,32,2176]{2,1,0:T(8,128)(2,1)}, u32[]{:S(2)}, u32[]{:S(2)}) %all-to-all-start.2) | async-done | bytes 4456480 | tf_op jit(solution)/shard_map/all_to_all | solution.py:454
  238.9 4.4 %combine.1 = (bf16[128,2048]{1,0:T(8,128)(2,1)}, bf16[8,128]{1,0:T(8,128)(2,1)}) custom-call(s32[8,128]{1,0:T(8,128)} %bitcast.20, bf16[8,128]{1,0:T(8,128)(2,1)} %bitcast.23, bf16[32,32,2176]{2,1,0:T(8,128)(2,1)} %all-to-all-done.2.back_ref), custom_call_target="tpu_custom_call" | custom-call | flops 12884901888 | bytes 106954752 | tf_op jit(solution)/shard_map/combine/pallas_call | solution.py:412
  243.2 1.1 collective-permute-done.14.refs_1_
  244.3 0.0 collective-permute-done.15.refs_3_
  244.3 1.0 copy-done
  245.4 0.4 copy-done.1
  245.8 5.5 %update1.1 = (bf16[2,512,768]{2,1,0:T(8,128)(2,1)}, bf16[2,512,768]{2,1,0:T(8,128)(2,1)}, bf16[2,512,768]{2,1,0:T(8,128)(2,1)}) custom-call(s32[1]{0:T(128)} %bitcast.15.where_ref, s32[2,3]{1,0:T(2,128)} %mask_ref.3, bf16[3,256,768]{2,1,0:T(8,128)(2,1)} %own10.1.refs_0_, ...), custom_call_target="tpu_custom_call", output_to_operand_aliasing={{0}: (9, {}), {1}: (10, {}), {2}: (11, {})} | custom-call | flops 47185920 | bytes 283115520 | tf_op jit(solution)/shard_map/update1/pallas_call | solution.py:326
  (23 shorter events, 0.0 us)
Async XLA Ops:
  5.4 62.0 %all-to-all-start = ((bf16[32,16,4096]{2,1,0:T(8,128)(2,1)}), bf16[32,16,4096]{2,1,0:T(8,128)(2,1)}, u32[]{:S(2)}, u32[]{:S(2)}) async-start(bf16[32,16,4096]{2,1,0:T(8,128)(2,1)} %bitcast.17), calls=%async_computation | async-start | bytes 8388608 | tf_op jit(solution)/shard_map/all_to_all | solution.py:454
  75.4 20.9 %collective-permute-start = (bf16[3,256,256]{2,1,0:T(8,128)(2,1)}, bf16[3,256,256]{2,1,0:T(8,128)(2,1)S(1)}, u32[]{:S(2)}, u32[]{:S(2)}) collective-permute-start(bf16[3,256,256]{2,1,0:T(8,128)(2,1)} %get-tuple-element.81), channel_id=1, source_target_pairs={{0,32},{32,64},{64,96},{96,0},{1,33},{33,65},{65,97},{97,1},{2,34}... | collective-permute-start | bytes 1179656 | tf_op jit(solution)/shard_map/ppermute | solution.py:445
  76.9 19.4 %collective-permute-start.1 = (bf16[3,256,256]{2,1,0:T(8,128)(2,1)}, bf16[3,256,256]{2,1,0:T(8,128)(2,1)S(1)}, u32[]{:S(2)}, u32[]{:S(2)}) collective-permute-start(bf16[3,256,256]{2,1,0:T(8,128)(2,1)} %get-tuple-element.82), channel_id=1, source_target_pairs={{0,96},{32,0},{64,32},{96,64},{1,97},{33,1},{65,33},{97,65},{2,98}... | collective-permute-start | bytes 1179656 | tf_op jit(solution)/shard_map/ppermute | solution.py:448
  86.7 27.8 %collective-permute-start.2 = (bf16[3,256,256]{2,1,0:T(8,128)(2,1)}, bf16[3,256,256]{2,1,0:T(8,128)(2,1)S(1)}, u32[]{:S(2)}, u32[]{:S(2)}) collective-permute-start(bf16[3,256,256]{2,1,0:T(8,128)(2,1)} %get-tuple-element.77.a_ref), channel_id=1, source_target_pairs={{0,32},{32,64},{64,96},{96,0},{1,33},{33,65},{65,97},{97,1},{2,34}... | collective-permute-start | bytes 1179656 | tf_op jit(solution)/shard_map/ppermute | solution.py:445
  87.1 30.7 %collective-permute-start.4 = (bf16[3,256,256]{2,1,0:T(8,128)(2,1)}, bf16[3,256,256]{2,1,0:T(8,128)(2,1)S(1)}, u32[]{:S(2)}, u32[]{:S(2)}) collective-permute-start(bf16[3,256,256]{2,1,0:T(8,128)(2,1)} %get-tuple-element.78.b_ref), channel_id=1, source_target_pairs={{0,96},{32,0},{64,32},{96,64},{1,97},{33,1},{65,33},{97,65},{2,98}... | collective-permute-start | bytes 1179656 | tf_op jit(solution)/shard_map/ppermute | solution.py:448
  91.3 58.4 %all-to-all-start.1 = ((bf16[32,16,4096]{2,1,0:T(8,128)(2,1)}), bf16[32,16,4096]{2,1,0:T(8,128)(2,1)}, u32[]{:S(2)}, u32[]{:S(2)}) async-start(bf16[32,16,4096]{2,1,0:T(8,128)(2,1)} %bitcast.16), calls=%async_computation.1 | async-start | bytes 8388608 | tf_op jit(solution)/shard_map/all_to_all | solution.py:454
  96.4 8.1 %copy-start.6 = (bf16[3,256,256]{2,1,0:T(8,128)(2,1)}, bf16[3,256,256]{2,1,0:T(8,128)(2,1)S(1)}, u32[]{:S(2)}) copy-start(bf16[3,256,256]{2,1,0:T(8,128)(2,1)S(1)} %collective-permute-done.refs_0_) | copy-start | bytes 1179652
  96.4 8.1 %copy-start.7 = (bf16[3,256,256]{2,1,0:T(8,128)(2,1)}, bf16[3,256,256]{2,1,0:T(8,128)(2,1)S(1)}, u32[]{:S(2)}) copy-start(bf16[3,256,256]{2,1,0:T(8,128)(2,1)S(1)} %collective-permute-done.1.refs_0_) | copy-start | bytes 1179652
  104.5 13.3 %collective-permute-start.3 = (bf16[3,256,256]{2,1,0:T(8,128)(2,1)}, bf16[3,256,256]{2,1,0:T(8,128)(2,1)S(1)}, u32[]{:S(2)}, u32[]{:S(2)}) collective-permute-start(bf16[3,256,256]{2,1,0:T(8,128)(2,1)} %get-tuple-element.91), channel_id=1, source_target_pairs={{0,32},{32,64},{64,96},{96,0},{1,33},{33,65},{65,97},{97,1},{2,34}... | collective-permute-start | bytes 1179656 | tf_op jit(solution)/shard_map/ppermute | solution.py:445
  104.6 13.3 %collective-permute-start.5 = (bf16[3,256,256]{2,1,0:T(8,128)(2,1)}, bf16[3,256,256]{2,1,0:T(8,128)(2,1)S(1)}, u32[]{:S(2)}, u32[]{:S(2)}) collective-permute-start(bf16[3,256,256]{2,1,0:T(8,128)(2,1)} %get-tuple-element.93), channel_id=1, source_target_pairs={{0,96},{32,0},{64,32},{96,64},{1,97},{33,1},{65,33},{97,65},{2,98}... | collective-permute-start | bytes 1179656 | tf_op jit(solution)/shard_map/ppermute | solution.py:448
  114.6 30.4 %collective-permute-start.6 = (bf16[3,256,768]{2,1,0:T(8,128)(2,1)}, bf16[3,256,768]{2,1,0:T(8,128)(2,1)}, u32[]{:S(2)}, u32[]{:S(2)}) collective-permute-start(bf16[3,256,768]{2,1,0:T(8,128)(2,1)} %get-tuple-element.95), channel_id=1, source_target_pairs={{0,32},{32,64},{64,96},{96,0},{1,33},{33,65},{65,97},{97,1},{2,34}... | collective-permute-start | bytes 3538952 | tf_op jit(solution)/shard_map/ppermute | solution.py:445
  114.6 8.1 %copy-start.8 = (bf16[3,256,256]{2,1,0:T(8,128)(2,1)}, bf16[3,256,256]{2,1,0:T(8,128)(2,1)S(1)}, u32[]{:S(2)}) copy-start(bf16[3,256,256]{2,1,0:T(8,128)(2,1)S(1)} %collective-permute-done.2.refs_1_) | copy-start | bytes 1179652
  114.6 30.4 %collective-permute-start.7 = (bf16[3,256,768]{2,1,0:T(8,128)(2,1)}, bf16[3,256,768]{2,1,0:T(8,128)(2,1)}, u32[]{:S(2)}, u32[]{:S(2)}) collective-permute-start(bf16[3,256,768]{2,1,0:T(8,128)(2,1)} %get-tuple-element.104), channel_id=1, source_target_pairs={{0,96},{32,0},{64,32},{96,64},{1,97},{33,1},{65,33},{97,65},{2,98}... | collective-permute-start | bytes 3538952 | tf_op jit(solution)/shard_map/ppermute | solution.py:448
  117.8 0.7 copy-start.9
  117.8 4.8 %copy-start.10 = (bf16[3,256,256]{2,1,0:T(8,128)(2,1)}, bf16[3,256,256]{2,1,0:T(8,128)(2,1)S(1)}, u32[]{:S(2)}) copy-start(bf16[3,256,256]{2,1,0:T(8,128)(2,1)S(1)} %collective-permute-done.3.refs_2_) | copy-start | bytes 1179652
  117.8 0.9 copy-start.11
  122.7 59.5 %collective-permute-start.9 = (bf16[3,256,768]{2,1,0:T(8,128)(2,1)}, bf16[3,256,768]{2,1,0:T(8,128)(2,1)}, u32[]{:S(2)}, u32[]{:S(2)}) collective-permute-start(bf16[3,256,768]{2,1,0:T(8,128)(2,1)} %down0.1), channel_id=1, source_target_pairs={{0,96},{32,0},{64,32},{96,64},{1,97},{33,1},{65,33},{97,65},{2,98}... | collective-permute-start | bytes 3538952 | tf_op jit(solution)/shard_map/ppermute | solution.py:448
  128.6 53.6 %collective-permute-start.8 = (bf16[3,256,768]{2,1,0:T(8,128)(2,1)}, bf16[3,256,768]{2,1,0:T(8,128)(2,1)}, u32[]{:S(2)}, u32[]{:S(2)}) collective-permute-start(bf16[3,256,768]{2,1,0:T(8,128)(2,1)} %up0.1), channel_id=1, source_target_pairs={{0,32},{32,64},{64,96},{96,0},{1,33},{33,65},{65,97},{97,1},{2,34}... | collective-permute-start | bytes 3538952 | tf_op jit(solution)/shard_map/ppermute | solution.py:445
  164.9 29.5 %collective-permute-start.12 = (bf16[3,256,768]{2,1,0:T(8,128)(2,1)}, bf16[3,256,768]{2,1,0:T(8,128)(2,1)S(1)}, u32[]{:S(2)}, u32[]{:S(2)}) collective-permute-start(bf16[3,256,768]{2,1,0:T(8,128)(2,1)} %get-tuple-element.110.a_ref), channel_id=1, source_target_pairs={{0,32},{32,64},{64,96},{96,0},{1,33},{33,65},{65,97},{97,1},{2,34}... | collective-permute-start | bytes 3538952 | tf_op jit(solution)/shard_map/ppermute | solution.py:445
  164.9 1.4 copy-start.2
  166.3 28.0 %collective-permute-start.13 = (bf16[3,256,768]{2,1,0:T(8,128)(2,1)S(1)}, bf16[3,256,768]{2,1,0:T(8,128)(2,1)S(1)}, u32[]{:S(2)}, u32[]{:S(2)}) collective-permute-start(bf16[3,256,768]{2,1,0:T(8,128)(2,1)S(1)} %copy-done.2), channel_id=1, source_target_pairs={{0,96},{32,0},{64,32},{96,64},{1,97},{33,1},{65,33},{97,65},{2,98}... | collective-permute-start | bytes 3538952 | tf_op jit(solution)/shard_map/ppermute | solution.py:448
  177.1 61.8 %all-to-all-start.2 = ((bf16[32,32,2176]{2,1,0:T(8,128)(2,1)}), bf16[32,32,2176]{2,1,0:T(8,128)(2,1)}, u32[]{:S(2)}, u32[]{:S(2)}) async-start(bf16[32,32,2176]{2,1,0:T(8,128)(2,1)} %dx1.1), calls=%async_computation.2 | async-start | bytes 8912896 | tf_op jit(solution)/shard_map/all_to_all | solution.py:454
  189.0 31.4 %collective-permute-start.11 = (bf16[3,256,768]{2,1,0:T(8,128)(2,1)}, bf16[3,256,768]{2,1,0:T(8,128)(2,1)}, u32[]{:S(2)}, u32[]{:S(2)}) collective-permute-start(bf16[3,256,768]{2,1,0:T(8,128)(2,1)} %get-tuple-element.117), channel_id=1, source_target_pairs={{0,32},{32,64},{64,96},{96,0},{1,33},{33,65},{65,97},{97,1},{2,34}... | collective-permute-start | bytes 3538952 | tf_op jit(solution)/shard_map/ppermute | solution.py:445
  189.0 35.3 %collective-permute-start.10 = (bf16[3,256,768]{2,1,0:T(8,128)(2,1)}, bf16[3,256,768]{2,1,0:T(8,128)(2,1)}, u32[]{:S(2)}, u32[]{:S(2)}) collective-permute-start(bf16[3,256,768]{2,1,0:T(8,128)(2,1)} %get-tuple-element.116), channel_id=1, source_target_pairs={{0,96},{32,0},{64,32},{96,64},{1,97},{33,1},{65,33},{97,65},{2,98}... | collective-permute-start | bytes 3538952 | tf_op jit(solution)/shard_map/ppermute | solution.py:448
  194.4 5.1 %copy-start.4 = (bf16[3,256,768]{2,1,0:T(8,128)(2,1)}, bf16[3,256,768]{2,1,0:T(8,128)(2,1)S(1)}, u32[]{:S(2)}) copy-start(bf16[3,256,768]{2,1,0:T(8,128)(2,1)S(1)} %collective-permute-done.12.refs_0_) | copy-start | bytes 3538948
  194.4 1.1 copy-start.5
  199.4 4.1 %copy-start.3 = (bf16[3,256,768]{2,1,0:T(8,128)(2,1)S(1)}, bf16[3,256,768]{2,1,0:T(8,128)(2,1)}, u32[]{:S(2)}) copy-start(bf16[3,256,768]{2,1,0:T(8,128)(2,1)} %down1.1) | copy-start | bytes 3538948
  203.5 40.8 %collective-permute-start.14 = (bf16[3,256,768]{2,1,0:T(8,128)(2,1)}, bf16[3,256,768]{2,1,0:T(8,128)(2,1)S(1)}, u32[]{:S(2)}, u32[]{:S(2)}) collective-permute-start(bf16[3,256,768]{2,1,0:T(8,128)(2,1)} %up1.1), channel_id=1, source_target_pairs={{0,32},{32,64},{64,96},{96,0},{1,33},{33,65},{65,97},{97,1},{2,34}... | collective-permute-start | bytes 3538952 | tf_op jit(solution)/shard_map/ppermute | solution.py:445
  203.5 40.8 %collective-permute-start.15 = (bf16[3,256,768]{2,1,0:T(8,128)(2,1)S(1)}, bf16[3,256,768]{2,1,0:T(8,128)(2,1)S(1)}, u32[]{:S(2)}, u32[]{:S(2)}) collective-permute-start(bf16[3,256,768]{2,1,0:T(8,128)(2,1)S(1)} %copy-done.3), channel_id=1, source_target_pairs={{0,96},{32,0},{64,32},{96,64},{1,97},{33,1},{65,33},{97,65},{2,98}... | collective-permute-start | bytes 3538952 | tf_op jit(solution)/shard_map/ppermute | solution.py:448
  244.3 1.0 copy-start
  244.3 1.4 copy-start.1

commit v10 on v8

--- a/solution.py
+++ b/solution.py
@@ -12,7 +12,7 @@
 LANES = 128
 F32 = jnp.float32
 BF16 = jnp.bfloat16
-VMEM_LIMIT = 60 * 1024 * 1024
+VMEM_LIMIT = 63 * 1024 * 1024
 
 
 def dot(a, b, dims):

time: 248 us -> 246 us (level)
  local copies, waits for them, and re-layouts: 3.6 us -> 0 us
    unnamed x18 -> x0, local copies, waits for them, and re-layouts: 3.6 us -> none
  transfers between devices with their start and end apart: 15 -> 15, of which waited for: 9 -> 9; matrix products, arithmetic and copies ran while one was open for 1% -> 0% of each run, Pallas kernels for 38% -> 38%
where the time goes in v10:
time: 246 us; the launch traced here: 245 us
  Pallas kernels  119 us (48%)
  waiting for transfers between devices  86.2 us (35%)
  starting transfers between devices  37.8 us (15%)
    all_to_all x3, waiting for transfers between devices, swap(): return lax.all_to_all(a, 'expert', split_axis=0, concat_axis=0, tiled=True)  66.5 us
    pallas_call x10, Pallas kernels, weight_grads(): pl.pallas_call(functools.partial(weight_kernel, len(adds), len(after)), g...  46 us
    pallas_call x2, Pallas kernels, hidden_grads(): pl.pallas_call(hidden_kernel, grid_spec=pltpu.PrefetchScalarGridSpec(num_...  30.4 us
    ppermute x6, waiting for transfers between devices, up(): lax.ppermute(a, 'dp', [(i, (i + 1) % n_group) for i in range(n_group)])  19.1 us
    all_to_all x3, starting transfers between devices, swap(): return lax.all_to_all(a, 'expert', split_axis=0, concat_axis=0, tiled=True)  18.3 us
    ppermute x6, starting transfers between devices, down(): lax.ppermute(a, 'dp', [(i, (i - 1) % n_group) for i in range(n_group)])  15.7 us
    pallas_call x2, Pallas kernels, input_grads(): pl.pallas_call(dx_kernel, grid=(5,), in_specs=[whole((n_rows, hidden)), w...  15.1 us
    pallas_call x2, Pallas kernels, update(): pl.pallas_call(functools.partial(update_kernel, chunk), grid_spec=pltpu.P...  11.2 us
  transfers between devices with their start and end apart: 15, of which 9 were waited for; matrix products, arithmetic and copies ran while one was open for 0% of the time, Pallas kernels for 38%

profile of v10, /device:TPU:0, one launch (start us, length us, event | category | flops | bytes accessed | tf_op | source)
XLA Modules:
  0.0 245.2 jit_solution(2416930048481351189)
XLA Ops:
  0.6 4.8 %dispatch0.1 = bf16[512,4096]{1,0:T(8,128)(2,1)} custom-call(s32[8,128]{1,0:T(8,128)} %bitcast.18, bf16[8,128]{1,0:T(8,128)(2,1)} %bitcast.21, bf16[128,2048]{1,0:T(8,128)(2,1)} %tok_ref.3, bf16[128,2048]{1,0:T(8,128)(2,1)} %grad_ref.3), custom_call_target="tpu_custom_call" | custom-call | flops 3758096384 | bytes 36700160 | tf_op jit(solution)/shard_map/dispatch0/pallas_call | solution.py:78
  5.4 8.5 %all-to-all-start = ((bf16[32,16,4096]{2,1,0:T(8,128)(2,1)}), bf16[32,16,4096]{2,1,0:T(8,128)(2,1)}, u32[]{:S(2)}, u32[]{:S(2)}) async-start(bf16[32,16,4096]{2,1,0:T(8,128)(2,1)} %bitcast.17), calls=%async_computation | async-start | bytes 8388608 | tf_op jit(solution)/shard_map/all_to_all | solution.py:373
  14.0 0.6 pad_add_fusion.where_ref
  14.5 4.7 %dispatch1.1 = bf16[512,4096]{1,0:T(8,128)(2,1)} custom-call(s32[8,128]{1,0:T(8,128)} %bitcast.19, bf16[8,128]{1,0:T(8,128)(2,1)} %bitcast.22, bf16[128,2048]{1,0:T(8,128)(2,1)} %tok_ref.3, bf16[128,2048]{1,0:T(8,128)(2,1)} %grad_ref.3), custom_call_target="tpu_custom_call" | custom-call | flops 3758096384 | bytes 36700160 | tf_op jit(solution)/shard_map/dispatch1/pallas_call | solution.py:78
  19.2 48.2 %all-to-all-done = bf16[32,16,4096]{2,1,0:T(8,128)(2,1)} async-done(((bf16[32,16,4096]{2,1,0:T(8,128)(2,1)}), bf16[32,16,4096]{2,1,0:T(8,128)(2,1)}, u32[]{:S(2)}, u32[]{:S(2)}) %all-to-all-start) | async-done | bytes 4194336 | tf_op jit(solution)/shard_map/all_to_all | solution.py:373
  67.4 15.2 %hidden0.1 = (bf16[512,768]{1,0:T(8,128)(2,1)}, bf16[512,768]{1,0:T(8,128)(2,1)}, bf16[512,768]{1,0:T(8,128)(2,1)}, bf16[512,128]{1,0:T(8,128)(2,1)}, bf16[3,256...) custom-call(s32[2]{0:T(128)} %pad_add_fusion.where_ref, ...), custom_call_target="tpu_custom_call" | custom-call | flops 45097156608 | bytes 111935488 | tf_op jit(solution)/shard_map/hidden0/pallas_call | solution.py:138
  82.6 1.5 collective-permute-start
  84.2 1.7 collective-permute-start.1
  85.9 1.3 mark0.1.refs_0_
  87.2 4.9 %all-to-all-start.1 = ((bf16[32,16,4096]{2,1,0:T(8,128)(2,1)}), bf16[32,16,4096]{2,1,0:T(8,128)(2,1)}, u32[]{:S(2)}, u32[]{:S(2)}) async-start(bf16[32,16,4096]{2,1,0:T(8,128)(2,1)} %bitcast.16), calls=%async_computation.1 | async-start | bytes 8388608 | tf_op jit(solution)/shard_map/all_to_all | solution.py:373
  92.1 0.6 pad_add_fusion.1.where_ref
  92.7 6.9 %near0.1 = (bf16[3,256,768]{2,1,0:T(8,128)(2,1)}, bf16[3,256,768]{2,1,0:T(8,128)(2,1)}) custom-call(s32[2]{0:T(128)} %pad_add_fusion.1.where_ref, bf16[512,4096]{1,0:T(8,128)(2,1)} %bitcast.5.x_ref.do_ref.xa_ref.xb_ref.da_col_ref.db_col_ref, bf16[512,4096]{1,0:T(8,128)(2,1)} %bitcast.5.x_ref.do_ref.xa_ref.xb_ref.da_col_ref.db_col_ref, ...), custom_call_target="tpu_custom_call" | custom-call | flops 8455716864 | bytes 33030144 | tf_op jit(solution)/shard_map/near0/pallas_call | solution.py:184
  99.6 0.3 collective-permute-start.2
  99.8 3.0 %collective-permute-start.3 = (bf16[3,256,768]{2,1,0:T(8,128)(2,1)}, bf16[3,256,768]{2,1,0:T(8,128)(2,1)}, u32[]{:S(2)}, u32[]{:S(2)}) collective-permute-start(bf16[3,256,768]{2,1,0:T(8,128)(2,1)} %get-tuple-element.66), channel_id=1, source_target_pairs={{0,96},{32,0},{64,32},{96,64},{1,97},{33,1},{65,33},{97,65},{2,98}... | collective-permute-start | bytes 3538952 | tf_op jit(solution)/shard_map/ppermute | solution.py:367
  102.8 10.3 %collective-permute-done.refs_0_ = bf16[3,256,768]{2,1,0:T(8,128)(2,1)} collective-permute-done((bf16[3,256,768]{2,1,0:T(8,128)(2,1)}, bf16[3,256,768]{2,1,0:T(8,128)(2,1)}, u32[]{:S(2)}, u32[]{:S(2)}) %collective-permute-start) | collective-permute-done | bytes 1179680 | tf_op jit(solution)/shard_map/ppermute | solution.py:364
  113.1 0.3 collective-permute-done.1.refs_0_
  113.4 4.0 %down0.1 = bf16[3,256,768]{2,1,0:T(8,128)(2,1)} custom-call(s32[1]{0:T(128)} %bitcast.11.where_ref, bf16[512,4096]{1,0:T(8,128)(2,1)} %bitcast.5.x_ref.do_ref.xa_ref.xb_ref.da_col_ref.db_col_ref, bf16[512,4096]{1,0:T(8,128)(2,1)} %bitcast.5.x_ref.do_ref.xa_ref.xb_ref.da_col_ref.db_col_ref, bf16[512,768]{1,0:T(8,128)(2,1)} %get-tuple-element.58.hid_ref, ...), custom_call_target="tpu_custom_call" | custom-call | flops 4227858432 | bytes 24772608 | tf_op jit(solution)/shard_map/down0/pallas_call | solution.py:184
  117.4 3.0 %collective-permute-start.5 = (bf16[3,256,768]{2,1,0:T(8,128)(2,1)}, bf16[3,256,768]{2,1,0:T(8,128)(2,1)}, u32[]{:S(2)}, u32[]{:S(2)}) collective-permute-start(bf16[3,256,768]{2,1,0:T(8,128)(2,1)} %down0.1), channel_id=1, source_target_pairs={{0,96},{32,0},{64,32},{96,64},{1,97},{33,1},{65,33},{97,65},{2,98}... | collective-permute-start | bytes 3538952 | tf_op jit(solution)/shard_map/ppermute | solution.py:367
  120.4 4.0 %up0.1 = bf16[3,256,768]{2,1,0:T(8,128)(2,1)} custom-call(s32[1]{0:T(128)} %bitcast.8.where_ref, bf16[512,4096]{1,0:T(8,128)(2,1)} %bitcast.5.x_ref.do_ref.xa_ref.xb_ref.da_col_ref.db_col_ref, bf16[512,4096]{1,0:T(8,128)(2,1)} %bitcast.5.x_ref.do_ref.xa_ref.xb_ref.da_col_ref.db_col_ref, bf16[512,768]{1,0:T(8,128)(2,1)} %get-tuple-element.58.hid_ref, ...), custom_call_target="tpu_custom_call" | custom-call | flops 4227858432 | bytes 24772608 | tf_op jit(solution)/shard_map/up0/pallas_call | solution.py:184
  124.4 0.0 collective-permute-start.4
  124.4 7.6 %dx0.1.refs_0_ = bf16[32,32,2176]{2,1,0:T(8,128)(2,1)} custom-call(bf16[512,768]{1,0:T(8,128)(2,1)} %get-tuple-element.64.da_ref, bf16[512,768]{1,0:T(8,128)(2,1)} %get-tuple-element.59.db_ref, bf16[512,128]{1,0:T(8,128)(2,1)} %get-tuple-element.65.s_ref, bf16[2,2048,768]{2,1,0:T(8,128)(2,1)} %refs_4_.3, bf16[2,2048,768]{2,1,0:T(8,128)(2,1)} %refs_5_.3), custom_call_target="tpu_custom_call" | custom-call | flops 22548578304 | bytes 69730304 | tf_op jit(solution)/shard_map/dx0/pallas_call | solution.py:287
  131.9 6.5 %collective-permute-done.2.refs_0_ = bf16[3,256,768]{2,1,0:T(8,128)(2,1)} collective-permute-done((bf16[3,256,768]{2,1,0:T(8,128)(2,1)}, bf16[3,256,768]{2,1,0:T(8,128)(2,1)}, u32[]{:S(2)}, u32[]{:S(2)}) %collective-permute-start.2) | collective-permute-done | bytes 1179680 | tf_op jit(solution)/shard_map/ppermute | solution.py:364
  138.4 0.3 collective-permute-done.3.refs_0_
  138.7 6.9 %all-to-all-done.1 = bf16[32,16,4096]{2,1,0:T(8,128)(2,1)} async-done(((bf16[32,16,4096]{2,1,0:T(8,128)(2,1)}), bf16[32,16,4096]{2,1,0:T(8,128)(2,1)}, u32[]{:S(2)}, u32[]{:S(2)}) %all-to-all-start.1) | async-done | bytes 4194336 | tf_op jit(solution)/shard_map/all_to_all | solution.py:373
  145.6 15.2 %hidden1.1 = (bf16[512,768]{1,0:T(8,128)(2,1)}, bf16[512,768]{1,0:T(8,128)(2,1)}, bf16[512,768]{1,0:T(8,128)(2,1)}, bf16[512,128]{1,0:T(8,128)(2,1)}, bf16[3,256...) custom-call(s32[2]{0:T(128)} %pad_add_fusion.where_ref, ...), custom_call_target="tpu_custom_call" | custom-call | flops 154618822656 | bytes 383778816 | tf_op jit(solution)/shard_map/hidden1/pallas_call | solution.py:138
  160.8 0.3 collective-permute-start.8
  161.1 1.3 mark1.1.refs_0_
  162.4 3.0 %collective-permute-start.9 = (bf16[3,256,768]{2,1,0:T(8,128)(2,1)}, bf16[3,256,768]{2,1,0:T(8,128)(2,1)}, u32[]{:S(2)}, u32[]{:S(2)}) collective-permute-start(bf16[3,256,768]{2,1,0:T(8,128)(2,1)} %get-tuple-element.73.b_ref), channel_id=1, source_target_pairs={{0,96},{32,0},{64,32},{96,64},{1,97},{33,1},{65,33},{97,65},{2,98}... | collective-permute-start | bytes 3538952 | tf_op jit(solution)/shard_map/ppermute | solution.py:367
  165.4 7.5 %dx1.1 = bf16[32,32,2176]{2,1,0:T(8,128)(2,1)} custom-call(bf16[512,768]{1,0:T(8,128)(2,1)} %get-tuple-element.68.da_ref, bf16[512,768]{1,0:T(8,128)(2,1)} %get-tuple-element.69.db_ref, bf16[512,128]{1,0:T(8,128)(2,1)} %get-tuple-element.70.s_ref, bf16[2,2048,768]{2,1,0:T(8,128)(2,1)} %refs_4_.3, ...), custom_call_target="tpu_custom_call", output_to_operand_aliasing={{}: (5, {})} | custom-call | flops 77309411328 | bytes 239075328 | tf_op jit(solution)/shard_map/dx1/pallas_call | solution.py:287
  172.9 4.8 %all-to-all-start.2 = ((bf16[32,32,2176]{2,1,0:T(8,128)(2,1)}), bf16[32,32,2176]{2,1,0:T(8,128)(2,1)}, u32[]{:S(2)}, u32[]{:S(2)}) async-start(bf16[32,32,2176]{2,1,0:T(8,128)(2,1)} %dx1.1), calls=%async_computation.2 | async-start | bytes 8912896 | tf_op jit(solution)/shard_map/all_to_all | solution.py:373
  177.8 0.0 collective-permute-done.5.refs_3_
  177.8 0.0 collective-permute-done.4.refs_1_
  177.8 6.9 %near1.1 = (bf16[3,256,768]{2,1,0:T(8,128)(2,1)}, bf16[3,256,768]{2,1,0:T(8,128)(2,1)}) custom-call(s32[2]{0:T(128)} %pad_add_fusion.1.where_ref, bf16[512,4096]{1,0:T(8,128)(2,1)} %bitcast.7.x_ref.do_ref.xa_ref.xb_ref.da_col_ref.db_col_ref, bf16[512,4096]{1,0:T(8,128)(2,1)} %bitcast.7.x_ref.do_ref.xa_ref.xb_ref.da_col_ref.db_col_ref, ...), custom_call_target="tpu_custom_call" | custom-call | flops 28991029248 | bytes 113246208 | tf_op jit(solution)/shard_map/near1/pallas_call | solution.py:184
  184.7 0.0 collective-permute-start.7
  184.7 3.2 %collective-permute-start.6 = (bf16[3,256,768]{2,1,0:T(8,128)(2,1)}, bf16[3,256,768]{2,1,0:T(8,128)(2,1)}, u32[]{:S(2)}, u32[]{:S(2)}) collective-permute-start(bf16[3,256,768]{2,1,0:T(8,128)(2,1)} %get-tuple-element.78), channel_id=1, source_target_pairs={{0,96},{32,0},{64,32},{96,64},{1,97},{33,1},{65,33},{97,65},{2,98}... | collective-permute-start | bytes 3538952 | tf_op jit(solution)/shard_map/ppermute | solution.py:367
  187.9 0.0 collective-permute-done.8.refs_0_
  187.9 0.0 collective-permute-done.9.refs_0_
  187.9 4.0 %down1.1 = bf16[3,256,768]{2,1,0:T(8,128)(2,1)} custom-call(s32[1]{0:T(128)} %bitcast.11.where_ref, bf16[512,4096]{1,0:T(8,128)(2,1)} %bitcast.7.x_ref.do_ref.xa_ref.xb_ref.da_col_ref.db_col_ref, bf16[512,4096]{1,0:T(8,128)(2,1)} %bitcast.7.x_ref.do_ref.xa_ref.xb_ref.da_col_ref.db_col_ref, bf16[512,768]{1,0:T(8,128)(2,1)} %get-tuple-element.76.hid_ref, ...), custom_call_target="tpu_custom_call" | custom-call | flops 14495514624 | bytes 84934656 | tf_op jit(solution)/shard_map/down1/pallas_call | solution.py:184
  192.0 4.1 %up1.1 = bf16[3,256,768]{2,1,0:T(8,128)(2,1)} custom-call(s32[1]{0:T(128)} %bitcast.8.where_ref, bf16[512,4096]{1,0:T(8,128)(2,1)} %bitcast.7.x_ref.do_ref.xa_ref.xb_ref.da_col_ref.db_col_ref, bf16[512,4096]{1,0:T(8,128)(2,1)} %bitcast.7.x_ref.do_ref.xa_ref.xb_ref.da_col_ref.db_col_ref, bf16[512,768]{1,0:T(8,128)(2,1)} %get-tuple-element.76.hid_ref, ...), custom_call_target="tpu_custom_call" | custom-call | flops 14495514624 | bytes 84934656 | tf_op jit(solution)/shard_map/up1/pallas_call | solution.py:184
  196.0 1.7 collective-permute-start.10
  197.7 1.9 collective-permute-start.11
  199.6 4.0 %own01.1.refs_2_ = bf16[3,256,768]{2,1,0:T(8,128)(2,1)} custom-call(s32[1]{0:T(128)} %bitcast.13.where_ref, bf16[512,4096]{1,0:T(8,128)(2,1)} %bitcast.5.x_ref.do_ref.xa_ref.xb_ref.da_col_ref.db_col_ref, bf16[512,4096]{1,0:T(8,128)(2,1)} %bitcast.5.x_ref.do_ref.xa_ref.xb_ref.da_col_ref.db_col_ref, bf16[512,768]{1,0:T(8,128)(2,1)} %get-tuple-element.58.hid_ref, ...), custom_call_target="tpu_custom_call" | custom-call | flops 4227858432 | bytes 24772608 | tf_op jit(solution)/shard_map/own01/pallas_call | solution.py:184
  203.7 4.0 %own00.1.refs_0_ = bf16[3,256,768]{2,1,0:T(8,128)(2,1)} custom-call(s32[1]{0:T(128)} %bitcast.12.where_ref, bf16[512,4096]{1,0:T(8,128)(2,1)} %bitcast.5.x_ref.do_ref.xa_ref.xb_ref.da_col_ref.db_col_ref, bf16[512,4096]{1,0:T(8,128)(2,1)} %bitcast.5.x_ref.do_ref.xa_ref.xb_ref.da_col_ref.db_col_ref, bf16[512,768]{1,0:T(8,128)(2,1)} %get-tuple-element.58.hid_ref, ...), custom_call_target="tpu_custom_call" | custom-call | flops 4227858432 | bytes 24772608 | tf_op jit(solution)/shard_map/own00/pallas_call | solution.py:184
  207.7 5.6 %update0.1 = (bf16[2,512,768]{2,1,0:T(8,128)(2,1)}, bf16[2,512,768]{2,1,0:T(8,128)(2,1)}, bf16[2,512,768]{2,1,0:T(8,128)(2,1)}) custom-call(s32[1]{0:T(128)} %bitcast.15.where_ref, s32[2,3]{1,0:T(2,128)} %mask_ref.3, bf16[3,256,768]{2,1,0:T(8,128)(2,1)} %own00.1.refs_0_, bf16[3,256,768]{2,1,0:T(8,128)(2,1)} %collective-permute-done.4.refs_1_, ...), custom_call_target="tpu_custom_call" | custom-call | flops 47185920 | bytes 283115520 | tf_op jit(solution)/shard_map/update0/pallas_call | solution.py:245
  213.3 1.8 collective-permute-done.7.refs_0_
  215.0 4.1 %own11.1.refs_2_ = bf16[3,256,768]{2,1,0:T(8,128)(2,1)} custom-call(s32[1]{0:T(128)} %bitcast.13.where_ref, bf16[512,4096]{1,0:T(8,128)(2,1)} %bitcast.7.x_ref.do_ref.xa_ref.xb_ref.da_col_ref.db_col_ref, bf16[512,4096]{1,0:T(8,128)(2,1)} %bitcast.7.x_ref.do_ref.xa_ref.xb_ref.da_col_ref.db_col_ref, bf16[512,768]{1,0:T(8,128)(2,1)} %get-tuple-element.76.hid_ref, ...), custom_call_target="tpu_custom_call" | custom-call | flops 14495514624 | bytes 84934656 | tf_op jit(solution)/shard_map/own11/pallas_call | solution.py:184
  219.1 0.0 collective-permute-done.6.refs_0_
  219.1 4.0 %own10.1.refs_0_ = bf16[3,256,768]{2,1,0:T(8,128)(2,1)} custom-call(s32[1]{0:T(128)} %bitcast.12.where_ref, bf16[512,4096]{1,0:T(8,128)(2,1)} %bitcast.7.x_ref.do_ref.xa_ref.xb_ref.da_col_ref.db_col_ref, bf16[512,4096]{1,0:T(8,128)(2,1)} %bitcast.7.x_ref.do_ref.xa_ref.xb_ref.da_col_ref.db_col_ref, bf16[512,768]{1,0:T(8,128)(2,1)} %get-tuple-element.76.hid_ref, ...), custom_call_target="tpu_custom_call" | custom-call | flops 14495514624 | bytes 84934656 | tf_op jit(solution)/shard_map/own10/pallas_call | solution.py:184
  223.1 11.4 %all-to-all-done.2.back_ref = bf16[32,32,2176]{2,1,0:T(8,128)(2,1)} async-done(((bf16[32,32,2176]{2,1,0:T(8,128)(2,1)}), bf16[32,32,2176]{2,1,0:T(8,128)(2,1)}, u32[]{:S(2)}, u32[]{:S(2)}) %all-to-all-start.2) | async-done | bytes 4456480 | tf_op jit(solution)/shard_map/all_to_all | solution.py:373
  234.5 4.4 %combine.1 = (bf16[128,2048]{1,0:T(8,128)(2,1)}, bf16[8,128]{1,0:T(8,128)(2,1)}) custom-call(s32[8,128]{1,0:T(8,128)} %bitcast.20, bf16[8,128]{1,0:T(8,128)(2,1)} %bitcast.23, bf16[32,32,2176]{2,1,0:T(8,128)(2,1)} %all-to-all-done.2.back_ref), custom_call_target="tpu_custom_call" | custom-call | flops 12884901888 | bytes 106954752 | tf_op jit(solution)/shard_map/combine/pallas_call | solution.py:331
  238.9 0.6 collective-permute-done.10.refs_1_
  239.5 0.0 collective-permute-done.11.refs_3_
  239.5 5.6 %update1.1 = (bf16[2,512,768]{2,1,0:T(8,128)(2,1)}, bf16[2,512,768]{2,1,0:T(8,128)(2,1)}, bf16[2,512,768]{2,1,0:T(8,128)(2,1)}) custom-call(s32[1]{0:T(128)} %bitcast.15.where_ref, s32[2,3]{1,0:T(2,128)} %mask_ref.3, bf16[3,256,768]{2,1,0:T(8,128)(2,1)} %own10.1.refs_0_, ...), custom_call_target="tpu_custom_call", output_to_operand_aliasing={{0}: (9, {}), {1}: (10, {}), {2}: (11, {})} | custom-call | flops 47185920 | bytes 283115520 | tf_op jit(solution)/shard_map/update1/pallas_call | solution.py:245
Async XLA Ops:
  5.4 62.0 %all-to-all-start = ((bf16[32,16,4096]{2,1,0:T(8,128)(2,1)}), bf16[32,16,4096]{2,1,0:T(8,128)(2,1)}, u32[]{:S(2)}, u32[]{:S(2)}) async-start(bf16[32,16,4096]{2,1,0:T(8,128)(2,1)} %bitcast.17), calls=%async_computation | async-start | bytes 8388608 | tf_op jit(solution)/shard_map/all_to_all | solution.py:373
  82.6 30.5 %collective-permute-start = (bf16[3,256,768]{2,1,0:T(8,128)(2,1)}, bf16[3,256,768]{2,1,0:T(8,128)(2,1)}, u32[]{:S(2)}, u32[]{:S(2)}) collective-permute-start(bf16[3,256,768]{2,1,0:T(8,128)(2,1)} %get-tuple-element.54.a_ref), channel_id=1, source_target_pairs={{0,32},{32,64},{64,96},{96,0},{1,33},{33,65},{65,97},{97,1},{2,34}... | collective-permute-start | bytes 3538952 | tf_op jit(solution)/shard_map/ppermute | solution.py:364
  84.2 29.2 %collective-permute-start.1 = (bf16[3,256,768]{2,1,0:T(8,128)(2,1)}, bf16[3,256,768]{2,1,0:T(8,128)(2,1)}, u32[]{:S(2)}, u32[]{:S(2)}) collective-permute-start(bf16[3,256,768]{2,1,0:T(8,128)(2,1)} %get-tuple-element.55.b_ref), channel_id=1, source_target_pairs={{0,96},{32,0},{64,32},{96,64},{1,97},{33,1},{65,33},{97,65},{2,98}... | collective-permute-start | bytes 3538952 | tf_op jit(solution)/shard_map/ppermute | solution.py:367
  87.2 58.3 %all-to-all-start.1 = ((bf16[32,16,4096]{2,1,0:T(8,128)(2,1)}), bf16[32,16,4096]{2,1,0:T(8,128)(2,1)}, u32[]{:S(2)}, u32[]{:S(2)}) async-start(bf16[32,16,4096]{2,1,0:T(8,128)(2,1)} %bitcast.16), calls=%async_computation.1 | async-start | bytes 8388608 | tf_op jit(solution)/shard_map/all_to_all | solution.py:373
  99.6 38.8 %collective-permute-start.2 = (bf16[3,256,768]{2,1,0:T(8,128)(2,1)}, bf16[3,256,768]{2,1,0:T(8,128)(2,1)}, u32[]{:S(2)}, u32[]{:S(2)}) collective-permute-start(bf16[3,256,768]{2,1,0:T(8,128)(2,1)} %get-tuple-element.61), channel_id=1, source_target_pairs={{0,32},{32,64},{64,96},{96,0},{1,33},{33,65},{65,97},{97,1},{2,34}... | collective-permute-start | bytes 3538952 | tf_op jit(solution)/shard_map/ppermute | solution.py:364
  99.8 38.8 %collective-permute-start.3 = (bf16[3,256,768]{2,1,0:T(8,128)(2,1)}, bf16[3,256,768]{2,1,0:T(8,128)(2,1)}, u32[]{:S(2)}, u32[]{:S(2)}) collective-permute-start(bf16[3,256,768]{2,1,0:T(8,128)(2,1)} %get-tuple-element.66), channel_id=1, source_target_pairs={{0,96},{32,0},{64,32},{96,64},{1,97},{33,1},{65,33},{97,65},{2,98}... | collective-permute-start | bytes 3538952 | tf_op jit(solution)/shard_map/ppermute | solution.py:367
  117.4 60.4 %collective-permute-start.5 = (bf16[3,256,768]{2,1,0:T(8,128)(2,1)}, bf16[3,256,768]{2,1,0:T(8,128)(2,1)}, u32[]{:S(2)}, u32[]{:S(2)}) collective-permute-start(bf16[3,256,768]{2,1,0:T(8,128)(2,1)} %down0.1), channel_id=1, source_target_pairs={{0,96},{32,0},{64,32},{96,64},{1,97},{33,1},{65,33},{97,65},{2,98}... | collective-permute-start | bytes 3538952 | tf_op jit(solution)/shard_map/ppermute | solution.py:367
  124.4 53.4 %collective-permute-start.4 = (bf16[3,256,768]{2,1,0:T(8,128)(2,1)}, bf16[3,256,768]{2,1,0:T(8,128)(2,1)}, u32[]{:S(2)}, u32[]{:S(2)}) collective-permute-start(bf16[3,256,768]{2,1,0:T(8,128)(2,1)} %up0.1), channel_id=1, source_target_pairs={{0,32},{32,64},{64,96},{96,0},{1,33},{33,65},{65,97},{97,1},{2,34}... | collective-permute-start | bytes 3538952 | tf_op jit(solution)/shard_map/ppermute | solution.py:364
  160.8 27.1 %collective-permute-start.8 = (bf16[3,256,768]{2,1,0:T(8,128)(2,1)}, bf16[3,256,768]{2,1,0:T(8,128)(2,1)}, u32[]{:S(2)}, u32[]{:S(2)}) collective-permute-start(bf16[3,256,768]{2,1,0:T(8,128)(2,1)} %get-tuple-element.72.a_ref), channel_id=1, source_target_pairs={{0,32},{32,64},{64,96},{96,0},{1,33},{33,65},{65,97},{97,1},{2,34}... | collective-permute-start | bytes 3538952 | tf_op jit(solution)/shard_map/ppermute | solution.py:364
  162.4 25.5 %collective-permute-start.9 = (bf16[3,256,768]{2,1,0:T(8,128)(2,1)}, bf16[3,256,768]{2,1,0:T(8,128)(2,1)}, u32[]{:S(2)}, u32[]{:S(2)}) collective-permute-start(bf16[3,256,768]{2,1,0:T(8,128)(2,1)} %get-tuple-element.73.b_ref), channel_id=1, source_target_pairs={{0,96},{32,0},{64,32},{96,64},{1,97},{33,1},{65,33},{97,65},{2,98}... | collective-permute-start | bytes 3538952 | tf_op jit(solution)/shard_map/ppermute | solution.py:367
  172.9 61.6 %all-to-all-start.2 = ((bf16[32,32,2176]{2,1,0:T(8,128)(2,1)}), bf16[32,32,2176]{2,1,0:T(8,128)(2,1)}, u32[]{:S(2)}, u32[]{:S(2)}) async-start(bf16[32,32,2176]{2,1,0:T(8,128)(2,1)} %dx1.1), calls=%async_computation.2 | async-start | bytes 8912896 | tf_op jit(solution)/shard_map/all_to_all | solution.py:373
  184.7 30.3 %collective-permute-start.7 = (bf16[3,256,768]{2,1,0:T(8,128)(2,1)}, bf16[3,256,768]{2,1,0:T(8,128)(2,1)}, u32[]{:S(2)}, u32[]{:S(2)}) collective-permute-start(bf16[3,256,768]{2,1,0:T(8,128)(2,1)} %get-tuple-element.79), channel_id=1, source_target_pairs={{0,32},{32,64},{64,96},{96,0},{1,33},{33,65},{65,97},{97,1},{2,34}... | collective-permute-start | bytes 3538952 | tf_op jit(solution)/shard_map/ppermute | solution.py:364
  184.7 34.4 %collective-permute-start.6 = (bf16[3,256,768]{2,1,0:T(8,128)(2,1)}, bf16[3,256,768]{2,1,0:T(8,128)(2,1)}, u32[]{:S(2)}, u32[]{:S(2)}) collective-permute-start(bf16[3,256,768]{2,1,0:T(8,128)(2,1)} %get-tuple-element.78), channel_id=1, source_target_pairs={{0,96},{32,0},{64,32},{96,64},{1,97},{33,1},{65,33},{97,65},{2,98}... | collective-permute-start | bytes 3538952 | tf_op jit(solution)/shard_map/ppermute | solution.py:367
  196.0 43.4 %collective-permute-start.10 = (bf16[3,256,768]{2,1,0:T(8,128)(2,1)}, bf16[3,256,768]{2,1,0:T(8,128)(2,1)}, u32[]{:S(2)}, u32[]{:S(2)}) collective-permute-start(bf16[3,256,768]{2,1,0:T(8,128)(2,1)} %up1.1), channel_id=1, source_target_pairs={{0,32},{32,64},{64,96},{96,0},{1,33},{33,65},{65,97},{97,1},{2,34}... | collective-permute-start | bytes 3538952 | tf_op jit(solution)/shard_map/ppermute | solution.py:364
  197.7 41.7 %collective-permute-start.11 = (bf16[3,256,768]{2,1,0:T(8,128)(2,1)}, bf16[3,256,768]{2,1,0:T(8,128)(2,1)}, u32[]{:S(2)}, u32[]{:S(2)}) collective-permute-start(bf16[3,256,768]{2,1,0:T(8,128)(2,1)} %down1.1), channel_id=1, source_target_pairs={{0,96},{32,0},{64,32},{96,64},{1,97},{33,1},{65,33},{97,65},{2,98}... | collective-permute-start | bytes 3538952 | tf_op jit(solution)/shard_map/ppermute | solution.py:367

commit v11 on v10

--- a/solution.py
+++ b/solution.py
@@ -229,13 +229,13 @@
                 grad = sum(g[m].astype(F32) for g in grads[2 * second : 2 * second + 2])
                 weight = weights[m][0].astype(F32)
                 rate = mask_ref[chunk, m].astype(F32)
-                outs[m][0] = (weight - step_size * grad - shrink_rate * rate * weight).astype(BF16)
+                outs[m][0] = (weight * (1.0 - shrink_rate * rate) - step_size * grad).astype(BF16)
 
 
 def update(chunk, where, mask, grads, weights, into):
     _, half, hidden = grads[0].shape
     local = weights[0].shape[0]
-    steps = 2
+    steps = 1
     block = half // steps
     early = pl.BlockSpec((3, block, hidden), lambda h, r, w: (0, r * (1 - h) + (steps - 1) * h, 0))
     late = pl.BlockSpec((3, block, hidden), lambda h, r, w: (0, r * h, 0))

time: 246 us -> 245 us (level)
  no operation moved by 1% of the time
where the time goes in v11:
time: 245 us; the launch traced here: 244 us
  Pallas kernels  118 us (48%)
  waiting for transfers between devices  86.8 us (35%)
  starting transfers between devices  37.8 us (15%)
    all_to_all x3, waiting for transfers between devices, swap(): return lax.all_to_all(a, 'expert', split_axis=0, concat_axis=0, tiled=True)  66.5 us
    pallas_call x10, Pallas kernels, weight_grads(): pl.pallas_call(functools.partial(weight_kernel, len(adds), len(after)), g...  46 us
    pallas_call x2, Pallas kernels, hidden_grads(): pl.pallas_call(hidden_kernel, grid_spec=pltpu.PrefetchScalarGridSpec(num_...  30.4 us
    ppermute x6, waiting for transfers between devices, up(): lax.ppermute(a, 'dp', [(i, (i + 1) % n_group) for i in range(n_group)])  19.8 us
    all_to_all x3, starting transfers between devices, swap(): return lax.all_to_all(a, 'expert', split_axis=0, concat_axis=0, tiled=True)  18.3 us
    ppermute x6, starting transfers between devices, down(): lax.ppermute(a, 'dp', [(i, (i - 1) % n_group) for i in range(n_group)])  15.7 us
    pallas_call x2, Pallas kernels, input_grads(): pl.pallas_call(dx_kernel, grid=(5,), in_specs=[whole((n_rows, hidden)), w...  15.1 us
    pallas_call x2, Pallas kernels, update(): pl.pallas_call(functools.partial(update_kernel, chunk), grid_spec=pltpu.P...  9.89 us
  transfers between devices with their start and end apart: 15, of which 9 were waited for; matrix products, arithmetic and copies ran while one was open for 0% of the time, Pallas kernels for 38%

profile of v11, /device:TPU:0, one launch (start us, length us, event | category | flops | bytes accessed | tf_op | source)
XLA Modules:
  0.0 244.5 jit_solution(1704658903193799253)
XLA Ops:
  0.6 4.8 %dispatch0.1 = bf16[512,4096]{1,0:T(8,128)(2,1)} custom-call(s32[8,128]{1,0:T(8,128)} %bitcast.18, bf16[8,128]{1,0:T(8,128)(2,1)} %bitcast.21, bf16[128,2048]{1,0:T(8,128)(2,1)} %tok_ref.3, bf16[128,2048]{1,0:T(8,128)(2,1)} %grad_ref.3), custom_call_target="tpu_custom_call" | custom-call | flops 3758096384 | bytes 36700160 | tf_op jit(solution)/shard_map/dispatch0/pallas_call | solution.py:78
  5.4 8.5 %all-to-all-start = ((bf16[32,16,4096]{2,1,0:T(8,128)(2,1)}), bf16[32,16,4096]{2,1,0:T(8,128)(2,1)}, u32[]{:S(2)}, u32[]{:S(2)}) async-start(bf16[32,16,4096]{2,1,0:T(8,128)(2,1)} %bitcast.17), calls=%async_computation | async-start | bytes 8388608 | tf_op jit(solution)/shard_map/all_to_all | solution.py:373
  14.0 0.6 pad_add_fusion.where_ref
  14.5 4.7 %dispatch1.1 = bf16[512,4096]{1,0:T(8,128)(2,1)} custom-call(s32[8,128]{1,0:T(8,128)} %bitcast.19, bf16[8,128]{1,0:T(8,128)(2,1)} %bitcast.22, bf16[128,2048]{1,0:T(8,128)(2,1)} %tok_ref.3, bf16[128,2048]{1,0:T(8,128)(2,1)} %grad_ref.3), custom_call_target="tpu_custom_call" | custom-call | flops 3758096384 | bytes 36700160 | tf_op jit(solution)/shard_map/dispatch1/pallas_call | solution.py:78
  19.2 48.2 %all-to-all-done = bf16[32,16,4096]{2,1,0:T(8,128)(2,1)} async-done(((bf16[32,16,4096]{2,1,0:T(8,128)(2,1)}), bf16[32,16,4096]{2,1,0:T(8,128)(2,1)}, u32[]{:S(2)}, u32[]{:S(2)}) %all-to-all-start) | async-done | bytes 4194336 | tf_op jit(solution)/shard_map/all_to_all | solution.py:373
  67.4 15.2 %hidden0.1 = (bf16[512,768]{1,0:T(8,128)(2,1)}, bf16[512,768]{1,0:T(8,128)(2,1)}, bf16[512,768]{1,0:T(8,128)(2,1)}, bf16[512,128]{1,0:T(8,128)(2,1)}, bf16[3,256...) custom-call(s32[2]{0:T(128)} %pad_add_fusion.where_ref, ...), custom_call_target="tpu_custom_call" | custom-call | flops 45097156608 | bytes 111935488 | tf_op jit(solution)/shard_map/hidden0/pallas_call | solution.py:138
  82.6 1.5 collective-permute-start
  84.2 1.7 collective-permute-start.1
  85.9 1.3 mark0.1.refs_0_
  87.2 4.9 %all-to-all-start.1 = ((bf16[32,16,4096]{2,1,0:T(8,128)(2,1)}), bf16[32,16,4096]{2,1,0:T(8,128)(2,1)}, u32[]{:S(2)}, u32[]{:S(2)}) async-start(bf16[32,16,4096]{2,1,0:T(8,128)(2,1)} %bitcast.16), calls=%async_computation.1 | async-start | bytes 8388608 | tf_op jit(solution)/shard_map/all_to_all | solution.py:373
  92.1 0.6 pad_add_fusion.1.where_ref
  92.7 6.9 %near0.1 = (bf16[3,256,768]{2,1,0:T(8,128)(2,1)}, bf16[3,256,768]{2,1,0:T(8,128)(2,1)}) custom-call(s32[2]{0:T(128)} %pad_add_fusion.1.where_ref, bf16[512,4096]{1,0:T(8,128)(2,1)} %bitcast.5.x_ref.do_ref.xa_ref.xb_ref.da_col_ref.db_col_ref, bf16[512,4096]{1,0:T(8,128)(2,1)} %bitcast.5.x_ref.do_ref.xa_ref.xb_ref.da_col_ref.db_col_ref, ...), custom_call_target="tpu_custom_call" | custom-call | flops 8455716864 | bytes 33030144 | tf_op jit(solution)/shard_map/near0/pallas_call | solution.py:184
  99.6 0.3 collective-permute-start.2
  99.8 3.0 %collective-permute-start.3 = (bf16[3,256,768]{2,1,0:T(8,128)(2,1)}, bf16[3,256,768]{2,1,0:T(8,128)(2,1)}, u32[]{:S(2)}, u32[]{:S(2)}) collective-permute-start(bf16[3,256,768]{2,1,0:T(8,128)(2,1)} %get-tuple-element.66), channel_id=1, source_target_pairs={{0,96},{32,0},{64,32},{96,64},{1,97},{33,1},{65,33},{97,65},{2,98}... | collective-permute-start | bytes 3538952 | tf_op jit(solution)/shard_map/ppermute | solution.py:367
  102.8 10.3 %collective-permute-done.refs_0_ = bf16[3,256,768]{2,1,0:T(8,128)(2,1)} collective-permute-done((bf16[3,256,768]{2,1,0:T(8,128)(2,1)}, bf16[3,256,768]{2,1,0:T(8,128)(2,1)}, u32[]{:S(2)}, u32[]{:S(2)}) %collective-permute-start) | collective-permute-done | bytes 1179680 | tf_op jit(solution)/shard_map/ppermute | solution.py:364
  113.1 0.3 collective-permute-done.1.refs_0_
  113.4 4.0 %down0.1 = bf16[3,256,768]{2,1,0:T(8,128)(2,1)} custom-call(s32[1]{0:T(128)} %bitcast.11.where_ref, bf16[512,4096]{1,0:T(8,128)(2,1)} %bitcast.5.x_ref.do_ref.xa_ref.xb_ref.da_col_ref.db_col_ref, bf16[512,4096]{1,0:T(8,128)(2,1)} %bitcast.5.x_ref.do_ref.xa_ref.xb_ref.da_col_ref.db_col_ref, bf16[512,768]{1,0:T(8,128)(2,1)} %get-tuple-element.58.hid_ref, ...), custom_call_target="tpu_custom_call" | custom-call | flops 4227858432 | bytes 24772608 | tf_op jit(solution)/shard_map/down0/pallas_call | solution.py:184
  117.4 3.0 %collective-permute-start.5 = (bf16[3,256,768]{2,1,0:T(8,128)(2,1)}, bf16[3,256,768]{2,1,0:T(8,128)(2,1)}, u32[]{:S(2)}, u32[]{:S(2)}) collective-permute-start(bf16[3,256,768]{2,1,0:T(8,128)(2,1)} %down0.1), channel_id=1, source_target_pairs={{0,96},{32,0},{64,32},{96,64},{1,97},{33,1},{65,33},{97,65},{2,98}... | collective-permute-start | bytes 3538952 | tf_op jit(solution)/shard_map/ppermute | solution.py:367
  120.4 4.0 %up0.1 = bf16[3,256,768]{2,1,0:T(8,128)(2,1)} custom-call(s32[1]{0:T(128)} %bitcast.8.where_ref, bf16[512,4096]{1,0:T(8,128)(2,1)} %bitcast.5.x_ref.do_ref.xa_ref.xb_ref.da_col_ref.db_col_ref, bf16[512,4096]{1,0:T(8,128)(2,1)} %bitcast.5.x_ref.do_ref.xa_ref.xb_ref.da_col_ref.db_col_ref, bf16[512,768]{1,0:T(8,128)(2,1)} %get-tuple-element.58.hid_ref, ...), custom_call_target="tpu_custom_call" | custom-call | flops 4227858432 | bytes 24772608 | tf_op jit(solution)/shard_map/up0/pallas_call | solution.py:184
  124.4 0.0 collective-permute-start.4
  124.4 7.6 %dx0.1.refs_0_ = bf16[32,32,2176]{2,1,0:T(8,128)(2,1)} custom-call(bf16[512,768]{1,0:T(8,128)(2,1)} %get-tuple-element.64.da_ref, bf16[512,768]{1,0:T(8,128)(2,1)} %get-tuple-element.59.db_ref, bf16[512,128]{1,0:T(8,128)(2,1)} %get-tuple-element.65.s_ref, bf16[2,2048,768]{2,1,0:T(8,128)(2,1)} %refs_4_.3, bf16[2,2048,768]{2,1,0:T(8,128)(2,1)} %refs_5_.3), custom_call_target="tpu_custom_call" | custom-call | flops 22548578304 | bytes 69730304 | tf_op jit(solution)/shard_map/dx0/pallas_call | solution.py:287
  131.9 6.5 %collective-permute-done.2.refs_0_ = bf16[3,256,768]{2,1,0:T(8,128)(2,1)} collective-permute-done((bf16[3,256,768]{2,1,0:T(8,128)(2,1)}, bf16[3,256,768]{2,1,0:T(8,128)(2,1)}, u32[]{:S(2)}, u32[]{:S(2)}) %collective-permute-start.2) | collective-permute-done | bytes 1179680 | tf_op jit(solution)/shard_map/ppermute | solution.py:364
  138.4 0.3 collective-permute-done.3.refs_0_
  138.7 6.9 %all-to-all-done.1 = bf16[32,16,4096]{2,1,0:T(8,128)(2,1)} async-done(((bf16[32,16,4096]{2,1,0:T(8,128)(2,1)}), bf16[32,16,4096]{2,1,0:T(8,128)(2,1)}, u32[]{:S(2)}, u32[]{:S(2)}) %all-to-all-start.1) | async-done | bytes 4194336 | tf_op jit(solution)/shard_map/all_to_all | solution.py:373
  145.6 15.2 %hidden1.1 = (bf16[512,768]{1,0:T(8,128)(2,1)}, bf16[512,768]{1,0:T(8,128)(2,1)}, bf16[512,768]{1,0:T(8,128)(2,1)}, bf16[512,128]{1,0:T(8,128)(2,1)}, bf16[3,256...) custom-call(s32[2]{0:T(128)} %pad_add_fusion.where_ref, ...), custom_call_target="tpu_custom_call" | custom-call | flops 154618822656 | bytes 383778816 | tf_op jit(solution)/shard_map/hidden1/pallas_call | solution.py:138
  160.8 0.3 collective-permute-start.8
  161.1 1.3 mark1.1.refs_0_
  162.4 3.0 %collective-permute-start.9 = (bf16[3,256,768]{2,1,0:T(8,128)(2,1)}, bf16[3,256,768]{2,1,0:T(8,128)(2,1)}, u32[]{:S(2)}, u32[]{:S(2)}) collective-permute-start(bf16[3,256,768]{2,1,0:T(8,128)(2,1)} %get-tuple-element.73.b_ref), channel_id=1, source_target_pairs={{0,96},{32,0},{64,32},{96,64},{1,97},{33,1},{65,33},{97,65},{2,98}... | collective-permute-start | bytes 3538952 | tf_op jit(solution)/shard_map/ppermute | solution.py:367
  165.4 7.5 %dx1.1 = bf16[32,32,2176]{2,1,0:T(8,128)(2,1)} custom-call(bf16[512,768]{1,0:T(8,128)(2,1)} %get-tuple-element.68.da_ref, bf16[512,768]{1,0:T(8,128)(2,1)} %get-tuple-element.69.db_ref, bf16[512,128]{1,0:T(8,128)(2,1)} %get-tuple-element.70.s_ref, bf16[2,2048,768]{2,1,0:T(8,128)(2,1)} %refs_4_.3, ...), custom_call_target="tpu_custom_call", output_to_operand_aliasing={{}: (5, {})} | custom-call | flops 77309411328 | bytes 239075328 | tf_op jit(solution)/shard_map/dx1/pallas_call | solution.py:287
  172.9 4.8 %all-to-all-start.2 = ((bf16[32,32,2176]{2,1,0:T(8,128)(2,1)}), bf16[32,32,2176]{2,1,0:T(8,128)(2,1)}, u32[]{:S(2)}, u32[]{:S(2)}) async-start(bf16[32,32,2176]{2,1,0:T(8,128)(2,1)} %dx1.1), calls=%async_computation.2 | async-start | bytes 8912896 | tf_op jit(solution)/shard_map/all_to_all | solution.py:373
  177.8 0.0 collective-permute-done.5.refs_3_
  177.8 0.0 collective-permute-done.4.refs_1_
  177.8 6.9 %near1.1 = (bf16[3,256,768]{2,1,0:T(8,128)(2,1)}, bf16[3,256,768]{2,1,0:T(8,128)(2,1)}) custom-call(s32[2]{0:T(128)} %pad_add_fusion.1.where_ref, bf16[512,4096]{1,0:T(8,128)(2,1)} %bitcast.7.x_ref.do_ref.xa_ref.xb_ref.da_col_ref.db_col_ref, bf16[512,4096]{1,0:T(8,128)(2,1)} %bitcast.7.x_ref.do_ref.xa_ref.xb_ref.da_col_ref.db_col_ref, ...), custom_call_target="tpu_custom_call" | custom-call | flops 28991029248 | bytes 113246208 | tf_op jit(solution)/shard_map/near1/pallas_call | solution.py:184
  184.7 0.0 collective-permute-start.7
  184.7 3.2 %collective-permute-start.6 = (bf16[3,256,768]{2,1,0:T(8,128)(2,1)}, bf16[3,256,768]{2,1,0:T(8,128)(2,1)}, u32[]{:S(2)}, u32[]{:S(2)}) collective-permute-start(bf16[3,256,768]{2,1,0:T(8,128)(2,1)} %get-tuple-element.78), channel_id=1, source_target_pairs={{0,96},{32,0},{64,32},{96,64},{1,97},{33,1},{65,33},{97,65},{2,98}... | collective-permute-start | bytes 3538952 | tf_op jit(solution)/shard_map/ppermute | solution.py:367
  187.9 0.0 collective-permute-done.8.refs_0_
  187.9 0.0 collective-permute-done.9.refs_0_
  187.9 4.0 %down1.1 = bf16[3,256,768]{2,1,0:T(8,128)(2,1)} custom-call(s32[1]{0:T(128)} %bitcast.11.where_ref, bf16[512,4096]{1,0:T(8,128)(2,1)} %bitcast.7.x_ref.do_ref.xa_ref.xb_ref.da_col_ref.db_col_ref, bf16[512,4096]{1,0:T(8,128)(2,1)} %bitcast.7.x_ref.do_ref.xa_ref.xb_ref.da_col_ref.db_col_ref, bf16[512,768]{1,0:T(8,128)(2,1)} %get-tuple-element.76.hid_ref, ...), custom_call_target="tpu_custom_call" | custom-call | flops 14495514624 | bytes 84934656 | tf_op jit(solution)/shard_map/down1/pallas_call | solution.py:184
  192.0 4.1 %up1.1 = bf16[3,256,768]{2,1,0:T(8,128)(2,1)} custom-call(s32[1]{0:T(128)} %bitcast.8.where_ref, bf16[512,4096]{1,0:T(8,128)(2,1)} %bitcast.7.x_ref.do_ref.xa_ref.xb_ref.da_col_ref.db_col_ref, bf16[512,4096]{1,0:T(8,128)(2,1)} %bitcast.7.x_ref.do_ref.xa_ref.xb_ref.da_col_ref.db_col_ref, bf16[512,768]{1,0:T(8,128)(2,1)} %get-tuple-element.76.hid_ref, ...), custom_call_target="tpu_custom_call" | custom-call | flops 14495514624 | bytes 84934656 | tf_op jit(solution)/shard_map/up1/pallas_call | solution.py:184
  196.0 1.7 collective-permute-start.10
  197.7 1.9 collective-permute-start.11
  199.6 4.0 %own01.1.refs_2_ = bf16[3,256,768]{2,1,0:T(8,128)(2,1)} custom-call(s32[1]{0:T(128)} %bitcast.13.where_ref, bf16[512,4096]{1,0:T(8,128)(2,1)} %bitcast.5.x_ref.do_ref.xa_ref.xb_ref.da_col_ref.db_col_ref, bf16[512,4096]{1,0:T(8,128)(2,1)} %bitcast.5.x_ref.do_ref.xa_ref.xb_ref.da_col_ref.db_col_ref, bf16[512,768]{1,0:T(8,128)(2,1)} %get-tuple-element.58.hid_ref, ...), custom_call_target="tpu_custom_call" | custom-call | flops 4227858432 | bytes 24772608 | tf_op jit(solution)/shard_map/own01/pallas_call | solution.py:184
  203.7 4.0 %own00.1.refs_0_ = bf16[3,256,768]{2,1,0:T(8,128)(2,1)} custom-call(s32[1]{0:T(128)} %bitcast.12.where_ref, bf16[512,4096]{1,0:T(8,128)(2,1)} %bitcast.5.x_ref.do_ref.xa_ref.xb_ref.da_col_ref.db_col_ref, bf16[512,4096]{1,0:T(8,128)(2,1)} %bitcast.5.x_ref.do_ref.xa_ref.xb_ref.da_col_ref.db_col_ref, bf16[512,768]{1,0:T(8,128)(2,1)} %get-tuple-element.58.hid_ref, ...), custom_call_target="tpu_custom_call" | custom-call | flops 4227858432 | bytes 24772608 | tf_op jit(solution)/shard_map/own00/pallas_call | solution.py:184
  207.7 5.0 %update0.1 = (bf16[2,512,768]{2,1,0:T(8,128)(2,1)}, bf16[2,512,768]{2,1,0:T(8,128)(2,1)}, bf16[2,512,768]{2,1,0:T(8,128)(2,1)}) custom-call(s32[1]{0:T(128)} %bitcast.15.where_ref, s32[2,3]{1,0:T(2,128)} %mask_ref.3, bf16[3,256,768]{2,1,0:T(8,128)(2,1)} %own00.1.refs_0_, bf16[3,256,768]{2,1,0:T(8,128)(2,1)} %collective-permute-done.4.refs_1_, ...), custom_call_target="tpu_custom_call" | custom-call | flops 47185920 | bytes 283115520 | tf_op jit(solution)/shard_map/update0/pallas_call | solution.py:245
  212.6 2.4 collective-permute-done.7.refs_0_
  215.0 4.1 %own11.1.refs_2_ = bf16[3,256,768]{2,1,0:T(8,128)(2,1)} custom-call(s32[1]{0:T(128)} %bitcast.13.where_ref, bf16[512,4096]{1,0:T(8,128)(2,1)} %bitcast.7.x_ref.do_ref.xa_ref.xb_ref.da_col_ref.db_col_ref, bf16[512,4096]{1,0:T(8,128)(2,1)} %bitcast.7.x_ref.do_ref.xa_ref.xb_ref.da_col_ref.db_col_ref, bf16[512,768]{1,0:T(8,128)(2,1)} %get-tuple-element.76.hid_ref, ...), custom_call_target="tpu_custom_call" | custom-call | flops 14495514624 | bytes 84934656 | tf_op jit(solution)/shard_map/own11/pallas_call | solution.py:184
  219.1 0.0 collective-permute-done.6.refs_0_
  219.1 4.0 %own10.1.refs_0_ = bf16[3,256,768]{2,1,0:T(8,128)(2,1)} custom-call(s32[1]{0:T(128)} %bitcast.12.where_ref, bf16[512,4096]{1,0:T(8,128)(2,1)} %bitcast.7.x_ref.do_ref.xa_ref.xb_ref.da_col_ref.db_col_ref, bf16[512,4096]{1,0:T(8,128)(2,1)} %bitcast.7.x_ref.do_ref.xa_ref.xb_ref.da_col_ref.db_col_ref, bf16[512,768]{1,0:T(8,128)(2,1)} %get-tuple-element.76.hid_ref, ...), custom_call_target="tpu_custom_call" | custom-call | flops 14495514624 | bytes 84934656 | tf_op jit(solution)/shard_map/own10/pallas_call | solution.py:184
  223.1 11.4 %all-to-all-done.2.back_ref = bf16[32,32,2176]{2,1,0:T(8,128)(2,1)} async-done(((bf16[32,32,2176]{2,1,0:T(8,128)(2,1)}), bf16[32,32,2176]{2,1,0:T(8,128)(2,1)}, u32[]{:S(2)}, u32[]{:S(2)}) %all-to-all-start.2) | async-done | bytes 4456480 | tf_op jit(solution)/shard_map/all_to_all | solution.py:373
  234.5 4.4 %combine.1 = (bf16[128,2048]{1,0:T(8,128)(2,1)}, bf16[8,128]{1,0:T(8,128)(2,1)}) custom-call(s32[8,128]{1,0:T(8,128)} %bitcast.20, bf16[8,128]{1,0:T(8,128)(2,1)} %bitcast.23, bf16[32,32,2176]{2,1,0:T(8,128)(2,1)} %all-to-all-done.2.back_ref), custom_call_target="tpu_custom_call" | custom-call | flops 12884901888 | bytes 106954752 | tf_op jit(solution)/shard_map/combine/pallas_call | solution.py:331
  238.9 0.6 collective-permute-done.10.refs_1_
  239.5 0.0 collective-permute-done.11.refs_3_
  239.5 4.9 %update1.1 = (bf16[2,512,768]{2,1,0:T(8,128)(2,1)}, bf16[2,512,768]{2,1,0:T(8,128)(2,1)}, bf16[2,512,768]{2,1,0:T(8,128)(2,1)}) custom-call(s32[1]{0:T(128)} %bitcast.15.where_ref, s32[2,3]{1,0:T(2,128)} %mask_ref.3, bf16[3,256,768]{2,1,0:T(8,128)(2,1)} %own10.1.refs_0_, ...), custom_call_target="tpu_custom_call", output_to_operand_aliasing={{0}: (9, {}), {1}: (10, {}), {2}: (11, {})} | custom-call | flops 47185920 | bytes 283115520 | tf_op jit(solution)/shard_map/update1/pallas_call | solution.py:245
Async XLA Ops:
  5.4 62.0 %all-to-all-start = ((bf16[32,16,4096]{2,1,0:T(8,128)(2,1)}), bf16[32,16,4096]{2,1,0:T(8,128)(2,1)}, u32[]{:S(2)}, u32[]{:S(2)}) async-start(bf16[32,16,4096]{2,1,0:T(8,128)(2,1)} %bitcast.17), calls=%async_computation | async-start | bytes 8388608 | tf_op jit(solution)/shard_map/all_to_all | solution.py:373
  82.6 30.5 %collective-permute-start = (bf16[3,256,768]{2,1,0:T(8,128)(2,1)}, bf16[3,256,768]{2,1,0:T(8,128)(2,1)}, u32[]{:S(2)}, u32[]{:S(2)}) collective-permute-start(bf16[3,256,768]{2,1,0:T(8,128)(2,1)} %get-tuple-element.54.a_ref), channel_id=1, source_target_pairs={{0,32},{32,64},{64,96},{96,0},{1,33},{33,65},{65,97},{97,1},{2,34}... | collective-permute-start | bytes 3538952 | tf_op jit(solution)/shard_map/ppermute | solution.py:364
  84.2 29.2 %collective-permute-start.1 = (bf16[3,256,768]{2,1,0:T(8,128)(2,1)}, bf16[3,256,768]{2,1,0:T(8,128)(2,1)}, u32[]{:S(2)}, u32[]{:S(2)}) collective-permute-start(bf16[3,256,768]{2,1,0:T(8,128)(2,1)} %get-tuple-element.55.b_ref), channel_id=1, source_target_pairs={{0,96},{32,0},{64,32},{96,64},{1,97},{33,1},{65,33},{97,65},{2,98}... | collective-permute-start | bytes 3538952 | tf_op jit(solution)/shard_map/ppermute | solution.py:367
  87.2 58.3 %all-to-all-start.1 = ((bf16[32,16,4096]{2,1,0:T(8,128)(2,1)}), bf16[32,16,4096]{2,1,0:T(8,128)(2,1)}, u32[]{:S(2)}, u32[]{:S(2)}) async-start(bf16[32,16,4096]{2,1,0:T(8,128)(2,1)} %bitcast.16), calls=%async_computation.1 | async-start | bytes 8388608 | tf_op jit(solution)/shard_map/all_to_all | solution.py:373
  99.6 38.8 %collective-permute-start.2 = (bf16[3,256,768]{2,1,0:T(8,128)(2,1)}, bf16[3,256,768]{2,1,0:T(8,128)(2,1)}, u32[]{:S(2)}, u32[]{:S(2)}) collective-permute-start(bf16[3,256,768]{2,1,0:T(8,128)(2,1)} %get-tuple-element.61), channel_id=1, source_target_pairs={{0,32},{32,64},{64,96},{96,0},{1,33},{33,65},{65,97},{97,1},{2,34}... | collective-permute-start | bytes 3538952 | tf_op jit(solution)/shard_map/ppermute | solution.py:364
  99.8 38.8 %collective-permute-start.3 = (bf16[3,256,768]{2,1,0:T(8,128)(2,1)}, bf16[3,256,768]{2,1,0:T(8,128)(2,1)}, u32[]{:S(2)}, u32[]{:S(2)}) collective-permute-start(bf16[3,256,768]{2,1,0:T(8,128)(2,1)} %get-tuple-element.66), channel_id=1, source_target_pairs={{0,96},{32,0},{64,32},{96,64},{1,97},{33,1},{65,33},{97,65},{2,98}... | collective-permute-start | bytes 3538952 | tf_op jit(solution)/shard_map/ppermute | solution.py:367
  117.4 60.4 %collective-permute-start.5 = (bf16[3,256,768]{2,1,0:T(8,128)(2,1)}, bf16[3,256,768]{2,1,0:T(8,128)(2,1)}, u32[]{:S(2)}, u32[]{:S(2)}) collective-permute-start(bf16[3,256,768]{2,1,0:T(8,128)(2,1)} %down0.1), channel_id=1, source_target_pairs={{0,96},{32,0},{64,32},{96,64},{1,97},{33,1},{65,33},{97,65},{2,98}... | collective-permute-start | bytes 3538952 | tf_op jit(solution)/shard_map/ppermute | solution.py:367
  124.4 53.4 %collective-permute-start.4 = (bf16[3,256,768]{2,1,0:T(8,128)(2,1)}, bf16[3,256,768]{2,1,0:T(8,128)(2,1)}, u32[]{:S(2)}, u32[]{:S(2)}) collective-permute-start(bf16[3,256,768]{2,1,0:T(8,128)(2,1)} %up0.1), channel_id=1, source_target_pairs={{0,32},{32,64},{64,96},{96,0},{1,33},{33,65},{65,97},{97,1},{2,34}... | collective-permute-start | bytes 3538952 | tf_op jit(solution)/shard_map/ppermute | solution.py:364
  160.8 27.1 %collective-permute-start.8 = (bf16[3,256,768]{2,1,0:T(8,128)(2,1)}, bf16[3,256,768]{2,1,0:T(8,128)(2,1)}, u32[]{:S(2)}, u32[]{:S(2)}) collective-permute-start(bf16[3,256,768]{2,1,0:T(8,128)(2,1)} %get-tuple-element.72.a_ref), channel_id=1, source_target_pairs={{0,32},{32,64},{64,96},{96,0},{1,33},{33,65},{65,97},{97,1},{2,34}... | collective-permute-start | bytes 3538952 | tf_op jit(solution)/shard_map/ppermute | solution.py:364
  162.4 25.5 %collective-permute-start.9 = (bf16[3,256,768]{2,1,0:T(8,128)(2,1)}, bf16[3,256,768]{2,1,0:T(8,128)(2,1)}, u32[]{:S(2)}, u32[]{:S(2)}) collective-permute-start(bf16[3,256,768]{2,1,0:T(8,128)(2,1)} %get-tuple-element.73.b_ref), channel_id=1, source_target_pairs={{0,96},{32,0},{64,32},{96,64},{1,97},{33,1},{65,33},{97,65},{2,98}... | collective-permute-start | bytes 3538952 | tf_op jit(solution)/shard_map/ppermute | solution.py:367
  172.9 61.6 %all-to-all-start.2 = ((bf16[32,32,2176]{2,1,0:T(8,128)(2,1)}), bf16[32,32,2176]{2,1,0:T(8,128)(2,1)}, u32[]{:S(2)}, u32[]{:S(2)}) async-start(bf16[32,32,2176]{2,1,0:T(8,128)(2,1)} %dx1.1), calls=%async_computation.2 | async-start | bytes 8912896 | tf_op jit(solution)/shard_map/all_to_all | solution.py:373
  184.7 30.3 %collective-permute-start.7 = (bf16[3,256,768]{2,1,0:T(8,128)(2,1)}, bf16[3,256,768]{2,1,0:T(8,128)(2,1)}, u32[]{:S(2)}, u32[]{:S(2)}) collective-permute-start(bf16[3,256,768]{2,1,0:T(8,128)(2,1)} %get-tuple-element.79), channel_id=1, source_target_pairs={{0,32},{32,64},{64,96},{96,0},{1,33},{33,65},{65,97},{97,1},{2,34}... | collective-permute-start | bytes 3538952 | tf_op jit(solution)/shard_map/ppermute | solution.py:364
  184.7 34.4 %collective-permute-start.6 = (bf16[3,256,768]{2,1,0:T(8,128)(2,1)}, bf16[3,256,768]{2,1,0:T(8,128)(2,1)}, u32[]{:S(2)}, u32[]{:S(2)}) collective-permute-start(bf16[3,256,768]{2,1,0:T(8,128)(2,1)} %get-tuple-element.78), channel_id=1, source_target_pairs={{0,96},{32,0},{64,32},{96,64},{1,97},{33,1},{65,33},{97,65},{2,98}... | collective-permute-start | bytes 3538952 | tf_op jit(solution)/shard_map/ppermute | solution.py:367
  196.0 43.4 %collective-permute-start.10 = (bf16[3,256,768]{2,1,0:T(8,128)(2,1)}, bf16[3,256,768]{2,1,0:T(8,128)(2,1)}, u32[]{:S(2)}, u32[]{:S(2)}) collective-permute-start(bf16[3,256,768]{2,1,0:T(8,128)(2,1)} %up1.1), channel_id=1, source_target_pairs={{0,32},{32,64},{64,96},{96,0},{1,33},{33,65},{65,97},{97,1},{2,34}... | collective-permute-start | bytes 3538952 | tf_op jit(solution)/shard_map/ppermute | solution.py:364
  197.7 41.7 %collective-permute-start.11 = (bf16[3,256,768]{2,1,0:T(8,128)(2,1)}, bf16[3,256,768]{2,1,0:T(8,128)(2,1)}, u32[]{:S(2)}, u32[]{:S(2)}) collective-permute-start(bf16[3,256,768]{2,1,0:T(8,128)(2,1)} %down1.1), channel_id=1, source_target_pairs={{0,96},{32,0},{64,32},{96,64},{1,97},{33,1},{65,33},{97,65},{2,98}... | collective-permute-start | bytes 3538952 | tf_op jit(solution)/shard_map/ppermute | solution.py:367
